TPU v7x, 32 devices: a whole 2x2x4 slice. The times are simulated.
32 devices in a mesh: section: 2 (over core), dp: 4 (over z), mp: 4 (over y, x).
Axes of the slice: x: 2, y: 2, z: 4, core: 2. Of those that a mesh axis runs over, the one named last changes fastest.
Arguments:
- tokens: bfloat16 [2, 8192, 1024], P(None, ('dp', 'mp')), may hold values from -6 to 6
- layout: int32 [2, 4], P(None, 'dp'), may hold values from 1 to 2, as said below
- cotangent: float32 [2, 8192, 1024], P(None, ('dp', 'mp')), may hold values from -6 to 6
- attn_gain: float32 [2, 1024], P('section'), may hold values from 0.5 to 1.5
- query_weight: bfloat16 [2, 1024, 1024], P('section', None, 'mp'), may hold values from -0.1875 to 0.1875
- key_weight: bfloat16 [2, 1024, 1024], P('section', None, 'mp'), may hold values from -0.1875 to 0.1875
- value_weight: bfloat16 [2, 1024, 1024], P('section', None, 'mp'), may hold values from -0.1875 to 0.1875
- out_weight: bfloat16 [2, 1024, 1024], P('section', 'mp'), may hold values from -1.5 to 1.5
- ffn_gain: float32 [2, 1024], P('section'), may hold values from 0.5 to 1.5
- gate_weight: bfloat16 [2, 1024, 2816], P('section', None, 'mp'), may hold values from -0.1875 to 0.1875
- up_weight: bfloat16 [2, 1024, 2816], P('section', None, 'mp'), may hold values from -0.1875 to 0.1875
- down_weight: bfloat16 [2, 2816, 1024], P('section', 'mp'), may hold values from -0.109375 to 0.109375
Outputs:
- layer_out: bfloat16 [2, 2, 8192, 1024], P('section', None, ('dp', 'mp'))
- input_grads: float32 [2, 2, 8192, 1024], P('section', None, ('dp', 'mp'))
- first_values: bfloat16 [2, 8192, 1024], P(None, 'dp', 'mp')
- value_norms: float32 [2, 16], replicated
- attn_gain_grad: float32 [2, 1024], P('section')
- query_grad: float32 [2, 1024, 1024], P('section', None, 'mp')
- key_grad: float32 [2, 1024, 1024], P('section', None, 'mp')
- value_grad: float32 [2, 1024, 1024], P('section', None, 'mp')
- out_grad: float32 [2, 1024, 1024], P('section', 'mp')
- ffn_gain_grad: float32 [2, 1024], P('section')
- gate_grad: float32 [2, 1024, 2816], P('section', None, 'mp')
- up_grad: float32 [2, 1024, 2816], P('section', None, 'mp')
- down_grad: float32 [2, 2816, 1024], P('section', 'mp')
Inputs may be any that keep to these rules, and one draw needn't show every extreme that they name: layout[m, d] is 1 or 2; for each data index d, 1 of the micro-batches hold 1.
All inputs are finite; a program needn't handle non-finite values.
Results may differ from a plain program's by a relative error of at most 0.028.
Values may be sent and summed in bfloat16 or wider, within the bound.
No kernel may reach another device: no remote copies, remote signals or barrier semaphores. Data moves between devices by JAX's collectives and lax.ppermute only.
A program may use at most 384 MiB of HBM per device.

v0:
```python
import jax
import jax.numpy as jnp
from jax import lax
from jax.sharding import PartitionSpec as P

HEAD_DIM = 64


def passed_along(value, axis, steps):
    count = lax.axis_size(axis)
    leading, last = (max(0, -steps), min(count, count - steps))
    return lax.ppermute(value, axis, [(source, source + steps) for source in range(leading, last)])


def normalize(rows_in, gain):
    return rows_in * lax.rsqrt(jnp.mean(rows_in * rows_in, axis=-1, keepdims=True) + 1e-05) * gain


def rotary(seq_rows, seg_len):
    positions = (jnp.arange(seq_rows, dtype=jnp.int32) % seg_len).astype(jnp.float32)
    inverse_freq = 10000.0 ** (-(jnp.arange(HEAD_DIM // 2, dtype=jnp.float32) * 2.0 / HEAD_DIM))
    angles = positions[:, None] * inverse_freq[None, :]
    return (jnp.cos(angles)[:, None, :], jnp.sin(angles)[:, None, :])


def rotate(tensor, cosine, sine_part):
    half_dim = tensor.shape[-1] // 2
    first_half = tensor[..., :half_dim]
    second_half = tensor[..., half_dim:]
    return jnp.concatenate(
        [
            first_half * cosine - second_half * sine_part,
            first_half * sine_part + second_half * cosine,
        ],
        axis=-1,
    )


def allowed_mask(seq_rows, seg_len, row_start, block_rows):
    query_index = row_start + jnp.arange(block_rows, dtype=jnp.int32)
    key_index = jnp.arange(seq_rows, dtype=jnp.int32)
    causal = key_index[None, :] <= query_index[:, None]
    same_seq = query_index[:, None] // seg_len == key_index[None, :] // seg_len
    return causal & same_seq


def block_scores(rows_q, keys_rot, seg_len, row_start):
    seq_rows = keys_rot.shape[0]
    block_rows = rows_q.shape[0]
    score_scale = keys_rot.shape[2] ** (-0.5)
    scores = (
        jnp.einsum("qhd,khd->hqk", rows_q, keys_rot, preferred_element_type=jnp.float32)
        * score_scale
    )
    return jnp.where(allowed_mask(seq_rows, seg_len, row_start, block_rows)[None], scores, -1e30)


def attend(queries, keys_rot, values_mix, seg_len):
    seq_rows, head_count, head_size = queries.shape
    block_rows = min(512, seq_rows)
    block_starts = jnp.arange(seq_rows // block_rows, dtype=jnp.int32) * block_rows

    def one_block(row_start):
        rows_q = lax.dynamic_slice_in_dim(queries, row_start, block_rows, 0)
        scores = block_scores(rows_q, keys_rot, seg_len, row_start)
        row_top = jnp.max(scores, axis=-1, keepdims=True)
        row_total = jnp.sum(jnp.exp(scores - row_top), axis=-1, keepdims=True)
        log_total = row_top + jnp.log(row_total)
        probabilities = jnp.exp(scores - log_total).astype(jnp.bfloat16)
        block_out = jnp.einsum(
            "hqk,khd->qhd", probabilities, values_mix, preferred_element_type=jnp.float32
        )
        return (block_out.astype(jnp.bfloat16), log_total[..., 0])

    blocks_out, log_totals = lax.map(one_block, block_starts)
    return (blocks_out.reshape(seq_rows, head_count * head_size), log_totals)


def attend_back(queries, keys_rot, values_mix, log_totals, grad_attended, seg_len):
    seq_rows, head_count, head_size = queries.shape
    block_rows = log_totals.shape[2]
    score_scale = head_size ** (-0.5)
    block_starts = jnp.arange(seq_rows // block_rows, dtype=jnp.int32) * block_rows

    def one_block(fold_state, items):
        grad_keys, grad_values = fold_state
        row_start, log_total = items
        rows_q = lax.dynamic_slice_in_dim(queries, row_start, block_rows, 0)
        rows_grad = lax.dynamic_slice_in_dim(grad_attended, row_start, block_rows, 0)
        scores = block_scores(rows_q, keys_rot, seg_len, row_start)
        probabilities = jnp.exp(scores - log_total[..., None])
        grad_values = grad_values + jnp.einsum(
            "hqk,qhd->khd",
            probabilities.astype(jnp.bfloat16),
            rows_grad,
            preferred_element_type=jnp.float32,
        )
        grad_probs = jnp.einsum(
            "qhd,khd->hqk", rows_grad, values_mix, preferred_element_type=jnp.float32
        )
        inner_sum = jnp.sum(probabilities * grad_probs, axis=-1, keepdims=True)
        grad_scores = (probabilities * (grad_probs - inner_sum)).astype(jnp.bfloat16)
        grad_rows_q = (
            jnp.einsum("hqk,khd->qhd", grad_scores, keys_rot, preferred_element_type=jnp.float32)
            * score_scale
        )
        grad_keys = (
            grad_keys
            + jnp.einsum("hqk,qhd->khd", grad_scores, rows_q, preferred_element_type=jnp.float32)
            * score_scale
        )
        return ((grad_keys, grad_values), grad_rows_q)

    zero_rows = jnp.zeros(queries.shape, jnp.float32)
    (grad_keys, grad_values), grad_queries = lax.scan(
        one_block, (zero_rows, zero_rows), (block_starts, log_totals)
    )
    return (grad_queries.reshape(seq_rows, head_count, head_size), grad_keys, grad_values)


def project_rows(normed, weight):
    gathered = lax.all_gather(normed, "mp", axis=0, tiled=True)
    return (jnp.dot(gathered, weight, preferred_element_type=jnp.float32), gathered)


def weight_grad(source, gradients):
    return lax.dot_general(
        source, gradients, (((0,), (0,)), ((), ())), preferred_element_type=jnp.float32
    )


def sum_branch(left_rows, weight, tok_rows):

    def term_rows(row_start, row_count):
        return jnp.dot(left_rows, weight, preferred_element_type=jnp.float32)

    return lax.psum_scatter(
        term_rows(jnp.int32(0), lax.axis_size("mp") * tok_rows).astype(jnp.bfloat16),
        "mp",
        scatter_dimension=0,
        tiled=True,
    ).astype(jnp.float32)


def sum_input(gradients, weight, tok_rows):

    def term_rows(row_start, row_count):
        return lax.dot_general(
            gradients, weight, (((1,), (1,)), ((), ())), preferred_element_type=jnp.float32
        )

    return lax.psum_scatter(
        term_rows(jnp.int32(0), lax.axis_size("mp") * tok_rows).astype(jnp.bfloat16),
        "mp",
        scatter_dimension=0,
        tiled=True,
    ).astype(jnp.float32)


def fold_branch(grad_rows, left_rows, weight):
    shard_rows = lax.all_gather(grad_rows, "mp", axis=0, tiled=True)
    part_back = lax.dot_general(
        shard_rows, weight, (((1,), (1,)), ((), ())), preferred_element_type=jnp.float32
    )
    weight_total = lax.dot_general(
        left_rows, shard_rows, (((0,), (0,)), ((), ())), preferred_element_type=jnp.float32
    )
    return (part_back, weight_total)


def layer_forward(inputs, first_in, mix_share, seg_len, weights):
    attn_gain, qkv_weight, out_weight, ffn_gain, inner_weight, down_weight, whole_weights = weights
    tok_rows = inputs.shape[0]
    state_rows = inputs.astype(jnp.float32)
    normed = normalize(state_rows, attn_gain).astype(jnp.bfloat16)
    projected, source_attn = project_rows(normed, qkv_weight)
    head_width = out_weight.shape[0]
    seq_rows = projected.shape[0]
    head_shape = (seq_rows, head_width // HEAD_DIM, HEAD_DIM)
    cosine, sine_part = rotary(seq_rows, seg_len)
    queries = rotate(projected[:, :head_width].reshape(head_shape), cosine, sine_part).astype(
        jnp.bfloat16
    )
    keys_rot = rotate(
        projected[:, head_width : 2 * head_width].reshape(head_shape), cosine, sine_part
    ).astype(jnp.bfloat16)
    values_mix = (
        (1.0 - mix_share) * projected[:, 2 * head_width :]
        + mix_share * first_in.astype(jnp.float32)
    ).astype(jnp.bfloat16)
    attended, log_totals = attend(queries, keys_rot, values_mix.reshape(head_shape), seg_len)
    middle = state_rows + sum_branch(attended, out_weight, tok_rows)
    normed_ffn = normalize(middle, ffn_gain).astype(jnp.bfloat16)
    inner_proj, source_ffn = project_rows(normed_ffn, inner_weight)
    hidden = down_weight.shape[0]
    gate_proj = inner_proj[:, :hidden]
    up_proj = inner_proj[:, hidden:]
    activated = (jax.nn.silu(gate_proj) * up_proj).astype(jnp.bfloat16)
    result = middle + sum_branch(activated, down_weight, tok_rows)
    kept_items = (
        inputs,
        source_attn,
        queries,
        keys_rot,
        values_mix,
        log_totals,
        attended,
        middle,
        source_ffn,
        gate_proj,
        up_proj,
        activated,
    )
    return (result, values_mix, kept_items)


def layer_backward(grad_result, grad_first_in, mix_share, seg_len, weights, kept_items):
    attn_gain, qkv_weight, out_weight, ffn_gain, inner_weight, down_weight, whole_weights = weights
    (
        inputs,
        source_attn,
        queries,
        keys_rot,
        values_mix,
        log_totals,
        attended,
        middle,
        source_ffn,
        gate_proj,
        up_proj,
        activated,
    ) = kept_items
    tok_rows = inputs.shape[0]
    seq_rows, head_count, head_size = queries.shape
    head_width = head_count * head_size
    grad_act, grad_down = fold_branch(grad_result.astype(jnp.bfloat16), activated, down_weight)
    unused, silu_back = jax.vjp(
        lambda gate_in, up_in: jax.nn.silu(gate_in) * up_in, gate_proj, up_proj
    )
    grad_gate, grad_up = silu_back(grad_act)
    grad_inner = jnp.concatenate([grad_gate, grad_up], 1).astype(jnp.bfloat16)
    grad_inner_weight = weight_grad(source_ffn, grad_inner)
    grad_normed_ffn = sum_input(grad_inner, inner_weight, tok_rows)
    unused, norm_back = jax.vjp(normalize, middle, ffn_gain)
    grad_middle_norm, grad_ffn_gain = norm_back(grad_normed_ffn)
    grad_middle = grad_result + grad_middle_norm
    grad_att, grad_out = fold_branch(grad_middle.astype(jnp.bfloat16), attended, out_weight)
    grad_att = grad_att.astype(jnp.bfloat16).reshape(seq_rows, head_count, head_size)
    grad_queries, grad_keys, grad_values = attend_back(
        queries,
        keys_rot,
        values_mix.reshape(seq_rows, head_count, head_size),
        log_totals,
        grad_att,
        seg_len,
    )
    cosine, sine_part = rotary(seq_rows, seg_len)
    unused, rot_back = jax.vjp(lambda tensor: rotate(tensor, cosine, sine_part), grad_queries)
    (grad_query_raw,) = rot_back(grad_queries)
    (grad_key_raw,) = rot_back(grad_keys)
    grad_value_mix = grad_values.reshape(seq_rows, head_width)
    grad_first_out = (mix_share * grad_value_mix).astype(jnp.bfloat16)
    grad_value_raw = (1.0 - mix_share) * grad_value_mix + grad_first_in.astype(jnp.float32)
    grad_qkv = jnp.concatenate(
        [
            grad_query_raw.reshape(seq_rows, head_width),
            grad_key_raw.reshape(seq_rows, head_width),
            grad_value_raw,
        ],
        1,
    ).astype(jnp.bfloat16)
    grad_qkv_weight = weight_grad(source_attn, grad_qkv)
    grad_normed = sum_input(grad_qkv, qkv_weight, tok_rows)
    unused, norm_back_attn = jax.vjp(normalize, inputs.astype(jnp.float32), attn_gain)
    grad_inputs_norm, grad_attn_gain = norm_back_attn(grad_normed)
    grad_inputs = grad_middle + grad_inputs_norm
    return (
        grad_inputs,
        grad_first_out,
        (grad_attn_gain, grad_qkv_weight, grad_out, grad_ffn_gain, grad_inner_weight, grad_down),
    )


def shards(
    tokens,
    layout,
    cotangent,
    attn_gain,
    query_weight,
    key_weight,
    value_weight,
    out_weight,
    ffn_gain,
    gate_weight,
    up_weight,
    down_weight,
):
    section_index = lax.axis_index("section")
    mix_share = section_index.astype(jnp.float32) * 0.5
    micro_count, tok_rows, model_width = tokens.shape
    seq_rows = tok_rows * lax.axis_size("mp")
    head_width = query_weight.shape[2]
    hidden = gate_weight.shape[2]
    own_layout = layout[:, 0]
    qkv_weight = jnp.concatenate([query_weight[0], key_weight[0], value_weight[0]], 1)
    inner_weight = jnp.concatenate([gate_weight[0], up_weight[0]], 1)
    whole_weights = (None, None, None, None)
    weights = (
        attn_gain[0],
        qkv_weight,
        out_weight[0],
        ffn_gain[0],
        inner_weight,
        down_weight[0],
        whole_weights,
    )

    def forward_tick(fold_state, tick_index):
        recv_rows, recv_first = fold_state
        micro_index = jnp.clip(tick_index - section_index, 0, micro_count - 1)
        own_rows = lax.dynamic_index_in_dim(tokens, micro_index, 0, keepdims=False)
        inputs = jnp.where(section_index == 0, own_rows, recv_rows)
        seg_len = seq_rows // lax.dynamic_index_in_dim(own_layout, micro_index, 0, keepdims=False)
        result, values_mix, kept_items = layer_forward(
            inputs, recv_first, mix_share, seg_len, weights
        )
        result = result.astype(jnp.bfloat16)
        sent_rows = passed_along(result, "section", 1)
        sent_first = passed_along(values_mix, "section", 1)
        first_seen = jnp.where(section_index == 0, values_mix, recv_first)
        return ((sent_rows, sent_first), (result, first_seen, kept_items))

    start_state = (
        jnp.zeros((tok_rows, model_width), jnp.bfloat16),
        jnp.zeros((seq_rows, head_width), jnp.bfloat16),
    )
    unused, (results, firsts, kept_all) = lax.scan(
        forward_tick, start_state, jnp.arange(micro_count + 1, dtype=jnp.int32)
    )
    layer_out = lax.dynamic_slice_in_dim(results, section_index, micro_count, 0)
    first_values = lax.dynamic_slice_in_dim(firsts, section_index, micro_count, 0)
    section_lag = 1 - section_index
    zero_totals = (
        jnp.zeros((model_width,), jnp.float32),
        jnp.zeros(qkv_weight.shape, jnp.float32),
        jnp.zeros(out_weight.shape[1:], jnp.float32),
        jnp.zeros((model_width,), jnp.float32),
        jnp.zeros(inner_weight.shape, jnp.float32),
        jnp.zeros(down_weight.shape[1:], jnp.float32),
    )

    def backward_tick(fold_state, tick_index):
        recv_grad, recv_first, totals = fold_state
        back_step = tick_index - section_lag
        micro_index = jnp.clip(micro_count - 1 - back_step, 0, micro_count - 1)
        is_valid = (back_step >= 0) & (back_step < micro_count)
        own_grad = lax.dynamic_index_in_dim(cotangent, micro_index, 0, keepdims=False)
        grad_result = jnp.where(section_index == 1, own_grad, recv_grad.astype(jnp.float32))
        seg_len = seq_rows // lax.dynamic_index_in_dim(own_layout, micro_index, 0, keepdims=False)
        kept_items = jax.tree.map(
            lambda stacked: lax.dynamic_index_in_dim(
                stacked, micro_index + section_index, 0, keepdims=False
            ),
            kept_all,
        )
        grad_inputs, grad_first, gradients = layer_backward(
            grad_result, recv_first, mix_share, seg_len, weights, kept_items
        )
        totals = jax.tree.map(
            lambda running, addend: running + jnp.where(is_valid, addend, 0.0), totals, gradients
        )
        sent_grad = passed_along(grad_inputs.astype(jnp.bfloat16), "section", -1)
        sent_first = passed_along(grad_first, "section", -1)
        return ((sent_grad, sent_first, totals), grad_inputs)

    back_start = (
        jnp.zeros((tok_rows, model_width), jnp.bfloat16),
        jnp.zeros((seq_rows, head_width), jnp.bfloat16),
        zero_totals,
    )
    (unused_grad, unused_first, totals), grad_ticks = lax.scan(
        backward_tick, back_start, jnp.arange(micro_count + 1, dtype=jnp.int32)
    )
    input_grads = jnp.flip(lax.dynamic_slice_in_dim(grad_ticks, section_lag, micro_count, 0), 0)
    attn_gain_grad, qkv_grad, out_grad, ffn_gain_grad, inner_grad, down_grad = totals
    qkv_grad, out_grad, inner_grad, down_grad = (
        lax.psum(qkv_grad.astype(jnp.bfloat16), "dp").astype(jnp.float32),
        lax.psum(out_grad.astype(jnp.bfloat16), "dp").astype(jnp.float32),
        lax.psum(inner_grad.astype(jnp.bfloat16), "dp").astype(jnp.float32),
        lax.psum(down_grad.astype(jnp.bfloat16), "dp").astype(jnp.float32),
    )
    heads_here = head_width // HEAD_DIM
    first_f32 = first_values.astype(jnp.float32).reshape(
        micro_count, seq_rows, heads_here, HEAD_DIM
    )
    squares = jnp.sum(first_f32 * first_f32, axis=(1, 3))
    placed = lax.dynamic_update_slice_in_dim(
        jnp.zeros((micro_count, heads_here * lax.axis_size("mp")), jnp.float32),
        squares,
        lax.axis_index("mp") * heads_here,
        1,
    )
    attn_gain_grad, ffn_gain_grad, value_norms = lax.psum(
        (attn_gain_grad, ffn_gain_grad, placed), ("dp", "mp")
    )
    return (
        layer_out[None],
        input_grads[None],
        first_values,
        value_norms,
        attn_gain_grad[None],
        qkv_grad[:, :head_width][None],
        qkv_grad[:, head_width : 2 * head_width][None],
        qkv_grad[:, 2 * head_width :][None],
        out_grad[None],
        ffn_gain_grad[None],
        inner_grad[:, :hidden][None],
        inner_grad[:, hidden:][None],
        down_grad[None],
    )


def solution(mesh):
    in_specs = (
        P(None, ("dp", "mp"), None),
        P(None, "dp"),
        P(None, ("dp", "mp"), None),
        P("section", None),
        P("section", None, "mp"),
        P("section", None, "mp"),
        P("section", None, "mp"),
        P("section", "mp", None),
        P("section", None),
        P("section", None, "mp"),
        P("section", None, "mp"),
        P("section", "mp", None),
    )
    out_specs = (
        P("section", None, ("dp", "mp"), None),
        P("section", None, ("dp", "mp"), None),
        P(None, "dp", "mp"),
        P(),
        P("section", None),
        P("section", None, "mp"),
        P("section", None, "mp"),
        P("section", None, "mp"),
        P("section", "mp", None),
        P("section", None),
        P("section", None, "mp"),
        P("section", None, "mp"),
        P("section", "mp", None),
    )
    return jax.shard_map(shards, mesh=mesh, in_specs=in_specs, out_specs=out_specs, check_vma=False)
```

profile of v0, /device:TPU:0, one launch (start us, length us, event | category | flops | bytes accessed | tf_op | source)
XLA Modules:
  0.0 3103.9 jit_solution(13223611022042671916)
XLA Ops:
  19.1 1059.4 %while.136 = (s32[]{:T(128)}, bf16[512,1024]{1,0:T(8,128)(2,1)S(1)}, bf16[2048,256]{0,1:T(8,128)(2,1)S(1)}, bf16[3,512,1024]{2,1,0:T(8,128)(2,1)}, bf16[3,2048,2...) while((s32[]{:T(128)}, bf16[512,1024]{1,0:T(8,128)(2,1)S(1)}, ...), condition=%wide.region_9.10_spmd, body=%wide.region_0.9_spmd.sunk | while | flops 14319849472 | bytes 413224832 | solution.py:337
  29.6 51.1 %all-gather.5.cloned.1.call-done = bf16[2048,1024]{1,0:T(8,128)(2,1)} async-done(((bf16[512,1024]{1,0:T(8,128)(2,1)}), bf16[2048,1024]{1,0:T(8,128)(2,1)}) %all-gather.5.cloned.1.call-update) | async-done | bytes 4194320 | tf_op jit(solution)/shard_map/while/body/eval_jaxpr/all_gather | solution.py:122
  90.6 75.8 %while.139 = (s32[]{:T(128)}, bf16[4,512,4,64]{1,3,2,0:T(8,128)(2,1)}, f32[4,4,512]{2,1,0:T(4,128)S(1)}, s32[4]{0:T(128)S(1)}, s32[]{:T(128)}, /*index=5*/s32[]{...) while((s32[]{:T(128)}, ...), condition=%wide.region_5.5_spmd, body=%wide.region_2.4_spmd.sunk | while | flops 1123174912 | bytes 61432540 | solution.py:75
  173.1 52.8 %reduce-scatter.5.cloned.1.call-done = bf16[512,1024]{1,0:T(8,128)(2,1)} async-done(((bf16[2048,1024]{1,0:T(8,128)(2,1)}), bf16[512,1024]{1,0:T(8,128)(2,1)}) %reduce-scatter.5.cloned.1.call-update) | async-done | bytes 1048592 | tf_op jit(solution)/shard_map/while/body/eval_jaxpr/reduce_scatter | solution.py:137
  230.3 52.8 %all-gather.7.cloned.1.call-done = bf16[2048,1024]{1,0:T(8,128)(2,1)} async-done(((bf16[512,1024]{1,0:T(8,128)(2,1)}), bf16[2048,1024]{1,0:T(8,128)(2,1)}) %all-gather.7.cloned.1.call-update) | async-done | bytes 4194320 | tf_op jit(solution)/shard_map/while/body/eval_jaxpr/all_gather | solution.py:122
  325.0 31.4 %reduce-scatter.7.cloned.1.call-done = bf16[512,1024]{1,0:T(8,128)(2,1)} async-done(((bf16[2048,1024]{1,0:T(8,128)(2,1)}), bf16[512,1024]{1,0:T(8,128)(2,1)}) %reduce-scatter.7.cloned.1.call-update) | async-done | bytes 1048592 | tf_op jit(solution)/shard_map/while/body/eval_jaxpr/reduce_scatter | solution.py:137
  384.4 48.4 %all-gather.5.cloned.1.call-done = bf16[2048,1024]{1,0:T(8,128)(2,1)} async-done(((bf16[512,1024]{1,0:T(8,128)(2,1)}), bf16[2048,1024]{1,0:T(8,128)(2,1)}) %all-gather.5.cloned.1.call-update) | async-done | bytes 4194320 | tf_op jit(solution)/shard_map/while/body/eval_jaxpr/all_gather | solution.py:122
  442.8 75.8 %while.139 = (s32[]{:T(128)}, bf16[4,512,4,64]{1,3,2,0:T(8,128)(2,1)}, f32[4,4,512]{2,1,0:T(4,128)S(1)}, s32[4]{0:T(128)S(1)}, s32[]{:T(128)}, /*index=5*/s32[]{...) while((s32[]{:T(128)}, ...), condition=%wide.region_5.5_spmd, body=%wide.region_2.4_spmd.sunk | while | flops 1123174912 | bytes 61432540 | solution.py:75
  525.3 52.8 %reduce-scatter.5.cloned.1.call-done = bf16[512,1024]{1,0:T(8,128)(2,1)} async-done(((bf16[2048,1024]{1,0:T(8,128)(2,1)}), bf16[512,1024]{1,0:T(8,128)(2,1)}) %reduce-scatter.5.cloned.1.call-update) | async-done | bytes 1048592 | tf_op jit(solution)/shard_map/while/body/eval_jaxpr/reduce_scatter | solution.py:137
  582.4 52.8 %all-gather.7.cloned.1.call-done = bf16[2048,1024]{1,0:T(8,128)(2,1)} async-done(((bf16[512,1024]{1,0:T(8,128)(2,1)}), bf16[2048,1024]{1,0:T(8,128)(2,1)}) %all-gather.7.cloned.1.call-update) | async-done | bytes 4194320 | tf_op jit(solution)/shard_map/while/body/eval_jaxpr/all_gather | solution.py:122
  677.1 31.4 %reduce-scatter.7.cloned.1.call-done = bf16[512,1024]{1,0:T(8,128)(2,1)} async-done(((bf16[2048,1024]{1,0:T(8,128)(2,1)}), bf16[512,1024]{1,0:T(8,128)(2,1)}) %reduce-scatter.7.cloned.1.call-update) | async-done | bytes 1048592 | tf_op jit(solution)/shard_map/while/body/eval_jaxpr/reduce_scatter | solution.py:137
  736.6 48.4 %all-gather.5.cloned.1.call-done = bf16[2048,1024]{1,0:T(8,128)(2,1)} async-done(((bf16[512,1024]{1,0:T(8,128)(2,1)}), bf16[2048,1024]{1,0:T(8,128)(2,1)}) %all-gather.5.cloned.1.call-update) | async-done | bytes 4194320 | tf_op jit(solution)/shard_map/while/body/eval_jaxpr/all_gather | solution.py:122
  794.9 75.8 %while.139 = (s32[]{:T(128)}, bf16[4,512,4,64]{1,3,2,0:T(8,128)(2,1)}, f32[4,4,512]{2,1,0:T(4,128)S(1)}, s32[4]{0:T(128)S(1)}, s32[]{:T(128)}, /*index=5*/s32[]{...) while((s32[]{:T(128)}, ...), condition=%wide.region_5.5_spmd, body=%wide.region_2.4_spmd.sunk | while | flops 1123174912 | bytes 61432540 | solution.py:75
  877.4 52.8 %reduce-scatter.5.cloned.1.call-done = bf16[512,1024]{1,0:T(8,128)(2,1)} async-done(((bf16[2048,1024]{1,0:T(8,128)(2,1)}), bf16[512,1024]{1,0:T(8,128)(2,1)}) %reduce-scatter.5.cloned.1.call-update) | async-done | bytes 1048592 | tf_op jit(solution)/shard_map/while/body/eval_jaxpr/reduce_scatter | solution.py:137
  934.5 52.8 %all-gather.7.cloned.1.call-done = bf16[2048,1024]{1,0:T(8,128)(2,1)} async-done(((bf16[512,1024]{1,0:T(8,128)(2,1)}), bf16[2048,1024]{1,0:T(8,128)(2,1)}) %all-gather.7.cloned.1.call-update) | async-done | bytes 4194320 | tf_op jit(solution)/shard_map/while/body/eval_jaxpr/all_gather | solution.py:122
  1029.3 31.3 %reduce-scatter.7.cloned.1.call-done = bf16[512,1024]{1,0:T(8,128)(2,1)} async-done(((bf16[2048,1024]{1,0:T(8,128)(2,1)}), bf16[512,1024]{1,0:T(8,128)(2,1)}) %reduce-scatter.7.cloned.1.call-update) | async-done | bytes 1048592 | tf_op jit(solution)/shard_map/while/body/eval_jaxpr/reduce_scatter | solution.py:137
  1084.7 1758.7 %while.138 = (s32[]{:T(128)}, bf16[512,1024]{1,0:T(8,128)(2,1)}, bf16[2048,256]{0,1:T(8,128)(2,1)}, f32[1024]{0:T(1024)}, f32[1024,768]{1,0:T(8,128)}, /*index=5...) while((s32[]{:T(128)}, bf16[512,1024]{1,0:T(8,128)(2,1)}, ...), condition=%wide.region_22.23_spmd.clone, body=%wide.region_10.22_spmd.clone.sunk | while | flops 29171040256 | bytes 634653184 | solution.py:381
  1098.5 52.8 %all-gather.9.cloned.1.call-done = bf16[2048,1024]{1,0:T(8,128)(2,1)} async-done(((bf16[512,1024]{1,0:T(8,128)(2,1)}), bf16[2048,1024]{1,0:T(8,128)(2,1)}) %all-gather.9.cloned.1.call-update) | async-done | bytes 4194320 | tf_op jit(solution)/shard_map/while/body/eval_jaxpr/all_gather | solution.py:161
  1176.7 51.0 %reduce-scatter.9.cloned.1.call-done = bf16[512,1024]{1,0:T(8,128)(2,1)} async-done(((bf16[2048,1024]{1,0:T(8,128)(2,1)}), bf16[512,1024]{1,0:T(8,128)(2,1)}) %reduce-scatter.9.cloned.1.call-update) | async-done | bytes 1048592 | tf_op jit(solution)/shard_map/while/body/eval_jaxpr/reduce_scatter | solution.py:152
  1246.2 42.6 %all-gather.11.cloned.1.call-done = bf16[2048,1024]{1,0:T(8,128)(2,1)} async-done(((bf16[512,1024]{1,0:T(8,128)(2,1)}), bf16[2048,1024]{1,0:T(8,128)(2,1)}) %all-gather.11.cloned.1.call-update) | async-done | bytes 4194320 | tf_op jit(solution)/shard_map/while/body/eval_jaxpr/all_gather | solution.py:161
  1293.3 289.5 %while.140 = (s32[]{:T(128)}, f32[2048,4,64]{0,2,1:T(8,128)}, f32[2048,4,64]{0,2,1:T(8,128)}, f32[4,512,4,64]{1,0,3,2:T(4,128)}, s32[4]{0:T(128)S(1)}, /*index=5...) while((s32[]{:T(128)}, f32[2048,4,64]{0,2,1:T(8,128)}, ...), condition=%wide.region_16.16_spmd.clone, body=%wide.region_14.15_spmd.clone.sunk | while | flops 2753186304 | bytes 187253072 | solution.py:115
  1307.3 12.5 multiply_reduce_fusion.6
  1319.7 12.1 multiply_convert_fusion.10
  1378.6 12.5 multiply_reduce_fusion.6
  1391.1 12.1 multiply_convert_fusion.10
  1425.2 12.5 fusion.242
  1451.2 12.5 multiply_reduce_fusion.6
  1463.7 12.1 multiply_convert_fusion.10
  1497.8 12.5 fusion.242
  1523.7 12.5 multiply_reduce_fusion.6
  1570.3 12.4 fusion.242
  1622.8 29.7 reduce-scatter.11.cloned.1.call-done
  1679.0 54.6 %all-gather.9.cloned.1.call-done = bf16[2048,1024]{1,0:T(8,128)(2,1)} async-done(((bf16[512,1024]{1,0:T(8,128)(2,1)}), bf16[2048,1024]{1,0:T(8,128)(2,1)}) %all-gather.9.cloned.1.call-update) | async-done | bytes 4194320 | tf_op jit(solution)/shard_map/while/body/eval_jaxpr/all_gather | solution.py:161
  1759.0 51.0 %reduce-scatter.9.cloned.1.call-done = bf16[512,1024]{1,0:T(8,128)(2,1)} async-done(((bf16[2048,1024]{1,0:T(8,128)(2,1)}), bf16[512,1024]{1,0:T(8,128)(2,1)}) %reduce-scatter.9.cloned.1.call-update) | async-done | bytes 1048592 | tf_op jit(solution)/shard_map/while/body/eval_jaxpr/reduce_scatter | solution.py:152
  1828.5 42.6 %all-gather.11.cloned.1.call-done = bf16[2048,1024]{1,0:T(8,128)(2,1)} async-done(((bf16[512,1024]{1,0:T(8,128)(2,1)}), bf16[2048,1024]{1,0:T(8,128)(2,1)}) %all-gather.11.cloned.1.call-update) | async-done | bytes 4194320 | tf_op jit(solution)/shard_map/while/body/eval_jaxpr/all_gather | solution.py:161
  1875.6 289.3 %while.140 = (s32[]{:T(128)}, f32[2048,4,64]{0,2,1:T(8,128)}, f32[2048,4,64]{0,2,1:T(8,128)}, f32[4,512,4,64]{1,0,3,2:T(4,128)}, s32[4]{0:T(128)S(1)}, /*index=5...) while((s32[]{:T(128)}, f32[2048,4,64]{0,2,1:T(8,128)}, ...), condition=%wide.region_16.16_spmd.clone, body=%wide.region_14.15_spmd.clone.sunk | while | flops 2753186304 | bytes 187253072 | solution.py:115
  1889.3 12.5 multiply_reduce_fusion.6
  1901.8 12.1 multiply_convert_fusion.10
  1960.7 12.5 multiply_reduce_fusion.6
  1973.2 12.1 multiply_convert_fusion.10
  2007.3 12.5 fusion.242
  2033.3 12.5 multiply_reduce_fusion.6
  2045.7 12.1 multiply_convert_fusion.10
  2079.9 12.5 fusion.242
  2105.8 12.5 multiply_reduce_fusion.6
  2118.3 12.1 multiply_convert_fusion.10
  2152.3 12.4 fusion.242
  2204.9 29.7 reduce-scatter.11.cloned.1.call-done
  2262.0 54.6 %all-gather.9.cloned.1.call-done = bf16[2048,1024]{1,0:T(8,128)(2,1)} async-done(((bf16[512,1024]{1,0:T(8,128)(2,1)}), bf16[2048,1024]{1,0:T(8,128)(2,1)}) %all-gather.9.cloned.1.call-update) | async-done | bytes 4194320 | tf_op jit(solution)/shard_map/while/body/eval_jaxpr/all_gather | solution.py:161
  2342.0 51.0 %reduce-scatter.9.cloned.1.call-done = bf16[512,1024]{1,0:T(8,128)(2,1)} async-done(((bf16[2048,1024]{1,0:T(8,128)(2,1)}), bf16[512,1024]{1,0:T(8,128)(2,1)}) %reduce-scatter.9.cloned.1.call-update) | async-done | bytes 1048592 | tf_op jit(solution)/shard_map/while/body/eval_jaxpr/reduce_scatter | solution.py:152
  2411.5 42.6 %all-gather.11.cloned.1.call-done = bf16[2048,1024]{1,0:T(8,128)(2,1)} async-done(((bf16[512,1024]{1,0:T(8,128)(2,1)}), bf16[2048,1024]{1,0:T(8,128)(2,1)}) %all-gather.11.cloned.1.call-update) | async-done | bytes 4194320 | tf_op jit(solution)/shard_map/while/body/eval_jaxpr/all_gather | solution.py:161
  2458.6 289.5 %while.140 = (s32[]{:T(128)}, f32[2048,4,64]{0,2,1:T(8,128)}, f32[2048,4,64]{0,2,1:T(8,128)}, f32[4,512,4,64]{1,0,3,2:T(4,128)}, s32[4]{0:T(128)S(1)}, /*index=5...) while((s32[]{:T(128)}, f32[2048,4,64]{0,2,1:T(8,128)}, ...), condition=%wide.region_16.16_spmd.clone, body=%wide.region_14.15_spmd.clone.sunk | while | flops 2753186304 | bytes 187253072 | solution.py:115
  2472.5 12.5 multiply_reduce_fusion.6
  2485.0 12.1 multiply_convert_fusion.10
  2543.9 12.5 multiply_reduce_fusion.6
  2556.4 12.1 multiply_convert_fusion.10
  2590.5 12.5 fusion.242
  2616.5 12.5 multiply_reduce_fusion.6
  2663.1 12.5 fusion.242
  2689.0 12.5 multiply_reduce_fusion.6
  2735.5 12.4 fusion.242
  2788.0 29.7 reduce-scatter.11.cloned.1.call-done
  2857.4 44.9 %all-reduce.4 = (f32[2,16]{1,0:T(2,128)}, f32[1,1024]{1,0:T(1,128)}, f32[1,1024]{1,0:T(1,128)}) all-reduce(f32[2,16]{1,0:T(2,128)S(1)} %dynamic_update_slice.137, f32[1,1024]{1,0:T(1,128)S(1)} %bitcast.409, f32[1,1024]{1,0:T(1,128)S(1)} %bitcast.410), channel_id=1, replica_groups=mesh['section'=2,'dp'=4,'mp'=4] {'dp','mp'}, use_global_device_ids=true, to_apply=%region_25.26 | all-reduce | flops 2080 | bytes 16640 | tf_op jit(solution)/shard_map/psum | solution.py:403
  2908.6 176.4 %all-reduce.8.cloned.1.call-done = (bf16[1024,768]{1,0:T(8,128)(2,1)}, bf16[1,256,1024]{2,1,0:T(8,128)(2,1)}, bf16[1024,1408]{0,1:T(8,128)(2,1)}, bf16[1,704,1024]{2,1,0:T(8,128)(2,1)}) async-done(((bf16[1024,768]{1,0:T(8,128)(2,1)}, bf16[1,256,1024]{2,1,0:T(8,128)(2,1)}, bf16[1024,1408]{0,1:T(8,128)(2,1)}, bf16[1,704,1024]{2,1,0:T(8,128)(2,1)}), (bf16[1024,768]{1,0:T(8,128)(2,1)}, ...) | async-done | bytes 6422544 | tf_op jit(solution)/shard_map/psum | solution.py:387
  (1021 shorter events, 1327.5 us)
Async XLA Ops:
  19.3 69.5 %copy-start.8 = (bf16[2048,256]{0,1:T(8,128)(2,1)}, bf16[2048,256]{0,1:T(8,128)(2,1)S(1)}, u32[]{:S(2)}) copy-start(bf16[2048,256]{0,1:T(8,128)(2,1)S(1)} %get-tuple-element.2638) | copy-start | bytes 3145732 | tf_op jit(solution)/shard_map/while
  19.3 61.4 %all-gather.5.cloned.1.call-start = ((), (), s32[]{:S(2)}) async-start(), calls=%async_computation.5 | async-start | bytes 5242880 | tf_op jit(solution)/shard_map/while/body/eval_jaxpr/all_gather | solution.py:122
  25.1 200.8 %reduce-scatter.5.cloned.1.call-start = ((), (), s32[]{:S(2)}) async-start(), calls=%async_computation.6 | async-start | bytes 5242880 | tf_op jit(solution)/shard_map/while/body/eval_jaxpr/reduce_scatter | solution.py:137
  173.1 110.0 %all-gather.7.cloned.1.call-start = ((), (), s32[]{:S(2)}) async-start(), calls=%async_computation.7 | async-start | bytes 5242880 | tf_op jit(solution)/shard_map/while/body/eval_jaxpr/all_gather | solution.py:122
  230.2 126.1 %reduce-scatter.7.cloned.1.call-start = ((), (), s32[]{:S(2)}) async-start(), calls=%async_computation.8 | async-start | bytes 5242880 | tf_op jit(solution)/shard_map/while/body/eval_jaxpr/reduce_scatter | solution.py:137
  305.1 16.9 collective-permute-start.3
  359.3 14.8 collective-permute-start.2
  374.2 66.8 %copy-start.8 = (bf16[2048,256]{0,1:T(8,128)(2,1)}, bf16[2048,256]{0,1:T(8,128)(2,1)S(1)}, u32[]{:S(2)}) copy-start(bf16[2048,256]{0,1:T(8,128)(2,1)S(1)} %get-tuple-element.2638) | copy-start | bytes 3145732 | tf_op jit(solution)/shard_map/while
  374.2 58.6 %all-gather.5.cloned.1.call-start = ((), (), s32[]{:S(2)}) async-start(), calls=%async_computation.5 | async-start | bytes 5242880 | tf_op jit(solution)/shard_map/while/body/eval_jaxpr/all_gather | solution.py:122
  380.0 198.1 %reduce-scatter.5.cloned.1.call-start = ((), (), s32[]{:S(2)}) async-start(), calls=%async_computation.6 | async-start | bytes 5242880 | tf_op jit(solution)/shard_map/while/body/eval_jaxpr/reduce_scatter | solution.py:137
  525.3 110.0 %all-gather.7.cloned.1.call-start = ((), (), s32[]{:S(2)}) async-start(), calls=%async_computation.7 | async-start | bytes 5242880 | tf_op jit(solution)/shard_map/while/body/eval_jaxpr/all_gather | solution.py:122
  582.4 126.1 %reduce-scatter.7.cloned.1.call-start = ((), (), s32[]{:S(2)}) async-start(), calls=%async_computation.8 | async-start | bytes 5242880 | tf_op jit(solution)/shard_map/while/body/eval_jaxpr/reduce_scatter | solution.py:137
  657.3 16.8 collective-permute-start.3
  711.5 14.8 collective-permute-start.2
  726.4 66.7 %copy-start.8 = (bf16[2048,256]{0,1:T(8,128)(2,1)}, bf16[2048,256]{0,1:T(8,128)(2,1)S(1)}, u32[]{:S(2)}) copy-start(bf16[2048,256]{0,1:T(8,128)(2,1)S(1)} %get-tuple-element.2638) | copy-start | bytes 3145732 | tf_op jit(solution)/shard_map/while
  726.4 58.6 %all-gather.5.cloned.1.call-start = ((), (), s32[]{:S(2)}) async-start(), calls=%async_computation.5 | async-start | bytes 5242880 | tf_op jit(solution)/shard_map/while/body/eval_jaxpr/all_gather | solution.py:122
  732.1 198.1 %reduce-scatter.5.cloned.1.call-start = ((), (), s32[]{:S(2)}) async-start(), calls=%async_computation.6 | async-start | bytes 5242880 | tf_op jit(solution)/shard_map/while/body/eval_jaxpr/reduce_scatter | solution.py:137
  877.4 110.0 %all-gather.7.cloned.1.call-start = ((), (), s32[]{:S(2)}) async-start(), calls=%async_computation.7 | async-start | bytes 5242880 | tf_op jit(solution)/shard_map/while/body/eval_jaxpr/all_gather | solution.py:122
  934.5 126.1 %reduce-scatter.7.cloned.1.call-start = ((), (), s32[]{:S(2)}) async-start(), calls=%async_computation.8 | async-start | bytes 5242880 | tf_op jit(solution)/shard_map/while/body/eval_jaxpr/reduce_scatter | solution.py:137
  1009.4 16.9 collective-permute-start.3
  1063.7 14.8 collective-permute-start.2
  1093.3 137.7 %copy-start.48 = (f32[1,1024]{1,0:T(1,128)}, f32[1,1024]{1,0:T(1,128)S(1)}, u32[]{:S(2)}) copy-start(f32[1,1024]{1,0:T(1,128)S(1)} %get-tuple-element.2827) | copy-start | bytes 12292 | tf_op jit(solution)/shard_map/while
  1093.3 58.1 %all-gather.9.cloned.1.call-start = ((), (), s32[]{:S(2)}) async-start(), calls=%async_computation.9 | async-start | bytes 5242880 | tf_op jit(solution)/shard_map/while/body/eval_jaxpr/all_gather | solution.py:161
  1098.5 129.2 %reduce-scatter.9.cloned.1.call-start = ((), (), s32[]{:S(2)}) async-start(), calls=%async_computation.10 | async-start | bytes 5242880 | tf_op jit(solution)/shard_map/while/body/eval_jaxpr/reduce_scatter | solution.py:152
  1174.8 113.9 %all-gather.11.cloned.1.call-start = ((), (), s32[]{:S(2)}) async-start(), calls=%async_computation.11 | async-start | bytes 5242880 | tf_op jit(solution)/shard_map/while/body/eval_jaxpr/all_gather | solution.py:161
  1236.0 416.5 %reduce-scatter.11.cloned.1.call-start = ((), (), s32[]{:S(2)}) async-start(), calls=%async_computation.12 | async-start | bytes 5242880 | tf_op jit(solution)/shard_map/while/body/eval_jaxpr/reduce_scatter | solution.py:152
  1293.7 13.5 copy-start.3
  1365.1 13.5 copy-start.3
  1437.7 13.5 copy-start.3
  1510.3 13.5 copy-start.3
  1609.6 42.9 %copy-start.39 = (f32[1,1024]{1,0:T(1,128)S(1)}, f32[1,1024]{1,0:T(1,128)}, u32[]{:S(2)}) copy-start(f32[1,1024]{1,0:T(1,128)} %get-tuple-element.2837) | copy-start | bytes 12292 | tf_op jit(solution)/shard_map/while
  1618.6 36.4 %copy-start.5 = (f32[512,1024]{1,0:T(8,128)S(1)}, f32[512,1024]{1,0:T(8,128)}, u32[]{:S(2)}) copy-start(f32[512,1024]{1,0:T(8,128)} %get-tuple-element.2466) | copy-start | bytes 6291460 | tf_op jit(solution)/shard_map/while
  1618.7 38.7 %copy-start.59 = (f32[1024]{0:T(1024)}, f32[1024]{0:T(1024)S(1)}, u32[]{:S(2)}) copy-start(f32[1024]{0:T(1024)S(1)} %select_add_fusion.12) | copy-start | bytes 12292 | tf_op jit(solution)/shard_map/while
  1621.5 47.9 %collective-permute-start.1 = (bf16[2048,256]{0,1:T(8,128)(2,1)}, bf16[2048,256]{0,1:T(8,128)(2,1)S(1)}, u32[]{:S(2)}, u32[]{:S(2)}) collective-permute-start(bf16[2048,256]{0,1:T(8,128)(2,1)} %bitcast.362), channel_id=1, source_target_pairs={{16,0},{17,1},{18,2},{19,3},{20,4},{21,5},{22,6},{23,7},{24,8},{25... | collective-permute-start | bytes 3145736 | tf_op jit(solution)/shard_map/while/body/eval_jaxpr/ppermute | solution.py:12
  1657.3 16.0 collective-permute-start
  1673.7 139.6 %copy-start.48 = (f32[1,1024]{1,0:T(1,128)}, f32[1,1024]{1,0:T(1,128)S(1)}, u32[]{:S(2)}) copy-start(f32[1,1024]{1,0:T(1,128)S(1)} %get-tuple-element.2827) | copy-start | bytes 12292 | tf_op jit(solution)/shard_map/while
  1673.7 59.9 %all-gather.9.cloned.1.call-start = ((), (), s32[]{:S(2)}) async-start(), calls=%async_computation.9 | async-start | bytes 5242880 | tf_op jit(solution)/shard_map/while/body/eval_jaxpr/all_gather | solution.py:161
  1679.0 131.0 %reduce-scatter.9.cloned.1.call-start = ((), (), s32[]{:S(2)}) async-start(), calls=%async_computation.10 | async-start | bytes 5242880 | tf_op jit(solution)/shard_map/while/body/eval_jaxpr/reduce_scatter | solution.py:152
  1757.1 114.0 %all-gather.11.cloned.1.call-start = ((), (), s32[]{:S(2)}) async-start(), calls=%async_computation.11 | async-start | bytes 5242880 | tf_op jit(solution)/shard_map/while/body/eval_jaxpr/all_gather | solution.py:161
  1818.2 416.3 %reduce-scatter.11.cloned.1.call-start = ((), (), s32[]{:S(2)}) async-start(), calls=%async_computation.12 | async-start | bytes 5242880 | tf_op jit(solution)/shard_map/while/body/eval_jaxpr/reduce_scatter | solution.py:152
  1875.8 13.5 copy-start.3
  1947.2 13.5 copy-start.3
  2019.8 13.5 copy-start.3
  2092.3 13.5 copy-start.3
  2191.7 42.9 %copy-start.39 = (f32[1,1024]{1,0:T(1,128)S(1)}, f32[1,1024]{1,0:T(1,128)}, u32[]{:S(2)}) copy-start(f32[1,1024]{1,0:T(1,128)} %get-tuple-element.2837) | copy-start | bytes 12292 | tf_op jit(solution)/shard_map/while
  2200.7 36.4 %copy-start.5 = (f32[512,1024]{1,0:T(8,128)S(1)}, f32[512,1024]{1,0:T(8,128)}, u32[]{:S(2)}) copy-start(f32[512,1024]{1,0:T(8,128)} %get-tuple-element.2466) | copy-start | bytes 6291460 | tf_op jit(solution)/shard_map/while
  2200.8 38.7 %copy-start.59 = (f32[1024]{0:T(1024)}, f32[1024]{0:T(1024)S(1)}, u32[]{:S(2)}) copy-start(f32[1024]{0:T(1024)S(1)} %select_add_fusion.12) | copy-start | bytes 12292 | tf_op jit(solution)/shard_map/while
  2203.6 49.0 %collective-permute-start.1 = (bf16[2048,256]{0,1:T(8,128)(2,1)}, bf16[2048,256]{0,1:T(8,128)(2,1)S(1)}, u32[]{:S(2)}, u32[]{:S(2)}) collective-permute-start(bf16[2048,256]{0,1:T(8,128)(2,1)} %bitcast.362), channel_id=1, source_target_pairs={{16,0},{17,1},{18,2},{19,3},{20,4},{21,5},{22,6},{23,7},{24,8},{25... | collective-permute-start | bytes 3145736 | tf_op jit(solution)/shard_map/while/body/eval_jaxpr/ppermute | solution.py:12
  2239.4 17.1 collective-permute-start
  2256.7 139.6 %copy-start.48 = (f32[1,1024]{1,0:T(1,128)}, f32[1,1024]{1,0:T(1,128)S(1)}, u32[]{:S(2)}) copy-start(f32[1,1024]{1,0:T(1,128)S(1)} %get-tuple-element.2827) | copy-start | bytes 12292 | tf_op jit(solution)/shard_map/while
  2256.7 59.9 %all-gather.9.cloned.1.call-start = ((), (), s32[]{:S(2)}) async-start(), calls=%async_computation.9 | async-start | bytes 5242880 | tf_op jit(solution)/shard_map/while/body/eval_jaxpr/all_gather | solution.py:161
  2261.9 131.0 %reduce-scatter.9.cloned.1.call-start = ((), (), s32[]{:S(2)}) async-start(), calls=%async_computation.10 | async-start | bytes 5242880 | tf_op jit(solution)/shard_map/while/body/eval_jaxpr/reduce_scatter | solution.py:152
  2340.1 113.9 %all-gather.11.cloned.1.call-start = ((), (), s32[]{:S(2)}) async-start(), calls=%async_computation.11 | async-start | bytes 5242880 | tf_op jit(solution)/shard_map/while/body/eval_jaxpr/all_gather | solution.py:161
  2401.2 416.5 %reduce-scatter.11.cloned.1.call-start = ((), (), s32[]{:S(2)}) async-start(), calls=%async_computation.12 | async-start | bytes 5242880 | tf_op jit(solution)/shard_map/while/body/eval_jaxpr/reduce_scatter | solution.py:152
  2459.0 13.5 copy-start.3
  2530.4 13.5 copy-start.3
  2603.0 13.5 copy-start.3
  2774.9 42.9 %copy-start.39 = (f32[1,1024]{1,0:T(1,128)S(1)}, f32[1,1024]{1,0:T(1,128)}, u32[]{:S(2)}) copy-start(f32[1,1024]{1,0:T(1,128)} %get-tuple-element.2837) | copy-start | bytes 12292 | tf_op jit(solution)/shard_map/while
  2783.9 36.4 %copy-start.5 = (f32[512,1024]{1,0:T(8,128)S(1)}, f32[512,1024]{1,0:T(8,128)}, u32[]{:S(2)}) copy-start(f32[512,1024]{1,0:T(8,128)} %get-tuple-element.2466) | copy-start | bytes 6291460 | tf_op jit(solution)/shard_map/while
  2783.9 38.7 %copy-start.59 = (f32[1024]{0:T(1024)}, f32[1024]{0:T(1024)S(1)}, u32[]{:S(2)}) copy-start(f32[1024]{0:T(1024)S(1)} %select_add_fusion.12) | copy-start | bytes 12292 | tf_op jit(solution)/shard_map/while
  2786.7 48.8 %collective-permute-start.1 = (bf16[2048,256]{0,1:T(8,128)(2,1)}, bf16[2048,256]{0,1:T(8,128)(2,1)S(1)}, u32[]{:S(2)}, u32[]{:S(2)}) collective-permute-start(bf16[2048,256]{0,1:T(8,128)(2,1)} %bitcast.362), channel_id=1, source_target_pairs={{16,0},{17,1},{18,2},{19,3},{20,4},{21,5},{22,6},{23,7},{24,8},{25... | collective-permute-start | bytes 3145736 | tf_op jit(solution)/shard_map/while/body/eval_jaxpr/ppermute | solution.py:12
  2822.6 16.9 collective-permute-start
  2843.5 241.6 %all-reduce.8.cloned.1.call-start = ((), (), s32[]{:S(2)}) async-start(), calls=%async_computation.4 | async-start | bytes 12845056 | tf_op jit(solution)/shard_map/psum | solution.py:387
  2853.5 48.8 %copy-start.43 = (bf16[3,512,1024]{2,1,0:T(8,128)(2,1)S(1)}, bf16[3,512,1024]{2,1,0:T(8,128)(2,1)}, u32[]{:S(2)}) copy-start(bf16[3,512,1024]{2,1,0:T(8,128)(2,1)} %get-tuple-element.2909) | copy-start | bytes 9437188
  (191 other events, 984.8 us)
Sparse Core Ops, SparseCore 0:
  25.3 55.3 all-gather.4
  173.2 52.6 reduce-scatter.4
  230.3 52.6 all-gather.6
  303.6 52.6 reduce-scatter.6
  380.1 52.6 all-gather.4
  525.4 52.6 reduce-scatter.4
  582.5 52.6 all-gather.6
  655.8 52.6 reduce-scatter.6
  732.3 52.6 all-gather.4
  877.5 52.6 reduce-scatter.4
  934.6 52.6 all-gather.6
  1007.9 52.6 reduce-scatter.6
  1098.6 52.6 all-gather.8
  1175.0 52.6 reduce-scatter.8
  1236.1 52.6 all-gather.10
  1599.7 52.6 reduce-scatter.10
  1679.1 54.4 all-gather.8
  1757.2 52.6 reduce-scatter.8
  1818.4 52.6 all-gather.10
  2181.8 52.6 reduce-scatter.10
  2262.0 54.4 all-gather.8
  2340.2 52.6 reduce-scatter.8
  2401.3 52.6 all-gather.10
  2765.0 52.6 reduce-scatter.10
Sparse Core Ops, SparseCore 1:
  2853.6 231.4 all-reduce.7
where the time goes:
time: 3110 us; the launch traced here: 3100 us
  waiting for transfers between devices  1270 us (41%)
  matrix products  892 us (29%)
  other arithmetic  430 us (14%)
  local copies, waits for them, and re-layouts  353 us (11%)
  loops' own time  77.7 us (2%)
  blocking collectives  44.9 us (1%)
    all_gather x6, waiting for transfers between devices, project_rows(): gathered = lax.all_gather(normed, 'mp', axis=0, tiled=True)  306 us
    all_gather x6, waiting for transfers between devices, fold_branch(): shard_rows = lax.all_gather(grad_rows, 'mp', axis=0, tiled=True)  290 us
    reduce_scatter x6, waiting for transfers between devices, sum_branch(): lax.psum_scatter(term_rows(jnp.int32(0), lax.axis_size('mp') * tok_rows)....  252 us
    reduce_scatter x6, waiting for transfers between devices, sum_input(): lax.psum_scatter(term_rows(jnp.int32(0), lax.axis_size('mp') * tok_rows)....  242 us
    psum x1, waiting for transfers between devices, shards(): lax.psum(qkv_grad.astype(jnp.bfloat16), 'dp').astype(jnp.float32)  176 us
    dot_general x24, matrix products, block_scores(): jnp.einsum('qhd,khd->hqk', rows_q, keys_rot, preferred_element_type=jnp.f...  167 us
    dot_general x12, matrix products, one_block(): jnp.einsum('qhd,khd->hqk', rows_grad, values_mix, preferred_element_type=...  150 us
    dot_general x12, matrix products, one_block(): jnp.einsum('hqk,qhd->khd', probabilities.astype(jnp.bfloat16), rows_grad,...  148 us
  transfers between devices with their start and end apart: 37, of which 25 were waited for; matrix products, arithmetic and copies ran while one was open for 8% of the time, Pallas kernels for 0%

commit v1 on v0

v1 whole, which is shorter than its diff:
```python
import functools

import jax
import jax.numpy as jnp
from jax import lax
from jax.experimental import pallas as pl
from jax.experimental.pallas import tpu as pltpu
from jax.sharding import PartitionSpec as P

HEAD_DIM = 64
HALF = HEAD_DIM // 2
EPS = 1e-05
SCALE = HEAD_DIM**-0.5
F32 = jnp.float32
BF16 = jnp.bfloat16
VMEM_BYTES = 56 * 1024 * 1024

NT = (((1,), (1,)), ((), ()))
NN = (((1,), (0,)), ((), ()))
TN = (((0,), (0,)), ((), ()))


def mm(left, right, dims=NN):
    return lax.dot_general(left, right, dims, preferred_element_type=F32)


def swap_halves(tensor):
    width = tensor.shape[1]
    if width % 128 == 0:
        lane = lax.broadcasted_iota(jnp.int32, tensor.shape, 1)
        ahead = pltpu.roll(tensor, width - HALF, 1)
        behind = pltpu.roll(tensor, HALF, 1)
        return jnp.where(lane % HEAD_DIM < HALF, ahead, behind)
    return jnp.concatenate([tensor[:, HALF:], tensor[:, :HALF]], axis=1)


def qkv_kernel(second, group, x_ref, w_ref, cos_ref, sin_ref, *refs):
    if second:
        first_ref, q_ref, k_ref, v_ref = refs
    else:
        q_ref, k_ref, v_ref = refs
    width = q_ref.shape[1]
    acc = mm(x_ref[...], w_ref[...])
    cosine, sine = cos_ref[...], sin_ref[...]
    for at in range(0, width, group):
        part = acc[:, at : at + group]
        turned = part * cosine + swap_halves(part) * sine
        q_ref[:, at : at + group] = (turned * SCALE).astype(BF16)
        part = acc[:, width + at : width + at + group]
        turned = part * cosine + swap_halves(part) * sine
        k_ref[:, at : at + group] = turned.astype(BF16)
    value = acc[:, 2 * width :]
    if second:
        value = 0.5 * value + 0.5 * first_ref[...].astype(F32)
    v_ref[...] = value.astype(BF16)


def project_qkv(normed, weight, cosine, sine, first):
    rows, model = normed.shape
    width = weight.shape[1] // 3
    group = min(width, 128)
    block = min(512, rows)
    second = first is not None
    row_spec = pl.BlockSpec((block, width), lambda i: (i, 0))
    in_specs = [
        pl.BlockSpec((block, model), lambda i: (i, 0)),
        pl.BlockSpec((model, 3 * width), lambda i: (0, 0)),
        pl.BlockSpec((block, group), lambda i: (i, 0)),
        pl.BlockSpec((block, group), lambda i: (i, 0)),
    ]
    args = [normed, weight, cosine, sine]
    if second:
        in_specs.append(row_spec)
        args.append(first)
    shape = jax.ShapeDtypeStruct((rows, width), BF16)
    return pl.pallas_call(
        functools.partial(qkv_kernel, second, group),
        grid=(rows // block,),
        in_specs=in_specs,
        out_specs=[row_spec] * 3,
        out_shape=[shape] * 3,
        compiler_params=pltpu.CompilerParams(vmem_limit_bytes=VMEM_BYTES),
        name="qkv_rope",
    )(*args)


def head_lanes(value, head, group):
    per = group // HEAD_DIM
    if per == 1:
        return value
    lane = lax.broadcasted_iota(jnp.int32, value.shape, 1)
    return jnp.where(lane // HEAD_DIM == head % per, value, jnp.zeros_like(value))


def attend_kernel(block, group, len_ref, q_ref, k_ref, v_ref, o_ref, lse_ref, acc_ref, top_ref, sum_ref):
    width = q_ref.shape[1]
    heads = width // HEAD_DIM
    per = group // HEAD_DIM
    step = pl.program_id(0)
    seg_len = len_ref[0]
    first = (step * block // seg_len) * (seg_len // block)
    q_heads = []
    for head in range(heads):
        at = head // per * group
        q_heads.append(head_lanes(q_ref[:, at : at + group], head, group))

    def one(col, masked, start):
        rows = pl.ds(pl.multiple_of(col * block, block), block)
        for pair in range(heads // per):
            at = pair * group
            keys = k_ref[rows, at : at + group]
            values = v_ref[rows, at : at + group]
            total = None
            shrink = None
            for sub in range(per):
                head = pair * per + sub
                scores = mm(q_heads[head], keys, NT)
                if masked:
                    r = lax.broadcasted_iota(jnp.int32, scores.shape, 0)
                    c = lax.broadcasted_iota(jnp.int32, scores.shape, 1)
                    scores = jnp.where(c <= r, scores, -1e30)
                top = jnp.max(scores, axis=1, keepdims=True)
                if not start:
                    old = top_ref[:, head : head + 1]
                    top = jnp.maximum(top, old)
                probs = jnp.exp(scores - top)
                count = jnp.sum(probs, axis=1, keepdims=True)
                if not start:
                    scale = jnp.exp(old - top)
                    count = count + sum_ref[:, head : head + 1] * scale
                    wide = jnp.broadcast_to(scale, (block, group))
                    if shrink is None:
                        shrink = wide
                    else:
                        lane = lax.broadcasted_iota(jnp.int32, wide.shape, 1)
                        shrink = jnp.where(lane // HEAD_DIM == sub, wide, shrink)
                top_ref[:, head : head + 1] = top
                sum_ref[:, head : head + 1] = count
                part = mm(probs.astype(BF16), head_lanes(values, head, group))
                total = part if total is None else total + part
            if start:
                acc_ref[:, at : at + group] = total
            else:
                acc_ref[:, at : at + group] = acc_ref[:, at : at + group] * shrink + total

    one(step, True, True)

    @pl.loop(first, step)
    def _(col):
        one(col, False, False)

    lane = lax.broadcasted_iota(jnp.int32, (block, 128), 1)
    columns = jnp.zeros((block, 128), F32)
    for head in range(heads):
        value = top_ref[:, head : head + 1] + jnp.log(sum_ref[:, head : head + 1])
        columns = jnp.where(lane == head, value, columns)
    lse_ref[...] = columns.T[: lse_ref.shape[0]]
    for pair in range(heads // per):
        at = pair * group
        over = None
        for sub in range(per):
            head = pair * per + sub
            wide = jnp.broadcast_to(1.0 / sum_ref[:, head : head + 1], (block, group))
            if over is None:
                over = wide
            else:
                sub_lane = lax.broadcasted_iota(jnp.int32, wide.shape, 1)
                over = jnp.where(sub_lane // HEAD_DIM == sub, wide, over)
        o_ref[:, at : at + group] = (acc_ref[:, at : at + group] * over).astype(BF16)


def attend(queries, keys, values, seg_len):
    rows, width = queries.shape
    group = min(width, 128)
    heads = width // HEAD_DIM
    block = min(512, rows // 2)
    whole = pl.BlockSpec((rows, width), lambda i, n: (0, 0))
    return pl.pallas_call(
        functools.partial(attend_kernel, block, group),
        grid_spec=pltpu.PrefetchScalarGridSpec(
            num_scalar_prefetch=1,
            grid=(rows // block,),
            in_specs=[pl.BlockSpec((block, width), lambda i, n: (i, 0)), whole, whole],
            out_specs=[
                pl.BlockSpec((block, width), lambda i, n: (i, 0)),
                pl.BlockSpec((heads, block), lambda i, n: (0, i)),
            ],
            scratch_shapes=[
                pltpu.VMEM((block, width), F32),
                pltpu.VMEM((block, 128), F32),
                pltpu.VMEM((block, 128), F32),
            ],
        ),
        out_shape=[
            jax.ShapeDtypeStruct((rows, width), BF16),
            jax.ShapeDtypeStruct((heads, rows), F32),
        ],
        compiler_params=pltpu.CompilerParams(vmem_limit_bytes=VMEM_BYTES),
        name="attend",
    )(seg_len, queries, keys, values)


def attend_back_kernel(second, block, group, len_ref, q_ref, k_ref, v_ref, o_ref, do_ref, lse_ref, cos_ref, sin_ref, *refs):
    if second:
        out_ref, dq_ref, dk_ref, dv_ref, delta_ref = refs
    else:
        first_ref, out_ref, dq_ref, dk_ref, dv_ref, delta_ref = refs
    rows, width = q_ref.shape
    heads = width // HEAD_DIM
    per = group // HEAD_DIM
    step = pl.program_id(0)
    steps = rows // block
    seg_len = len_ref[0]
    per_seg = seg_len // block
    last = (step // per_seg + 1) * per_seg

    @pl.when(step == 0)
    def _():
        dq_ref[...] = jnp.zeros_like(dq_ref)
        head = lax.broadcasted_iota(jnp.int32, (8, width), 0)
        lane = lax.broadcasted_iota(jnp.int32, (8, width), 1)
        pick = jnp.where(lane // HEAD_DIM == head, 1.0, 0.0).astype(F32)
        for at in range(0, rows, block):
            prod = do_ref[at : at + block, :].astype(F32) * o_ref[at : at + block, :].astype(F32)
            delta_ref[:, at : at + block] = lax.dot_general(
                pick, prod, NT, precision=lax.Precision.HIGHEST, preferred_element_type=F32
            )

    key_rows = pl.ds(pl.multiple_of(step * block, block), block)

    def one(row, masked):
        query_rows = pl.ds(pl.multiple_of(row * block, block), block)
        for pair in range(heads // per):
            at = pair * group
            keys = k_ref[key_rows, at : at + group]
            values = v_ref[key_rows, at : at + group]
            queries = q_ref[query_rows, at : at + group]
            grads = do_ref[query_rows, at : at + group]
            dq = dk = dv = None
            for sub in range(per):
                head = pair * per + sub
                q_one = head_lanes(queries, head, group)
                do_one = head_lanes(grads, head, group)
                scores = mm(keys, q_one, NT)
                probs = jnp.exp(scores - lse_ref[head : head + 1, query_rows])
                if masked:
                    r = lax.broadcasted_iota(jnp.int32, scores.shape, 0)
                    c = lax.broadcasted_iota(jnp.int32, scores.shape, 1)
                    probs = jnp.where(r <= c, probs, 0.0)
                g_probs = mm(values, do_one, NT)
                g_scores = (probs * (g_probs - delta_ref[head : head + 1, query_rows])).astype(BF16)
                dv_one = mm(probs.astype(BF16), do_one)
                dk_one = mm(g_scores, q_one)
                dq_one = mm(g_scores, head_lanes(keys, head, group), TN)
                dq = dq_one if dq is None else dq + dq_one
                dk = dk_one if dk is None else dk + dk_one
                dv = dv_one if dv is None else dv + dv_one
            dq_ref[query_rows, at : at + group] += dq
            if masked:
                dk_ref[:, at : at + group] = dk
                dv_ref[:, at : at + group] = dv
            else:
                dk_ref[:, at : at + group] += dk
                dv_ref[:, at : at + group] += dv

    one(step, True)

    @pl.loop(step + 1, last)
    def _(row):
        one(row, False)

    def turn_back(value, at_rows):
        return value * cos_ref[at_rows, :] - swap_halves(value) * sin_ref[at_rows, :]

    for at in range(0, width, group):
        out_ref[key_rows, width + at : width + at + group] = turn_back(dk_ref[:, at : at + group], key_rows).astype(BF16)
        out_ref[key_rows, at : at + group] = turn_back(dq_ref[key_rows, at : at + group] * SCALE, key_rows).astype(BF16)
    if second:
        g_value = 0.5 * dv_ref[...]
    else:
        g_value = dv_ref[...] + first_ref[key_rows, :].astype(F32)
    out_ref[key_rows, 2 * width :] = g_value.astype(BF16)


def attend_back(queries, keys, values, attended, grads, lse, cosine, sine, g_first, seg_len):
    rows, width = queries.shape
    group = min(width, 128)
    heads = width // HEAD_DIM
    block = min(512, rows // 2)
    second = g_first is None
    whole = pl.BlockSpec((rows, width), lambda i, n: (0, 0))
    table = pl.BlockSpec((rows, group), lambda i, n: (0, 0))
    in_specs = [whole] * 5 + [pl.BlockSpec((heads, rows), lambda i, n: (0, 0)), table, table]
    args = [queries, keys, values, attended, grads, lse, cosine, sine]
    if not second:
        in_specs.append(whole)
        args.append(g_first)
    return pl.pallas_call(
        functools.partial(attend_back_kernel, second, block, group),
        grid_spec=pltpu.PrefetchScalarGridSpec(
            num_scalar_prefetch=1,
            grid=(rows // block,),
            in_specs=in_specs,
            out_specs=pl.BlockSpec((rows, 3 * width), lambda i, n: (0, 0)),
            scratch_shapes=[
                pltpu.VMEM((rows, width), F32),
                pltpu.VMEM((block, width), F32),
                pltpu.VMEM((block, width), F32),
                pltpu.VMEM((8, rows), F32),
            ],
        ),
        out_shape=jax.ShapeDtypeStruct((rows, 3 * width), BF16),
        compiler_params=pltpu.CompilerParams(vmem_limit_bytes=VMEM_BYTES),
        name="attend_back",
    )(seg_len, *args)


def normalize(rows_in, gain):
    scale = lax.rsqrt(jnp.mean(rows_in * rows_in, axis=-1, keepdims=True) + EPS)
    return rows_in * scale * gain


def normalize_back(rows_in, gain, grad):
    scale = lax.rsqrt(jnp.mean(rows_in * rows_in, axis=-1, keepdims=True) + EPS)
    gained = grad * gain
    inner = jnp.mean(gained * rows_in, axis=-1, keepdims=True)
    g_rows = scale * (gained - rows_in * (scale * scale * inner))
    return g_rows, jnp.sum(grad * (rows_in * scale), axis=0)


def rotary_tables(rows, seg_len, lanes):
    positions = (jnp.arange(rows, dtype=jnp.int32) % seg_len).astype(F32)
    inverse_freq = 10000.0 ** (-(jnp.arange(HALF, dtype=F32) * 2.0 / HEAD_DIM))
    angles = positions[:, None] * inverse_freq[None, :]
    cosine, sine = jnp.cos(angles), jnp.sin(angles)
    cosine = jnp.concatenate([cosine, cosine] * (lanes // HEAD_DIM), axis=1)
    sine = jnp.concatenate([-sine, sine] * (lanes // HEAD_DIM), axis=1)
    return cosine, sine


def swap_cores(value):
    return lax.ppermute(value, "section", [(0, 1), (1, 0)])


def pick_half(value, which, axis=0):
    size = value.shape[axis] // 2
    return lax.dynamic_slice_in_dim(value, which * size, size, axis)


def shards(
    tokens,
    layout,
    cotangent,
    attn_gain,
    query_weight,
    key_weight,
    value_weight,
    out_weight,
    ffn_gain,
    gate_weight,
    up_weight,
    down_weight,
):
    core = lax.axis_index("section")
    is_low = core == 0
    micro_count, tok_rows, model = tokens.shape
    mp = lax.axis_size("mp")
    seq_rows = tok_rows * mp
    width = query_weight.shape[2]
    hidden = gate_weight.shape[2]
    hid_half = hidden // 2
    out_half = width // 2
    group = min(width, 128)

    def in_order(own, other):
        return jnp.where(is_low, own, other), jnp.where(is_low, other, own)

    inputs = lax.dynamic_index_in_dim(tokens, core, 0, keepdims=False)
    g_top = lax.dynamic_index_in_dim(cotangent, core, 0, keepdims=False)
    pack_layout = lax.dynamic_index_in_dim(layout[:, 0], core, 0, keepdims=False)
    seg_len = (seq_rows // pack_layout).astype(jnp.int32)
    seg_arg = seg_len.reshape(1)
    cosine, sine = rotary_tables(seq_rows, seg_len, group)

    own_qkv = jnp.concatenate([query_weight[0], key_weight[0], value_weight[0]], axis=1)
    qkv_weights = in_order(own_qkv, swap_cores(own_qkv))
    gains = jnp.concatenate([attn_gain, ffn_gain], axis=0)
    gain_first, gain_second = in_order(gains, swap_cores(gains))
    halves = jnp.concatenate(
        [
            gate_weight[0].T.reshape(2, hid_half, model),
            up_weight[0].T.reshape(2, hid_half, model),
            down_weight[0].reshape(2, hid_half, model),
            out_weight[0].reshape(2, out_half, model),
        ],
        axis=1,
    )
    kept = lax.dynamic_index_in_dim(halves, core, 0, keepdims=False)
    sent = lax.dynamic_index_in_dim(halves, 1 - core, 0, keepdims=False)
    packs = in_order(kept, swap_cores(sent))
    pack_rows = packs[0].shape[0]

    def unpack(pack):
        parts = pack.reshape(mp, pack_rows, model)
        gate_t = parts[:, :hid_half].reshape(mp * hid_half, model)
        up_t = parts[:, hid_half : 2 * hid_half].reshape(mp * hid_half, model)
        down = parts[:, 2 * hid_half : 3 * hid_half].reshape(mp * hid_half, model)
        return gate_t, up_t, down, parts[:, 3 * hid_half :]

    def gathered(pack):
        own = lax.all_gather(pack, "mp", axis=0, tiled=True)
        other = swap_cores(own)
        own, other = unpack(own), unpack(other)
        low, high = in_order(own[3], other[3])
        out_full = jnp.concatenate([low, high], axis=1).reshape(mp * width, model)
        return own[:3], other[:3], out_full

    layers = []
    for layer in range(2):
        gain_pair = (gain_first, gain_second)[layer]
        own, other, out_full = gathered(packs[layer])
        layers.append((gain_pair[0], gain_pair[1], qkv_weights[layer], own, other, out_full))

    def to_owners(value):
        blocks = value.reshape(mp, tok_rows, width)
        moved = lax.all_to_all(blocks, "mp", 0, 0)
        return jnp.transpose(moved, (1, 0, 2)).reshape(tok_rows, mp * width)

    def to_heads(value):
        blocks = jnp.transpose(value.reshape(tok_rows, mp, width), (1, 0, 2))
        return lax.all_to_all(blocks, "mp", 0, 0).reshape(seq_rows, width)

    def forward(rows_low, first, weights):
        gain_a, gain_f, qkv_w, own, other, out_full = weights
        state = rows_low.astype(F32)
        normed = normalize(state, gain_a).astype(BF16)
        normed_all = lax.all_gather(normed, "mp", axis=0, tiled=True)
        queries, keys, values = project_qkv(normed_all, qkv_w, cosine, sine, first)
        attended, lse = attend(queries, keys, values, seg_arg)
        att_rows = to_owners(attended)
        middle = state + mm(att_rows, out_full)
        normed_ffn = normalize(middle, gain_f).astype(BF16)
        result = middle
        inner = []
        for gate_t, up_t, down in (own, other):
            gate = mm(normed_ffn, gate_t, NT)
            up = mm(normed_ffn, up_t, NT)
            activated = (jax.nn.silu(gate) * up).astype(BF16)
            result = result + mm(activated, down)
            inner.append((gate, up, activated))
        kept_items = (state, normed_all, queries, keys, values, attended, lse, att_rows, middle, normed_ffn, inner)
        return result.astype(BF16), values, kept_items

    def backward(g_result, g_first, weights, kept_items):
        gain_a, gain_f, qkv_w, own, other, out_full = weights
        state, normed_all, queries, keys, values, attended, lse, att_rows, middle, normed_ffn, inner = kept_items
        g_branch = g_result.astype(BF16)
        g_normed = None
        g_inner = []
        for (gate, up, activated), (gate_t, up_t, down) in zip(inner, (own, other)):
            g_act = mm(g_branch, down, NT)
            sig = jax.nn.sigmoid(gate)
            g_up = (g_act * (gate * sig)).astype(BF16)
            g_gate = (g_act * up * (sig * (1.0 + gate * (1.0 - sig)))).astype(BF16)
            part = mm(g_gate, gate_t) + mm(g_up, up_t)
            g_normed = part if g_normed is None else g_normed + part
            g_inner.append((g_gate, g_up, activated))
        g_norm, g_gain_f = normalize_back(middle, gain_f, g_normed)
        g_middle = g_result + g_norm
        g_mid_low = g_middle.astype(BF16)
        g_att = to_heads(mm(g_mid_low, out_full, NT).astype(BF16))
        g_qkv = attend_back(queries, keys, values, attended, g_att, lse, cosine, sine, g_first, seg_arg)
        g_normed_part = mm(g_qkv, qkv_w, NT).astype(BF16)
        g_normed_attn = lax.psum_scatter(g_normed_part, "mp", scatter_dimension=0, tiled=True).astype(F32)
        g_norm, g_gain_a = normalize_back(state, gain_a, g_normed_attn)
        g_inputs = g_middle + g_norm

        sent_rows = jnp.concatenate(list(g_inner[1]) + [normed_ffn, g_branch], axis=1)
        got = swap_cores(sent_rows)
        hid_all = mp * hid_half
        got_gate, got_up, got_act = (got[:, i * hid_all : (i + 1) * hid_all] for i in range(3))
        got_normed = got[:, 3 * hid_all : 3 * hid_all + model]
        got_branch = got[:, 3 * hid_all + model :]
        gate_grad = mm(g_inner[0][0], normed_ffn, TN) + mm(got_gate, got_normed, TN)
        up_grad = mm(g_inner[0][1], normed_ffn, TN) + mm(got_up, got_normed, TN)
        down_grad = mm(g_inner[0][2], g_branch, TN) + mm(got_act, got_branch, TN)
        out_grad = mm(att_rows, g_mid_low, TN).astype(BF16).reshape(mp, 2, out_half, model)
        out_kept = lax.dynamic_index_in_dim(out_grad, core, 1, keepdims=False)
        out_sent = lax.dynamic_index_in_dim(out_grad, 1 - core, 1, keepdims=False)
        out_grad = out_kept.astype(F32) + swap_cores(out_sent).astype(F32)
        grads = jnp.concatenate(
            [
                gate_grad.astype(BF16).reshape(mp, hid_half, model),
                up_grad.astype(BF16).reshape(mp, hid_half, model),
                down_grad.astype(BF16).reshape(mp, hid_half, model),
                out_grad.astype(BF16),
            ],
            axis=1,
        ).reshape(mp * pack_rows, model)
        grads = lax.psum_scatter(grads, "mp", scatter_dimension=0, tiled=True)
        grads = lax.psum(grads, "dp")
        qkv_grad = mm(normed_all, g_qkv, TN).astype(BF16)
        qkv_grad = pick_half(qkv_grad, core).astype(F32) + swap_cores(pick_half(qkv_grad, 1 - core)).astype(F32)
        qkv_grad = lax.psum(qkv_grad.astype(BF16), "dp")
        return g_inputs, g_qkv[:, 2 * width :], (grads, qkv_grad, g_gain_a, g_gain_f)

    h_first, first_values, kept_first = forward(inputs, None, layers[0])
    h_second, unused, kept_second = forward(h_first, first_values, layers[1])
    g_second, g_first, grads_second = backward(g_top, None, layers[1], kept_second)
    g_tokens, unused, grads_first = backward(g_second.astype(BF16).astype(F32), g_first, layers[0], kept_first)

    def by_layer(low, high, wire):
        mine = jnp.where(is_low, low, high)
        theirs = swap_cores(jnp.where(is_low, high, low).astype(wire)).astype(mine.dtype)
        return in_order(mine, theirs)

    layer_out = jnp.stack(by_layer(h_first, h_second, BF16))
    input_grads = jnp.stack(by_layer(g_tokens, g_second, BF16))
    all_first = jnp.stack(in_order(first_values, swap_cores(first_values)))

    grads_low, grads_high = by_layer(grads_first[0], grads_second[0], BF16)
    qkv_low, qkv_high = by_layer(grads_first[1], grads_second[1], BF16)

    def joined(start, size):
        return jnp.concatenate([grads_low[start : start + size], grads_high[start : start + size]], axis=0).astype(F32)

    gate_grad = joined(0, hid_half).T
    up_grad = joined(hid_half, hid_half).T
    down_grad = joined(2 * hid_half, hid_half)
    out_grad = joined(3 * hid_half, out_half)
    qkv_grad = jnp.concatenate([qkv_low, qkv_high], axis=0).astype(F32)

    heads_here = width // HEAD_DIM
    first_f32 = first_values.astype(F32).reshape(seq_rows, heads_here, HEAD_DIM)
    squares = jnp.sum(first_f32 * first_f32, axis=(0, 2))
    placed = lax.dynamic_update_slice(
        jnp.zeros((micro_count, heads_here * mp), F32),
        squares[None],
        (core, lax.axis_index("mp") * heads_here),
    )
    gain_grads = jnp.stack([grads_first[2], grads_second[2], grads_first[3], grads_second[3]])
    gain_grads, value_norms = lax.psum((gain_grads, placed), ("section", "dp", "mp"))
    attn_gain_grad = lax.dynamic_slice_in_dim(gain_grads, core, 1, 0)
    ffn_gain_grad = lax.dynamic_slice_in_dim(gain_grads, 2 + core, 1, 0)
    return (
        layer_out[None],
        input_grads[None],
        all_first,
        value_norms,
        attn_gain_grad,
        qkv_grad[:, :width][None],
        qkv_grad[:, width : 2 * width][None],
        qkv_grad[:, 2 * width :][None],
        out_grad[None],
        ffn_gain_grad,
        gate_grad[None],
        up_grad[None],
        down_grad[None],
    )


def solution(mesh):
    in_specs = (
        P(None, ("dp", "mp"), None),
        P(None, "dp"),
        P(None, ("dp", "mp"), None),
        P("section", None),
        P("section", None, "mp"),
        P("section", None, "mp"),
        P("section", None, "mp"),
        P("section", "mp", None),
        P("section", None),
        P("section", None, "mp"),
        P("section", None, "mp"),
        P("section", "mp", None),
    )
    out_specs = (
        P("section", None, ("dp", "mp"), None),
        P("section", None, ("dp", "mp"), None),
        P(None, "dp", "mp"),
        P(),
        P("section", None),
        P("section", None, "mp"),
        P("section", None, "mp"),
        P("section", None, "mp"),
        P("section", "mp", None),
        P("section", None),
        P("section", None, "mp"),
        P("section", None, "mp"),
        P("section", "mp", None),
    )
    return jax.shard_map(shards, mesh=mesh, in_specs=in_specs, out_specs=out_specs, check_vma=False)
```

time: 3110 us -> 1180 us (0.38)
  matrix products: 892 us -> 141 us
  waiting for transfers between devices: 1270 us -> 588 us
  other arithmetic: 430 us -> 112 us
  local copies, waits for them, and re-layouts: 353 us -> 70.4 us
  Pallas kernels: 0 us -> 171 us
  loops' own time: 77.7 us -> 0 us
    dot_general x120 -> x46, matrix products: 892 us -> 141 us  [mm(): return lax.dot_general(left, right, dims, preferred_element_type=F32)]
    reduce_scatter x12 -> x4, waiting for transfers between devices: 495 us -> 95.1 us  [the longest x2 54.5 us: backward(): lax.psum_scatter(g_normed_part, 'mp', scatter_dimension=0, tiled=True)]
    all_gather x12 -> x4, waiting for transfers between devices: 596 us -> 231 us  [the longest x2 155 us: gathered(): own = lax.all_gather(pack, 'mp', axis=0, tiled=True)]
    dynamic_update_slice x46 -> x1, local copies, waits for them, and re-layouts: 209 us -> 0.37 us  [shards(): lax.dynamic_update_slice(jnp.zeros((micro_count, heads_here * mp), F32),...]
    convert_element_type x39 -> x14, other arithmetic: 203 us -> 19.6 us  [the longest x2 4.54 us: backward(): qkv_grad = lax.psum(qkv_grad.astype(BF16), 'dp')]
    pallas_call x0 -> x6, Pallas kernels: none -> 171 us  [the longest x2 78.6 us: attend_back(): pl.pallas_call(functools.partial(attend_back_kernel, second, block, group...]
    reduce_sum x32 -> x5, other arithmetic: 89 us -> 5.44 us  [the longest x2 4.74 us: normalize_back(): return (g_rows, jnp.sum(grad * (rows_in * scale), axis=0))]
    another operation x8 -> x0, loops' own time: 77.7 us -> none  [the longest x3 23.3 us: attend(): blocks_out, log_totals = lax.map(one_block, block_starts)]
  transfers between devices with their start and end apart: 37 -> 28, of which waited for: 25 -> 12; matrix products, arithmetic and copies ran while one was open for 8% -> 21% of each run, Pallas kernels for 0% -> 11%
where the time goes in v1:
time: 1180 us; the launch traced here: 1170 us
  waiting for transfers between devices  588 us (50%)
  Pallas kernels  171 us (14%)
  matrix products  141 us (12%)
  other arithmetic  112 us (9%)
  local copies, waits for them, and re-layouts  70.4 us (6%)
  blocking collectives  58.4 us (5%)
  between operations  17.3 us (1%)
  starting transfers between devices  15.6 us (1%)
    psum x1, waiting for transfers between devices, backward(): qkv_grad = lax.psum(qkv_grad.astype(BF16), 'dp')  225 us
    all_gather x2, waiting for transfers between devices, gathered(): own = lax.all_gather(pack, 'mp', axis=0, tiled=True)  155 us
    dot_general x46, matrix products, mm(): return lax.dot_general(left, right, dims, preferred_element_type=F32)  141 us
    pallas_call x2, Pallas kernels, attend_back(): pl.pallas_call(functools.partial(attend_back_kernel, second, block, group...  78.6 us
    all_gather x2, waiting for transfers between devices, forward(): normed_all = lax.all_gather(normed, 'mp', axis=0, tiled=True)  76 us
    pallas_call x2, Pallas kernels, attend(): pl.pallas_call(functools.partial(attend_kernel, block, group), grid_spec=...  75.8 us
    reduce_scatter x2, waiting for transfers between devices, backward(): lax.psum_scatter(g_normed_part, 'mp', scatter_dimension=0, tiled=True)  54.5 us
    reduce_scatter x2, waiting for transfers between devices, backward(): grads = lax.psum_scatter(grads, 'mp', scatter_dimension=0, tiled=True)  40.5 us
  transfers between devices with their start and end apart: 28, of which 12 were waited for; matrix products, arithmetic and copies ran while one was open for 21% of the time, Pallas kernels for 11%

profile of v1, /device:TPU:0, one launch (start us, length us, event | category | flops | bytes accessed | tf_op | source)
XLA Modules:
  0.0 1173.8 jit_solution(9426955513214215671)
XLA Ops:
  7.2 2.6 pad_maximum_fusion.2
  14.2 4.5 collective-permute-done.2
  18.6 4.2 bitcast_select_fusion
  28.0 96.2 %all-gather.7.cloned.1.call-done = bf16[4736,1024]{1,0:T(8,128)(2,1)} async-done(((bf16[1184,1024]{1,0:T(8,128)(2,1)}), bf16[4736,1024]{1,0:T(8,128)(2,1)}) %all-gather.7.cloned.1.call-update) | async-done | bytes 9699344 | tf_op jit(solution)/shard_map/all_gather | solution.py:411
  128.6 3.7 fusion.47
  132.4 3.0 pad_maximum_fusion.7
  135.4 6.2 collective-permute-done.1
  141.6 3.7 broadcast_select_fusion.4
  145.3 34.0 %all-gather.5.cloned.1.call-done.x_ref = bf16[2048,1024]{1,0:T(8,128)(2,1)} async-done(((bf16[512,1024]{1,0:T(8,128)(2,1)}), bf16[2048,1024]{1,0:T(8,128)(2,1)}) %all-gather.5.cloned.1.call-update) | async-done | bytes 4194320 | tf_op jit(solution)/shard_map/all_gather | solution.py:437
  179.3 8.5 qkv_rope.2
  187.9 38.1 %attend.2 = (bf16[2048,256]{1,0:T(8,128)(2,1)}, f32[4,2048]{1,0:T(4,128)}) custom-call(s32[1]{0:T(128)} %bitcast.3.len_ref, bf16[2048,256]{1,0:T(8,128)(2,1)} %get-tuple-element.23.q_ref, bf16[2048,256]{1,0:T(8,128)(2,1)} %get-tuple-element.24.k_ref, bf16[2048,256]{1,0:T(8,128)(2,1)} %get-tuple-element.25.v_ref.refs_0_), custom_call_target="tpu_custom_call" | custom-call | tf_op jit(solution)/shard_map/attend/pallas_call | solution.py:178
  226.0 4.2 all-to-all-start
  230.3 59.0 %all-gather.11.cloned.1.call-done = bf16[4736,1024]{1,0:T(8,128)(2,1)} async-done(((bf16[1184,1024]{1,0:T(8,128)(2,1)}), bf16[4736,1024]{1,0:T(8,128)(2,1)}) %all-gather.11.cloned.1.call-update) | async-done | bytes 9699344 | tf_op jit(solution)/shard_map/all_gather | solution.py:411
  289.4 6.2 fusion.64
  295.6 3.0 broadcast_select_fusion.9
  298.6 5.8 fusion.63
  304.4 4.6 multiply_reduce_fusion.6
  313.9 3.4 multiply_convert_fusion.11
  319.7 3.5 multiply_convert_fusion.10
  326.5 6.3 fusion.62
  337.5 42.0 %all-gather.9.cloned.1.call-done.x_ref = bf16[2048,1024]{1,0:T(8,128)(2,1)} async-done(((bf16[512,1024]{1,0:T(8,128)(2,1)}), bf16[2048,1024]{1,0:T(8,128)(2,1)}) %all-gather.9.cloned.1.call-update) | async-done | bytes 4194320 | tf_op jit(solution)/shard_map/all_gather | solution.py:437
  379.5 8.2 qkv_rope.3
  387.7 37.7 %attend.3 = (bf16[2048,256]{1,0:T(8,128)(2,1)}, f32[4,2048]{1,0:T(4,128)}) custom-call(s32[1]{0:T(128)} %bitcast.3.len_ref, bf16[2048,256]{1,0:T(8,128)(2,1)} %get-tuple-element.27.q_ref, bf16[2048,256]{1,0:T(8,128)(2,1)} %get-tuple-element.28.k_ref, bf16[2048,256]{1,0:T(8,128)(2,1)} %get-tuple-element.29.v_ref), custom_call_target="tpu_custom_call" | custom-call | tf_op jit(solution)/shard_map/attend/pallas_call | solution.py:178
  425.4 4.2 all-to-all-start.1
  429.7 6.0 fusion.61
  437.4 5.0 fusion.41
  442.4 3.2 multiply_reduce_fusion.5
  450.5 3.7 constant_dynamic-update-slice_fusion.8
  456.2 2.6 constant_dynamic-update-slice_fusion.6
  460.7 3.4 fusion.72
  467.2 5.2 multiply_convert_fusion.6
  476.1 2.9 multiply_reduce_fusion
  484.7 19.0 %all_to_all.20 = bf16[4,512,256]{2,1,0:T(8,128)(2,1)} all-to-all(bf16[4,512,256]{2,1,0:T(8,128)(2,1)S(1)} %bitcast.255), channel_id=1, replica_groups=mesh['section'=2,'dp'=4,'mp'=4] {'mp'}, dimensions={0} | all-to-all | bytes 2097152 | tf_op jit(solution)/shard_map/all_to_all | solution.py:431
  503.7 38.9 %attend_back.2 = bf16[2048,768]{1,0:T(8,128)(2,1)} custom-call(s32[1]{0:T(128)} %bitcast.3.len_ref, bf16[2048,256]{1,0:T(8,128)(2,1)} %get-tuple-element.27.q_ref, bf16[2048,256]{1,0:T(8,128)(2,1)} %get-tuple-element.28.k_ref, bf16[2048,256]{1,0:T(8,128)(2,1)} %get-tuple-element.29.v_ref, bf16[2048,256]{1,0:T(8,128)(2,1)} %get-tuple-element.30.o_ref, ...), custom_call_target="tpu_custom_call" | custom-call | tf_op jit(solution)/shard_map/attend_back/pallas_call | solution.py:298
  542.6 6.9 convolution_convert_fusion.1
  552.1 3.3 convolution_convert_fusion.2
  555.6 3.4 fusion.45
  562.9 3.7 add_convert_fusion
  566.6 3.6 add_convert_fusion.1
  570.3 3.5 add_convert_fusion.2
  573.8 14.7 %pad_maximum_fusion.1 = bf16[4,1184,1024]{2,1,0:T(8,128)(2,1)} fusion(bf16[4,128,1024]{2,1,0:T(8,128)(2,1)S(1)} %fusion.22, bf16[4,352,1024]{2,1,0:T(8,128)(2,1)S(1)} %bitcast.242, bf16[4,352,1024]{2,1,0:T(8,128)(2,1)S(1)} %bitcast.244, bf16[4,352,1024]{2,1,0:T(8,128)(2,1)S(1)} %bitcast.246), kind=kLoop, calls=%fused_computation.1 | loop fusion | flops 38797312 | bytes 19398656 | tf_op jit(solution)/shard_map/concatenate | solution.py:491
  588.6 12.3 %reduce-scatter.5.cloned.1.call-done = bf16[512,1024]{1,0:T(8,128)(2,1)} async-done(((bf16[2048,1024]{1,0:T(8,128)(2,1)}), bf16[512,1024]{1,0:T(8,128)(2,1)}) %reduce-scatter.5.cloned.1.call-update) | async-done | bytes 1048592 | tf_op jit(solution)/shard_map/reduce_scatter | solution.py:474
  603.3 3.3 fusion.59
  606.6 5.7 constant_dynamic-update-slice_fusion.4
  621.8 4.2 fusion.80
  627.2 2.6 multiply_convert_fusion.2
  646.0 3.8 add_convert_fusion.3
  649.9 3.7 add_convert_fusion.4
  653.6 3.6 add_convert_fusion.5
  657.1 14.3 %pad_maximum_fusion = bf16[4,1184,1024]{2,1,0:T(8,128)(2,1)} fusion(bf16[4,128,1024]{2,1,0:T(8,128)(2,1)S(1)} %fusion.23, bf16[4,352,1024]{2,1,0:T(8,128)(2,1)S(1)} %bitcast.243, bf16[4,352,1024]{2,1,0:T(8,128)(2,1)S(1)} %bitcast.245, bf16[4,352,1024]{2,1,0:T(8,128)(2,1)S(1)} %bitcast.247), kind=kLoop, calls=%fused_computation | loop fusion | flops 38797312 | bytes 19398656 | tf_op jit(solution)/shard_map/concatenate | solution.py:491
  677.2 3.5 all-to-all-start.3
  683.0 23.5 %all-to-all-done.3 = bf16[4,512,256]{2,1,0:T(8,128)(2,1)S(1)} async-done(((bf16[4,512,256]{2,1,0:T(8,128)(2,1)}), bf16[4,512,256]{2,1,0:T(8,128)(2,1)S(1)}, u32[]{:S(2)}, u32[]{:S(2)}) %all-to-all-start.3) | async-done | bytes 1048608 | tf_op jit(solution)/shard_map/all_to_all | solution.py:431
  707.4 39.7 %attend_back.3 = bf16[2048,768]{1,0:T(8,128)(2,1)} custom-call(s32[1]{0:T(128)} %bitcast.3.len_ref, bf16[2048,256]{1,0:T(8,128)(2,1)} %get-tuple-element.23.q_ref, bf16[2048,256]{1,0:T(8,128)(2,1)} %get-tuple-element.24.k_ref, bf16[2048,256]{1,0:T(8,128)(2,1)} %get-tuple-element.25.v_ref.refs_0_, bf16[2048,256]{1,0:T(8,128)(2,1)} %get-tuple-element.26.o_ref, ...), custom_call_target="tpu_custom_call" | custom-call | tf_op jit(solution)/shard_map/attend_back/pallas_call | solution.py:298
  747.2 6.9 convolution_convert_fusion
  754.3 7.1 convolution_convert_fusion.4
  762.5 3.7 convolution_convert_fusion.5
  772.7 40.5 %reduce-scatter.9.cloned.1.call-done = bf16[1184,1024]{1,0:T(8,128)(2,1)} async-done(((bf16[4736,1024]{1,0:T(8,128)(2,1)}), bf16[1184,1024]{1,0:T(8,128)(2,1)}) %reduce-scatter.9.cloned.1.call-update) | async-done | bytes 2424848 | tf_op jit(solution)/shard_map/reduce_scatter | solution.py:500
  824.2 3.3 broadcast_select_fusion.11
  827.5 42.2 %reduce-scatter.7.cloned.1.call-done = bf16[512,1024]{1,0:T(8,128)(2,1)} async-done(((bf16[2048,1024]{1,0:T(8,128)(2,1)}), bf16[512,1024]{1,0:T(8,128)(2,1)}) %reduce-scatter.7.cloned.1.call-update) | async-done | bytes 1048592 | tf_op jit(solution)/shard_map/reduce_scatter | solution.py:474
  872.2 4.5 select_convert_fusion
  876.7 225.0 %all-reduce.4.cloned.1.call-done = (bf16[512,768]{1,0:T(8,128)(2,1)}, bf16[512,768]{1,0:T(8,128)(2,1)}, bf16[1184,1024]{1,0:T(8,128)(2,1)}, bf16[1184,1024]{1,0:T(8,128)(2,1)}) async-done(((bf16[512,768]{1,0:T(8,128)(2,1)}, bf16[512,768]{1,0:T(8,128)(2,1)}, bf16[1184,1024]{1,0:T(8,128)(2,1)}, bf16[1184,1024]{1,0:T(8,128)(2,1)}), (bf16[512,768]{1,0:T(8,128)(2,1)}, bf16[512,768]{1,0:T(8,128)(2,1)}, ...) | async-done | bytes 6422544 | tf_op jit(solution)/shard_map/psum | solution.py:504
  1101.7 3.5 broadcast_select_fusion.2
  1108.1 39.4 %all-reduce = (f32[2,16]{1,0:T(2,128)}, f32[4,1024]{1,0:T(4,128)S(1)}) all-reduce(f32[2,16]{1,0:T(2,128)S(1)} %dynamic_update_slice.3, f32[4,1024]{1,0:T(4,128)S(1)} %pad_maximum_fusion.9), channel_id=1, replica_groups=mesh['section'=2,'dp'=4,'mp'=4] {'section','dp','mp'}, use_global_device_ids=true, to_apply=%region_12.13 | all-reduce | flops 4128 | bytes 33024 | tf_op jit(solution)/shard_map/psum | solution.py:542
  1151.1 2.6 maximum_bitcast_fusion
  (333 shorter events, 135.4 us)
Async XLA Ops:
  7.2 117.0 %all-gather.7.cloned.1.call-start = ((), (), s32[]{:S(2)}) async-start(), calls=%async_computation.9 | async-start | bytes 12124160 | tf_op jit(solution)/shard_map/all_gather | solution.py:411
  13.7 4.9 collective-permute-start.2
  14.2 8.8 copy-start.78
  14.2 8.8 copy-start.79
  22.9 156.4 %all-gather.5.cloned.1.call-start = ((), (), s32[]{:S(2)}) async-start(), calls=%async_computation.8 | async-start | bytes 5242880 | tf_op jit(solution)/shard_map/all_gather | solution.py:437
  23.0 1.8 collective-permute-start
  24.7 99.4 %copy-start.52 = (bf16[1,1024,256]{2,1,0:T(8,128)(2,1)S(1)}, bf16[1,1024,256]{2,1,0:T(8,128)(2,1)}, u32[]{:S(2)}) copy-start(bf16[1,1024,256]{2,1,0:T(8,128)(2,1)} %param.18) | copy-start | bytes 1572868
  24.7 99.4 %copy-start.53 = (bf16[1,1024,256]{2,1,0:T(8,128)(2,1)S(1)}, bf16[1,1024,256]{2,1,0:T(8,128)(2,1)}, u32[]{:S(2)}) copy-start(bf16[1,1024,256]{2,1,0:T(8,128)(2,1)} %param.17) | copy-start | bytes 1572868
  25.3 283.7 %copy-start.67 = (f32[1,1024]{1,0:T(1,128)}, f32[1,1024]{1,0:T(1,128)S(1)}, u32[]{:S(2)}) copy-start(f32[1,1024]{1,0:T(1,128)S(1)} %get-tuple-element.135) | copy-start | bytes 12292
  27.2 98.7 %copy-start.82 = (s32[2,1]{0,1:T(1,128)S(1)}, s32[2,1]{0,1:T(1,128)}, u32[]{:S(2)}) copy-start(s32[2,1]{0,1:T(1,128)} %param.13) | copy-start | bytes 28
  27.2 262.1 %all-gather.11.cloned.1.call-start = ((), (), s32[]{:S(2)}) async-start(), calls=%async_computation.11 | async-start | bytes 12124160 | tf_op jit(solution)/shard_map/all_gather | solution.py:411
  124.2 171.4 %collective-permute-start.3 = (bf16[4736,1024]{1,0:T(8,128)(2,1)}, bf16[4736,1024]{1,0:T(8,128)(2,1)}, u32[]{:S(2)}, u32[]{:S(2)}) collective-permute-start(bf16[4736,1024]{1,0:T(8,128)(2,1)} %all-gather.7.cloned.1.call-done), channel_id=1, source_target_pairs={{0,16},{16,0},{1,17},{17,1},{2,18},{18,2},{3,19},{19,3},{4,20},{20... | collective-permute-start | bytes 29097992 | tf_op jit(solution)/shard_map/ppermute | solution.py:342
  125.3 16.3 %collective-permute-start.1 = (bf16[1024,768]{1,0:T(8,128)(2,1)S(1)}, bf16[1024,768]{1,0:T(8,128)(2,1)}, u32[]{:S(2)}, u32[]{:S(2)}) collective-permute-start(bf16[1024,768]{1,0:T(8,128)(2,1)S(1)} %pad_maximum_fusion.6), channel_id=1, source_target_pairs={{0,16},{16,0},{1,17},{17,1},{2,18},{18,2},{3,19},{19,3},{4,20},{20... | collective-permute-start | bytes 4718600 | tf_op jit(solution)/shard_map/ppermute | solution.py:342
  132.3 9.3 copy-start.54
  226.0 78.4 %all-to-all-start = ((bf16[4,512,256]{2,1,0:T(8,128)(2,1)}), bf16[4,512,256]{2,1,0:T(8,128)(2,1)}, u32[]{:S(2)}, u32[]{:S(2)}) async-start(bf16[4,512,256]{2,1,0:T(8,128)(2,1)} %bitcast.252), calls=%async_computation | async-start | bytes 2097152 | tf_op jit(solution)/shard_map/all_to_all | solution.py:426
  230.3 149.2 %all-gather.9.cloned.1.call-start = ((), (), s32[]{:S(2)}) async-start(), calls=%async_computation.10 | async-start | bytes 5242880 | tf_op jit(solution)/shard_map/all_gather | solution.py:437
  289.3 43.4 %collective-permute-start.4 = (bf16[4736,1024]{1,0:T(8,128)(2,1)}, bf16[4736,1024]{1,0:T(8,128)(2,1)}, u32[]{:S(2)}, u32[]{:S(2)}) collective-permute-start(bf16[4736,1024]{1,0:T(8,128)(2,1)} %all-gather.11.cloned.1.call-done), channel_id=1, source_target_pairs={{0,16},{16,0},{1,17},{17,1},{2,18},{18,2},{3,19},{19,3},{4,20},{20... | collective-permute-start | bytes 29097992 | tf_op jit(solution)/shard_map/ppermute | solution.py:342
  304.4 4.9 copy-start.8
  308.9 14.2 %copy-start = (f32[512,1024]{1,0:T(8,128)}, f32[512,1024]{1,0:T(8,128)S(1)}, u32[]{:S(2)}) copy-start(f32[512,1024]{1,0:T(8,128)S(1)} %get-tuple-element.119) | copy-start | bytes 6291460
  309.2 9.9 copy-start.61
  311.1 8.1 copy-start.31
  313.7 3.6 copy-start.91
  313.9 3.4 copy-start.42
  319.7 3.5 copy-start.45
  325.1 278.1 %copy-start.6 = (bf16[512,1024]{1,0:T(8,128)(2,1)}, bf16[512,1024]{1,0:T(8,128)(2,1)S(1)}, u32[]{:S(2)}) copy-start(bf16[512,1024]{1,0:T(8,128)(2,1)S(1)} %get-tuple-element.125) | copy-start | bytes 3145732
  425.4 17.0 %all-to-all-start.1 = ((bf16[4,512,256]{2,1,0:T(8,128)(2,1)}), bf16[4,512,256]{2,1,0:T(8,128)(2,1)}, u32[]{:S(2)}, u32[]{:S(2)}) async-start(bf16[4,512,256]{2,1,0:T(8,128)(2,1)} %bitcast.256), calls=%async_computation.1 | async-start | bytes 2097152 | tf_op jit(solution)/shard_map/all_to_all | solution.py:426
  429.7 171.2 %reduce-scatter.5.cloned.1.call-start = ((), (), s32[]{:S(2)}) async-start(), calls=%async_computation.12 | async-start | bytes 5242880 | tf_op jit(solution)/shard_map/reduce_scatter | solution.py:474
  445.9 14.8 %copy-start.63 = (bf16[512,1024]{1,0:T(8,128)(2,1)}, bf16[512,1024]{1,0:T(8,128)(2,1)S(1)}, u32[]{:S(2)}) copy-start(bf16[512,1024]{1,0:T(8,128)(2,1)S(1)} %multiply_convert_fusion.12) | copy-start | bytes 3145732
  481.5 81.4 %collective-permute-start.13 = (bf16[512,6272]{1,0:T(8,128)(2,1)}, bf16[512,6272]{1,0:T(8,128)(2,1)}, u32[]{:S(2)}, u32[]{:S(2)}) collective-permute-start(bf16[512,6272]{1,0:T(8,128)(2,1)} %fusion.46), channel_id=1, source_target_pairs={{0,16},{16,0},{1,17},{17,1},{2,18},{18,2},{3,19},{19,3},{4,20},{20... | collective-permute-start | bytes 19267592 | tf_op jit(solution)/shard_map/ppermute | solution.py:342
  503.7 38.9 %copy-start.22 = (bf16[1024,768]{1,0:T(8,128)(2,1)S(1)}, bf16[1024,768]{1,0:T(8,128)(2,1)}, u32[]{:S(2)}) copy-start(bf16[1024,768]{1,0:T(8,128)(2,1)} %get-tuple-element.93.w_ref) | copy-start | bytes 4718596
  549.5 223.1 %reduce-scatter.11.cloned.1.call-start = ((), (), s32[]{:S(2)}) async-start(), calls=%async_computation.15 | async-start | bytes 12124160 | tf_op jit(solution)/shard_map/reduce_scatter | solution.py:500
  552.1 3.4 copy-start.89
  555.5 7.0 collective-permute-start.14
  555.5 3.5 copy-start.64
  555.6 3.5 copy-start.88
  588.6 224.6 %reduce-scatter.9.cloned.1.call-start = ((), (), s32[]{:S(2)}) async-start(), calls=%async_computation.14 | async-start | bytes 12124160 | tf_op jit(solution)/shard_map/reduce_scatter | solution.py:500
  606.6 11.6 copy-start.13
  619.3 26.7 %collective-permute-start.11 = (bf16[512,6272]{1,0:T(8,128)(2,1)}, bf16[512,6272]{1,0:T(8,128)(2,1)}, u32[]{:S(2)}, u32[]{:S(2)}) collective-permute-start(bf16[512,6272]{1,0:T(8,128)(2,1)} %constant_dynamic-update-slice_fusion), channel_id=1, source_target_pairs={{0,16},{16,0},{1,17},{17,1},{2,18},{18,2},{3,19},{19,3},{4,20},{20... | collective-permute-start | bytes 19267592 | tf_op jit(solution)/shard_map/ppermute | solution.py:342
  621.7 4.2 copy-start.14
  621.8 4.2 copy-start.43
  621.8 4.6 copy-start.92
  621.8 5.4 copy-start.93
  639.6 6.0 collective-permute-start.12
  677.2 29.3 %all-to-all-start.3 = ((bf16[4,512,256]{2,1,0:T(8,128)(2,1)}), bf16[4,512,256]{2,1,0:T(8,128)(2,1)S(1)}, u32[]{:S(2)}, u32[]{:S(2)}) async-start(bf16[4,512,256]{2,1,0:T(8,128)(2,1)} %bitcast.254), calls=%async_computation.4 | async-start | bytes 2097152 | tf_op jit(solution)/shard_map/all_to_all | solution.py:431
  680.7 189.1 %reduce-scatter.7.cloned.1.call-start = ((), (), s32[]{:S(2)}) async-start(), calls=%async_computation.13 | async-start | bytes 5242880 | tf_op jit(solution)/shard_map/reduce_scatter | solution.py:474
  707.4 39.7 %copy-start.21 = (bf16[1024,768]{1,0:T(8,128)(2,1)S(1)}, bf16[1024,768]{1,0:T(8,128)(2,1)}, u32[]{:S(2)}) copy-start(bf16[1024,768]{1,0:T(8,128)(2,1)} %get-tuple-element.94.w_ref) | copy-start | bytes 4718596
  754.1 347.6 %all-reduce.4.cloned.1.call-start = ((), (), s32[]{:S(2)}) async-start(), calls=%async_computation.16 | async-start | bytes 12845056 | tf_op jit(solution)/shard_map/psum | solution.py:504
  754.3 8.2 copy-start.27
  754.3 8.2 copy-start.30
  761.5 4.7 copy-start.55
  762.5 5.6 collective-permute-start.9
  767.6 2.9 collective-permute-start.8
  814.4 2.8 collective-permute-start.7
  824.2 45.6 %copy-start.72 = (f32[1,1024]{1,0:T(1,128)S(1)}, f32[1,1024]{1,0:T(1,128)}, u32[]{:S(2)}) copy-start(f32[1,1024]{1,0:T(1,128)} %copy-done.71) | copy-start | bytes 12292
  824.2 45.6 %copy-start.74 = (f32[512]{0:T(512)S(1)}, f32[512]{0:T(512)}, u32[]{:S(2)}) copy-start(f32[512]{0:T(512)} %copy-done.73) | copy-start | bytes 6148
  824.2 48.0 %copy-start.76 = (f32[512]{0:T(512)S(1)}, f32[512]{0:T(512)}, u32[]{:S(2)}) copy-start(f32[512]{0:T(512)} %copy-done.75) | copy-start | bytes 6148
  827.5 44.7 %copy-start.5 = (f32[512,1024]{1,0:T(8,128)S(1)}, f32[512,1024]{1,0:T(8,128)}, u32[]{:S(2)}) copy-start(f32[512,1024]{1,0:T(8,128)} %get-tuple-element.60) | copy-start | bytes 6291460
  827.5 277.6 %collective-permute-start.5 = (bf16[512,1024]{1,0:T(8,128)(2,1)}, bf16[512,1024]{1,0:T(8,128)(2,1)}, u32[]{:S(2)}, u32[]{:S(2)}) collective-permute-start(bf16[512,1024]{1,0:T(8,128)(2,1)} %get-tuple-element.129), channel_id=1, source_target_pairs={{0,16},{16,0},{1,17},{17,1},{2,18},{18,2},{3,19},{19,3},{4,20},{20... | collective-permute-start | bytes 3145736 | tf_op jit(solution)/shard_map/ppermute | solution.py:342
  876.7 271.9 %collective-permute-start.6 = (bf16[512,1024]{1,0:T(8,128)(2,1)}, bf16[512,1024]{1,0:T(8,128)(2,1)}, u32[]{:S(2)}, u32[]{:S(2)}) collective-permute-start(bf16[512,1024]{1,0:T(8,128)(2,1)} %get-tuple-element.57), channel_id=1, source_target_pairs={{0,16},{16,0},{1,17},{17,1},{2,18},{18,2},{3,19},{19,3},{4,20},{20... | collective-permute-start | bytes 3145736 | tf_op jit(solution)/shard_map/ppermute | solution.py:342
  1101.7 3.5 copy-start.66
  1105.1 50.7 %collective-permute-start.15 = (bf16[1184,1024]{1,0:T(8,128)(2,1)}, bf16[1184,1024]{1,0:T(8,128)(2,1)}, u32[]{:S(2)}, u32[]{:S(2)}) collective-permute-start(bf16[1184,1024]{1,0:T(8,128)(2,1)} %broadcast_select_fusion.2), channel_id=1, source_target_pairs={{0,16},{16,0},{1,17},{17,1},{2,18},{18,2},{3,19},{19,3},{4,20},{20... | collective-permute-start | bytes 7274504 | tf_op jit(solution)/shard_map/ppermute | solution.py:342
  1106.6 40.9 %copy-start.28 = (bf16[512,768]{1,0:T(8,128)(2,1)S(1)}, bf16[512,768]{1,0:T(8,128)(2,1)}, u32[]{:S(2)}) copy-start(bf16[512,768]{1,0:T(8,128)(2,1)} %get-tuple-element.43) | copy-start | bytes 2359300
  1147.6 6.1 collective-permute-start.10
  1154.1 3.5 copy-start.12
  (58 other events, 118.0 us)
Sparse Core Ops, SparseCore 0:
  23.0 101.1 all-gather.6
  126.6 52.6 all-gather.4
  181.8 107.5 all-gather.10
  326.6 52.8 all-gather.8
  549.6 51.2 reduce-scatter.4
  604.2 108.3 reduce-scatter.10
  716.0 97.1 reduce-scatter.8
  817.0 52.6 reduce-scatter.6
  873.5 228.0 all-reduce.3

commit v2 on v1

v2 whole, which is shorter than its diff:
```python
import functools

import jax
import jax.numpy as jnp
from jax import lax
from jax.experimental import pallas as pl
from jax.experimental.pallas import tpu as pltpu
from jax.sharding import PartitionSpec as P

HEAD_DIM = 64
HALF = HEAD_DIM // 2
EPS = 1e-05
SCALE = HEAD_DIM**-0.5
F32 = jnp.float32
BF16 = jnp.bfloat16
VMEM_BYTES = 56 * 1024 * 1024

NT = (((1,), (1,)), ((), ()))
NN = (((1,), (0,)), ((), ()))
TN = (((0,), (0,)), ((), ()))


def cost(micros):
    return pl.CostEstimate(flops=int(micros * 1.15e9), transcendentals=0, bytes_accessed=1 << 20)


def mm(left, right, dims=NN):
    return lax.dot_general(left, right, dims, preferred_element_type=F32)


def swap_halves(tensor):
    width = tensor.shape[1]
    if width % 128 == 0:
        lane = lax.broadcasted_iota(jnp.int32, tensor.shape, 1)
        ahead = pltpu.roll(tensor, width - HALF, 1)
        behind = pltpu.roll(tensor, HALF, 1)
        return jnp.where(lane % HEAD_DIM < HALF, ahead, behind)
    return jnp.concatenate([tensor[:, HALF:], tensor[:, :HALF]], axis=1)


def qkv_kernel(second, group, parts, fresh, place_ref, *refs):
    piece_refs, refs = refs[:parts], refs[parts:]
    w_ref, cos_ref, sin_ref = refs[:3]
    refs = refs[3:]
    if second:
        first_ref, refs = refs[0], refs[1:]
    if not fresh:
        refs = refs[3:]
    q_ref, k_ref, v_ref = refs
    width = q_ref.shape[1]
    rows = piece_refs[0][...]
    if parts == 2:
        rows = jnp.where(pl.program_id(0) == 0, rows, piece_refs[1][...])
    acc = mm(rows, w_ref[...])
    cosine, sine = cos_ref[...], sin_ref[...]
    for at in range(0, width, group):
        part = acc[:, at : at + group]
        turned = part * cosine + swap_halves(part) * sine
        q_ref[:, at : at + group] = (turned * SCALE).astype(BF16)
        part = acc[:, width + at : width + at + group]
        turned = part * cosine + swap_halves(part) * sine
        k_ref[:, at : at + group] = turned.astype(BF16)
    value = acc[:, 2 * width :]
    if second:
        value = 0.5 * value + 0.5 * first_ref[...].astype(F32)
    v_ref[...] = value.astype(BF16)


def project_qkv(pieces, place, weight, cosine, sine, first, held):
    rows, model = cosine.shape[0], weight.shape[0]
    width = weight.shape[1] // 3
    group = min(width, 128)
    chunk = sum(piece.shape[0] for piece in pieces)
    parts = len(pieces)
    block = pieces[0].shape[0] if parts == 2 else min(512, chunk)
    steps = chunk // block
    second = first is not None
    fresh = held is None

    def at_place(i, place_ref):
        return (place_ref[0] * steps + i, 0)

    row_spec = pl.BlockSpec((block, width), at_place)
    if parts == 2:
        piece_specs = [pl.BlockSpec((block, model), lambda i, p: (0, 0))] * 2
    else:
        piece_specs = [pl.BlockSpec((block, model), lambda i, p: (i, 0))]
    in_specs = piece_specs + [
        pl.BlockSpec((model, 3 * width), lambda i, p: (0, 0)),
        pl.BlockSpec((block, group), at_place),
        pl.BlockSpec((block, group), at_place),
    ]
    args = [*pieces, weight, cosine, sine]
    if second:
        in_specs.append(row_spec)
        args.append(first)
    aliases = {}
    if not fresh:
        aliases = {1 + len(args) + i: i for i in range(3)}
        in_specs += [pl.BlockSpec(memory_space=pl.ANY)] * 3
        args += list(held)
    shape = jax.ShapeDtypeStruct((rows, width), BF16)
    return pl.pallas_call(
        functools.partial(qkv_kernel, second, group, parts, fresh),
        grid_spec=pltpu.PrefetchScalarGridSpec(
            num_scalar_prefetch=1,
            grid=(steps,),
            in_specs=in_specs,
            out_specs=[row_spec] * 3,
        ),
        out_shape=[shape] * 3,
        input_output_aliases=aliases,
        compiler_params=pltpu.CompilerParams(vmem_limit_bytes=VMEM_BYTES),
        cost_estimate=cost(4),
        name="qkv_rope",
    )(place, *args)


def head_lanes(value, head, group):
    per = group // HEAD_DIM
    if per == 1:
        return value
    lane = lax.broadcasted_iota(jnp.int32, value.shape, 1)
    return jnp.where(lane // HEAD_DIM == head % per, value, jnp.zeros_like(value))


def attend_kernel(block, group, parts, info_ref, q_ref, k_ref, v_ref, *refs):
    o_refs, refs = refs[:parts], refs[parts:]
    lse_ref, vt_ref, acc_ref, top_ref, sum_ref, all_ref = refs
    rows, width = k_ref.shape
    heads = width // HEAD_DIM
    per = group // HEAD_DIM
    chunk = rows // parts
    small = min(block, chunk)
    step = pl.program_id(0)
    seg_len = info_ref[0]
    place = info_ref[1]

    @pl.when(step == 0)
    def _():
        for at in range(0, rows, small):
            vt_ref[:, at : at + small] = v_ref[at : at + small, :].astype(F32).T.astype(BF16)

    q_heads = []
    for head in range(heads):
        at = head // per * group
        q_heads.append(head_lanes(q_ref[:, at : at + group], head, group))

    def one(col, masked):
        key_rows = pl.ds(pl.multiple_of(col * block, block), block)
        for head in range(heads):
            at = head // per * group
            own = slice(head * HEAD_DIM, (head + 1) * HEAD_DIM)
            scores = mm(k_ref[key_rows, at : at + group], q_heads[head], NT)
            if masked:
                r = lax.broadcasted_iota(jnp.int32, scores.shape, 0)
                c = lax.broadcasted_iota(jnp.int32, scores.shape, 1)
                scores = jnp.where(r <= c, scores, -1e30)
            top = jnp.max(scores, axis=0, keepdims=True)
            if not masked:
                old = top_ref[head : head + 1, :]
                top = jnp.maximum(top, old)
            probs = jnp.exp(scores - top)
            count = jnp.sum(probs, axis=0, keepdims=True)
            total = mm(vt_ref[own, key_rows], probs.astype(BF16))
            if not masked:
                shrink = jnp.exp(old - top)
                count = count + sum_ref[head : head + 1, :] * shrink
                total = total + acc_ref[own, :] * shrink
            acc_ref[own, :] = total
            top_ref[head : head + 1, :] = top
            sum_ref[head : head + 1, :] = count

    one(step, True)

    @pl.loop(step * block // seg_len * (seg_len // block), step)
    def _(col):
        one(col, False)

    lse_ref[...] = top_ref[:heads, :] + jnp.log(sum_ref[:heads, :])
    for head in range(heads):
        own = slice(head * HEAD_DIM, (head + 1) * HEAD_DIM)
        acc_ref[own, :] = acc_ref[own, :] * (1.0 / sum_ref[head : head + 1, :])
    for at in range(0, block, small):
        turned = acc_ref[:, at : at + small].T.astype(BF16)
        if parts == 1:
            target = step * block + at
        else:
            target = jnp.bitwise_xor(step * (block // chunk) + at // chunk, place) * chunk + at % chunk
        all_ref[pl.ds(pl.multiple_of(target, small), small), :] = turned

    @pl.when(step == pl.num_programs(0) - 1)
    def _():
        for part in range(parts):
            o_refs[part][...] = all_ref[part * chunk : (part + 1) * chunk, :]


def attend(queries, keys, values, info, parts):
    rows, width = queries.shape
    group = min(width, 128)
    heads = width // HEAD_DIM
    block = rows // 2
    chunk = rows // parts
    whole = pl.BlockSpec((rows, width), lambda i, n: (0, 0))
    results = pl.pallas_call(
        functools.partial(attend_kernel, block, group, parts),
        grid_spec=pltpu.PrefetchScalarGridSpec(
            num_scalar_prefetch=1,
            grid=(rows // block,),
            in_specs=[pl.BlockSpec((block, width), lambda i, n: (i, 0)), whole, whole],
            out_specs=[pl.BlockSpec((chunk, width), lambda i, n: (0, 0))] * parts
            + [pl.BlockSpec((heads, block), lambda i, n: (0, i))],
            scratch_shapes=[
                pltpu.VMEM((width, rows), BF16),
                pltpu.VMEM((width, block), F32),
                pltpu.VMEM((8, block), F32),
                pltpu.VMEM((8, block), F32),
                pltpu.VMEM((rows, width), BF16),
            ],
        ),
        out_shape=[jax.ShapeDtypeStruct((chunk, width), BF16)] * parts
        + [jax.ShapeDtypeStruct((heads, rows), F32)],
        compiler_params=pltpu.CompilerParams(vmem_limit_bytes=VMEM_BYTES),
        cost_estimate=cost(18),
        name="attend",
    )(info, queries, keys, values)
    return results[:parts], results[parts]


def attend_back_kernel(second, block, strip, group, parts, info_ref, q_ref, k_ref, v_ref, lse_ref, cos_ref, sin_ref, *refs):
    o_refs, refs = refs[:parts], refs[parts:]
    do_refs, refs = refs[:parts], refs[parts:]
    if not second:
        first_refs, refs = refs[:parts], refs[parts:]
    out_refs, refs = refs[:parts], refs[parts:]
    do_ref, all_ref, dq_ref, dk_ref, dv_ref, delta_ref = refs
    rows, width = q_ref.shape
    heads = width // HEAD_DIM
    per = group // HEAD_DIM
    chunk = rows // parts
    small = min(block, chunk)
    step = pl.program_id(0)
    steps = rows // block
    seg_len = info_ref[0]
    place = info_ref[1]

    @pl.when(step == 0)
    def _():
        dq_ref[...] = jnp.zeros_like(dq_ref)
        head = lax.broadcasted_iota(jnp.int32, (8, width), 0)
        lane = lax.broadcasted_iota(jnp.int32, (8, width), 1)
        pick = jnp.where(lane // HEAD_DIM == head, 1.0, 0.0).astype(F32)
        for part in range(parts):
            for at in range(0, chunk, small):
                grads = do_refs[part][at : at + small, :]
                prod = grads.astype(F32) * o_refs[part][at : at + small, :].astype(F32)
                delta = lax.dot_general(
                    pick, prod, NT, precision=lax.Precision.HIGHEST, preferred_element_type=F32
                )
                if parts == 1:
                    target = at
                else:
                    target = jnp.bitwise_xor(part, place) * chunk + at
                target = pl.ds(pl.multiple_of(target, small), small)
                do_ref[target, :] = grads
                delta_ref[:, target] = delta
            if not second:
                all_ref[part * chunk : (part + 1) * chunk, 2 * width :] = first_refs[part][...]

    dk_ref[...] = jnp.zeros_like(dk_ref)
    dv_ref[...] = jnp.zeros_like(dv_ref)
    base = step * block

    def one(key_off, key_size, query_start, query_size, masked):
        key_rows = pl.ds(pl.multiple_of(base + key_off, strip), key_size)
        query_rows = pl.ds(pl.multiple_of(query_start, strip), query_size)
        for pair in range(heads // per):
            at = pair * group
            keys = k_ref[key_rows, at : at + group]
            values = v_ref[key_rows, at : at + group]
            queries = q_ref[query_rows, at : at + group]
            grads = do_ref[query_rows, at : at + group]
            dq = dk = dv = None
            for sub in range(per):
                head = pair * per + sub
                q_one = head_lanes(queries, head, group)
                do_one = head_lanes(grads, head, group)
                scores = mm(keys, q_one, NT)
                if masked:
                    r = lax.broadcasted_iota(jnp.int32, scores.shape, 0)
                    c = lax.broadcasted_iota(jnp.int32, scores.shape, 1)
                    scores = jnp.where(r <= c, scores, -1e30)
                probs = jnp.exp(scores - lse_ref[head : head + 1, query_rows])
                g_probs = mm(values, do_one, NT)
                g_scores = (probs * (g_probs - delta_ref[head : head + 1, query_rows])).astype(BF16)
                dv_one = mm(probs.astype(BF16), do_one)
                dk_one = mm(g_scores, q_one)
                dq_one = mm(g_scores, head_lanes(keys, head, group), TN)
                dq = dq_one if dq is None else dq + dq_one
                dk = dk_one if dk is None else dk + dk_one
                dv = dv_one if dv is None else dv + dv_one
            dq_ref[query_rows, at : at + group] += dq
            dk_ref[key_off : key_off + key_size, at : at + group] += dk
            dv_ref[key_off : key_off + key_size, at : at + group] += dv

    for off in range(0, block, strip):
        one(off, strip, base + off, block - off, True)

    per_seg = seg_len // block

    @pl.loop(step + 1, (step // per_seg + 1) * per_seg)
    def _(row):
        one(0, block, row * block, block, False)

    def turn_back(value, at_rows):
        return value * cos_ref[at_rows, :] - swap_halves(value) * sin_ref[at_rows, :]

    for off in range(0, block, small):
        here = pl.ds(pl.multiple_of(base + off, small), small)
        if parts == 1:
            target = base + off
        else:
            target = jnp.bitwise_xor(step * (block // chunk) + off // chunk, place) * chunk + off % chunk
        target = pl.ds(pl.multiple_of(target, small), small)
        for at in range(0, width, group):
            g_query = turn_back(dq_ref[here, at : at + group] * SCALE, here)
            g_key = turn_back(dk_ref[off : off + small, at : at + group], here)
            all_ref[target, at : at + group] = g_query.astype(BF16)
            all_ref[target, width + at : width + at + group] = g_key.astype(BF16)
        g_value = dv_ref[off : off + small, :]
        if second:
            g_value = 0.5 * g_value
        else:
            g_value = g_value + all_ref[target, 2 * width :].astype(F32)
        all_ref[target, 2 * width :] = g_value.astype(BF16)

    @pl.when(step == steps - 1)
    def _():
        for part in range(parts):
            out_refs[part][...] = all_ref[part * chunk : (part + 1) * chunk, :]


def attend_back(queries, keys, values, lse, cosine, sine, attended, grads, g_first, info):
    rows, width = queries.shape
    parts = len(attended)
    group = min(width, 128)
    heads = width // HEAD_DIM
    block = rows // 2
    chunk = rows // parts
    second = g_first is None
    whole = pl.BlockSpec((rows, width), lambda i, n: (0, 0))
    table = pl.BlockSpec((rows, group), lambda i, n: (0, 0))
    piece = pl.BlockSpec((chunk, width), lambda i, n: (0, 0))
    in_specs = [whole] * 3 + [pl.BlockSpec((heads, rows), lambda i, n: (0, 0)), table, table] + [piece] * (2 * parts)
    args = [queries, keys, values, lse, cosine, sine, *attended, *grads]
    if not second:
        values_at = 2 if width % 128 == 0 else 0
        if values_at == 0:
            g_first = [part[:, 2 * width :] for part in g_first]
        in_specs += [pl.BlockSpec((chunk, width), lambda i, n: (0, values_at))] * parts
        args += list(g_first)
    return pl.pallas_call(
        functools.partial(attend_back_kernel, second, block, min(256, block), group, parts),
        grid_spec=pltpu.PrefetchScalarGridSpec(
            num_scalar_prefetch=1,
            grid=(rows // block,),
            in_specs=in_specs,
            out_specs=[pl.BlockSpec((chunk, 3 * width), lambda i, n: (0, 0))] * parts,
            scratch_shapes=[
                pltpu.VMEM((rows, width), BF16),
                pltpu.VMEM((rows, 3 * width), BF16),
                pltpu.VMEM((rows, width), F32),
                pltpu.VMEM((block, width), F32),
                pltpu.VMEM((block, width), F32),
                pltpu.VMEM((8, rows), F32),
            ],
        ),
        out_shape=[jax.ShapeDtypeStruct((chunk, 3 * width), BF16)] * parts,
        compiler_params=pltpu.CompilerParams(vmem_limit_bytes=VMEM_BYTES),
        cost_estimate=cost(36),
        name="attend_back",
    )(info, *args)


def out_kernel(info_ref, own_ref, other_ref, state_ref, gain_ref, *refs):
    att_refs = refs[:-3]
    middle_ref, normed_ref, full_ref = refs[-3:]
    mp, out_half, model = own_ref.shape
    low_core = info_ref[2] == 0
    square = mp == 4
    for at in range(mp):
        source = jnp.bitwise_xor(at, info_ref[1]) if square else at
        own, other = own_ref[source], other_ref[source]
        base = at * 2 * out_half
        full_ref[base : base + out_half, :] = jnp.where(low_core, own, other)
        full_ref[base + out_half : base + 2 * out_half, :] = jnp.where(low_core, other, own)
    total = state_ref[...].astype(F32)
    size = mp * 2 * out_half // len(att_refs)
    for part, att_ref in enumerate(att_refs):
        total = total + mm(att_ref[...], full_ref[part * size : (part + 1) * size, :])
    middle_ref[...] = total
    normed_ref[...] = normalize(total, gain_ref[...]).astype(BF16)


def out_project(attended, own, other, state, gain, info):
    rows, model = state.shape
    mp, out_half = own.shape[:2]
    whole = pl.BlockSpec((rows, model), lambda i, n: (0, 0))
    share = pl.BlockSpec(own.shape, lambda i, n: (0, 0, 0))
    full = (mp * 2 * out_half, model)
    return pl.pallas_call(
        out_kernel,
        grid_spec=pltpu.PrefetchScalarGridSpec(
            num_scalar_prefetch=1,
            grid=(1,),
            in_specs=[share, share, whole, pl.BlockSpec((1, model), lambda i, n: (0, 0))]
            + [pl.BlockSpec(part.shape, lambda i, n: (0, 0)) for part in attended],
            out_specs=[whole, whole, pl.BlockSpec(full, lambda i, n: (0, 0))],
        ),
        out_shape=[
            jax.ShapeDtypeStruct((rows, model), F32),
            jax.ShapeDtypeStruct((rows, model), BF16),
            jax.ShapeDtypeStruct(full, BF16),
        ],
        compiler_params=pltpu.CompilerParams(vmem_limit_bytes=VMEM_BYTES),
        cost_estimate=cost(5),
        name="out_project",
    )(info, own, other, state, gain.reshape(1, model), *attended)


def weight_copies(pieces_ref, wide_ref, sems):
    count, hidden, model = wide_ref.shape
    mp = pieces_ref.shape[0]
    size = hidden // mp
    groups = []
    for at in range(count):
        copies = []
        for part in range(mp):
            copies.append(
                pltpu.make_async_copy(
                    pieces_ref.at[part, pl.ds(at * size, size), :],
                    wide_ref.at[at, pl.ds(part * size, size), :],
                    sems.at[at, part],
                )
            )
        groups.append(copies)
    return groups


def ffn_kernel(x_ref, base_ref, pieces_ref, out_ref, silu_ref, slope_ref, act_ref, wide_ref, sems):
    groups = weight_copies(pieces_ref, wide_ref, sems)
    for copies in groups:
        for copy in copies:
            copy.start()
    for copy in groups[0]:
        copy.wait()
    gate = mm(x_ref[...], wide_ref[0], NT)
    for copy in groups[1]:
        copy.wait()
    up = mm(x_ref[...], wide_ref[1], NT)
    sig = 0.5 + 0.5 * jnp.tanh(0.5 * gate)
    silu = gate * sig
    act = (silu * up).astype(BF16)
    silu_ref[...] = silu.astype(BF16)
    slope_ref[...] = (up * (sig + silu * (1.0 - sig))).astype(BF16)
    act_ref[...] = act
    for copy in groups[2]:
        copy.wait()
    out_ref[...] = base_ref[...] + mm(act, wide_ref[2])


def ffn_forward(normed, base, pieces, hidden):
    rows, model = normed.shape
    mp = pieces.shape[0]
    whole = pl.BlockSpec((rows, model), lambda j: (0, 0))
    inner = pl.BlockSpec((rows, hidden), lambda j: (0, 0))
    shape = jax.ShapeDtypeStruct((rows, hidden), BF16)
    return pl.pallas_call(
        ffn_kernel,
        grid=(1,),
        in_specs=[whole, whole, pl.BlockSpec(memory_space=pl.ANY)],
        out_specs=[whole, inner, inner, inner],
        out_shape=[jax.ShapeDtypeStruct((rows, model), F32), shape, shape, shape],
        scratch_shapes=[pltpu.VMEM((3, hidden, model), BF16), pltpu.SemaphoreType.DMA((3, mp))],
        compiler_params=pltpu.CompilerParams(vmem_limit_bytes=VMEM_BYTES),
        cost_estimate=cost(9),
        name="ffn",
    )(normed, base, pieces)


def ffn_back_kernel(more, *refs):
    if more:
        base_ref, refs = refs[0], refs[1:]
    g_ref, silu_ref, slope_ref, pieces_ref, out_ref, g_gate_ref, g_up_ref, wide_ref, sems = refs
    groups = weight_copies(pieces_ref, wide_ref, sems)
    for at in (2, 0, 1):
        for copy in groups[at]:
            copy.start()
    for copy in groups[2]:
        copy.wait()
    g_act = mm(g_ref[...], wide_ref[2], NT)
    g_up = (g_act * silu_ref[...].astype(F32)).astype(BF16)
    g_gate = (g_act * slope_ref[...].astype(F32)).astype(BF16)
    g_gate_ref[...] = g_gate
    g_up_ref[...] = g_up
    for copy in groups[0]:
        copy.wait()
    total = mm(g_gate, wide_ref[0])
    for copy in groups[1]:
        copy.wait()
    total = total + mm(g_up, wide_ref[1])
    out_ref[...] = base_ref[...] + total if more else total


def ffn_backward(g_branch, base, silu, slope, pieces):
    rows, model = g_branch.shape
    hidden = silu.shape[1]
    mp = pieces.shape[0]
    whole = pl.BlockSpec((rows, model), lambda j: (0, 0))
    inner = pl.BlockSpec((rows, hidden), lambda j: (0, 0))
    shape = jax.ShapeDtypeStruct((rows, hidden), BF16)
    more = base is not None
    args = [g_branch, silu, slope, pieces]
    in_specs = [whole, inner, inner, pl.BlockSpec(memory_space=pl.ANY)]
    if more:
        args, in_specs = [base] + args, [whole] + in_specs
    return pl.pallas_call(
        functools.partial(ffn_back_kernel, more),
        grid=(1,),
        in_specs=in_specs,
        out_specs=[whole, inner, inner],
        out_shape=[jax.ShapeDtypeStruct((rows, model), F32), shape, shape],
        scratch_shapes=[pltpu.VMEM((3, hidden, model), BF16), pltpu.SemaphoreType.DMA((3, mp))],
        compiler_params=pltpu.CompilerParams(vmem_limit_bytes=VMEM_BYTES),
        cost_estimate=cost(9),
        name="ffn_back",
    )(*args)


def pack_grads_kernel(size, *refs):
    gate, got_gate, up, got_up, act, got_act, x_ref, got_x, g_ref, got_g, out_grad, pack_ref = refs
    count = pack_ref.shape[0]
    jobs = ((gate, x_ref, got_gate, got_x), (up, x_ref, got_up, got_x), (act, g_ref, got_act, got_g))
    for at, (left, right, left_two, right_two) in enumerate(jobs):
        acc = mm(left[...], right[...], TN) + mm(left_two[...], right_two[...], TN)
        for part in range(count):
            pack_ref[part, at * size : (at + 1) * size, :] = acc[part * size : (part + 1) * size].astype(BF16)
    for part in range(count):
        pack_ref[part, 3 * size :, :] = out_grad[part]


def pack_grads(inner, got_inner, normed, got_normed, g_branch, got_branch, out_grad):
    rows, model = normed.shape
    hidden = inner[0].shape[1]
    mp, out_half = out_grad.shape[:2]
    size = hidden // mp
    block = min(512, model)
    left = pl.BlockSpec((rows, hidden), lambda j: (0, 0))
    right = pl.BlockSpec((rows, block), lambda j: (0, j))
    pack_rows = 3 * size + out_half
    args = []
    for own, got in zip(inner, got_inner):
        args += [own, got]
    return pl.pallas_call(
        functools.partial(pack_grads_kernel, size),
        grid=(model // block,),
        in_specs=[left] * 6 + [right] * 4 + [pl.BlockSpec((mp, out_half, block), lambda j: (0, 0, j))],
        out_specs=pl.BlockSpec((mp, pack_rows, block), lambda j: (0, 0, j)),
        out_shape=jax.ShapeDtypeStruct((mp, pack_rows, model), BF16),
        compiler_params=pltpu.CompilerParams(vmem_limit_bytes=VMEM_BYTES),
        cost_estimate=cost(15),
        name="pack_grads",
    )(*args, normed, got_normed, g_branch, got_branch, out_grad)


def place_kernel(which_ref, first_ref, second_ref, out_ref):
    @pl.when(pl.program_id(0) == 0)
    def _():
        out_ref[...] = first_ref[...]

    @pl.when(pl.program_id(0) == 1)
    def _():
        out_ref[...] = second_ref[...]


def place_rows(first, second, which):
    rows, model = first.shape
    if rows % 16:
        ordered = jnp.where(which == 0, first, second), jnp.where(which == 0, second, first)
        return jnp.concatenate(ordered, axis=0)
    whole = pl.BlockSpec((rows, model), lambda i, w: (0, 0))
    return pl.pallas_call(
        place_kernel,
        grid_spec=pltpu.PrefetchScalarGridSpec(
            num_scalar_prefetch=1,
            grid=(2,),
            in_specs=[whole, whole],
            out_specs=pl.BlockSpec((rows, model), lambda i, w: (jnp.bitwise_xor(w[0], i), 0)),
        ),
        out_shape=jax.ShapeDtypeStruct((2 * rows, model), first.dtype),
        compiler_params=pltpu.CompilerParams(vmem_limit_bytes=VMEM_BYTES),
        cost_estimate=cost(2),
        name="place_rows",
    )(which.astype(jnp.int32).reshape(1), first, second)


def qkv_grad_kernel(count, *refs):
    out_ref = refs[-1]
    acc = None
    at = 0
    whole = count
    grads = refs[whole:-1]
    part = 0
    for i in range(count):
        size = refs[i].shape[0]
        chunk = grads[part].shape[0]
        product = mm(refs[i][...], grads[part][at : at + size, :], TN)
        acc = product if acc is None else acc + product
        at += size
        if at == chunk:
            at, part = 0, part + 1
    out_ref[...] = acc.astype(BF16)


def qkv_grad_sum(pieces, grads):
    model = pieces[0].shape[1]
    width = grads[0].shape[1]
    block = min(512, model)
    return pl.pallas_call(
        functools.partial(qkv_grad_kernel, len(pieces)),
        grid=(model // block,),
        in_specs=[pl.BlockSpec((piece.shape[0], block), lambda i: (0, i)) for piece in pieces]
        + [pl.BlockSpec(part.shape, lambda i: (0, 0)) for part in grads],
        out_specs=pl.BlockSpec((block, width), lambda i: (i, 0)),
        out_shape=jax.ShapeDtypeStruct((model, width), BF16),
        compiler_params=pltpu.CompilerParams(vmem_limit_bytes=VMEM_BYTES),
        cost_estimate=cost(7),
        name="qkv_grad",
    )(*pieces, *grads)


def normalize(rows_in, gain):
    scale = lax.rsqrt(jnp.mean(rows_in * rows_in, axis=-1, keepdims=True) + EPS)
    return rows_in * scale * gain


def normalize_back(rows_in, gain, grad):
    scale = lax.rsqrt(jnp.mean(rows_in * rows_in, axis=-1, keepdims=True) + EPS)
    gained = grad * gain
    inner = jnp.mean(gained * rows_in, axis=-1, keepdims=True)
    g_rows = scale * (gained - rows_in * (scale * scale * inner))
    return g_rows, jnp.sum(grad * (rows_in * scale), axis=0)


def rotary_tables(rows, seg_len, lanes):
    positions = (jnp.arange(rows, dtype=jnp.int32) % seg_len).astype(F32)
    inverse_freq = 10000.0 ** (-(jnp.arange(HALF, dtype=F32) * 2.0 / HEAD_DIM))
    angles = positions[:, None] * inverse_freq[None, :]
    cosine, sine = jnp.cos(angles), jnp.sin(angles)
    cosine = jnp.concatenate([cosine, cosine] * (lanes // HEAD_DIM), axis=1)
    sine = jnp.concatenate([-sine, sine] * (lanes // HEAD_DIM), axis=1)
    return cosine, sine


def swap_cores(value):
    return lax.ppermute(value, "section", [(0, 1), (1, 0)])


def across(value, axis, bits):
    return lax.ppermute(value, axis, [(i, i ^ bits) for i in range(lax.axis_size(axis))])


def is_square():
    return lax.axis_size("mp") == 4


def spread_rows(value):
    if not is_square():
        return [[lax.all_gather(value, "mp", axis=0, tiled=True)]]
    half = value.shape[0] // 2
    from_x, from_y = across(value, "mp", 1), across(value, "mp", 2)
    far_low, far_high = across(from_y[:half], "mp", 1), across(from_x[half:], "mp", 2)
    return [[value], [from_x], [from_y], [far_low, far_high]]


def sum_rows_to_owner(parts):
    if not is_square():
        total = lax.psum_scatter(jnp.concatenate(parts, axis=0), "mp", scatter_dimension=0, tiled=True)
        return total.astype(F32)
    half = parts[0].shape[0] // 2
    own, to_x, to_y, to_far = parts
    far_low = across(to_far[:half], "mp", 1)
    far_high = across(to_far[half:], "mp", 2)
    x_low = across(to_x[:half], "mp", 1)
    y_high = across(to_y[half:], "mp", 2)
    passed_x = (to_x[half:].astype(F32) + far_high.astype(F32)).astype(BF16)
    passed_y = (to_y[:half].astype(F32) + far_low.astype(F32)).astype(BF16)
    x_high = across(passed_x, "mp", 1)
    y_low = across(passed_y, "mp", 2)
    own = own.astype(F32)
    low = own[:half] + x_low.astype(F32) + y_low.astype(F32)
    high = own[half:] + x_high.astype(F32) + y_high.astype(F32)
    return jnp.concatenate([low, high], axis=0)


def group_steps():
    return 4 if lax.axis_size("dp") == 4 else 1


def sum_groups_step(step, state):
    if lax.axis_size("dp") != 4:
        return (lax.psum(state[0], "dp"), None)
    index = lax.axis_index("dp")
    low, high = index % 2, index // 2
    kept, got = state
    bits, which = ((1, low), (2, high), (2, high), (1, low))[step]
    if step < 2:
        whole = kept if got is None else (kept.astype(F32) + got.astype(F32)).astype(BF16)
        size = whole.shape[0] // 2
        kept = lax.dynamic_slice_in_dim(whole, which * size, size, 0)
        sent = lax.dynamic_slice_in_dim(whole, (1 - which) * size, size, 0)
        return kept, across(sent, "dp", bits)
    if step == 2:
        whole = (kept.astype(F32) + got.astype(F32)).astype(BF16)
    else:
        whole = place_rows(kept, got, high)
    return whole, across(whole, "dp", bits)


def sum_groups_end(state):
    if lax.axis_size("dp") != 4:
        return state[0]
    return place_rows(state[0], state[1], lax.axis_index("dp") % 2)


def sum_groups(value, state=None, start=0):
    if state is None:
        state = (value, None)
    for step in range(start, group_steps()):
        state = sum_groups_step(step, state)
    return sum_groups_end(state)


class Hook:
    def __init__(self, value):
        self.state = (value, None)
        self.step = 0

    def tie(self, value):
        value, self.state = lax.optimization_barrier((value, self.state))
        if self.step < group_steps():
            self.state = sum_groups_step(self.step, self.state)
            self.step += 1
        return value

    def end(self):
        return sum_groups(None, self.state, self.step)


def by_distance(blocks, place):
    if not is_square():
        return blocks
    blocks = jnp.where(place % 2 == 0, blocks, jnp.stack([blocks[i] for i in (1, 0, 3, 2)]))
    return jnp.where(place < 2, blocks, jnp.stack([blocks[i] for i in (2, 3, 0, 1)]))


def sum_all(value):
    if not is_square() or lax.axis_size("dp") != 4:
        return lax.psum(value, ("section", "dp", "mp"))
    value = value + across(value, "section", 1)
    for axis in ("mp", "dp"):
        for bits in (1, 2):
            value = value + across(value, axis, bits)
    return value


def pick_half(value, which, axis=0):
    size = value.shape[axis] // 2
    return lax.dynamic_slice_in_dim(value, which * size, size, axis)


def shards(
    tokens,
    layout,
    cotangent,
    attn_gain,
    query_weight,
    key_weight,
    value_weight,
    out_weight,
    ffn_gain,
    gate_weight,
    up_weight,
    down_weight,
):
    core = lax.axis_index("section")
    is_low = core == 0
    micro_count, tok_rows, model = tokens.shape
    mp = lax.axis_size("mp")
    place = lax.axis_index("mp").astype(jnp.int32)
    square = is_square()
    parts = mp if square else 1
    seq_rows = tok_rows * mp
    width = query_weight.shape[2]
    hidden = gate_weight.shape[2]
    hid_half = hidden // 2
    out_half = width // 2
    group = min(width, 128)

    def in_order(own, other):
        return jnp.where(is_low, own, other), jnp.where(is_low, other, own)

    inputs = lax.dynamic_index_in_dim(tokens, core, 0, keepdims=False)
    g_top = lax.dynamic_index_in_dim(cotangent, core, 0, keepdims=False)
    pack_layout = lax.dynamic_index_in_dim(layout[:, 0], core, 0, keepdims=False)
    seg_len = (seq_rows // pack_layout).astype(jnp.int32)
    info = jnp.stack([seg_len, place, core.astype(jnp.int32)])
    cosine, sine = rotary_tables(seq_rows, seg_len, group)

    own_qkv = jnp.concatenate([query_weight[0], key_weight[0], value_weight[0]], axis=1)
    qkv_weights = in_order(own_qkv, swap_cores(own_qkv))
    gains = jnp.concatenate([attn_gain, ffn_gain], axis=0)
    layer_gains = in_order(gains, swap_cores(gains))

    halves = jnp.concatenate(
        [
            gate_weight[0].T.reshape(2, hid_half, model),
            up_weight[0].T.reshape(2, hid_half, model),
            down_weight[0].reshape(2, hid_half, model),
            out_weight[0].reshape(2, out_half, model),
        ],
        axis=1,
    )
    kept = lax.dynamic_index_in_dim(halves, core, 0, keepdims=False)
    sent = lax.dynamic_index_in_dim(halves, 1 - core, 0, keepdims=False)
    packs = in_order(kept, swap_cores(sent))
    pack_rows = packs[0].shape[0]

    all_pieces = [lax.all_gather(pack, "mp", axis=0, tiled=False) for pack in packs]

    hid_all = mp * hid_half

    def whole_rows(pieces):
        if hid_half % 16 == 0:
            return pieces
        starts = [i * hid_half for i in range(3)]
        parts = [pieces[:, at : at + hid_half].reshape(hid_all, model) for at in starts]
        return jnp.concatenate(parts, axis=0)[None]

    def to_owners(attended):
        if not square:
            blocks = attended[0].reshape(mp, tok_rows, width)
            moved = lax.all_to_all(blocks, "mp", 0, 0)
            return [jnp.transpose(moved, (1, 0, 2)).reshape(tok_rows, mp * width)]
        moved = {i: across(attended[i], "mp", i) for i in (3, 1, 2)}
        return [attended[0], moved[1], moved[2], moved[3]]

    def to_heads(value):
        if not square:
            blocks = jnp.transpose(value.reshape(tok_rows, mp, width), (1, 0, 2))
            return [lax.all_to_all(blocks, "mp", 0, 0).reshape(seq_rows, width)]
        blocks = [value[:, i * width : (i + 1) * width] for i in range(mp)]
        moved = {i: across(blocks[i], "mp", i) for i in (3, 1, 2)}
        return [blocks[0], moved[1], moved[2], moved[3]]

    def forward(rows_low, first, weights):
        gain_a, gain_f, qkv_w, pieces_w = weights
        state = rows_low.astype(F32)
        normed = normalize(state, gain_a).astype(BF16)
        pieces = spread_rows(normed)
        held = None
        for index, piece in enumerate(pieces):
            spot = jnp.bitwise_xor(place, index) if square else jnp.int32(0)
            held = project_qkv(piece, spot.reshape(1), qkv_w, cosine, sine, first, held)
        queries, keys, values = held
        attended, lse = attend(queries, keys, values, info, parts)
        attended, pieces_w = lax.optimization_barrier((attended, pieces_w))
        out_own = pieces_w[:, 3 * hid_half :]
        out_other = swap_cores(out_own)
        own, other = whole_rows(pieces_w), whole_rows(swap_cores(pieces_w))
        att_rows = to_owners(attended)
        middle, normed_ffn, out_full = out_project(att_rows, out_own, out_other, rows_low, gain_f, info)
        result = middle
        inner = []
        for share in (own, other):
            result, silu, slope, activated = ffn_forward(normed_ffn, result, share, hid_all)
            inner.append((silu, slope, activated))
        flat = [part for piece in pieces for part in piece]
        kept_items = (state, flat, queries, keys, values, attended, lse, att_rows, middle, normed_ffn, inner)
        kept_items += (own, other, out_full)
        return result.astype(BF16), values, kept_items

    def backward(g_result, g_first, weights, kept_items, hook=None):
        tie = hook.tie if hook is not None else lambda value: value

        gain_a, gain_f, qkv_w, unused = weights
        state, pieces, queries, keys, values, attended, lse, att_rows, middle, normed_ffn, inner = kept_items[:11]
        own, other, out_full = kept_items[11:]
        g_branch = g_result.astype(BF16)
        got_normed, got_branch, got_act = swap_cores(normed_ffn), swap_cores(g_branch), swap_cores(inner[1][2])
        g_normed = None
        g_inner = []
        for (silu, slope, activated), share in zip(inner, (own, other)):
            g_normed, g_gate, g_up = ffn_backward(g_branch, g_normed, silu, slope, share)
            g_inner.append((g_gate, g_up, activated))
        got_gate, got_up = swap_cores(g_inner[1][0]), swap_cores(g_inner[1][1])
        g_normed = tie(g_normed)
        g_norm, g_gain_f = normalize_back(middle, gain_f, g_normed)
        g_middle = g_result + g_norm
        g_mid_low = g_middle.astype(BF16)
        g_att = to_heads(mm(g_mid_low, out_full, NT).astype(BF16))
        g_att = tie(g_att)
        g_qkv = attend_back(queries, keys, values, lse, cosine, sine, attended, g_att, g_first, info)
        g_qkv = tie(g_qkv)
        g_parts = [mm(part, qkv_w, NT).astype(BF16) for part in g_qkv]
        if not square:
            g_parts = [g_parts[0][i * tok_rows : (i + 1) * tok_rows] for i in range(mp)]
        g_norm, g_gain_a = normalize_back(state, gain_a, tie(sum_rows_to_owner(g_parts)))
        g_inputs = g_middle + g_norm

        att_whole = jnp.concatenate(att_rows, axis=1)
        out_grad = mm(att_whole, g_mid_low, TN).astype(BF16).reshape(mp, 2, out_half, model)
        out_kept = lax.dynamic_index_in_dim(out_grad, core, 1, keepdims=False)
        out_sent = lax.dynamic_index_in_dim(out_grad, 1 - core, 1, keepdims=False)
        out_grad = (out_kept.astype(F32) + swap_cores(out_sent).astype(F32)).astype(BF16)
        pack = pack_grads(
            g_inner[0],
            (got_gate, got_up, got_act),
            normed_ffn,
            got_normed,
            g_branch,
            got_branch,
            by_distance(out_grad, place),
        )
        ffn_grads = lax.psum_scatter(pack.reshape(mp * pack_rows, model), "mp", scatter_dimension=0, tiled=True)
        qkv_grad = qkv_grad_sum(pieces, g_qkv)
        qkv_grad = pick_half(qkv_grad, core).astype(F32) + swap_cores(pick_half(qkv_grad, 1 - core)).astype(F32)
        return g_inputs, g_qkv, (ffn_grads, qkv_grad, g_gain_a, g_gain_f)

    layers = [
        (layer_gains[i][0], layer_gains[i][1], qkv_weights[i], all_pieces[i]) for i in range(2)
    ]
    h_first, first_values, kept_first = forward(inputs, None, layers[0])
    h_second, unused, kept_second = forward(h_first, first_values, layers[1])
    g_second, g_qkv_second, grads_second = backward(g_top, None, layers[1], kept_second)
    hook = Hook(grads_second[0])
    g_tokens, unused, grads_first = backward(
        g_second.astype(BF16).astype(F32), g_qkv_second, layers[0], kept_first, hook
    )

    def flat_rows(value):
        return value.reshape(-1, model).astype(BF16)

    totals_second = [hook.end(), sum_groups(flat_rows(grads_second[1]))]
    cut = pack_rows // 64 * 32
    totals_first = [
        jnp.concatenate([sum_groups(grads_first[0][:cut]), sum_groups(grads_first[0][cut:])], axis=0),
        sum_groups(flat_rows(grads_first[1])),
    ]

    def by_layer(low, high, wire):
        mine = jnp.where(is_low, low, high)
        theirs = swap_cores(jnp.where(is_low, high, low).astype(wire)).astype(mine.dtype)
        return in_order(mine, theirs)

    layer_out = jnp.stack(by_layer(h_first, h_second, BF16))
    input_grads = jnp.stack(by_layer(g_tokens, g_second, BF16))
    all_first = jnp.stack(in_order(first_values, swap_cores(first_values)))

    low, high = by_layer(totals_first[0], totals_second[0], BF16)
    qkv_low, qkv_high = by_layer(totals_first[1], totals_second[1], BF16)

    def joined(start, size):
        return jnp.concatenate([low[start : start + size], high[start : start + size]], axis=0).astype(F32)

    gate_grad = joined(0, hid_half)
    up_grad = joined(hid_half, hid_half)
    down_grad = joined(2 * hid_half, hid_half)
    out_grad = joined(3 * hid_half, out_half)
    qkv_grad = jnp.concatenate([qkv_low, qkv_high], axis=0).astype(F32).reshape(model, 3 * width)

    heads_here = width // HEAD_DIM
    first_f32 = first_values.astype(F32).reshape(seq_rows, heads_here, HEAD_DIM)
    squares = jnp.sum(first_f32 * first_f32, axis=(0, 2))
    placed = lax.dynamic_update_slice(
        jnp.zeros((micro_count, heads_here * mp), F32), squares[None], (core, place * heads_here)
    )
    sums = [grads_first[2], grads_second[2], grads_first[3], grads_second[3], placed.reshape(-1)]
    sums = sum_all(jnp.concatenate(sums))
    gain_grads = sums[: 4 * model].reshape(4, model)
    value_norms = sums[4 * model :].reshape(placed.shape)
    attn_gain_grad = lax.dynamic_slice_in_dim(gain_grads, core, 1, 0)
    ffn_gain_grad = lax.dynamic_slice_in_dim(gain_grads, 2 + core, 1, 0)
    return (
        layer_out[None],
        input_grads[None],
        all_first,
        value_norms,
        attn_gain_grad,
        qkv_grad[:, :width][None],
        qkv_grad[:, width : 2 * width][None],
        qkv_grad[:, 2 * width :][None],
        out_grad[None],
        ffn_gain_grad,
        gate_grad.T[None],
        up_grad.T[None],
        down_grad[None],
    )


def solution(mesh):
    in_specs = (
        P(None, ("dp", "mp"), None),
        P(None, "dp"),
        P(None, ("dp", "mp"), None),
        P("section", None),
        P("section", None, "mp"),
        P("section", None, "mp"),
        P("section", None, "mp"),
        P("section", "mp", None),
        P("section", None),
        P("section", None, "mp"),
        P("section", None, "mp"),
        P("section", "mp", None),
    )
    out_specs = (
        P("section", None, ("dp", "mp"), None),
        P("section", None, ("dp", "mp"), None),
        P(None, "dp", "mp"),
        P(),
        P("section", None),
        P("section", None, "mp"),
        P("section", None, "mp"),
        P("section", None, "mp"),
        P("section", "mp", None),
        P("section", None),
        P("section", None, "mp"),
        P("section", None, "mp"),
        P("section", "mp", None),
    )
    return jax.shard_map(shards, mesh=mesh, in_specs=in_specs, out_specs=out_specs, check_vma=False)
```

time: 1180 us -> 972 us (0.82)
  waiting for transfers between devices: 588 us -> 400 us
  matrix products: 141 us -> 19.6 us
  Pallas kernels: 171 us -> 281 us
  starting transfers between devices: 15.6 us -> 101 us
  blocking collectives: 58.4 us -> 0 us
  other arithmetic: 112 us -> 87.8 us
  local copies, waits for them, and re-layouts: 70.4 us -> 55.3 us
    ppermute x0 -> x57, waiting for transfers between devices: none -> 351 us  [across(): lax.ppermute(value, axis, [(i, i ^ bits) for i in range(lax.axis_size(axi...]
    psum x1 -> x0, waiting for transfers between devices: 225 us -> none  [backward(): qkv_grad = lax.psum(qkv_grad.astype(BF16), 'dp')]
    all_gather x4 -> x2, waiting for transfers between devices: 231 us -> 30.2 us  [shards(): lax.all_gather(pack, 'mp', axis=0, tiled=False)]
    dot_general x46 -> x12, matrix products: 141 us -> 19.6 us  [mm(): return lax.dot_general(left, right, dims, preferred_element_type=F32)]
    pallas_call x6 -> x34, Pallas kernels: 171 us -> 281 us  [the longest x2 52.1 us: attend_back(): pl.pallas_call(functools.partial(attend_back_kernel, second, block, min(2...]
    reduce_scatter x4 -> x2, waiting for transfers between devices: 95.1 us -> 0.02 us  [backward(): lax.psum_scatter(pack.reshape(mp * pack_rows, model), 'mp', scatter_dimen...]
    ppermute x0 -> x57, starting transfers between devices: none -> 71.5 us  [across(): lax.ppermute(value, axis, [(i, i ^ bits) for i in range(lax.axis_size(axi...]
    psum x1 -> x0, blocking collectives: 39.4 us -> none  [shards(): lax.psum((gain_grads, placed), ('section', 'dp', 'mp'))]
  transfers between devices with their start and end apart: 28 -> 87, of which waited for: 12 -> 51; matrix products, arithmetic and copies ran while one was open for 21% -> 12% of each run, Pallas kernels for 11% -> 23%
where the time goes in v2:
time: 972 us; the launch traced here: 962 us
  waiting for transfers between devices  400 us (41%)
  Pallas kernels  281 us (29%)
  starting transfers between devices  101 us (10%)
  other arithmetic  87.8 us (9%)
  local copies, waits for them, and re-layouts  55.3 us (6%)
  matrix products  19.6 us (2%)
  between operations  17.8 us (2%)
    ppermute x57, waiting for transfers between devices, across(): lax.ppermute(value, axis, [(i, i ^ bits) for i in range(lax.axis_size(axi...  351 us
    ppermute x57, starting transfers between devices, across(): lax.ppermute(value, axis, [(i, i ^ bits) for i in range(lax.axis_size(axi...  71.5 us
    pallas_call x2, Pallas kernels, attend_back(): pl.pallas_call(functools.partial(attend_back_kernel, second, block, min(2...  52.1 us
    pallas_call x4, Pallas kernels, ffn_backward(): pl.pallas_call(functools.partial(ffn_back_kernel, more), grid=(1,), in_sp...  45.5 us
    pallas_call x4, Pallas kernels, ffn_forward(): pl.pallas_call(ffn_kernel, grid=(1,), in_specs=[whole, whole, pl.BlockSpe...  44.7 us
    pallas_call x2, Pallas kernels, pack_grads(): pl.pallas_call(functools.partial(pack_grads_kernel, size), grid=(model //...  33 us
    pallas_call x8, Pallas kernels, project_qkv(): pl.pallas_call(functools.partial(qkv_kernel, second, group, parts, fresh)...  32.5 us
    all_gather x2, waiting for transfers between devices, shards(): lax.all_gather(pack, 'mp', axis=0, tiled=False)  30.2 us
  transfers between devices with their start and end apart: 87, of which 51 were waited for; matrix products, arithmetic and copies ran while one was open for 12% of the time, Pallas kernels for 23%

profile of v2, /device:TPU:0, one launch (start us, length us, event | category | flops | bytes accessed | tf_op | source)
XLA Modules:
  0.0 961.8 jit_solution(443848644994943682)
XLA Ops:
  13.2 4.5 collective-permute-done.6
  17.7 4.2 bitcast_select_fusion
  42.6 33.7 %collective-permute-done.1.refs_0_.refs_2_ = bf16[512,1024]{1,0:T(8,128)(2,1)} collective-permute-done((bf16[512,1024]{1,0:T(8,128)(2,1)}, bf16[512,1024]{1,0:T(8,128)(2,1)}, u32[]{:S(2)}, u32[]{:S(2)}) %collective-permute-start.1) | collective-permute-done | bytes 1048608 | tf_op jit(solution)/shard_map/ppermute | solution.py:670
  84.8 3.8 qkv_rope.8
  88.6 3.8 qkv_rope.9
  92.4 4.1 qkv_rope.10
  97.6 4.5 qkv_rope.11
  102.0 13.6 %attend.2 = (bf16[512,256]{1,0:T(8,128)(2,1)}, bf16[512,256]{1,0:T(8,128)(2,1)}, bf16[512,256]{1,0:T(8,128)(2,1)}, bf16[512,256]{1,0:T(8,128)(2,1)}, f32[4,2048]{1,0:T(4,128)}) custom-call(s32[3]{0:T(128)} %pad_add_fusion.info_ref, bf16[2048,256]{1,0:T(8,128)(2,1)} %get-tuple-element.125.q_ref, bf16[2048,256]{1,0:T(8,128)(2,1)} %get-tuple-element.126.k_ref, ...), custom_call_target="tpu_custom_call" | custom-call | flops 20700000256 | bytes 1048576 | tf_op jit(solution)/shard_map/attend/pallas_call | solution.py:205
  115.6 30.2 %all-gather.5.cloned.1.call-done = bf16[4736,1024]{1,0:T(8,128)(2,1)} async-done(((bf16[1184,1024]{1,0:T(8,128)(2,1)}), bf16[4736,1024]{1,0:T(8,128)(2,1)}) %all-gather.5.cloned.1.call-update) | async-done | bytes 9699344 | tf_op jit(solution)/shard_map/all_gather | solution.py:839
  151.4 6.6 collective-permute-done.10.refs_3_
  158.0 7.7 collective-permute-done.8.refs_1_
  166.9 6.5 out_project.2
  173.5 11.1 %ffn.4 = (f32[512,1024]{1,0:T(8,128)}, bf16[512,1408]{1,0:T(8,128)(2,1)}, bf16[512,1408]{1,0:T(8,128)(2,1)}, bf16[512,1408]{1,0:T(8,128)(2,1)}) custom-call(bf16[512,1024]{1,0:T(8,128)(2,1)} %get-tuple-element.137.x_ref.refs_6_, f32[512,1024]{1,0:T(8,128)} %get-tuple-element.138.base_ref, bf16[4,1184,1024]{2,1,0:T(8,128)(2,1)} %bitcast.135), custom_call_target="tpu_custom_call" | custom-call | flops 10350000128 | bytes 1048576 | tf_op jit(solution)/shard_map/ffn/pallas_call | solution.py:478
  184.6 11.1 %ffn.5 = (f32[512,1024]{1,0:T(8,128)}, bf16[512,1408]{1,0:T(8,128)(2,1)}, bf16[512,1408]{1,0:T(8,128)(2,1)}, bf16[512,1408]{1,0:T(8,128)(2,1)}) custom-call(bf16[512,1024]{1,0:T(8,128)(2,1)} %get-tuple-element.137.x_ref.refs_6_, f32[512,1024]{1,0:T(8,128)} %get-tuple-element.139.base_ref, bf16[4,1184,1024]{2,1,0:T(8,128)(2,1)} %collective-permute-done.11.pieces_ref.refs_4_), custom_call_target="tpu_custom_call" | custom-call | flops 10350000128 | bytes 1048576 | tf_op jit(solution)/shard_map/ffn/pallas_call | solution.py:478
  200.4 4.3 qkv_rope.12
  204.7 42.4 %collective-permute-done.12.refs_0_.refs_2_ = bf16[512,1024]{1,0:T(8,128)(2,1)S(1)} collective-permute-done((bf16[512,1024]{1,0:T(8,128)(2,1)S(1)}, bf16[512,1024]{1,0:T(8,128)(2,1)S(1)}, u32[]{:S(2)}, u32[]{:S(2)}) %collective-permute-start.12) | collective-permute-done | bytes 1048608 | tf_op jit(solution)/shard_map/ppermute | solution.py:670
  249.4 3.9 qkv_rope.13
  253.3 3.9 qkv_rope.14
  257.2 15.3 %collective-permute-done.13.refs_0_.refs_3_ = bf16[256,1024]{1,0:T(8,128)(2,1)S(1)} collective-permute-done((bf16[256,1024]{1,0:T(8,128)(2,1)S(1)}, bf16[256,1024]{1,0:T(8,128)(2,1)S(1)}, u32[]{:S(2)}, u32[]{:S(2)}) %collective-permute-start.13) | collective-permute-done | bytes 524320 | tf_op jit(solution)/shard_map/ppermute | solution.py:670
  274.7 4.2 qkv_rope.15
  278.9 13.7 %attend.3 = (bf16[512,256]{1,0:T(8,128)(2,1)}, bf16[512,256]{1,0:T(8,128)(2,1)}, bf16[512,256]{1,0:T(8,128)(2,1)}, bf16[512,256]{1,0:T(8,128)(2,1)}, f32[4,2048]{1,0:T(4,128)}) custom-call(s32[3]{0:T(128)} %pad_add_fusion.info_ref, bf16[2048,256]{1,0:T(8,128)(2,1)} %get-tuple-element.150.q_ref, bf16[2048,256]{1,0:T(8,128)(2,1)} %get-tuple-element.151.k_ref, ...), custom_call_target="tpu_custom_call" | custom-call | flops 20700000256 | bytes 1048576 | tf_op jit(solution)/shard_map/attend/pallas_call | solution.py:205
  292.6 4.6 collective-permute-start.20
  307.8 4.6 collective-permute-done.18.refs_2_
  314.3 6.5 out_project.3
  322.7 11.1 %ffn.6 = (f32[512,1024]{1,0:T(8,128)}, bf16[512,1408]{1,0:T(8,128)(2,1)}, bf16[512,1408]{1,0:T(8,128)(2,1)}, bf16[512,1408]{1,0:T(8,128)(2,1)}) custom-call(bf16[512,1024]{1,0:T(8,128)(2,1)} %get-tuple-element.162.x_ref.refs_6_, f32[512,1024]{1,0:T(8,128)} %get-tuple-element.163.base_ref, bf16[4,1184,1024]{2,1,0:T(8,128)(2,1)} %bitcast.139), custom_call_target="tpu_custom_call" | custom-call | flops 10350000128 | bytes 1048576 | tf_op jit(solution)/shard_map/ffn/pallas_call | solution.py:478
  333.8 11.0 %ffn_back.4 = (f32[512,1024]{1,0:T(8,128)}, bf16[512,1408]{1,0:T(8,128)(2,1)}, bf16[512,1408]{1,0:T(8,128)(2,1)}) custom-call(bf16[512,1024]{1,0:T(8,128)(2,1)} %bitcast_convert_fusion.refs_0_.refs_1_.refs_8_, bf16[512,1408]{1,0:T(8,128)(2,1)} %get-tuple-element.166.refs_1_, bf16[512,1408]{1,0:T(8,128)(2,1)} %get-tuple-element.167.refs_2_, ...), custom_call_target="tpu_custom_call" | custom-call | flops 10350000128 | bytes 1048576 | tf_op jit(solution)/shard_map/ffn_back/pallas_call | solution.py:527
  344.8 11.3 %ffn.7 = (f32[512,1024]{1,0:T(8,128)}, bf16[512,1408]{1,0:T(8,128)(2,1)}, bf16[512,1408]{1,0:T(8,128)(2,1)}, bf16[512,1408]{1,0:T(8,128)(2,1)}) custom-call(bf16[512,1024]{1,0:T(8,128)(2,1)} %get-tuple-element.162.x_ref.refs_6_, f32[512,1024]{1,0:T(8,128)} %get-tuple-element.164.base_ref, bf16[4,1184,1024]{2,1,0:T(8,128)(2,1)} %collective-permute-done.20.pieces_ref.refs_4_), custom_call_target="tpu_custom_call" | custom-call | flops 10350000128 | bytes 1048576 | tf_op jit(solution)/shard_map/ffn/pallas_call | solution.py:478
  356.2 11.7 %ffn_back.5 = (f32[512,1024]{1,0:T(8,128)}, bf16[512,1408]{1,0:T(8,128)(2,1)}, bf16[512,1408]{1,0:T(8,128)(2,1)}) custom-call(f32[512,1024]{1,0:T(8,128)} %get-tuple-element.168.refs_0_, bf16[512,1024]{1,0:T(8,128)(2,1)} %bitcast_convert_fusion.refs_0_.refs_1_.refs_8_, bf16[512,1408]{1,0:T(8,128)(2,1)} %get-tuple-element.169.refs_2_, ...), custom_call_target="tpu_custom_call" | custom-call | flops 10350000128 | bytes 1048576 | tf_op jit(solution)/shard_map/ffn_back/pallas_call | solution.py:527
  388.9 16.7 %pack_grads.2 = bf16[4,1184,1024]{2,1,0:T(8,128)(2,1)} custom-call(bf16[512,1408]{1,0:T(8,128)(2,1)} %get-tuple-element.184.refs_0_, bf16[512,1408]{1,0:T(8,128)(2,1)} %collective-permute-done.31.refs_1_, bf16[512,1408]{1,0:T(8,128)(2,1)} %get-tuple-element.186.refs_2_, bf16[512,1408]{1,0:T(8,128)(2,1)} %collective-permute-done.32.refs_3_, ...), custom_call_target="tpu_custom_call" | custom-call | flops 17250000896 | bytes 1048576 | tf_op jit(solution)/shard_map/pack_grads/pallas_call | solution.py:564
  413.1 9.1 collective-permute-done.22.refs_5_
  422.2 3.8 collective-permute-done.23.refs_6_
  426.1 7.8 collective-permute-done.24.refs_7_
  434.6 25.8 %attend_back.2 = (bf16[512,768]{1,0:T(8,128)(2,1)}, bf16[512,768]{1,0:T(8,128)(2,1)}, bf16[512,768]{1,0:T(8,128)(2,1)}, bf16[512,768]{1,0:T(8,128)(2,1)}) custom-call(s32[3]{0:T(128)} %pad_add_fusion.info_ref, bf16[2048,256]{1,0:T(8,128)(2,1)} %get-tuple-element.150.q_ref, bf16[2048,256]{1,0:T(8,128)(2,1)} %get-tuple-element.151.k_ref, ...), custom_call_target="tpu_custom_call" | custom-call | flops 41400000512 | bytes 1048576 | tf_op jit(solution)/shard_map/attend_back/pallas_call | solution.py:362
  469.0 16.0 %collective-permute-done.28 = bf16[256,1024]{1,0:T(8,128)(2,1)S(1)} collective-permute-done((bf16[256,1024]{1,0:T(8,128)(2,1)S(1)}, bf16[256,1024]{1,0:T(8,128)(2,1)S(1)}, u32[]{:S(2)}, u32[]{:S(2)}) %collective-permute-start.28) | collective-permute-done | bytes 524320 | tf_op jit(solution)/shard_map/ppermute | solution.py:670
  485.8 11.8 %collective-permute-done.26 = bf16[256,1024]{1,0:T(8,128)(2,1)S(1)} collective-permute-done((bf16[256,1024]{1,0:T(8,128)(2,1)S(1)}, bf16[256,1024]{1,0:T(8,128)(2,1)S(1)}, u32[]{:S(2)}, u32[]{:S(2)}) %collective-permute-start.26) | collective-permute-done | bytes 524320 | tf_op jit(solution)/shard_map/ppermute | solution.py:670
  500.4 19.7 %collective-permute-done.29 = bf16[256,1024]{1,0:T(8,128)(2,1)S(1)} collective-permute-done((bf16[256,1024]{1,0:T(8,128)(2,1)S(1)}, bf16[256,1024]{1,0:T(8,128)(2,1)S(1)}, u32[]{:S(2)}, u32[]{:S(2)}) %collective-permute-start.29) | collective-permute-done | bytes 524320 | tf_op jit(solution)/shard_map/ppermute | solution.py:670
  526.9 11.0 %ffn_back.6 = (f32[512,1024]{1,0:T(8,128)}, bf16[512,1408]{1,0:T(8,128)(2,1)}, bf16[512,1408]{1,0:T(8,128)(2,1)}) custom-call(bf16[512,1024]{1,0:T(8,128)(2,1)} %get-tuple-element.229.refs_0_.refs_1_.refs_8_, bf16[512,1408]{1,0:T(8,128)(2,1)} %get-tuple-element.178.refs_1_, bf16[512,1408]{1,0:T(8,128)(2,1)} %get-tuple-element.179.refs_2_, ...), custom_call_target="tpu_custom_call" | custom-call | flops 10350000128 | bytes 1048576 | tf_op jit(solution)/shard_map/ffn_back/pallas_call | solution.py:527
  538.0 11.8 %ffn_back.7 = (f32[512,1024]{1,0:T(8,128)}, bf16[512,1408]{1,0:T(8,128)(2,1)}, bf16[512,1408]{1,0:T(8,128)(2,1)}) custom-call(f32[512,1024]{1,0:T(8,128)} %get-tuple-element.180.refs_0_, bf16[512,1024]{1,0:T(8,128)(2,1)} %get-tuple-element.229.refs_0_.refs_1_.refs_8_, bf16[512,1408]{1,0:T(8,128)(2,1)} %get-tuple-element.181.refs_2_, ...), custom_call_target="tpu_custom_call" | custom-call | flops 10350000128 | bytes 1048576 | tf_op jit(solution)/shard_map/ffn_back/pallas_call | solution.py:527
  556.7 8.3 collective-permute-start.72
  569.7 5.3 collective-permute-done.70.refs_7_
  578.4 16.3 %pack_grads.3 = bf16[4,1184,1024]{2,1,0:T(8,128)(2,1)} custom-call(bf16[512,1408]{1,0:T(8,128)(2,1)} %get-tuple-element.211.refs_0_, bf16[512,1408]{1,0:T(8,128)(2,1)} %copy-done.74, bf16[512,1408]{1,0:T(8,128)(2,1)} %get-tuple-element.213.refs_2_, bf16[512,1408]{1,0:T(8,128)(2,1)} %copy-done.75, bf16[512,1408]{1,0:T(8,128)(2,1)} %get-tuple-element.215.refs_4_, ...), custom_call_target="tpu_custom_call" | custom-call | flops 17250000896 | bytes 1048576 | tf_op jit(solution)/shard_map/pack_grads/pallas_call | solution.py:564
  594.7 7.4 qkv_grad.3
  613.1 8.2 collective-permute-start.62
  624.5 6.2 collective-permute-done.62
  631.2 11.3 %collective-permute-done.63 = bf16[96,1024]{1,0:T(8,128)(2,1)S(1)} collective-permute-done((bf16[96,1024]{1,0:T(8,128)(2,1)S(1)}, bf16[96,1024]{1,0:T(8,128)(2,1)S(1)}, u32[]{:S(2)}, u32[]{:S(2)}) %collective-permute-start.63) | collective-permute-done | bytes 196640 | tf_op jit(solution)/shard_map/ppermute | solution.py:670
  655.7 6.8 collective-permute-done.37.refs_5_
  664.5 7.8 collective-permute-done.39.refs_7_
  672.3 4.2 collective-permute-done.40
  677.2 26.4 %attend_back.3 = (bf16[512,768]{1,0:T(8,128)(2,1)}, bf16[512,768]{1,0:T(8,128)(2,1)}, bf16[512,768]{1,0:T(8,128)(2,1)}, bf16[512,768]{1,0:T(8,128)(2,1)}) custom-call(s32[3]{0:T(128)} %pad_add_fusion.info_ref, bf16[2048,256]{1,0:T(8,128)(2,1)} %get-tuple-element.125.q_ref, bf16[2048,256]{1,0:T(8,128)(2,1)} %get-tuple-element.126.k_ref, ...), custom_call_target="tpu_custom_call" | custom-call | flops 41400000512 | bytes 1048576 | tf_op jit(solution)/shard_map/attend_back/pallas_call | solution.py:362
  716.3 7.4 qkv_grad.2
  724.8 8.7 collective-permute-start.56
  757.8 13.7 %collective-permute-done.48 = bf16[296,1024]{1,0:T(8,128)(2,1)} collective-permute-done((bf16[296,1024]{1,0:T(8,128)(2,1)S(1)}, bf16[296,1024]{1,0:T(8,128)(2,1)}, u32[]{:S(2)}, u32[]{:S(2)}) %collective-permute-start.48) | collective-permute-done | bytes 606240 | tf_op jit(solution)/shard_map/ppermute | solution.py:670
  785.2 7.9 collective-permute-done.73
  793.4 3.8 collective-permute-start.74
  797.2 15.6 %collective-permute-done.77 = bf16[304,1024]{1,0:T(8,128)(2,1)S(1)} collective-permute-done((bf16[304,1024]{1,0:T(8,128)(2,1)S(1)}, bf16[304,1024]{1,0:T(8,128)(2,1)S(1)}, u32[]{:S(2)}, u32[]{:S(2)}) %collective-permute-start.77) | collective-permute-done | bytes 622624 | tf_op jit(solution)/shard_map/ppermute | solution.py:670
  813.1 3.8 collective-permute-start.78
  816.9 19.9 %collective-permute-done.74 = bf16[144,1024]{1,0:T(8,128)(2,1)S(1)} collective-permute-done((bf16[144,1024]{1,0:T(8,128)(2,1)S(1)}, bf16[144,1024]{1,0:T(8,128)(2,1)S(1)}, u32[]{:S(2)}, u32[]{:S(2)}) %collective-permute-start.74) | collective-permute-done | bytes 294944 | tf_op jit(solution)/shard_map/ppermute | solution.py:670
  847.1 14.2 %collective-permute-done.58 = bf16[96,1024]{1,0:T(8,128)(2,1)S(1)} collective-permute-done((bf16[96,1024]{1,0:T(8,128)(2,1)S(1)}, bf16[96,1024]{1,0:T(8,128)(2,1)S(1)}, u32[]{:S(2)}, u32[]{:S(2)}) %collective-permute-start.58) | collective-permute-done | bytes 196640 | tf_op jit(solution)/shard_map/ppermute | solution.py:670
  861.4 12.9 %collective-permute-done.75.second_ref = bf16[144,1024]{1,0:T(8,128)(2,1)S(1)} collective-permute-done((bf16[144,1024]{1,0:T(8,128)(2,1)S(1)}, bf16[144,1024]{1,0:T(8,128)(2,1)S(1)}, u32[]{:S(2)}, u32[]{:S(2)}) %collective-permute-start.75) | collective-permute-done | bytes 294944 | tf_op jit(solution)/shard_map/ppermute | solution.py:670
  876.9 8.3 collective-permute-done.79
  885.3 4.1 collective-permute-done.59.second_ref
  896.6 5.4 collective-permute-done.76.second_ref
  905.2 10.3 %collective-permute-done.80.second_ref = bf16[304,1024]{1,0:T(8,128)(2,1)} collective-permute-done((bf16[304,1024]{1,0:T(8,128)(2,1)S(1)}, bf16[304,1024]{1,0:T(8,128)(2,1)}, u32[]{:S(2)}, u32[]{:S(2)}) %collective-permute-start.80) | collective-permute-done | bytes 622624 | tf_op jit(solution)/shard_map/ppermute | solution.py:670
  917.8 4.0 broadcast_select_fusion.2
  (549 shorter events, 268.1 us)
Async XLA Ops:
  7.2 138.6 %all-gather.5.cloned.1.call-start = ((), (), s32[]{:S(2)}) async-start(), calls=%async_computation.4 | async-start | bytes 12124160 | tf_op jit(solution)/shard_map/all_gather | solution.py:839
  22.0 270.7 %all-gather.7.cloned.1.call-start = ((), (), s32[]{:S(2)}) async-start(), calls=%async_computation.5 | async-start | bytes 12124160 | tf_op jit(solution)/shard_map/all_gather | solution.py:839
  24.6 56.5 %collective-permute-start.5 = (bf16[1024,768]{1,0:T(8,128)(2,1)}, bf16[1024,768]{1,0:T(8,128)(2,1)}, u32[]{:S(2)}, u32[]{:S(2)}) collective-permute-start(bf16[1024,768]{1,0:T(8,128)(2,1)} %pad_maximum_fusion.5), channel_id=1, source_target_pairs={{0,16},{16,0},{1,17},{17,1},{2,18},{18,2},{3,19},{19,3},{4,20},{20... | collective-permute-start | bytes 4718600 | tf_op jit(solution)/shard_map/ppermute | solution.py:666
  28.3 49.2 %collective-permute-start.3 = (bf16[512,1024]{1,0:T(8,128)(2,1)}, bf16[512,1024]{1,0:T(8,128)(2,1)}, u32[]{:S(2)}, u32[]{:S(2)}) collective-permute-start(bf16[512,1024]{1,0:T(8,128)(2,1)} %fusion.6.refs_0_), channel_id=1, source_target_pairs={{0,1},{1,0},{2,3},{3,2},{4,5},{5,4},{6,7},{7,6},{8,9},{9,8},{10,11... | collective-permute-start | bytes 3145736 | tf_op jit(solution)/shard_map/ppermute | solution.py:670
  30.9 45.4 %collective-permute-start.1 = (bf16[512,1024]{1,0:T(8,128)(2,1)}, bf16[512,1024]{1,0:T(8,128)(2,1)}, u32[]{:S(2)}, u32[]{:S(2)}) collective-permute-start(bf16[512,1024]{1,0:T(8,128)(2,1)} %fusion.6.refs_0_), channel_id=1, source_target_pairs={{0,2},{1,3},{2,0},{3,1},{4,6},{5,7},{6,4},{7,5},{8,10},{9,11},{10,... | collective-permute-start | bytes 3145736 | tf_op jit(solution)/shard_map/ppermute | solution.py:670
  77.4 19.2 %collective-permute-start.2 = (bf16[256,1024]{1,0:T(8,128)(2,1)S(1)}, bf16[256,1024]{1,0:T(8,128)(2,1)S(1)}, u32[]{:S(2)}, u32[]{:S(2)}) collective-permute-start(bf16[256,1024]{1,0:T(8,128)(2,1)S(1)} %slice.264), channel_id=1, source_target_pairs={{0,1},{1,0},{2,3},{3,2},{4,5},{5,4},{6,7},{7,6},{8,9},{9,8},{10,11... | collective-permute-start | bytes 1572872 | tf_op jit(solution)/shard_map/ppermute | solution.py:670
  78.5 18.0 %collective-permute-start.4 = (bf16[256,1024]{1,0:T(8,128)(2,1)S(1)}, bf16[256,1024]{1,0:T(8,128)(2,1)S(1)}, u32[]{:S(2)}, u32[]{:S(2)}) collective-permute-start(bf16[256,1024]{1,0:T(8,128)(2,1)S(1)} %slice.265), channel_id=1, source_target_pairs={{0,2},{1,3},{2,0},{3,1},{4,6},{5,7},{6,4},{7,5},{8,10},{9,11},{10,... | collective-permute-start | bytes 1572872 | tf_op jit(solution)/shard_map/ppermute | solution.py:670
  145.8 38.8 %collective-permute-start.11 = (bf16[4,1184,1024]{2,1,0:T(8,128)(2,1)}, bf16[4,1184,1024]{2,1,0:T(8,128)(2,1)}, u32[]{:S(2)}, u32[]{:S(2)}) collective-permute-start(bf16[4,1184,1024]{2,1,0:T(8,128)(2,1)} %bitcast.133), channel_id=1, source_target_pairs={{0,16},{16,0},{1,17},{17,1},{2,18},{18,2},{3,19},{19,3},{4,20},{20... | collective-permute-start | bytes 29097992 | tf_op jit(solution)/shard_map/ppermute | solution.py:666
  145.9 403.9 %reduce-scatter.3.cloned.1.call-start = ((), (), s32[]{:S(2)}) async-start(), calls=%async_computation.2 | async-start | bytes 12124160 | tf_op jit(solution)/shard_map/reduce_scatter | solution.py:935
  147.4 18.4 %collective-permute-start.7 = (bf16[4,128,1024]{2,1,0:T(8,128)(2,1)S(1)}, bf16[4,128,1024]{2,1,0:T(8,128)(2,1)S(1)}, u32[]{:S(2)}, u32[]{:S(2)}) collective-permute-start(bf16[4,128,1024]{2,1,0:T(8,128)(2,1)S(1)} %slice.204.own_ref), channel_id=1, source_target_pairs={{0,16},{16,0},{1,17},{17,1},{2,18},{18,2},{3,19},{19,3},{4,20},{20... | collective-permute-start | bytes 3145736 | tf_op jit(solution)/shard_map/ppermute | solution.py:666
  149.4 16.3 %collective-permute-start.8 = (bf16[512,256]{1,0:T(8,128)(2,1)S(1)}, bf16[512,256]{1,0:T(8,128)(2,1)S(1)}, u32[]{:S(2)}, u32[]{:S(2)}) collective-permute-start(bf16[512,256]{1,0:T(8,128)(2,1)S(1)} %copy-done.88), channel_id=1, source_target_pairs={{0,1},{1,0},{2,3},{3,2},{4,5},{5,4},{6,7},{7,6},{8,9},{9,8},{10,11... | collective-permute-start | bytes 786440 | tf_op jit(solution)/shard_map/ppermute | solution.py:670
  150.9 14.8 %collective-permute-start.9 = (bf16[512,256]{1,0:T(8,128)(2,1)S(1)}, bf16[512,256]{1,0:T(8,128)(2,1)S(1)}, u32[]{:S(2)}, u32[]{:S(2)}) collective-permute-start(bf16[512,256]{1,0:T(8,128)(2,1)S(1)} %copy-done.89), channel_id=1, source_target_pairs={{0,2},{1,3},{2,0},{3,1},{4,6},{5,7},{6,4},{7,5},{8,10},{9,11},{10,... | collective-permute-start | bytes 786440 | tf_op jit(solution)/shard_map/ppermute | solution.py:670
  199.2 48.0 %collective-permute-start.12 = (bf16[512,1024]{1,0:T(8,128)(2,1)S(1)}, bf16[512,1024]{1,0:T(8,128)(2,1)S(1)}, u32[]{:S(2)}, u32[]{:S(2)}) collective-permute-start(bf16[512,1024]{1,0:T(8,128)(2,1)S(1)} %fusion.4.refs_0_), channel_id=1, source_target_pairs={{0,2},{1,3},{2,0},{3,1},{4,6},{5,7},{6,4},{7,5},{8,10},{9,11},{10,... | collective-permute-start | bytes 3145736 | tf_op jit(solution)/shard_map/ppermute | solution.py:670
  200.4 48.0 %collective-permute-start.14 = (bf16[512,1024]{1,0:T(8,128)(2,1)S(1)}, bf16[512,1024]{1,0:T(8,128)(2,1)S(1)}, u32[]{:S(2)}, u32[]{:S(2)}) collective-permute-start(bf16[512,1024]{1,0:T(8,128)(2,1)S(1)} %fusion.4.refs_0_), channel_id=1, source_target_pairs={{0,1},{1,0},{2,3},{3,2},{4,5},{5,4},{6,7},{7,6},{8,9},{9,8},{10,11... | collective-permute-start | bytes 3145736 | tf_op jit(solution)/shard_map/ppermute | solution.py:670
  247.2 25.3 %collective-permute-start.13 = (bf16[256,1024]{1,0:T(8,128)(2,1)S(1)}, bf16[256,1024]{1,0:T(8,128)(2,1)S(1)}, u32[]{:S(2)}, u32[]{:S(2)}) collective-permute-start(bf16[256,1024]{1,0:T(8,128)(2,1)S(1)} %slice.268), channel_id=1, source_target_pairs={{0,1},{1,0},{2,3},{3,2},{4,5},{5,4},{6,7},{7,6},{8,9},{9,8},{10,11... | collective-permute-start | bytes 1572872 | tf_op jit(solution)/shard_map/ppermute | solution.py:670
  248.5 25.4 %collective-permute-start.15 = (bf16[256,1024]{1,0:T(8,128)(2,1)S(1)}, bf16[256,1024]{1,0:T(8,128)(2,1)S(1)}, u32[]{:S(2)}, u32[]{:S(2)}) collective-permute-start(bf16[256,1024]{1,0:T(8,128)(2,1)S(1)} %slice.269), channel_id=1, source_target_pairs={{0,2},{1,3},{2,0},{3,1},{4,6},{5,7},{6,4},{7,5},{8,10},{9,11},{10,... | collective-permute-start | bytes 1572872 | tf_op jit(solution)/shard_map/ppermute | solution.py:670
  292.6 52.2 %collective-permute-start.20 = (bf16[4,1184,1024]{2,1,0:T(8,128)(2,1)}, bf16[4,1184,1024]{2,1,0:T(8,128)(2,1)}, u32[]{:S(2)}, u32[]{:S(2)}) collective-permute-start(bf16[4,1184,1024]{2,1,0:T(8,128)(2,1)} %bitcast.137), channel_id=1, source_target_pairs={{0,16},{16,0},{1,17},{17,1},{2,18},{18,2},{3,19},{19,3},{4,20},{20... | collective-permute-start | bytes 29097992 | tf_op jit(solution)/shard_map/ppermute | solution.py:666
  298.5 14.9 %collective-permute-start.16 = (bf16[4,128,1024]{2,1,0:T(8,128)(2,1)S(1)}, bf16[4,128,1024]{2,1,0:T(8,128)(2,1)S(1)}, u32[]{:S(2)}, u32[]{:S(2)}) collective-permute-start(bf16[4,128,1024]{2,1,0:T(8,128)(2,1)S(1)} %slice.209.own_ref), channel_id=1, source_target_pairs={{0,16},{16,0},{1,17},{17,1},{2,18},{18,2},{3,19},{19,3},{4,20},{20... | collective-permute-start | bytes 3145736 | tf_op jit(solution)/shard_map/ppermute | solution.py:666
  299.1 13.4 %collective-permute-start.18 = (bf16[512,256]{1,0:T(8,128)(2,1)S(1)}, bf16[512,256]{1,0:T(8,128)(2,1)S(1)}, u32[]{:S(2)}, u32[]{:S(2)}) collective-permute-start(bf16[512,256]{1,0:T(8,128)(2,1)S(1)} %copy-done.98), channel_id=1, source_target_pairs={{0,2},{1,3},{2,0},{3,1},{4,6},{5,7},{6,4},{7,5},{8,10},{9,11},{10,... | collective-permute-start | bytes 786440 | tf_op jit(solution)/shard_map/ppermute | solution.py:670
  300.9 12.2 %collective-permute-start.19 = (bf16[512,256]{1,0:T(8,128)(2,1)S(1)}, bf16[512,256]{1,0:T(8,128)(2,1)S(1)}, u32[]{:S(2)}, u32[]{:S(2)}) collective-permute-start(bf16[512,256]{1,0:T(8,128)(2,1)S(1)} %copy-done.99), channel_id=1, source_target_pairs={{0,3},{1,2},{2,1},{3,0},{4,7},{5,6},{6,5},{7,4},{8,11},{9,10},{10,... | collective-permute-start | bytes 786440 | tf_op jit(solution)/shard_map/ppermute | solution.py:670
  405.7 369.8 %reduce-scatter.5.cloned.1.call-start = ((), (), s32[]{:S(2)}) async-start(), calls=%async_computation.3 | async-start | bytes 12124160 | tf_op jit(solution)/shard_map/reduce_scatter | solution.py:935
  409.4 12.8 %collective-permute-start.22 = (bf16[512,256]{1,0:T(8,128)(2,1)S(1)}, bf16[512,256]{1,0:T(8,128)(2,1)S(1)}, u32[]{:S(2)}, u32[]{:S(2)}) collective-permute-start(bf16[512,256]{1,0:T(8,128)(2,1)S(1)} %get-tuple-element.290), channel_id=1, source_target_pairs={{0,1},{1,0},{2,3},{3,2},{4,5},{5,4},{6,7},{7,6},{8,9},{9,8},{10,11... | collective-permute-start | bytes 786440 | tf_op jit(solution)/shard_map/ppermute | solution.py:670
  410.8 15.3 %collective-permute-start.23 = (bf16[512,256]{1,0:T(8,128)(2,1)S(1)}, bf16[512,256]{1,0:T(8,128)(2,1)S(1)}, u32[]{:S(2)}, u32[]{:S(2)}) collective-permute-start(bf16[512,256]{1,0:T(8,128)(2,1)S(1)} %get-tuple-element.289), channel_id=1, source_target_pairs={{0,2},{1,3},{2,0},{3,1},{4,6},{5,7},{6,4},{7,5},{8,10},{9,11},{10,... | collective-permute-start | bytes 786440 | tf_op jit(solution)/shard_map/ppermute | solution.py:670
  411.6 22.2 %collective-permute-start.24 = (bf16[512,256]{1,0:T(8,128)(2,1)S(1)}, bf16[512,256]{1,0:T(8,128)(2,1)S(1)}, u32[]{:S(2)}, u32[]{:S(2)}) collective-permute-start(bf16[512,256]{1,0:T(8,128)(2,1)S(1)} %get-tuple-element.288), channel_id=1, source_target_pairs={{0,3},{1,2},{2,1},{3,0},{4,7},{5,6},{6,5},{7,4},{8,11},{9,10},{10,... | collective-permute-start | bytes 786440 | tf_op jit(solution)/shard_map/ppermute | solution.py:670
  462.6 22.3 %collective-permute-start.28 = (bf16[256,1024]{1,0:T(8,128)(2,1)S(1)}, bf16[256,1024]{1,0:T(8,128)(2,1)S(1)}, u32[]{:S(2)}, u32[]{:S(2)}) collective-permute-start(bf16[256,1024]{1,0:T(8,128)(2,1)S(1)} %get-tuple-element.287), channel_id=1, source_target_pairs={{0,2},{1,3},{2,0},{3,1},{4,6},{5,7},{6,4},{7,5},{8,10},{9,11},{10,... | collective-permute-start | bytes 1572872 | tf_op jit(solution)/shard_map/ppermute | solution.py:670
  464.7 35.6 %collective-permute-start.25 = (bf16[256,1024]{1,0:T(8,128)(2,1)S(1)}, bf16[256,1024]{1,0:T(8,128)(2,1)S(1)}, u32[]{:S(2)}, u32[]{:S(2)}) collective-permute-start(bf16[256,1024]{1,0:T(8,128)(2,1)S(1)} %slice.276), channel_id=1, source_target_pairs={{0,1},{1,0},{2,3},{3,2},{4,5},{5,4},{6,7},{7,6},{8,9},{9,8},{10,11... | collective-permute-start | bytes 1572872 | tf_op jit(solution)/shard_map/ppermute | solution.py:670
  466.6 31.0 %collective-permute-start.26 = (bf16[256,1024]{1,0:T(8,128)(2,1)S(1)}, bf16[256,1024]{1,0:T(8,128)(2,1)S(1)}, u32[]{:S(2)}, u32[]{:S(2)}) collective-permute-start(bf16[256,1024]{1,0:T(8,128)(2,1)S(1)} %get-tuple-element.286), channel_id=1, source_target_pairs={{0,1},{1,0},{2,3},{3,2},{4,5},{5,4},{6,7},{7,6},{8,9},{9,8},{10,11... | collective-permute-start | bytes 1572872 | tf_op jit(solution)/shard_map/ppermute | solution.py:670
  467.9 32.5 %collective-permute-start.30 = (bf16[256,1024]{1,0:T(8,128)(2,1)S(1)}, bf16[256,1024]{1,0:T(8,128)(2,1)S(1)}, u32[]{:S(2)}, u32[]{:S(2)}) collective-permute-start(bf16[256,1024]{1,0:T(8,128)(2,1)S(1)} %slice.282), channel_id=1, source_target_pairs={{0,2},{1,3},{2,0},{3,1},{4,6},{5,7},{6,4},{7,5},{8,10},{9,11},{10,... | collective-permute-start | bytes 1572872 | tf_op jit(solution)/shard_map/ppermute | solution.py:670
  485.1 35.0 %collective-permute-start.29 = (bf16[256,1024]{1,0:T(8,128)(2,1)S(1)}, bf16[256,1024]{1,0:T(8,128)(2,1)S(1)}, u32[]{:S(2)}, u32[]{:S(2)}) collective-permute-start(bf16[256,1024]{1,0:T(8,128)(2,1)S(1)} %add_convert_fusion.8), channel_id=1, source_target_pairs={{0,1},{1,0},{2,3},{3,2},{4,5},{5,4},{6,7},{7,6},{8,9},{9,8},{10,11... | collective-permute-start | bytes 1572872 | tf_op jit(solution)/shard_map/ppermute | solution.py:670
  497.8 25.4 %collective-permute-start.27 = (bf16[256,1024]{1,0:T(8,128)(2,1)S(1)}, bf16[256,1024]{1,0:T(8,128)(2,1)S(1)}, u32[]{:S(2)}, u32[]{:S(2)}) collective-permute-start(bf16[256,1024]{1,0:T(8,128)(2,1)S(1)} %add_convert_fusion.9), channel_id=1, source_target_pairs={{0,2},{1,3},{2,0},{3,1},{4,6},{5,7},{6,4},{7,5},{8,10},{9,11},{10,... | collective-permute-start | bytes 1572872 | tf_op jit(solution)/shard_map/ppermute | solution.py:670
  604.6 16.7 %collective-permute-start.50 = (bf16[2048,256]{1,0:T(8,128)(2,1)}, bf16[2048,256]{1,0:T(8,128)(2,1)}, u32[]{:S(2)}, u32[]{:S(2)}) collective-permute-start(bf16[2048,256]{1,0:T(8,128)(2,1)} %get-tuple-element.127.v_ref.refs_4_.refs_5_), channel_id=1, source_target_pairs={{0,16},{16,0},{1,17},{17,1},{2,18},{18,2},{3,19},{19,3},{4,20},{20... | collective-permute-start | bytes 3145736 | tf_op jit(solution)/shard_map/ppermute | solution.py:666
  613.1 17.6 %collective-permute-start.62 = (bf16[192,1024]{1,0:T(8,128)(2,1)S(1)}, bf16[192,1024]{1,0:T(8,128)(2,1)S(1)}, u32[]{:S(2)}, u32[]{:S(2)}) collective-permute-start(bf16[192,1024]{1,0:T(8,128)(2,1)S(1)} %constant_dynamic-slice_fusion.6), channel_id=1, source_target_pairs={{0,4},{4,0},{8,12},{12,8},{1,5},{5,1},{9,13},{13,9},{2,6},{6,2},{1... | collective-permute-start | bytes 1179656 | tf_op jit(solution)/shard_map/ppermute | solution.py:670
  630.8 11.7 %collective-permute-start.63 = (bf16[96,1024]{1,0:T(8,128)(2,1)S(1)}, bf16[96,1024]{1,0:T(8,128)(2,1)S(1)}, u32[]{:S(2)}, u32[]{:S(2)}) collective-permute-start(bf16[96,1024]{1,0:T(8,128)(2,1)S(1)} %constant_dynamic-slice_fusion.5), channel_id=1, source_target_pairs={{0,8},{4,12},{8,0},{12,4},{1,9},{5,13},{9,1},{13,5},{2,10},{6,14},... | collective-permute-start | bytes 589832 | tf_op jit(solution)/shard_map/ppermute | solution.py:670
  631.1 18.7 %collective-permute-start.21 = (bf16[512,1024]{1,0:T(8,128)(2,1)S(1)}, bf16[512,1024]{1,0:T(8,128)(2,1)S(1)}, u32[]{:S(2)}, u32[]{:S(2)}) collective-permute-start(bf16[512,1024]{1,0:T(8,128)(2,1)S(1)} %broadcast_select_fusion.7), channel_id=1, source_target_pairs={{0,16},{16,0},{1,17},{17,1},{2,18},{18,2},{3,19},{19,3},{4,20},{20... | collective-permute-start | bytes 3145736 | tf_op jit(solution)/shard_map/ppermute | solution.py:666
  644.0 32.5 %collective-permute-start.40 = (bf16[592,1024]{1,0:T(8,128)(2,1)}, bf16[592,1024]{1,0:T(8,128)(2,1)S(1)}, u32[]{:S(2)}, u32[]{:S(2)}) collective-permute-start(bf16[592,1024]{1,0:T(8,128)(2,1)} %get-tuple-element.254), channel_id=1, source_target_pairs={{0,4},{4,0},{8,12},{12,8},{1,5},{5,1},{9,13},{13,9},{2,6},{6,2},{1... | collective-permute-start | bytes 3637256 | tf_op jit(solution)/shard_map/ppermute | solution.py:670
  647.8 14.8 %collective-permute-start.37 = (bf16[512,256]{1,0:T(8,128)(2,1)S(1)}, bf16[512,256]{1,0:T(8,128)(2,1)S(1)}, u32[]{:S(2)}, u32[]{:S(2)}) collective-permute-start(bf16[512,256]{1,0:T(8,128)(2,1)S(1)} %get-tuple-element.278), channel_id=1, source_target_pairs={{0,1},{1,0},{2,3},{3,2},{4,5},{5,4},{6,7},{7,6},{8,9},{9,8},{10,11... | collective-permute-start | bytes 786440 | tf_op jit(solution)/shard_map/ppermute | solution.py:670
  648.9 15.7 %collective-permute-start.38 = (bf16[512,256]{1,0:T(8,128)(2,1)S(1)}, bf16[512,256]{1,0:T(8,128)(2,1)S(1)}, u32[]{:S(2)}, u32[]{:S(2)}) collective-permute-start(bf16[512,256]{1,0:T(8,128)(2,1)S(1)} %get-tuple-element.277), channel_id=1, source_target_pairs={{0,2},{1,3},{2,0},{3,1},{4,6},{5,7},{6,4},{7,5},{8,10},{9,11},{10,... | collective-permute-start | bytes 786440 | tf_op jit(solution)/shard_map/ppermute | solution.py:670
  649.8 22.5 %collective-permute-start.39 = (bf16[512,256]{1,0:T(8,128)(2,1)S(1)}, bf16[512,256]{1,0:T(8,128)(2,1)S(1)}, u32[]{:S(2)}, u32[]{:S(2)}) collective-permute-start(bf16[512,256]{1,0:T(8,128)(2,1)S(1)} %get-tuple-element.276), channel_id=1, source_target_pairs={{0,3},{1,2},{2,1},{3,0},{4,7},{5,6},{6,5},{7,4},{8,11},{9,10},{10,... | collective-permute-start | bytes 786440 | tf_op jit(solution)/shard_map/ppermute | solution.py:670
  677.1 27.3 %collective-permute-start.41 = (bf16[296,1024]{1,0:T(8,128)(2,1)S(1)}, bf16[296,1024]{1,0:T(8,128)(2,1)S(1)}, u32[]{:S(2)}, u32[]{:S(2)}) collective-permute-start(bf16[296,1024]{1,0:T(8,128)(2,1)S(1)} %get-tuple-element.266), channel_id=1, source_target_pairs={{0,8},{4,12},{8,0},{12,4},{1,9},{5,13},{9,1},{13,5},{2,10},{6,14},... | collective-permute-start | bytes 1818632 | tf_op jit(solution)/shard_map/ppermute | solution.py:670
  708.5 28.4 %collective-permute-start.45 = (bf16[256,1024]{1,0:T(8,128)(2,1)}, bf16[256,1024]{1,0:T(8,128)(2,1)S(1)}, u32[]{:S(2)}, u32[]{:S(2)}) collective-permute-start(bf16[256,1024]{1,0:T(8,128)(2,1)} %get-tuple-element.275), channel_id=1, source_target_pairs={{0,2},{1,3},{2,0},{3,1},{4,6},{5,7},{6,4},{7,5},{8,10},{9,11},{10,... | collective-permute-start | bytes 1572872 | tf_op jit(solution)/shard_map/ppermute | solution.py:670
  710.9 37.5 %collective-permute-start.42 = (bf16[256,1024]{1,0:T(8,128)(2,1)}, bf16[256,1024]{1,0:T(8,128)(2,1)}, u32[]{:S(2)}, u32[]{:S(2)}) collective-permute-start(bf16[256,1024]{1,0:T(8,128)(2,1)} %slice.294), channel_id=1, source_target_pairs={{0,1},{1,0},{2,3},{3,2},{4,5},{5,4},{6,7},{7,6},{8,9},{9,8},{10,11... | collective-permute-start | bytes 1572872 | tf_op jit(solution)/shard_map/ppermute | solution.py:670
  712.5 26.6 %collective-permute-start.43 = (bf16[256,1024]{1,0:T(8,128)(2,1)}, bf16[256,1024]{1,0:T(8,128)(2,1)}, u32[]{:S(2)}, u32[]{:S(2)}) collective-permute-start(bf16[256,1024]{1,0:T(8,128)(2,1)} %get-tuple-element.274), channel_id=1, source_target_pairs={{0,1},{1,0},{2,3},{3,2},{4,5},{5,4},{6,7},{7,6},{8,9},{9,8},{10,11... | collective-permute-start | bytes 1572872 | tf_op jit(solution)/shard_map/ppermute | solution.py:670
  714.8 35.5 %collective-permute-start.47 = (bf16[256,1024]{1,0:T(8,128)(2,1)}, bf16[256,1024]{1,0:T(8,128)(2,1)}, u32[]{:S(2)}, u32[]{:S(2)}) collective-permute-start(bf16[256,1024]{1,0:T(8,128)(2,1)} %slice.300), channel_id=1, source_target_pairs={{0,2},{1,3},{2,0},{3,1},{4,6},{5,7},{6,4},{7,5},{8,10},{9,11},{10,... | collective-permute-start | bytes 1572872 | tf_op jit(solution)/shard_map/ppermute | solution.py:670
  724.8 17.4 %collective-permute-start.56 = (bf16[512,768]{1,0:T(8,128)(2,1)S(1)}, bf16[512,768]{1,0:T(8,128)(2,1)S(1)}, u32[]{:S(2)}, u32[]{:S(2)}) collective-permute-start(bf16[512,768]{1,0:T(8,128)(2,1)S(1)} %constant_dynamic-slice_fusion.10), channel_id=1, source_target_pairs={{0,16},{16,0},{1,17},{17,1},{2,18},{18,2},{3,19},{19,3},{4,20},{20... | collective-permute-start | bytes 2359304 | tf_op jit(solution)/shard_map/ppermute | solution.py:666
  738.0 14.2 %collective-permute-start.46 = (bf16[256,1024]{1,0:T(8,128)(2,1)}, bf16[256,1024]{1,0:T(8,128)(2,1)}, u32[]{:S(2)}, u32[]{:S(2)}) collective-permute-start(bf16[256,1024]{1,0:T(8,128)(2,1)} %add_convert_fusion.6), channel_id=1, source_target_pairs={{0,1},{1,0},{2,3},{3,2},{4,5},{5,4},{6,7},{7,6},{8,9},{9,8},{10,11... | collective-permute-start | bytes 1572872 | tf_op jit(solution)/shard_map/ppermute | solution.py:670
  741.1 13.9 %collective-permute-start.44 = (bf16[256,1024]{1,0:T(8,128)(2,1)}, bf16[256,1024]{1,0:T(8,128)(2,1)}, u32[]{:S(2)}, u32[]{:S(2)}) collective-permute-start(bf16[256,1024]{1,0:T(8,128)(2,1)} %add_convert_fusion.7), channel_id=1, source_target_pairs={{0,2},{1,3},{2,0},{3,1},{4,6},{5,7},{6,4},{7,5},{8,10},{9,11},{10,... | collective-permute-start | bytes 1572872 | tf_op jit(solution)/shard_map/ppermute | solution.py:670
  742.2 29.3 %collective-permute-start.48 = (bf16[296,1024]{1,0:T(8,128)(2,1)S(1)}, bf16[296,1024]{1,0:T(8,128)(2,1)}, u32[]{:S(2)}, u32[]{:S(2)}) collective-permute-start(bf16[296,1024]{1,0:T(8,128)(2,1)S(1)} %add_convert_fusion.4), channel_id=1, source_target_pairs={{0,8},{4,12},{8,0},{12,4},{1,9},{5,13},{9,1},{13,5},{2,10},{6,14},... | collective-permute-start | bytes 1818632 | tf_op jit(solution)/shard_map/ppermute | solution.py:670
  748.4 175.0 %collective-permute-start.65 = (bf16[192,1024]{1,0:T(8,128)(2,1)}, bf16[192,1024]{1,0:T(8,128)(2,1)}, u32[]{:S(2)}, u32[]{:S(2)}) collective-permute-start(bf16[192,1024]{1,0:T(8,128)(2,1)} %place_rows.10.first_ref), channel_id=1, source_target_pairs={{0,4},{4,0},{8,12},{12,8},{1,5},{5,1},{9,13},{13,9},{2,6},{6,2},{1... | collective-permute-start | bytes 1179656 | tf_op jit(solution)/shard_map/ppermute | solution.py:670
  750.3 33.7 %collective-permute-start.57 = (bf16[192,1024]{1,0:T(8,128)(2,1)}, bf16[192,1024]{1,0:T(8,128)(2,1)}, u32[]{:S(2)}, u32[]{:S(2)}) collective-permute-start(bf16[192,1024]{1,0:T(8,128)(2,1)} %constant_dynamic-slice_fusion.9), channel_id=1, source_target_pairs={{0,4},{4,0},{8,12},{12,8},{1,5},{5,1},{9,13},{13,9},{2,6},{6,2},{1... | collective-permute-start | bytes 1179656 | tf_op jit(solution)/shard_map/ppermute | solution.py:670
  776.9 16.2 %collective-permute-start.73 = (bf16[288,1024]{1,0:T(8,128)(2,1)S(1)}, bf16[288,1024]{1,0:T(8,128)(2,1)S(1)}, u32[]{:S(2)}, u32[]{:S(2)}) collective-permute-start(bf16[288,1024]{1,0:T(8,128)(2,1)S(1)} %constant_dynamic-slice_fusion.4), channel_id=1, source_target_pairs={{0,4},{4,0},{8,12},{12,8},{1,5},{5,1},{9,13},{13,9},{2,6},{6,2},{1... | collective-permute-start | bytes 1769480 | tf_op jit(solution)/shard_map/ppermute | solution.py:670
  780.3 32.5 %collective-permute-start.77 = (bf16[304,1024]{1,0:T(8,128)(2,1)S(1)}, bf16[304,1024]{1,0:T(8,128)(2,1)S(1)}, u32[]{:S(2)}, u32[]{:S(2)}) collective-permute-start(bf16[304,1024]{1,0:T(8,128)(2,1)S(1)} %constant_dynamic-slice_fusion.2), channel_id=1, source_target_pairs={{0,4},{4,0},{8,12},{12,8},{1,5},{5,1},{9,13},{13,9},{2,6},{6,2},{1... | collective-permute-start | bytes 1867784 | tf_op jit(solution)/shard_map/ppermute | solution.py:670
  782.6 109.3 %collective-permute-start.81 = (bf16[592,1024]{1,0:T(8,128)(2,1)S(1)}, bf16[592,1024]{1,0:T(8,128)(2,1)}, u32[]{:S(2)}, u32[]{:S(2)}) collective-permute-start(bf16[592,1024]{1,0:T(8,128)(2,1)S(1)} %pad_maximum_fusion.6.first_ref), channel_id=1, source_target_pairs={{0,4},{4,0},{8,12},{12,8},{1,5},{5,1},{9,13},{13,9},{2,6},{6,2},{1... | collective-permute-start | bytes 3637256 | tf_op jit(solution)/shard_map/ppermute | solution.py:670
  784.0 148.3 %collective-permute-start.49 = (bf16[512,1024]{1,0:T(8,128)(2,1)}, bf16[512,1024]{1,0:T(8,128)(2,1)S(1)}, u32[]{:S(2)}, u32[]{:S(2)}) collective-permute-start(bf16[512,1024]{1,0:T(8,128)(2,1)} %get-tuple-element.227), channel_id=1, source_target_pairs={{0,16},{16,0},{1,17},{17,1},{2,18},{18,2},{3,19},{19,3},{4,20},{20... | collective-permute-start | bytes 3145736 | tf_op jit(solution)/shard_map/ppermute | solution.py:666
  793.4 43.4 %collective-permute-start.74 = (bf16[144,1024]{1,0:T(8,128)(2,1)S(1)}, bf16[144,1024]{1,0:T(8,128)(2,1)S(1)}, u32[]{:S(2)}, u32[]{:S(2)}) collective-permute-start(bf16[144,1024]{1,0:T(8,128)(2,1)S(1)} %constant_dynamic-slice_fusion.3), channel_id=1, source_target_pairs={{0,8},{4,12},{8,0},{12,4},{1,9},{5,13},{9,1},{13,5},{2,10},{6,14},... | collective-permute-start | bytes 884744 | tf_op jit(solution)/shard_map/ppermute | solution.py:670
  813.1 30.5 %collective-permute-start.78 = (bf16[152,1024]{1,0:T(8,128)(2,1)S(1)}, bf16[152,1024]{1,0:T(8,128)(2,1)S(1)}, u32[]{:S(2)}, u32[]{:S(2)}) collective-permute-start(bf16[152,1024]{1,0:T(8,128)(2,1)S(1)} %constant_dynamic-slice_fusion.1), channel_id=1, source_target_pairs={{0,8},{4,12},{8,0},{12,4},{1,9},{5,13},{9,1},{13,5},{2,10},{6,14},... | collective-permute-start | bytes 933896 | tf_op jit(solution)/shard_map/ppermute | solution.py:670
  836.8 24.5 %collective-permute-start.58 = (bf16[96,1024]{1,0:T(8,128)(2,1)S(1)}, bf16[96,1024]{1,0:T(8,128)(2,1)S(1)}, u32[]{:S(2)}, u32[]{:S(2)}) collective-permute-start(bf16[96,1024]{1,0:T(8,128)(2,1)S(1)} %constant_dynamic-slice_fusion.8), channel_id=1, source_target_pairs={{0,8},{4,12},{8,0},{12,4},{1,9},{5,13},{9,1},{13,5},{2,10},{6,14},... | collective-permute-start | bytes 589832 | tf_op jit(solution)/shard_map/ppermute | solution.py:670
  843.5 30.8 %collective-permute-start.75 = (bf16[144,1024]{1,0:T(8,128)(2,1)S(1)}, bf16[144,1024]{1,0:T(8,128)(2,1)S(1)}, u32[]{:S(2)}, u32[]{:S(2)}) collective-permute-start(bf16[144,1024]{1,0:T(8,128)(2,1)S(1)} %add_convert_fusion.13.first_ref), channel_id=1, source_target_pairs={{0,8},{4,12},{8,0},{12,4},{1,9},{5,13},{9,1},{13,5},{2,10},{6,14},... | collective-permute-start | bytes 884744 | tf_op jit(solution)/shard_map/ppermute | solution.py:670
  861.3 23.9 %collective-permute-start.79 = (bf16[152,1024]{1,0:T(8,128)(2,1)S(1)}, bf16[152,1024]{1,0:T(8,128)(2,1)S(1)}, u32[]{:S(2)}, u32[]{:S(2)}) collective-permute-start(bf16[152,1024]{1,0:T(8,128)(2,1)S(1)} %add_convert_fusion.12), channel_id=1, source_target_pairs={{0,8},{4,12},{8,0},{12,4},{1,9},{5,13},{9,1},{13,5},{2,10},{6,14},... | collective-permute-start | bytes 933896 | tf_op jit(solution)/shard_map/ppermute | solution.py:670
  874.3 15.1 %collective-permute-start.59 = (bf16[96,1024]{1,0:T(8,128)(2,1)S(1)}, bf16[96,1024]{1,0:T(8,128)(2,1)S(1)}, u32[]{:S(2)}, u32[]{:S(2)}) collective-permute-start(bf16[96,1024]{1,0:T(8,128)(2,1)S(1)} %add_convert_fusion.15.first_ref), channel_id=1, source_target_pairs={{0,8},{4,12},{8,0},{12,4},{1,9},{5,13},{9,1},{13,5},{2,10},{6,14},... | collective-permute-start | bytes 589832 | tf_op jit(solution)/shard_map/ppermute | solution.py:670
  885.2 16.9 %collective-permute-start.76 = (bf16[288,1024]{1,0:T(8,128)(2,1)}, bf16[288,1024]{1,0:T(8,128)(2,1)S(1)}, u32[]{:S(2)}, u32[]{:S(2)}) collective-permute-start(bf16[288,1024]{1,0:T(8,128)(2,1)} %place_rows.12.first_ref), channel_id=1, source_target_pairs={{0,4},{4,0},{8,12},{12,8},{1,5},{5,1},{9,13},{13,9},{2,6},{6,2},{1... | collective-permute-start | bytes 1769480 | tf_op jit(solution)/shard_map/ppermute | solution.py:670
  889.4 26.1 %collective-permute-start.80 = (bf16[304,1024]{1,0:T(8,128)(2,1)S(1)}, bf16[304,1024]{1,0:T(8,128)(2,1)}, u32[]{:S(2)}, u32[]{:S(2)}) collective-permute-start(bf16[304,1024]{1,0:T(8,128)(2,1)S(1)} %pad_maximum_fusion.9.first_ref), channel_id=1, source_target_pairs={{0,4},{4,0},{8,12},{12,8},{1,5},{5,1},{9,13},{13,9},{2,6},{6,2},{1... | collective-permute-start | bytes 1867784 | tf_op jit(solution)/shard_map/ppermute | solution.py:670
  891.9 31.5 %collective-permute-start.54 = (f32[4128]{0:T(1024)S(1)}, f32[4128]{0:T(1024)S(1)}, u32[]{:S(2)}, u32[]{:S(2)}) collective-permute-start(f32[4128]{0:T(1024)S(1)} %add.311), channel_id=1, source_target_pairs={{0,4},{4,0},{8,12},{12,8},{1,5},{5,1},{9,13},{13,9},{2,6},{6,2},{1... | collective-permute-start | bytes 49544 | tf_op jit(solution)/shard_map/ppermute | solution.py:670
  902.0 26.8 %collective-permute-start.60 = (bf16[192,1024]{1,0:T(8,128)(2,1)}, bf16[192,1024]{1,0:T(8,128)(2,1)}, u32[]{:S(2)}, u32[]{:S(2)}) collective-permute-start(bf16[192,1024]{1,0:T(8,128)(2,1)} %place_rows.8.first_ref), channel_id=1, source_target_pairs={{0,4},{4,0},{8,12},{12,8},{1,5},{5,1},{9,13},{13,9},{2,6},{6,2},{1... | collective-permute-start | bytes 1179656 | tf_op jit(solution)/shard_map/ppermute | solution.py:670
  921.9 21.0 %collective-permute-start.82 = (bf16[1184,1024]{1,0:T(8,128)(2,1)}, bf16[1184,1024]{1,0:T(8,128)(2,1)}, u32[]{:S(2)}, u32[]{:S(2)}) collective-permute-start(bf16[1184,1024]{1,0:T(8,128)(2,1)} %broadcast_select_fusion.2), channel_id=1, source_target_pairs={{0,16},{16,0},{1,17},{17,1},{2,18},{18,2},{3,19},{19,3},{4,20},{20... | collective-permute-start | bytes 7274504 | tf_op jit(solution)/shard_map/ppermute | solution.py:666
  (145 other events, 1145.2 us)
Sparse Core Ops, SparseCore 0:
  22.1 123.6 all-gather.4
  148.2 134.4 all-gather.6
  405.8 131.8 reduce-scatter.2
  594.9 113.0 reduce-scatter.4

commit v3 on v2

--- a/solution.py
+++ b/solution.py
@@ -532,13 +532,15 @@
         out_shape=[jax.ShapeDtypeStruct((rows, model), F32), shape, shape],
         scratch_shapes=[pltpu.VMEM((3, hidden, model), BF16), pltpu.SemaphoreType.DMA((3, mp))],
         compiler_params=pltpu.CompilerParams(vmem_limit_bytes=VMEM_BYTES),
-        cost_estimate=cost(9),
+        cost_estimate=cost(1),
         name="ffn_back",
     )(*args)
 
 
-def pack_grads_kernel(size, *refs):
-    gate, got_gate, up, got_up, act, got_act, x_ref, got_x, g_ref, got_g, out_grad, pack_ref = refs
+def pack_grads_kernel(size, plain, halves, info_ref, *refs):
+    gate, got_gate, up, got_up, act, got_act, x_ref, got_x, g_ref, got_g, out_grad = refs[:11]
+    out_refs = refs[11:]
+    pack_ref = out_refs[-1]
     count = pack_ref.shape[0]
     jobs = ((gate, x_ref, got_gate, got_x), (up, x_ref, got_up, got_x), (act, g_ref, got_act, got_g))
     for at, (left, right, left_two, right_two) in enumerate(jobs):
@@ -547,30 +549,57 @@
             pack_ref[part, at * size : (at + 1) * size, :] = acc[part * size : (part + 1) * size].astype(BF16)
     for part in range(count):
         pack_ref[part, 3 * size :, :] = out_grad[part]
-
-
-def pack_grads(inner, got_inner, normed, got_normed, g_branch, got_branch, out_grad):
+    if plain:
+        out_refs[0][...] = pack_ref[:, :plain, :]
+        out_refs = out_refs[1:]
+    if halves:
+        cut = plain + halves
+
+        @pl.when(info_ref[0] == 0)
+        def _():
+            out_refs[0][...] = pack_ref[:, plain:cut, :]
+            out_refs[1][...] = pack_ref[:, cut:, :]
+
+        @pl.when(info_ref[0] == 1)
+        def _():
+            out_refs[0][...] = pack_ref[:, cut:, :]
+            out_refs[1][...] = pack_ref[:, plain:cut, :]
+
+
+def pack_grads(inner, got_inner, normed, got_normed, g_branch, got_branch, out_grad, plain, first):
     rows, model = normed.shape
     hidden = inner[0].shape[1]
     mp, out_half = out_grad.shape[:2]
     size = hidden // mp
     block = min(512, model)
-    left = pl.BlockSpec((rows, hidden), lambda j: (0, 0))
-    right = pl.BlockSpec((rows, block), lambda j: (0, j))
+    left = pl.BlockSpec((rows, hidden), lambda j, n: (0, 0))
+    right = pl.BlockSpec((rows, block), lambda j, n: (0, j))
     pack_rows = 3 * size + out_half
     args = []
     for own, got in zip(inner, got_inner):
         args += [own, got]
+    halves = (pack_rows - plain) // 2
+    if halves == 0:
+        plain, sizes, scratch = 0, [pack_rows], []
+    else:
+        sizes = ([plain] if plain else []) + [halves, halves]
+        scratch = [pltpu.VMEM((mp, pack_rows, block), BF16)]
     return pl.pallas_call(
-        functools.partial(pack_grads_kernel, size),
-        grid=(model // block,),
-        in_specs=[left] * 6 + [right] * 4 + [pl.BlockSpec((mp, out_half, block), lambda j: (0, 0, j))],
-        out_specs=pl.BlockSpec((mp, pack_rows, block), lambda j: (0, 0, j)),
-        out_shape=jax.ShapeDtypeStruct((mp, pack_rows, model), BF16),
+        functools.partial(pack_grads_kernel, size, plain, halves),
+        grid_spec=pltpu.PrefetchScalarGridSpec(
+            num_scalar_prefetch=1,
+            grid=(model // block,),
+            in_specs=[left] * 6
+            + [right] * 4
+            + [pl.BlockSpec((mp, out_half, block), lambda j, n: (0, 0, j))],
+            out_specs=[pl.BlockSpec((mp, part, block), lambda j, n: (0, 0, j)) for part in sizes],
+            scratch_shapes=scratch,
+        ),
+        out_shape=[jax.ShapeDtypeStruct((mp, part, model), BF16) for part in sizes],
         compiler_params=pltpu.CompilerParams(vmem_limit_bytes=VMEM_BYTES),
         cost_estimate=cost(15),
         name="pack_grads",
-    )(*args, normed, got_normed, g_branch, got_branch, out_grad)
+    )(first.astype(jnp.int32).reshape(1), *args, normed, got_normed, g_branch, got_branch, out_grad)
 
 
 def place_kernel(which_ref, first_ref, second_ref, out_ref):
@@ -583,24 +612,30 @@
         out_ref[...] = second_ref[...]
 
 
-def place_rows(first, second, which):
+def place_two(first, second, which, axis):
     rows, model = first.shape
-    if rows % 16:
+    if (rows, model)[axis] % (16, 128)[axis]:
         ordered = jnp.where(which == 0, first, second), jnp.where(which == 0, second, first)
-        return jnp.concatenate(ordered, axis=0)
+        return jnp.concatenate(ordered, axis=axis)
     whole = pl.BlockSpec((rows, model), lambda i, w: (0, 0))
+
+    def target(i, w):
+        spot = jnp.bitwise_xor(w[0], i)
+        return (spot, 0) if axis == 0 else (0, spot)
+
+    shape = (2 * rows, model) if axis == 0 else (rows, 2 * model)
     return pl.pallas_call(
         place_kernel,
         grid_spec=pltpu.PrefetchScalarGridSpec(
             num_scalar_prefetch=1,
             grid=(2,),
             in_specs=[whole, whole],
-            out_specs=pl.BlockSpec((rows, model), lambda i, w: (jnp.bitwise_xor(w[0], i), 0)),
+            out_specs=pl.BlockSpec((rows, model), target),
         ),
-        out_shape=jax.ShapeDtypeStruct((2 * rows, model), first.dtype),
+        out_shape=jax.ShapeDtypeStruct(shape, first.dtype),
         compiler_params=pltpu.CompilerParams(vmem_limit_bytes=VMEM_BYTES),
         cost_estimate=cost(2),
-        name="place_rows",
+        name="place_two",
     )(which.astype(jnp.int32).reshape(1), first, second)
 
 
@@ -716,21 +751,21 @@
     bits, which = ((1, low), (2, high), (2, high), (1, low))[step]
     if step < 2:
         whole = kept if got is None else (kept.astype(F32) + got.astype(F32)).astype(BF16)
-        size = whole.shape[0] // 2
-        kept = lax.dynamic_slice_in_dim(whole, which * size, size, 0)
-        sent = lax.dynamic_slice_in_dim(whole, (1 - which) * size, size, 0)
+        size = whole.shape[1] // 2
+        kept = lax.dynamic_slice_in_dim(whole, which * size, size, 1)
+        sent = lax.dynamic_slice_in_dim(whole, (1 - which) * size, size, 1)
         return kept, across(sent, "dp", bits)
     if step == 2:
         whole = (kept.astype(F32) + got.astype(F32)).astype(BF16)
     else:
-        whole = place_rows(kept, got, high)
+        whole = place_two(kept, got, high, 1)
     return whole, across(whole, "dp", bits)
 
 
 def sum_groups_end(state):
     if lax.axis_size("dp") != 4:
         return state[0]
-    return place_rows(state[0], state[1], lax.axis_index("dp") % 2)
+    return place_two(state[0], state[1], lax.axis_index("dp") % 2, 1)
 
 
 def sum_groups(value, state=None, start=0):
@@ -741,20 +776,53 @@
     return sum_groups_end(state)
 
 
-class Hook:
-    def __init__(self, value):
-        self.state = (value, None)
-        self.step = 0
+def add_low(left, right):
+    return (left.astype(F32) + right.astype(F32)).astype(BF16)
+
+
+def scatter_parts(parts):
+    rows = parts.reshape(-1, parts.shape[2])
+    return lax.psum_scatter(rows, "mp", scatter_dimension=0, tiled=True)
+
+
+class Chain:
+    def __init__(self, state, steps, last):
+        self.state, self.steps, self.last = state, list(steps), last
 
     def tie(self, value):
-        value, self.state = lax.optimization_barrier((value, self.state))
-        if self.step < group_steps():
-            self.state = sum_groups_step(self.step, self.state)
-            self.step += 1
+        if self.steps:
+            value, self.state = lax.optimization_barrier((value, self.state))
+            self.state = self.steps.pop(0)(self.state)
         return value
 
     def end(self):
-        return sum_groups(None, self.state, self.step)
+        while self.steps:
+            self.state = self.steps.pop(0)(self.state)
+        return self.last(self.state)
+
+
+def groups_chain(parts):
+    steps = [lambda state: sum_groups_step(0, (state, None))]
+    steps += [functools.partial(sum_groups_step, step) for step in range(1, group_steps())]
+    return Chain(scatter_parts(parts), steps, sum_groups_end)
+
+
+def plain_chain(value):
+    steps = [functools.partial(sum_groups_step, step) for step in range(1, group_steps())]
+    return Chain(sum_groups_step(0, (value, None)), steps, sum_groups_end)
+
+
+def halves_chain(kept, sent):
+    steps = [
+        lambda state: scatter_parts(add_low(*state)),
+        lambda state: (state, across(state, "dp", 2)),
+        lambda state: (lambda total: (total, across(total, "dp", 1)))(add_low(*state)),
+    ]
+    return Chain(
+        (kept, across(sent, "dp", 1)),
+        steps,
+        lambda state: place_two(state[0], state[1], lax.axis_index("dp") % 2, 0),
+    )
 
 
 def by_distance(blocks, place):
@@ -822,6 +890,10 @@
     gains = jnp.concatenate([attn_gain, ffn_gain], axis=0)
     layer_gains = in_order(gains, swap_cores(gains))
 
+    first_normed = normalize(inputs.astype(F32), layer_gains[0][0]).astype(BF16)
+    first_normed, gate_weight, up_weight, down_weight, out_weight = lax.optimization_barrier(
+        (first_normed, gate_weight, up_weight, down_weight, out_weight)
+    )
     halves = jnp.concatenate(
         [
             gate_weight[0].T.reshape(2, hid_half, model),
@@ -863,10 +935,11 @@
         moved = {i: across(blocks[i], "mp", i) for i in (3, 1, 2)}
         return [blocks[0], moved[1], moved[2], moved[3]]
 
-    def forward(rows_low, first, weights):
+    def forward(rows_low, first, weights, normed=None):
         gain_a, gain_f, qkv_w, pieces_w = weights
         state = rows_low.astype(F32)
-        normed = normalize(state, gain_a).astype(BF16)
+        if normed is None:
+            normed = normalize(state, gain_a).astype(BF16)
         pieces = spread_rows(normed)
         held = None
         for index, piece in enumerate(pieces):
@@ -890,8 +963,18 @@
         kept_items += (own, other, out_full)
         return result.astype(BF16), values, kept_items
 
-    def backward(g_result, g_first, weights, kept_items, hook=None):
-        tie = hook.tie if hook is not None else lambda value: value
+    split = square and lax.axis_size("dp") == 4
+    plain_rows = {False: pack_rows, True: pack_rows}
+    if split:
+        plain_rows = {False: 0, True: pack_rows // 64 * 32 + 32}
+
+    def tied(chains, value):
+        for chain in chains:
+            value = chain.tie(value)
+        return value
+
+    def backward(g_result, g_first, weights, kept_items, earlier=()):
+        late = len(earlier) > 0
 
         gain_a, gain_f, qkv_w, unused = weights
         state, pieces, queries, keys, values, attended, lse, att_rows, middle, normed_ffn, inner = kept_items[:11]
@@ -904,59 +987,80 @@
             g_normed, g_gate, g_up = ffn_backward(g_branch, g_normed, silu, slope, share)
             g_inner.append((g_gate, g_up, activated))
         got_gate, got_up = swap_cores(g_inner[1][0]), swap_cores(g_inner[1][1])
-        g_normed = tie(g_normed)
+        if late:
+            g_normed = tied(earlier[0], g_normed)
         g_norm, g_gain_f = normalize_back(middle, gain_f, g_normed)
         g_middle = g_result + g_norm
         g_mid_low = g_middle.astype(BF16)
-        g_att = to_heads(mm(g_mid_low, out_full, NT).astype(BF16))
-        g_att = tie(g_att)
+        g_att_rows = mm(g_mid_low, out_full, NT).astype(BF16)
+        g_att_rows, got_gate, got_up = lax.optimization_barrier((g_att_rows, got_gate, got_up))
+        g_att = to_heads(g_att_rows)
+
+        def make_packs():
+            att_whole = jnp.concatenate(att_rows, axis=1)
+            out_grad = mm(att_whole, g_mid_low, TN).astype(BF16).reshape(mp, 2, out_half, model)
+            out_kept = lax.dynamic_index_in_dim(out_grad, core, 1, keepdims=False)
+            out_sent = lax.dynamic_index_in_dim(out_grad, 1 - core, 1, keepdims=False)
+            out_grad = (out_kept.astype(F32) + swap_cores(out_sent).astype(F32)).astype(BF16)
+            return pack_grads(
+                g_inner[0],
+                (got_gate, got_up, got_act),
+                normed_ffn,
+                got_normed,
+                g_branch,
+                got_branch,
+                by_distance(out_grad, place),
+                plain_rows[late],
+                lax.axis_index("dp") % 2,
+            )
+
+        if not late:
+            hidden_packs = make_packs()
+            g_att, hidden_packs = lax.optimization_barrier((g_att, hidden_packs))
+        if late:
+            g_att = tied(earlier[1], g_att)
         g_qkv = attend_back(queries, keys, values, lse, cosine, sine, attended, g_att, g_first, info)
-        g_qkv = tie(g_qkv)
+        packs = hidden_packs if not late else make_packs()
+        own_chains = [groups_chain(packs[0])] if len(packs) != 2 else []
+        if split:
+            own_chains.append(halves_chain(packs[-2], packs[-1]))
+        if late:
+            g_qkv = tied(earlier[2] + own_chains[:1], g_qkv)
         g_parts = [mm(part, qkv_w, NT).astype(BF16) for part in g_qkv]
         if not square:
             g_parts = [g_parts[0][i * tok_rows : (i + 1) * tok_rows] for i in range(mp)]
-        g_norm, g_gain_a = normalize_back(state, gain_a, tie(sum_rows_to_owner(g_parts)))
+        g_rows = tied(earlier[3] if late else (), sum_rows_to_owner(g_parts))
+        g_norm, g_gain_a = normalize_back(state, gain_a, g_rows)
         g_inputs = g_middle + g_norm
-
-        att_whole = jnp.concatenate(att_rows, axis=1)
-        out_grad = mm(att_whole, g_mid_low, TN).astype(BF16).reshape(mp, 2, out_half, model)
-        out_kept = lax.dynamic_index_in_dim(out_grad, core, 1, keepdims=False)
-        out_sent = lax.dynamic_index_in_dim(out_grad, 1 - core, 1, keepdims=False)
-        out_grad = (out_kept.astype(F32) + swap_cores(out_sent).astype(F32)).astype(BF16)
-        pack = pack_grads(
-            g_inner[0],
-            (got_gate, got_up, got_act),
-            normed_ffn,
-            got_normed,
-            g_branch,
-            got_branch,
-            by_distance(out_grad, place),
-        )
-        ffn_grads = lax.psum_scatter(pack.reshape(mp * pack_rows, model), "mp", scatter_dimension=0, tiled=True)
-        qkv_grad = qkv_grad_sum(pieces, g_qkv)
+        qkv_grad = qkv_grad_sum(pieces, tied(own_chains[1:], g_qkv) if late else g_qkv)
         qkv_grad = pick_half(qkv_grad, core).astype(F32) + swap_cores(pick_half(qkv_grad, 1 - core)).astype(F32)
-        return g_inputs, g_qkv, (ffn_grads, qkv_grad, g_gain_a, g_gain_f)
+        qkv_grad = qkv_grad.reshape(-1, model).astype(BF16)
+        if late:
+            qkv_grad = plain_chain(qkv_grad)
+        else:
+            qkv_grad = Chain(qkv_grad, [lambda state: lax.psum(state, "dp")], lambda state: state)
+        return g_inputs, g_qkv, (own_chains, qkv_grad, g_gain_a, g_gain_f)
 
     layers = [
         (layer_gains[i][0], layer_gains[i][1], qkv_weights[i], all_pieces[i]) for i in range(2)
     ]
-    h_first, first_values, kept_first = forward(inputs, None, layers[0])
+    h_first, first_values, kept_first = forward(inputs, None, layers[0], first_normed)
     h_second, unused, kept_second = forward(h_first, first_values, layers[1])
     g_second, g_qkv_second, grads_second = backward(g_top, None, layers[1], kept_second)
-    hook = Hook(grads_second[0])
+    chains = grads_second[0]
     g_tokens, unused, grads_first = backward(
-        g_second.astype(BF16).astype(F32), g_qkv_second, layers[0], kept_first, hook
+        g_second.astype(BF16).astype(F32),
+        g_qkv_second,
+        layers[0],
+        kept_first,
+        (chains, chains, [grads_second[1]], chains),
     )
 
-    def flat_rows(value):
-        return value.reshape(-1, model).astype(BF16)
-
-    totals_second = [hook.end(), sum_groups(flat_rows(grads_second[1]))]
-    cut = pack_rows // 64 * 32
-    totals_first = [
-        jnp.concatenate([sum_groups(grads_first[0][:cut]), sum_groups(grads_first[0][cut:])], axis=0),
-        sum_groups(flat_rows(grads_first[1])),
-    ]
+    def ended(chains):
+        return jnp.concatenate([chain.end() for chain in chains], axis=0)
+
+    totals_first = (ended(grads_first[0]), grads_first[1].end())
+    totals_second = (ended(grads_second[0]), grads_second[1].end())
 
     def by_layer(low, high, wire):
         mine = jnp.where(is_low, low, high)

time: 972 us -> 919 us (0.945)
  waiting for transfers between devices: 400 us -> 350 us
  other arithmetic: 87.8 us -> 108 us
  starting transfers between devices: 101 us -> 82.5 us
    ppermute x57 -> x51, waiting for transfers between devices: 351 us -> 270 us  [across(): lax.ppermute(value, axis, [(i, i ^ bits) for i in range(lax.axis_size(axi...]
    reduce_scatter x2 -> x3, waiting for transfers between devices: 0.02 us -> 33.9 us  [scatter_parts(): return lax.psum_scatter(rows, 'mp', scatter_dimension=0, tiled=True)]
    ppermute x26, starting transfers between devices: 28.9 us -> 9.71 us  [swap_cores(): return lax.ppermute(value, 'section', [(0, 1), (1, 0)])]
    convert_element_type x4 -> x9, other arithmetic: 4.97 us -> 23.6 us  [the longest x4 17 us: add_low(): return (left.astype(F32) + right.astype(F32)).astype(BF16)]
    pallas_call x10 -> x8, Pallas kernels: 50.6 us -> 48.1 us  [the longest x2 34.3 us: pack_grads(): pl.pallas_call(functools.partial(pack_grads_kernel, size, plain, halves),...]
    ppermute x57 -> x51, starting transfers between devices: 71.5 us -> 72.3 us  [across(): lax.ppermute(value, axis, [(i, i ^ bits) for i in range(lax.axis_size(axi...]
    unnamed x248 -> x234, local copies, waits for them, and re-layouts: 19.4 us -> 20 us
  transfers between devices with their start and end apart: 87 -> 83, of which waited for: 51 -> 34; matrix products, arithmetic and copies ran while one was open for 12% -> 13% of each run, Pallas kernels for 23% -> 28%
where the time goes in v3:
time: 919 us; the launch traced here: 909 us
  waiting for transfers between devices  350 us (38%)
  Pallas kernels  278 us (30%)
  other arithmetic  108 us (12%)
  starting transfers between devices  82.5 us (9%)
  local copies, waits for them, and re-layouts  50.7 us (6%)
  matrix products  21.5 us (2%)
  between operations  18 us (2%)
    ppermute x51, waiting for transfers between devices, across(): lax.ppermute(value, axis, [(i, i ^ bits) for i in range(lax.axis_size(axi...  270 us
    ppermute x51, starting transfers between devices, across(): lax.ppermute(value, axis, [(i, i ^ bits) for i in range(lax.axis_size(axi...  72.3 us
    pallas_call x2, Pallas kernels, attend_back(): pl.pallas_call(functools.partial(attend_back_kernel, second, block, min(2...  51.7 us
    pallas_call x4, Pallas kernels, ffn_backward(): pl.pallas_call(functools.partial(ffn_back_kernel, more), grid=(1,), in_sp...  45.5 us
    pallas_call x4, Pallas kernels, ffn_forward(): pl.pallas_call(ffn_kernel, grid=(1,), in_specs=[whole, whole, pl.BlockSpe...  44.8 us
    all_gather x2, waiting for transfers between devices, shards(): lax.all_gather(pack, 'mp', axis=0, tiled=False)  36.5 us
    pallas_call x2, Pallas kernels, pack_grads(): pl.pallas_call(functools.partial(pack_grads_kernel, size, plain, halves),...  34.3 us
    reduce_scatter x3, waiting for transfers between devices, scatter_parts(): return lax.psum_scatter(rows, 'mp', scatter_dimension=0, tiled=True)  33.9 us
  transfers between devices with their start and end apart: 83, of which 34 were waited for; matrix products, arithmetic and copies ran while one was open for 13% of the time, Pallas kernels for 28%

profile of v3, /device:TPU:0, one launch (start us, length us, event | category | flops | bytes accessed | tf_op | source)
XLA Modules:
  0.0 908.8 jit_solution(6876264185982535115)
XLA Ops:
  14.6 4.6 collective-permute-done.6
  31.0 3.7 fusion.46
  34.7 3.0 pad_maximum_fusion.6
  37.8 29.4 %collective-permute-done.1.refs_0_.refs_2_ = bf16[512,1024]{1,0:T(8,128)(2,1)} collective-permute-done((bf16[512,1024]{1,0:T(8,128)(2,1)}, bf16[512,1024]{1,0:T(8,128)(2,1)}, u32[]{:S(2)}, u32[]{:S(2)}) %collective-permute-start.1) | collective-permute-done | bytes 1048608 | tf_op jit(solution)/shard_map/ppermute | solution.py:705
  71.9 3.7 broadcast_select_fusion.4
  75.7 3.8 qkv_rope.8
  79.5 3.8 qkv_rope.9
  83.3 3.8 qkv_rope.10
  89.3 5.4 qkv_rope.11
  94.8 13.5 %attend.2 = (bf16[512,256]{1,0:T(8,128)(2,1)}, bf16[512,256]{1,0:T(8,128)(2,1)}, bf16[512,256]{1,0:T(8,128)(2,1)}, bf16[512,256]{1,0:T(8,128)(2,1)}, f32[4,2048]{1,0:T(4,128)}) custom-call(s32[3]{0:T(128)} %pad_add_fusion.info_ref, bf16[2048,256]{1,0:T(8,128)(2,1)} %get-tuple-element.158.q_ref, bf16[2048,256]{1,0:T(8,128)(2,1)} %get-tuple-element.159.k_ref, ...), custom_call_target="tpu_custom_call" | custom-call | flops 20700000256 | bytes 1048576 | tf_op jit(solution)/shard_map/attend/pallas_call | solution.py:205
  108.3 36.5 %all-gather.5.cloned.1.call-done = bf16[4736,1024]{1,0:T(8,128)(2,1)} async-done(((bf16[1184,1024]{1,0:T(8,128)(2,1)}), bf16[4736,1024]{1,0:T(8,128)(2,1)}) %all-gather.5.cloned.1.call-update) | async-done | bytes 9699344 | tf_op jit(solution)/shard_map/all_gather | solution.py:911
  150.4 6.6 collective-permute-done.10.refs_3_
  157.0 7.9 collective-permute-done.8.refs_1_
  166.1 6.5 out_project.2
  172.7 11.1 %ffn.4 = (f32[512,1024]{1,0:T(8,128)}, bf16[512,1408]{1,0:T(8,128)(2,1)}, bf16[512,1408]{1,0:T(8,128)(2,1)}, bf16[512,1408]{1,0:T(8,128)(2,1)}) custom-call(bf16[512,1024]{1,0:T(8,128)(2,1)} %get-tuple-element.174.x_ref.refs_6_, f32[512,1024]{1,0:T(8,128)} %get-tuple-element.175.base_ref, bf16[4,1184,1024]{2,1,0:T(8,128)(2,1)} %bitcast.121), custom_call_target="tpu_custom_call" | custom-call | flops 10350000128 | bytes 1048576 | tf_op jit(solution)/shard_map/ffn/pallas_call | solution.py:478
  183.8 11.2 %ffn.5 = (f32[512,1024]{1,0:T(8,128)}, bf16[512,1408]{1,0:T(8,128)(2,1)}, bf16[512,1408]{1,0:T(8,128)(2,1)}, bf16[512,1408]{1,0:T(8,128)(2,1)}) custom-call(bf16[512,1024]{1,0:T(8,128)(2,1)} %get-tuple-element.174.x_ref.refs_6_, f32[512,1024]{1,0:T(8,128)} %get-tuple-element.176.base_ref, bf16[4,1184,1024]{2,1,0:T(8,128)(2,1)} %collective-permute-done.11.pieces_ref.refs_4_), custom_call_target="tpu_custom_call" | custom-call | flops 10350000128 | bytes 1048576 | tf_op jit(solution)/shard_map/ffn/pallas_call | solution.py:478
  200.5 4.3 qkv_rope.12
  204.8 41.5 %collective-permute-done.12.refs_0_.refs_2_ = bf16[512,1024]{1,0:T(8,128)(2,1)S(1)} collective-permute-done((bf16[512,1024]{1,0:T(8,128)(2,1)S(1)}, bf16[512,1024]{1,0:T(8,128)(2,1)S(1)}, u32[]{:S(2)}, u32[]{:S(2)}) %collective-permute-start.12) | collective-permute-done | bytes 1048608 | tf_op jit(solution)/shard_map/ppermute | solution.py:705
  248.6 3.9 qkv_rope.13
  252.5 3.9 qkv_rope.14
  256.4 15.2 %collective-permute-done.13.refs_0_.refs_3_ = bf16[256,1024]{1,0:T(8,128)(2,1)S(1)} collective-permute-done((bf16[256,1024]{1,0:T(8,128)(2,1)S(1)}, bf16[256,1024]{1,0:T(8,128)(2,1)S(1)}, u32[]{:S(2)}, u32[]{:S(2)}) %collective-permute-start.13) | collective-permute-done | bytes 524320 | tf_op jit(solution)/shard_map/ppermute | solution.py:705
  273.9 4.2 qkv_rope.15
  278.1 13.7 %attend.3 = (bf16[512,256]{1,0:T(8,128)(2,1)}, bf16[512,256]{1,0:T(8,128)(2,1)}, bf16[512,256]{1,0:T(8,128)(2,1)}, bf16[512,256]{1,0:T(8,128)(2,1)}, f32[4,2048]{1,0:T(4,128)}) custom-call(s32[3]{0:T(128)} %pad_add_fusion.info_ref, bf16[2048,256]{1,0:T(8,128)(2,1)} %get-tuple-element.187.q_ref, bf16[2048,256]{1,0:T(8,128)(2,1)} %get-tuple-element.188.k_ref, ...), custom_call_target="tpu_custom_call" | custom-call | flops 20700000256 | bytes 1048576 | tf_op jit(solution)/shard_map/attend/pallas_call | solution.py:205
  291.9 4.6 collective-permute-start.20
  307.0 5.4 collective-permute-done.18.refs_2_
  313.6 6.5 out_project.3
  320.1 11.1 %ffn.6 = (f32[512,1024]{1,0:T(8,128)}, bf16[512,1408]{1,0:T(8,128)(2,1)}, bf16[512,1408]{1,0:T(8,128)(2,1)}, bf16[512,1408]{1,0:T(8,128)(2,1)}) custom-call(bf16[512,1024]{1,0:T(8,128)(2,1)} %get-tuple-element.199.x_ref.refs_6_, f32[512,1024]{1,0:T(8,128)} %get-tuple-element.200.base_ref, bf16[4,1184,1024]{2,1,0:T(8,128)(2,1)} %bitcast.125), custom_call_target="tpu_custom_call" | custom-call | flops 10350000128 | bytes 1048576 | tf_op jit(solution)/shard_map/ffn/pallas_call | solution.py:478
  331.3 11.1 %ffn_back.4 = (f32[512,1024]{1,0:T(8,128)}, bf16[512,1408]{1,0:T(8,128)(2,1)}, bf16[512,1408]{1,0:T(8,128)(2,1)}) custom-call(bf16[512,1024]{1,0:T(8,128)(2,1)} %bitcast_convert_fusion.refs_0_.refs_1_.refs_8_, bf16[512,1408]{1,0:T(8,128)(2,1)} %get-tuple-element.203.refs_1_, bf16[512,1408]{1,0:T(8,128)(2,1)} %get-tuple-element.204.refs_2_, ...), custom_call_target="tpu_custom_call" | custom-call | flops 1150000000 | bytes 1048576 | tf_op jit(solution)/shard_map/ffn_back/pallas_call | solution.py:527
  342.6 11.3 %ffn.7 = (f32[512,1024]{1,0:T(8,128)}, bf16[512,1408]{1,0:T(8,128)(2,1)}, bf16[512,1408]{1,0:T(8,128)(2,1)}, bf16[512,1408]{1,0:T(8,128)(2,1)}) custom-call(bf16[512,1024]{1,0:T(8,128)(2,1)} %get-tuple-element.199.x_ref.refs_6_, f32[512,1024]{1,0:T(8,128)} %get-tuple-element.201.base_ref, bf16[4,1184,1024]{2,1,0:T(8,128)(2,1)} %collective-permute-done.20.pieces_ref.refs_4_), custom_call_target="tpu_custom_call" | custom-call | flops 10350000128 | bytes 1048576 | tf_op jit(solution)/shard_map/ffn/pallas_call | solution.py:478
  354.0 11.6 %ffn_back.5 = (f32[512,1024]{1,0:T(8,128)}, bf16[512,1408]{1,0:T(8,128)(2,1)}, bf16[512,1408]{1,0:T(8,128)(2,1)}) custom-call(f32[512,1024]{1,0:T(8,128)} %get-tuple-element.205.refs_0_, bf16[512,1024]{1,0:T(8,128)(2,1)} %bitcast_convert_fusion.refs_0_.refs_1_.refs_8_, bf16[512,1408]{1,0:T(8,128)(2,1)} %get-tuple-element.206.refs_2_, ...), custom_call_target="tpu_custom_call" | custom-call | flops 1150000000 | bytes 1048576 | tf_op jit(solution)/shard_map/ffn_back/pallas_call | solution.py:527
  375.0 3.0 convolution_convert_fusion.11
  382.2 3.5 collective-permute-done.23.refs_3_
  391.5 17.0 %pack_grads.2 = (bf16[4,592,1024]{2,1,0:T(8,128)(2,1)}, bf16[4,592,1024]{2,1,0:T(8,128)(2,1)}) custom-call(s32[1]{0:T(128)} %bitcast.31.info_ref.which_ref, bf16[512,1408]{1,0:T(8,128)(2,1)} %get-tuple-element.214.refs_0_, bf16[512,1408]{1,0:T(8,128)(2,1)} %copy-done.68, bf16[512,1408]{1,0:T(8,128)(2,1)} %get-tuple-element.216.refs_2_, ...), custom_call_target="tpu_custom_call" | custom-call | flops 17250000896 | bytes 1048576 | tf_op jit(solution)/shard_map/pack_grads/pallas_call | solution.py:587
  408.6 3.5 collective-permute-start.37
  412.1 25.7 %attend_back.2 = (bf16[512,768]{1,0:T(8,128)(2,1)}, bf16[512,768]{1,0:T(8,128)(2,1)}, bf16[512,768]{1,0:T(8,128)(2,1)}, bf16[512,768]{1,0:T(8,128)(2,1)}) custom-call(s32[3]{0:T(128)} %pad_add_fusion.info_ref, bf16[2048,256]{1,0:T(8,128)(2,1)} %get-tuple-element.187.q_ref, bf16[2048,256]{1,0:T(8,128)(2,1)} %get-tuple-element.188.k_ref, ...), custom_call_target="tpu_custom_call" | custom-call | flops 41400000512 | bytes 1048576 | tf_op jit(solution)/shard_map/attend_back/pallas_call | solution.py:362
  450.6 8.9 collective-permute-done.32
  461.5 9.2 %collective-permute-done.35 = bf16[256,1024]{1,0:T(8,128)(2,1)S(1)} collective-permute-done((bf16[256,1024]{1,0:T(8,128)(2,1)S(1)}, bf16[256,1024]{1,0:T(8,128)(2,1)S(1)}, u32[]{:S(2)}, u32[]{:S(2)}) %collective-permute-start.35) | collective-permute-done | bytes 524320 | tf_op jit(solution)/shard_map/ppermute | solution.py:705
  475.5 10.9 %ffn_back.6 = (f32[512,1024]{1,0:T(8,128)}, bf16[512,1408]{1,0:T(8,128)(2,1)}, bf16[512,1408]{1,0:T(8,128)(2,1)}) custom-call(bf16[512,1024]{1,0:T(8,128)(2,1)} %get-tuple-element.293.refs_0_.refs_1_.refs_8_, bf16[512,1408]{1,0:T(8,128)(2,1)} %get-tuple-element.230.refs_1_, bf16[512,1408]{1,0:T(8,128)(2,1)} %get-tuple-element.231.refs_2_, ...), custom_call_target="tpu_custom_call" | custom-call | flops 1150000000 | bytes 1048576 | tf_op jit(solution)/shard_map/ffn_back/pallas_call | solution.py:527
  486.5 11.8 %ffn_back.7 = (f32[512,1024]{1,0:T(8,128)}, bf16[512,1408]{1,0:T(8,128)(2,1)}, bf16[512,1408]{1,0:T(8,128)(2,1)}) custom-call(f32[512,1024]{1,0:T(8,128)} %get-tuple-element.232.refs_0_, bf16[512,1024]{1,0:T(8,128)(2,1)} %get-tuple-element.293.refs_0_.refs_1_.refs_8_, bf16[512,1408]{1,0:T(8,128)(2,1)} %get-tuple-element.233.refs_2_, ...), custom_call_target="tpu_custom_call" | custom-call | flops 1150000000 | bytes 1048576 | tf_op jit(solution)/shard_map/ffn_back/pallas_call | solution.py:527
  498.3 18.2 %collective-permute-done.37 = bf16[4,592,1024]{2,1,0:T(8,128)(2,1)} collective-permute-done((bf16[4,592,1024]{2,1,0:T(8,128)(2,1)}, bf16[4,592,1024]{2,1,0:T(8,128)(2,1)}, u32[]{:S(2)}, u32[]{:S(2)}) %collective-permute-start.37) | collective-permute-done | bytes 4849696 | tf_op jit(solution)/shard_map/ppermute | solution.py:705
  516.5 8.6 add_convert_fusion
  542.3 17.3 %pack_grads.3 = (bf16[4,608,1024]{2,1,0:T(8,128)(2,1)}, bf16[4,288,1024]{2,1,0:T(8,128)(2,1)}, bf16[4,288,1024]{2,1,0:T(8,128)(2,1)}) custom-call(s32[1]{0:T(128)} %bitcast.31.info_ref.which_ref, bf16[512,1408]{1,0:T(8,128)(2,1)} %get-tuple-element.258.refs_0_, bf16[512,1408]{1,0:T(8,128)(2,1)} %copy-done.66, bf16[512,1408]{1,0:T(8,128)(2,1)} %get-tuple-element.260.refs_2_, ...), custom_call_target="tpu_custom_call" | custom-call | flops 17250000896 | bytes 1048576 | tf_op jit(solution)/shard_map/pack_grads/pallas_call | solution.py:587
  559.7 7.5 qkv_grad.2
  581.7 5.2 collective-permute-done.40.refs_5_
  588.3 6.2 collective-permute-done.42.refs_7_
  594.4 26.0 %attend_back.3 = (bf16[512,768]{1,0:T(8,128)(2,1)}, bf16[512,768]{1,0:T(8,128)(2,1)}, bf16[512,768]{1,0:T(8,128)(2,1)}, bf16[512,768]{1,0:T(8,128)(2,1)}) custom-call(s32[3]{0:T(128)} %pad_add_fusion.info_ref, bf16[2048,256]{1,0:T(8,128)(2,1)} %get-tuple-element.158.q_ref, bf16[2048,256]{1,0:T(8,128)(2,1)} %get-tuple-element.159.k_ref, ...), custom_call_target="tpu_custom_call" | custom-call | flops 41400000512 | bytes 1048576 | tf_op jit(solution)/shard_map/attend_back/pallas_call | solution.py:362
  620.5 33.9 %reduce-scatter.6.cloned.1.call-done = bf16[608,1024]{1,0:T(8,128)(2,1)} async-done(((bf16[2432,1024]{1,0:T(8,128)(2,1)}), bf16[608,1024]{1,0:T(8,128)(2,1)}) %reduce-scatter.6.cloned.1.call-update) | async-done | bytes 1245200 | tf_op jit(solution)/shard_map/reduce_scatter | solution.py:785
  654.4 4.9 add_convert_fusion.1
  681.3 7.4 qkv_grad.3
  688.7 3.5 fusion.23
  694.2 15.8 %collective-permute-done.69 = bf16[608,512]{1,0:T(8,128)(2,1)} collective-permute-done((bf16[608,512]{1,0:T(8,128)(2,1)S(1)}, bf16[608,512]{1,0:T(8,128)(2,1)}, u32[]{:S(2)}, u32[]{:S(2)}) %collective-permute-start.69) | collective-permute-done | bytes 622624 | tf_op jit(solution)/shard_map/ppermute | solution.py:705
  720.9 28.7 %collective-permute-done.70 = bf16[608,256]{1,0:T(8,128)(2,1)S(1)} collective-permute-done((bf16[608,256]{1,0:T(8,128)(2,1)S(1)}, bf16[608,256]{1,0:T(8,128)(2,1)S(1)}, u32[]{:S(2)}, u32[]{:S(2)}) %collective-permute-start.70) | collective-permute-done | bytes 311328 | tf_op jit(solution)/shard_map/ppermute | solution.py:705
  757.7 3.4 collective-permute-start.71
  767.8 3.3 add_convert_fusion.2.first_ref
  780.5 3.4 collective-permute-start.73
  787.2 33.5 %collective-permute-done.65 = bf16[384,256]{1,0:T(8,128)(2,1)S(1)} collective-permute-done((bf16[384,256]{1,0:T(8,128)(2,1)S(1)}, bf16[384,256]{1,0:T(8,128)(2,1)S(1)}, u32[]{:S(2)}, u32[]{:S(2)}) %collective-permute-start.65) | collective-permute-done | bytes 196640 | tf_op jit(solution)/shard_map/ppermute | solution.py:705
  820.7 4.1 collective-permute-start.72
  825.2 17.5 %collective-permute-done.66.second_ref = bf16[384,256]{1,0:T(8,128)(2,1)S(1)} collective-permute-done((bf16[384,256]{1,0:T(8,128)(2,1)S(1)}, bf16[384,256]{1,0:T(8,128)(2,1)S(1)}, u32[]{:S(2)}, u32[]{:S(2)}) %collective-permute-start.66) | collective-permute-done | bytes 196640 | tf_op jit(solution)/shard_map/ppermute | solution.py:705
  850.9 3.2 place_two.11
  854.0 5.0 collective-permute-done.74.second_ref
  862.1 4.4 broadcast_select_fusion.2
  868.0 3.4 collective-permute-start.61
  884.8 3.0 reshape.277
  891.4 3.1 broadcast_select_fusion.1
  (513 shorter events, 223.9 us)
Async XLA Ops:
  7.2 137.6 %all-gather.5.cloned.1.call-start = ((), (), s32[]{:S(2)}) async-start(), calls=%async_computation.7 | async-start | bytes 12124160 | tf_op jit(solution)/shard_map/all_gather | solution.py:911
  21.7 270.2 %all-gather.7.cloned.1.call-start = ((), (), s32[]{:S(2)}) async-start(), calls=%async_computation.8 | async-start | bytes 12124160 | tf_op jit(solution)/shard_map/all_gather | solution.py:911
  23.1 48.8 %collective-permute-start.5 = (bf16[1024,768]{1,0:T(8,128)(2,1)S(1)}, bf16[1024,768]{1,0:T(8,128)(2,1)}, u32[]{:S(2)}, u32[]{:S(2)}) collective-permute-start(bf16[1024,768]{1,0:T(8,128)(2,1)S(1)} %pad_maximum_fusion.5), channel_id=1, source_target_pairs={{0,16},{16,0},{1,17},{17,1},{2,18},{18,2},{3,19},{19,3},{4,20},{20... | collective-permute-start | bytes 4718600 | tf_op jit(solution)/shard_map/ppermute | solution.py:701
  23.3 45.0 %collective-permute-start.3 = (bf16[512,1024]{1,0:T(8,128)(2,1)}, bf16[512,1024]{1,0:T(8,128)(2,1)}, u32[]{:S(2)}, u32[]{:S(2)}) collective-permute-start(bf16[512,1024]{1,0:T(8,128)(2,1)} %fusion.6.refs_0_), channel_id=1, source_target_pairs={{0,1},{1,0},{2,3},{3,2},{4,5},{5,4},{6,7},{7,6},{8,9},{9,8},{10,11... | collective-permute-start | bytes 3145736 | tf_op jit(solution)/shard_map/ppermute | solution.py:705
  26.2 40.9 %collective-permute-start.1 = (bf16[512,1024]{1,0:T(8,128)(2,1)}, bf16[512,1024]{1,0:T(8,128)(2,1)}, u32[]{:S(2)}, u32[]{:S(2)}) collective-permute-start(bf16[512,1024]{1,0:T(8,128)(2,1)} %fusion.6.refs_0_), channel_id=1, source_target_pairs={{0,2},{1,3},{2,0},{3,1},{4,6},{5,7},{6,4},{7,5},{8,10},{9,11},{10,... | collective-permute-start | bytes 3145736 | tf_op jit(solution)/shard_map/ppermute | solution.py:705
  68.2 18.9 %collective-permute-start.2 = (bf16[256,1024]{1,0:T(8,128)(2,1)S(1)}, bf16[256,1024]{1,0:T(8,128)(2,1)S(1)}, u32[]{:S(2)}, u32[]{:S(2)}) collective-permute-start(bf16[256,1024]{1,0:T(8,128)(2,1)S(1)} %slice.257), channel_id=1, source_target_pairs={{0,1},{1,0},{2,3},{3,2},{4,5},{5,4},{6,7},{7,6},{8,9},{9,8},{10,11... | collective-permute-start | bytes 1572872 | tf_op jit(solution)/shard_map/ppermute | solution.py:705
  69.4 19.2 %collective-permute-start.4 = (bf16[256,1024]{1,0:T(8,128)(2,1)S(1)}, bf16[256,1024]{1,0:T(8,128)(2,1)S(1)}, u32[]{:S(2)}, u32[]{:S(2)}) collective-permute-start(bf16[256,1024]{1,0:T(8,128)(2,1)S(1)} %slice.258), channel_id=1, source_target_pairs={{0,2},{1,3},{2,0},{3,1},{4,6},{5,7},{6,4},{7,5},{8,10},{9,11},{10,... | collective-permute-start | bytes 1572872 | tf_op jit(solution)/shard_map/ppermute | solution.py:705
  144.8 39.0 %collective-permute-start.11 = (bf16[4,1184,1024]{2,1,0:T(8,128)(2,1)}, bf16[4,1184,1024]{2,1,0:T(8,128)(2,1)}, u32[]{:S(2)}, u32[]{:S(2)}) collective-permute-start(bf16[4,1184,1024]{2,1,0:T(8,128)(2,1)} %bitcast.119), channel_id=1, source_target_pairs={{0,16},{16,0},{1,17},{17,1},{2,18},{18,2},{3,19},{19,3},{4,20},{20... | collective-permute-start | bytes 29097992 | tf_op jit(solution)/shard_map/ppermute | solution.py:701
  144.8 449.6 %reduce-scatter.4.cloned.1.call-start = ((), (), s32[]{:S(2)}) async-start(), calls=%async_computation.3 | async-start | bytes 6062080 | tf_op jit(solution)/shard_map/reduce_scatter | solution.py:785
  146.4 18.6 %collective-permute-start.7 = (bf16[4,128,1024]{2,1,0:T(8,128)(2,1)S(1)}, bf16[4,128,1024]{2,1,0:T(8,128)(2,1)S(1)}, u32[]{:S(2)}, u32[]{:S(2)}) collective-permute-start(bf16[4,128,1024]{2,1,0:T(8,128)(2,1)S(1)} %slice.199.own_ref), channel_id=1, source_target_pairs={{0,16},{16,0},{1,17},{17,1},{2,18},{18,2},{3,19},{19,3},{4,20},{20... | collective-permute-start | bytes 3145736 | tf_op jit(solution)/shard_map/ppermute | solution.py:701
  148.4 16.6 %collective-permute-start.8 = (bf16[512,256]{1,0:T(8,128)(2,1)S(1)}, bf16[512,256]{1,0:T(8,128)(2,1)S(1)}, u32[]{:S(2)}, u32[]{:S(2)}) collective-permute-start(bf16[512,256]{1,0:T(8,128)(2,1)S(1)} %copy-done.85), channel_id=1, source_target_pairs={{0,1},{1,0},{2,3},{3,2},{4,5},{5,4},{6,7},{7,6},{8,9},{9,8},{10,11... | collective-permute-start | bytes 786440 | tf_op jit(solution)/shard_map/ppermute | solution.py:705
  149.9 15.1 %collective-permute-start.9 = (bf16[512,256]{1,0:T(8,128)(2,1)S(1)}, bf16[512,256]{1,0:T(8,128)(2,1)S(1)}, u32[]{:S(2)}, u32[]{:S(2)}) collective-permute-start(bf16[512,256]{1,0:T(8,128)(2,1)S(1)} %copy-done.86), channel_id=1, source_target_pairs={{0,2},{1,3},{2,0},{3,1},{4,6},{5,7},{6,4},{7,5},{8,10},{9,11},{10,... | collective-permute-start | bytes 786440 | tf_op jit(solution)/shard_map/ppermute | solution.py:705
  198.3 48.0 %collective-permute-start.12 = (bf16[512,1024]{1,0:T(8,128)(2,1)S(1)}, bf16[512,1024]{1,0:T(8,128)(2,1)S(1)}, u32[]{:S(2)}, u32[]{:S(2)}) collective-permute-start(bf16[512,1024]{1,0:T(8,128)(2,1)S(1)} %fusion.4.refs_0_), channel_id=1, source_target_pairs={{0,2},{1,3},{2,0},{3,1},{4,6},{5,7},{6,4},{7,5},{8,10},{9,11},{10,... | collective-permute-start | bytes 3145736 | tf_op jit(solution)/shard_map/ppermute | solution.py:705
  199.6 48.0 %collective-permute-start.14 = (bf16[512,1024]{1,0:T(8,128)(2,1)S(1)}, bf16[512,1024]{1,0:T(8,128)(2,1)S(1)}, u32[]{:S(2)}, u32[]{:S(2)}) collective-permute-start(bf16[512,1024]{1,0:T(8,128)(2,1)S(1)} %fusion.4.refs_0_), channel_id=1, source_target_pairs={{0,1},{1,0},{2,3},{3,2},{4,5},{5,4},{6,7},{7,6},{8,9},{9,8},{10,11... | collective-permute-start | bytes 3145736 | tf_op jit(solution)/shard_map/ppermute | solution.py:705
  246.3 25.3 %collective-permute-start.13 = (bf16[256,1024]{1,0:T(8,128)(2,1)S(1)}, bf16[256,1024]{1,0:T(8,128)(2,1)S(1)}, u32[]{:S(2)}, u32[]{:S(2)}) collective-permute-start(bf16[256,1024]{1,0:T(8,128)(2,1)S(1)} %slice.261), channel_id=1, source_target_pairs={{0,1},{1,0},{2,3},{3,2},{4,5},{5,4},{6,7},{7,6},{8,9},{9,8},{10,11... | collective-permute-start | bytes 1572872 | tf_op jit(solution)/shard_map/ppermute | solution.py:705
  247.7 25.4 %collective-permute-start.15 = (bf16[256,1024]{1,0:T(8,128)(2,1)S(1)}, bf16[256,1024]{1,0:T(8,128)(2,1)S(1)}, u32[]{:S(2)}, u32[]{:S(2)}) collective-permute-start(bf16[256,1024]{1,0:T(8,128)(2,1)S(1)} %slice.262), channel_id=1, source_target_pairs={{0,2},{1,3},{2,0},{3,1},{4,6},{5,7},{6,4},{7,5},{8,10},{9,11},{10,... | collective-permute-start | bytes 1572872 | tf_op jit(solution)/shard_map/ppermute | solution.py:705
  291.9 50.8 %collective-permute-start.20 = (bf16[4,1184,1024]{2,1,0:T(8,128)(2,1)}, bf16[4,1184,1024]{2,1,0:T(8,128)(2,1)}, u32[]{:S(2)}, u32[]{:S(2)}) collective-permute-start(bf16[4,1184,1024]{2,1,0:T(8,128)(2,1)} %bitcast.123), channel_id=1, source_target_pairs={{0,16},{16,0},{1,17},{17,1},{2,18},{18,2},{3,19},{19,3},{4,20},{20... | collective-permute-start | bytes 29097992 | tf_op jit(solution)/shard_map/ppermute | solution.py:701
  297.8 14.9 %collective-permute-start.16 = (bf16[4,128,1024]{2,1,0:T(8,128)(2,1)S(1)}, bf16[4,128,1024]{2,1,0:T(8,128)(2,1)S(1)}, u32[]{:S(2)}, u32[]{:S(2)}) collective-permute-start(bf16[4,128,1024]{2,1,0:T(8,128)(2,1)S(1)} %slice.204.own_ref), channel_id=1, source_target_pairs={{0,16},{16,0},{1,17},{17,1},{2,18},{18,2},{3,19},{19,3},{4,20},{20... | collective-permute-start | bytes 3145736 | tf_op jit(solution)/shard_map/ppermute | solution.py:701
  298.3 14.1 %collective-permute-start.18 = (bf16[512,256]{1,0:T(8,128)(2,1)S(1)}, bf16[512,256]{1,0:T(8,128)(2,1)S(1)}, u32[]{:S(2)}, u32[]{:S(2)}) collective-permute-start(bf16[512,256]{1,0:T(8,128)(2,1)S(1)} %copy-done.95), channel_id=1, source_target_pairs={{0,2},{1,3},{2,0},{3,1},{4,6},{5,7},{6,4},{7,5},{8,10},{9,11},{10,... | collective-permute-start | bytes 786440 | tf_op jit(solution)/shard_map/ppermute | solution.py:705
  300.2 12.2 %collective-permute-start.19 = (bf16[512,256]{1,0:T(8,128)(2,1)S(1)}, bf16[512,256]{1,0:T(8,128)(2,1)S(1)}, u32[]{:S(2)}, u32[]{:S(2)}) collective-permute-start(bf16[512,256]{1,0:T(8,128)(2,1)S(1)} %copy-done.96), channel_id=1, source_target_pairs={{0,3},{1,2},{2,1},{3,0},{4,7},{5,6},{6,5},{7,4},{8,11},{9,10},{10,... | collective-permute-start | bytes 786440 | tf_op jit(solution)/shard_map/ppermute | solution.py:705
  374.0 14.8 %collective-permute-start.29 = (bf16[512,1024]{1,0:T(8,128)(2,1)S(1)}, bf16[512,1024]{1,0:T(8,128)(2,1)}, u32[]{:S(2)}, u32[]{:S(2)}) collective-permute-start(bf16[512,1024]{1,0:T(8,128)(2,1)S(1)} %copy-done.9), channel_id=1, source_target_pairs={{0,16},{16,0},{1,17},{17,1},{2,18},{18,2},{3,19},{19,3},{4,20},{20... | collective-permute-start | bytes 3145736 | tf_op jit(solution)/shard_map/ppermute | solution.py:701
  374.4 15.7 %collective-permute-start.28 = (bf16[512,1024]{1,0:T(8,128)(2,1)}, bf16[512,1024]{1,0:T(8,128)(2,1)S(1)}, u32[]{:S(2)}, u32[]{:S(2)}) collective-permute-start(bf16[512,1024]{1,0:T(8,128)(2,1)} %get-tuple-element.199.x_ref.refs_6_), channel_id=1, source_target_pairs={{0,16},{16,0},{1,17},{17,1},{2,18},{18,2},{3,19},{19,3},{4,20},{20... | collective-permute-start | bytes 3145736 | tf_op jit(solution)/shard_map/ppermute | solution.py:701
  374.9 10.8 %collective-permute-start.23 = (bf16[512,1408]{1,0:T(8,128)(2,1)}, bf16[512,1408]{1,0:T(8,128)(2,1)S(1)}, u32[]{:S(2)}, u32[]{:S(2)}) collective-permute-start(bf16[512,1408]{1,0:T(8,128)(2,1)} %get-tuple-element.212), channel_id=1, source_target_pairs={{0,16},{16,0},{1,17},{17,1},{2,18},{18,2},{3,19},{19,3},{4,20},{20... | collective-permute-start | bytes 4325384 | tf_op jit(solution)/shard_map/ppermute | solution.py:701
  378.1 12.0 %collective-permute-start.27 = (bf16[512,1408]{1,0:T(8,128)(2,1)S(1)}, bf16[512,1408]{1,0:T(8,128)(2,1)S(1)}, u32[]{:S(2)}, u32[]{:S(2)}) collective-permute-start(bf16[512,1408]{1,0:T(8,128)(2,1)S(1)} %copy-done.65), channel_id=1, source_target_pairs={{0,16},{16,0},{1,17},{17,1},{2,18},{18,2},{3,19},{19,3},{4,20},{20... | collective-permute-start | bytes 4325384 | tf_op jit(solution)/shard_map/ppermute | solution.py:701
  386.6 21.9 %collective-permute-start.24 = (bf16[512,256]{1,0:T(8,128)(2,1)S(1)}, bf16[512,256]{1,0:T(8,128)(2,1)S(1)}, u32[]{:S(2)}, u32[]{:S(2)}) collective-permute-start(bf16[512,256]{1,0:T(8,128)(2,1)S(1)} %get-tuple-element.348), channel_id=1, source_target_pairs={{0,1},{1,0},{2,3},{3,2},{4,5},{5,4},{6,7},{7,6},{8,9},{9,8},{10,11... | collective-permute-start | bytes 786440 | tf_op jit(solution)/shard_map/ppermute | solution.py:705
  388.0 20.6 %collective-permute-start.25 = (bf16[512,256]{1,0:T(8,128)(2,1)S(1)}, bf16[512,256]{1,0:T(8,128)(2,1)S(1)}, u32[]{:S(2)}, u32[]{:S(2)}) collective-permute-start(bf16[512,256]{1,0:T(8,128)(2,1)S(1)} %get-tuple-element.347), channel_id=1, source_target_pairs={{0,2},{1,3},{2,0},{3,1},{4,6},{5,7},{6,4},{7,5},{8,10},{9,11},{10,... | collective-permute-start | bytes 786440 | tf_op jit(solution)/shard_map/ppermute | solution.py:705
  388.8 19.7 %collective-permute-start.26 = (bf16[512,256]{1,0:T(8,128)(2,1)S(1)}, bf16[512,256]{1,0:T(8,128)(2,1)S(1)}, u32[]{:S(2)}, u32[]{:S(2)}) collective-permute-start(bf16[512,256]{1,0:T(8,128)(2,1)S(1)} %get-tuple-element.346), channel_id=1, source_target_pairs={{0,3},{1,2},{2,1},{3,0},{4,7},{5,6},{6,5},{7,4},{8,11},{9,10},{10,... | collective-permute-start | bytes 786440 | tf_op jit(solution)/shard_map/ppermute | solution.py:705
  408.6 107.9 %collective-permute-start.37 = (bf16[4,592,1024]{2,1,0:T(8,128)(2,1)}, bf16[4,592,1024]{2,1,0:T(8,128)(2,1)}, u32[]{:S(2)}, u32[]{:S(2)}) collective-permute-start(bf16[4,592,1024]{2,1,0:T(8,128)(2,1)} %get-tuple-element.237), channel_id=1, source_target_pairs={{0,4},{4,0},{8,12},{12,8},{1,5},{5,1},{9,13},{13,9},{2,6},{6,2},{1... | collective-permute-start | bytes 14549000 | tf_op jit(solution)/shard_map/ppermute | solution.py:705
  442.5 19.0 %collective-permute-start.31 = (bf16[256,1024]{1,0:T(8,128)(2,1)S(1)}, bf16[256,1024]{1,0:T(8,128)(2,1)S(1)}, u32[]{:S(2)}, u32[]{:S(2)}) collective-permute-start(bf16[256,1024]{1,0:T(8,128)(2,1)S(1)} %slice.271), channel_id=1, source_target_pairs={{0,1},{1,0},{2,3},{3,2},{4,5},{5,4},{6,7},{7,6},{8,9},{9,8},{10,11... | collective-permute-start | bytes 1572872 | tf_op jit(solution)/shard_map/ppermute | solution.py:705
  443.4 16.1 %collective-permute-start.32 = (bf16[256,1024]{1,0:T(8,128)(2,1)S(1)}, bf16[256,1024]{1,0:T(8,128)(2,1)S(1)}, u32[]{:S(2)}, u32[]{:S(2)}) collective-permute-start(bf16[256,1024]{1,0:T(8,128)(2,1)S(1)} %get-tuple-element.338), channel_id=1, source_target_pairs={{0,1},{1,0},{2,3},{3,2},{4,5},{5,4},{6,7},{7,6},{8,9},{9,8},{10,11... | collective-permute-start | bytes 1572872 | tf_op jit(solution)/shard_map/ppermute | solution.py:705
  445.7 15.8 %collective-permute-start.36 = (bf16[256,1024]{1,0:T(8,128)(2,1)S(1)}, bf16[256,1024]{1,0:T(8,128)(2,1)S(1)}, u32[]{:S(2)}, u32[]{:S(2)}) collective-permute-start(bf16[256,1024]{1,0:T(8,128)(2,1)S(1)} %slice.277), channel_id=1, source_target_pairs={{0,2},{1,3},{2,0},{3,1},{4,6},{5,7},{6,4},{7,5},{8,10},{9,11},{10,... | collective-permute-start | bytes 1572872 | tf_op jit(solution)/shard_map/ppermute | solution.py:705
  449.5 21.3 %collective-permute-start.35 = (bf16[256,1024]{1,0:T(8,128)(2,1)S(1)}, bf16[256,1024]{1,0:T(8,128)(2,1)S(1)}, u32[]{:S(2)}, u32[]{:S(2)}) collective-permute-start(bf16[256,1024]{1,0:T(8,128)(2,1)S(1)} %add_convert_fusion.9), channel_id=1, source_target_pairs={{0,1},{1,0},{2,3},{3,2},{4,5},{5,4},{6,7},{7,6},{8,9},{9,8},{10,11... | collective-permute-start | bytes 1572872 | tf_op jit(solution)/shard_map/ppermute | solution.py:705
  459.7 12.1 %collective-permute-start.33 = (bf16[256,1024]{1,0:T(8,128)(2,1)S(1)}, bf16[256,1024]{1,0:T(8,128)(2,1)S(1)}, u32[]{:S(2)}, u32[]{:S(2)}) collective-permute-start(bf16[256,1024]{1,0:T(8,128)(2,1)S(1)} %add_convert_fusion.10), channel_id=1, source_target_pairs={{0,2},{1,3},{2,0},{3,1},{4,6},{5,7},{6,4},{7,5},{8,10},{9,11},{10,... | collective-permute-start | bytes 1572872 | tf_op jit(solution)/shard_map/ppermute | solution.py:705
  525.1 129.3 %reduce-scatter.6.cloned.1.call-start = ((), (), s32[]{:S(2)}) async-start(), calls=%async_computation.4 | async-start | bytes 6225920 | tf_op jit(solution)/shard_map/reduce_scatter | solution.py:785
  527.2 10.3 %collective-permute-start.39 = (bf16[512,1408]{1,0:T(8,128)(2,1)}, bf16[512,1408]{1,0:T(8,128)(2,1)S(1)}, u32[]{:S(2)}, u32[]{:S(2)}) collective-permute-start(bf16[512,1408]{1,0:T(8,128)(2,1)} %get-tuple-element.242), channel_id=1, source_target_pairs={{0,16},{16,0},{1,17},{17,1},{2,18},{18,2},{3,19},{19,3},{4,20},{20... | collective-permute-start | bytes 4325384 | tf_op jit(solution)/shard_map/ppermute | solution.py:701
  559.6 220.9 %reduce-scatter.8.cloned.1.call-start = ((), (), s32[]{:S(2)}) async-start(), calls=%async_computation.6 | async-start | bytes 2949120 | tf_op jit(solution)/shard_map/reduce_scatter | solution.py:785
  571.9 15.1 %collective-permute-start.40 = (bf16[512,256]{1,0:T(8,128)(2,1)}, bf16[512,256]{1,0:T(8,128)(2,1)}, u32[]{:S(2)}, u32[]{:S(2)}) collective-permute-start(bf16[512,256]{1,0:T(8,128)(2,1)} %get-tuple-element.336), channel_id=1, source_target_pairs={{0,1},{1,0},{2,3},{3,2},{4,5},{5,4},{6,7},{7,6},{8,9},{9,8},{10,11... | collective-permute-start | bytes 786440 | tf_op jit(solution)/shard_map/ppermute | solution.py:705
  573.4 14.8 %collective-permute-start.41 = (bf16[512,256]{1,0:T(8,128)(2,1)}, bf16[512,256]{1,0:T(8,128)(2,1)}, u32[]{:S(2)}, u32[]{:S(2)}) collective-permute-start(bf16[512,256]{1,0:T(8,128)(2,1)} %get-tuple-element.335), channel_id=1, source_target_pairs={{0,2},{1,3},{2,0},{3,1},{4,6},{5,7},{6,4},{7,5},{8,10},{9,11},{10,... | collective-permute-start | bytes 786440 | tf_op jit(solution)/shard_map/ppermute | solution.py:705
  574.7 19.7 %collective-permute-start.42 = (bf16[512,256]{1,0:T(8,128)(2,1)S(1)}, bf16[512,256]{1,0:T(8,128)(2,1)}, u32[]{:S(2)}, u32[]{:S(2)}) collective-permute-start(bf16[512,256]{1,0:T(8,128)(2,1)S(1)} %get-tuple-element.334), channel_id=1, source_target_pairs={{0,3},{1,2},{2,1},{3,0},{4,7},{5,6},{6,5},{7,4},{8,11},{9,10},{10,... | collective-permute-start | bytes 786440 | tf_op jit(solution)/shard_map/ppermute | solution.py:705
  580.0 74.4 %collective-permute-start.62 = (bf16[4,288,1024]{2,1,0:T(8,128)(2,1)}, bf16[4,288,1024]{2,1,0:T(8,128)(2,1)}, u32[]{:S(2)}, u32[]{:S(2)}) collective-permute-start(bf16[4,288,1024]{2,1,0:T(8,128)(2,1)} %get-tuple-element.272), channel_id=1, source_target_pairs={{0,4},{4,0},{8,12},{12,8},{1,5},{5,1},{9,13},{13,9},{2,6},{6,2},{1... | collective-permute-start | bytes 7077896 | tf_op jit(solution)/shard_map/ppermute | solution.py:705
  659.3 216.6 %all-reduce.2.cloned.1.call-start = ((), (), s32[]{:S(2)}) async-start(), calls=%async_computation.5 | async-start | bytes 1572864 | tf_op jit(solution)/shard_map/psum | solution.py:1041
  667.8 98.0 %collective-permute-start.54 = (bf16[592,1024]{1,0:T(8,128)(2,1)}, bf16[592,1024]{1,0:T(8,128)(2,1)}, u32[]{:S(2)}, u32[]{:S(2)}) collective-permute-start(bf16[592,1024]{1,0:T(8,128)(2,1)} %reduce-scatter.4.cloned.1.call-done), channel_id=1, source_target_pairs={{0,8},{4,12},{8,0},{12,4},{1,9},{5,13},{9,1},{13,5},{2,10},{6,14},... | collective-permute-start | bytes 3637256 | tf_op jit(solution)/shard_map/ppermute | solution.py:705
  674.5 35.4 %collective-permute-start.69 = (bf16[608,512]{1,0:T(8,128)(2,1)S(1)}, bf16[608,512]{1,0:T(8,128)(2,1)}, u32[]{:S(2)}, u32[]{:S(2)}) collective-permute-start(bf16[608,512]{1,0:T(8,128)(2,1)S(1)} %constant_dynamic-slice_fusion.2), channel_id=1, source_target_pairs={{0,4},{4,0},{8,12},{12,8},{1,5},{5,1},{9,13},{13,9},{2,6},{6,2},{1... | collective-permute-start | bytes 1867784 | tf_op jit(solution)/shard_map/ppermute | solution.py:705
  677.1 35.0 %collective-permute-start.51 = (bf16[256,1024]{1,0:T(8,128)(2,1)}, bf16[256,1024]{1,0:T(8,128)(2,1)}, u32[]{:S(2)}, u32[]{:S(2)}) collective-permute-start(bf16[256,1024]{1,0:T(8,128)(2,1)} %get-tuple-element.327), channel_id=1, source_target_pairs={{0,2},{1,3},{2,0},{3,1},{4,6},{5,7},{6,4},{7,5},{8,10},{9,11},{10,... | collective-permute-start | bytes 1572872 | tf_op jit(solution)/shard_map/ppermute | solution.py:705
  679.3 77.8 %collective-permute-start.48 = (bf16[256,1024]{1,0:T(8,128)(2,1)}, bf16[256,1024]{1,0:T(8,128)(2,1)}, u32[]{:S(2)}, u32[]{:S(2)}) collective-permute-start(bf16[256,1024]{1,0:T(8,128)(2,1)} %slice.285), channel_id=1, source_target_pairs={{0,1},{1,0},{2,3},{3,2},{4,5},{5,4},{6,7},{7,6},{8,9},{9,8},{10,11... | collective-permute-start | bytes 1572872 | tf_op jit(solution)/shard_map/ppermute | solution.py:705
  680.0 36.9 %collective-permute-start.49 = (bf16[256,1024]{1,0:T(8,128)(2,1)}, bf16[256,1024]{1,0:T(8,128)(2,1)}, u32[]{:S(2)}, u32[]{:S(2)}) collective-permute-start(bf16[256,1024]{1,0:T(8,128)(2,1)} %get-tuple-element.326), channel_id=1, source_target_pairs={{0,1},{1,0},{2,3},{3,2},{4,5},{5,4},{6,7},{7,6},{8,9},{9,8},{10,11... | collective-permute-start | bytes 1572872 | tf_op jit(solution)/shard_map/ppermute | solution.py:705
  709.9 10.3 %collective-permute-start.63 = (bf16[512,768]{1,0:T(8,128)(2,1)S(1)}, bf16[512,768]{1,0:T(8,128)(2,1)S(1)}, u32[]{:S(2)}, u32[]{:S(2)}) collective-permute-start(bf16[512,768]{1,0:T(8,128)(2,1)S(1)} %constant_dynamic-slice_fusion.5), channel_id=1, source_target_pairs={{0,16},{16,0},{1,17},{17,1},{2,18},{18,2},{3,19},{19,3},{4,20},{20... | collective-permute-start | bytes 2359304 | tf_op jit(solution)/shard_map/ppermute | solution.py:701
  712.1 37.5 %collective-permute-start.70 = (bf16[608,256]{1,0:T(8,128)(2,1)S(1)}, bf16[608,256]{1,0:T(8,128)(2,1)S(1)}, u32[]{:S(2)}, u32[]{:S(2)}) collective-permute-start(bf16[608,256]{1,0:T(8,128)(2,1)S(1)} %constant_dynamic-slice_fusion.1), channel_id=1, source_target_pairs={{0,8},{4,12},{8,0},{12,4},{1,9},{5,13},{9,1},{13,5},{2,10},{6,14},... | collective-permute-start | bytes 933896 | tf_op jit(solution)/shard_map/ppermute | solution.py:705
  716.8 40.3 %collective-permute-start.53 = (bf16[256,1024]{1,0:T(8,128)(2,1)}, bf16[256,1024]{1,0:T(8,128)(2,1)}, u32[]{:S(2)}, u32[]{:S(2)}) collective-permute-start(bf16[256,1024]{1,0:T(8,128)(2,1)} %slice.291), channel_id=1, source_target_pairs={{0,2},{1,3},{2,0},{3,1},{4,6},{5,7},{6,4},{7,5},{8,10},{9,11},{10,... | collective-permute-start | bytes 1572872 | tf_op jit(solution)/shard_map/ppermute | solution.py:705
  720.2 37.5 %collective-permute-start.52 = (bf16[256,1024]{1,0:T(8,128)(2,1)}, bf16[256,1024]{1,0:T(8,128)(2,1)}, u32[]{:S(2)}, u32[]{:S(2)}) collective-permute-start(bf16[256,1024]{1,0:T(8,128)(2,1)} %add_convert_fusion.7), channel_id=1, source_target_pairs={{0,1},{1,0},{2,3},{3,2},{4,5},{5,4},{6,7},{7,6},{8,9},{9,8},{10,11... | collective-permute-start | bytes 1572872 | tf_op jit(solution)/shard_map/ppermute | solution.py:705
  749.6 13.4 %collective-permute-start.50 = (bf16[256,1024]{1,0:T(8,128)(2,1)}, bf16[256,1024]{1,0:T(8,128)(2,1)}, u32[]{:S(2)}, u32[]{:S(2)}) collective-permute-start(bf16[256,1024]{1,0:T(8,128)(2,1)} %add_convert_fusion.8), channel_id=1, source_target_pairs={{0,2},{1,3},{2,0},{3,1},{4,6},{5,7},{6,4},{7,5},{8,10},{9,11},{10,... | collective-permute-start | bytes 1572872 | tf_op jit(solution)/shard_map/ppermute | solution.py:705
  757.1 109.4 %collective-permute-start.21 = (bf16[512,1024]{1,0:T(8,128)(2,1)}, bf16[512,1024]{1,0:T(8,128)(2,1)}, u32[]{:S(2)}, u32[]{:S(2)}) collective-permute-start(bf16[512,1024]{1,0:T(8,128)(2,1)} %broadcast_select_fusion.7), channel_id=1, source_target_pairs={{0,16},{16,0},{1,17},{17,1},{2,18},{18,2},{3,19},{19,3},{4,20},{20... | collective-permute-start | bytes 3145736 | tf_op jit(solution)/shard_map/ppermute | solution.py:701
  757.2 23.3 %collective-permute-start.64 = (bf16[384,512]{1,0:T(8,128)(2,1)S(1)}, bf16[384,512]{1,0:T(8,128)(2,1)S(1)}, u32[]{:S(2)}, u32[]{:S(2)}) collective-permute-start(bf16[384,512]{1,0:T(8,128)(2,1)S(1)} %constant_dynamic-slice_fusion.4), channel_id=1, source_target_pairs={{0,4},{4,0},{8,12},{12,8},{1,5},{5,1},{9,13},{13,9},{2,6},{6,2},{1... | collective-permute-start | bytes 1179656 | tf_op jit(solution)/shard_map/ppermute | solution.py:705
  757.7 27.3 %collective-permute-start.71 = (bf16[608,256]{1,0:T(8,128)(2,1)}, bf16[608,256]{1,0:T(8,128)(2,1)}, u32[]{:S(2)}, u32[]{:S(2)}) collective-permute-start(bf16[608,256]{1,0:T(8,128)(2,1)} %add_convert_fusion.12.first_ref), channel_id=1, source_target_pairs={{0,8},{4,12},{8,0},{12,4},{1,9},{5,13},{9,1},{13,5},{2,10},{6,14},... | collective-permute-start | bytes 933896 | tf_op jit(solution)/shard_map/ppermute | solution.py:705
  771.1 78.5 %collective-permute-start.75 = (bf16[592,1024]{1,0:T(8,128)(2,1)}, bf16[592,1024]{1,0:T(8,128)(2,1)}, u32[]{:S(2)}, u32[]{:S(2)}) collective-permute-start(bf16[592,1024]{1,0:T(8,128)(2,1)} %add_convert_fusion.2.first_ref), channel_id=1, source_target_pairs={{0,4},{4,0},{8,12},{12,8},{1,5},{5,1},{9,13},{13,9},{2,6},{6,2},{1... | collective-permute-start | bytes 3637256 | tf_op jit(solution)/shard_map/ppermute | solution.py:705
  779.9 98.1 %collective-permute-start.55 = (bf16[512,1024]{1,0:T(8,128)(2,1)}, bf16[512,1024]{1,0:T(8,128)(2,1)}, u32[]{:S(2)}, u32[]{:S(2)}) collective-permute-start(bf16[512,1024]{1,0:T(8,128)(2,1)} %get-tuple-element.291), channel_id=1, source_target_pairs={{0,16},{16,0},{1,17},{17,1},{2,18},{18,2},{3,19},{19,3},{4,20},{20... | collective-permute-start | bytes 3145736 | tf_op jit(solution)/shard_map/ppermute | solution.py:701
  780.5 44.4 %collective-permute-start.73 = (bf16[288,1024]{1,0:T(8,128)(2,1)}, bf16[288,1024]{1,0:T(8,128)(2,1)S(1)}, u32[]{:S(2)}, u32[]{:S(2)}) collective-permute-start(bf16[288,1024]{1,0:T(8,128)(2,1)} %reduce-scatter.8.cloned.1.call-done), channel_id=1, source_target_pairs={{0,8},{4,12},{8,0},{12,4},{1,9},{5,13},{9,1},{13,5},{2,10},{6,14},... | collective-permute-start | bytes 1769480 | tf_op jit(solution)/shard_map/ppermute | solution.py:705
  785.0 35.7 %collective-permute-start.65 = (bf16[384,256]{1,0:T(8,128)(2,1)S(1)}, bf16[384,256]{1,0:T(8,128)(2,1)S(1)}, u32[]{:S(2)}, u32[]{:S(2)}) collective-permute-start(bf16[384,256]{1,0:T(8,128)(2,1)S(1)} %constant_dynamic-slice_fusion.3), channel_id=1, source_target_pairs={{0,8},{4,12},{8,0},{12,4},{1,9},{5,13},{9,1},{13,5},{2,10},{6,14},... | collective-permute-start | bytes 589832 | tf_op jit(solution)/shard_map/ppermute | solution.py:705
  820.7 25.6 %collective-permute-start.72 = (bf16[608,512]{1,0:T(8,128)(2,1)}, bf16[608,512]{1,0:T(8,128)(2,1)S(1)}, u32[]{:S(2)}, u32[]{:S(2)}) collective-permute-start(bf16[608,512]{1,0:T(8,128)(2,1)} %place_two.8.first_ref), channel_id=1, source_target_pairs={{0,4},{4,0},{8,12},{12,8},{1,5},{5,1},{9,13},{13,9},{2,6},{6,2},{1... | collective-permute-start | bytes 1867784 | tf_op jit(solution)/shard_map/ppermute | solution.py:705
  824.9 17.8 %collective-permute-start.66 = (bf16[384,256]{1,0:T(8,128)(2,1)S(1)}, bf16[384,256]{1,0:T(8,128)(2,1)S(1)}, u32[]{:S(2)}, u32[]{:S(2)}) collective-permute-start(bf16[384,256]{1,0:T(8,128)(2,1)S(1)} %add_convert_fusion.13.first_ref), channel_id=1, source_target_pairs={{0,8},{4,12},{8,0},{12,4},{1,9},{5,13},{9,1},{13,5},{2,10},{6,14},... | collective-permute-start | bytes 589832 | tf_op jit(solution)/shard_map/ppermute | solution.py:705
  842.7 16.3 %collective-permute-start.74 = (bf16[288,1024]{1,0:T(8,128)(2,1)S(1)}, bf16[288,1024]{1,0:T(8,128)(2,1)S(1)}, u32[]{:S(2)}, u32[]{:S(2)}) collective-permute-start(bf16[288,1024]{1,0:T(8,128)(2,1)S(1)} %add_convert_fusion.6.first_ref), channel_id=1, source_target_pairs={{0,4},{4,0},{8,12},{12,8},{1,5},{5,1},{9,13},{13,9},{2,6},{6,2},{1... | collective-permute-start | bytes 1769480 | tf_op jit(solution)/shard_map/ppermute | solution.py:705
  846.4 21.6 %collective-permute-start.60 = (f32[4128]{0:T(1024)S(1)}, f32[4128]{0:T(1024)S(1)}, u32[]{:S(2)}, u32[]{:S(2)}) collective-permute-start(f32[4128]{0:T(1024)S(1)} %copy-done.45), channel_id=1, source_target_pairs={{0,4},{4,0},{8,12},{12,8},{1,5},{5,1},{9,13},{13,9},{2,6},{6,2},{1... | collective-permute-start | bytes 49544 | tf_op jit(solution)/shard_map/ppermute | solution.py:705
  849.6 24.3 %collective-permute-start.67 = (bf16[384,512]{1,0:T(8,128)(2,1)S(1)}, bf16[384,512]{1,0:T(8,128)(2,1)}, u32[]{:S(2)}, u32[]{:S(2)}) collective-permute-start(bf16[384,512]{1,0:T(8,128)(2,1)S(1)} %copy-done.84), channel_id=1, source_target_pairs={{0,4},{4,0},{8,12},{12,8},{1,5},{5,1},{9,13},{13,9},{2,6},{6,2},{1... | collective-permute-start | bytes 1179656 | tf_op jit(solution)/shard_map/ppermute | solution.py:705
  866.5 23.1 %collective-permute-start.76 = (bf16[1184,1024]{1,0:T(8,128)(2,1)}, bf16[1184,1024]{1,0:T(8,128)(2,1)}, u32[]{:S(2)}, u32[]{:S(2)}) collective-permute-start(bf16[1184,1024]{1,0:T(8,128)(2,1)} %broadcast_select_fusion.2), channel_id=1, source_target_pairs={{0,16},{16,0},{1,17},{17,1},{2,18},{18,2},{3,19},{19,3},{4,20},{20... | collective-permute-start | bytes 7274504 | tf_op jit(solution)/shard_map/ppermute | solution.py:701
  (134 other events, 807.6 us)
Sparse Core Ops, SparseCore 0:
  21.8 122.9 all-gather.4
  147.2 134.2 all-gather.6
  525.2 65.8 reduce-scatter.3
  594.0 60.3 reduce-scatter.5
  659.4 47.7 reduce-scatter.7
  709.5 65.2 all-reduce.1

commit v4 on v3

--- a/solution.py
+++ b/solution.py
@@ -807,6 +807,12 @@
     return Chain(scatter_parts(parts), steps, sum_groups_end)
 
 
+def waiting_chain(value):
+    steps = [lambda state: sum_groups_step(0, (state, None))]
+    steps += [functools.partial(sum_groups_step, step) for step in range(1, group_steps())]
+    return Chain(value, steps, sum_groups_end)
+
+
 def plain_chain(value):
     steps = [functools.partial(sum_groups_step, step) for step in range(1, group_steps())]
     return Chain(sum_groups_step(0, (value, None)), steps, sum_groups_end)
@@ -1038,7 +1044,7 @@
         if late:
             qkv_grad = plain_chain(qkv_grad)
         else:
-            qkv_grad = Chain(qkv_grad, [lambda state: lax.psum(state, "dp")], lambda state: state)
+            qkv_grad = waiting_chain(qkv_grad)
         return g_inputs, g_qkv, (own_chains, qkv_grad, g_gain_a, g_gain_f)
 
     layers = [
@@ -1053,8 +1059,16 @@
         g_qkv_second,
         layers[0],
         kept_first,
-        (chains, chains, [grads_second[1]], chains),
+        (chains, chains + [grads_second[1]], [], chains + [grads_second[1]]),
     )
+
+    large, small = grads_first[0][0], grads_first[1]
+    while len(large.steps) > 1:
+        large.state = large.steps.pop(0)(large.state)
+    if large.steps:
+        large.state = large.steps.pop(0)(large.state)
+        small.state = small.steps.pop(0)(small.state)
+        large.state, small.state = lax.optimization_barrier((large.state, small.state))
 
     def ended(chains):
         return jnp.concatenate([chain.end() for chain in chains], axis=0)

time: 919 us -> 925 us (level)
    ppermute x51 -> x55, waiting for transfers between devices: 270 us -> 287 us  [across(): lax.ppermute(value, axis, [(i, i ^ bits) for i in range(lax.axis_size(axi...]
    reduce_scatter x3, waiting for transfers between devices: 33.9 us -> 18.8 us  [scatter_parts(): return lax.psum_scatter(rows, 'mp', scatter_dimension=0, tiled=True)]
    ppermute x51 -> x55, starting transfers between devices: 72.3 us -> 75.4 us  [across(): lax.ppermute(value, axis, [(i, i ^ bits) for i in range(lax.axis_size(axi...]
    unnamed x234 -> x266, local copies, waits for them, and re-layouts: 20 us -> 21.2 us
  transfers between devices with their start and end apart: 83 -> 86, of which waited for: 34 -> 38; matrix products, arithmetic and copies ran while one was open for 13% -> 13% of each run, Pallas kernels for 28% -> 29%
where the time goes in v4:
time: 925 us; the launch traced here: 914 us
  waiting for transfers between devices  351 us (38%)
  Pallas kernels  284 us (31%)
  other arithmetic  101 us (11%)
  starting transfers between devices  86.7 us (9%)
  local copies, waits for them, and re-layouts  52.7 us (6%)
  matrix products  21.1 us (2%)
  between operations  17.7 us (2%)
    ppermute x55, waiting for transfers between devices, across(): lax.ppermute(value, axis, [(i, i ^ bits) for i in range(lax.axis_size(axi...  287 us
    ppermute x55, starting transfers between devices, across(): lax.ppermute(value, axis, [(i, i ^ bits) for i in range(lax.axis_size(axi...  75.4 us
    pallas_call x2, Pallas kernels, attend_back(): pl.pallas_call(functools.partial(attend_back_kernel, second, block, min(2...  52.3 us
    pallas_call x4, Pallas kernels, ffn_backward(): pl.pallas_call(functools.partial(ffn_back_kernel, more), grid=(1,), in_sp...  45.5 us
    pallas_call x4, Pallas kernels, ffn_forward(): pl.pallas_call(ffn_kernel, grid=(1,), in_specs=[whole, whole, pl.BlockSpe...  44.8 us
    all_gather x2, waiting for transfers between devices, shards(): lax.all_gather(pack, 'mp', axis=0, tiled=False)  36.4 us
    pallas_call x2, Pallas kernels, pack_grads(): pl.pallas_call(functools.partial(pack_grads_kernel, size, plain, halves),...  34.3 us
    pallas_call x8, Pallas kernels, project_qkv(): pl.pallas_call(functools.partial(qkv_kernel, second, group, parts, fresh)...  33.1 us
  transfers between devices with their start and end apart: 86, of which 38 were waited for; matrix products, arithmetic and copies ran while one was open for 13% of the time, Pallas kernels for 29%

profile of v4, /device:TPU:0, one launch (start us, length us, event | category | flops | bytes accessed | tf_op | source)
XLA Modules:
  0.0 914.3 jit_solution(12525684898386112201)
XLA Ops:
  14.6 4.6 collective-permute-done.6
  31.0 3.7 fusion.46
  37.8 29.4 %collective-permute-done.1.refs_0_.refs_2_ = bf16[512,1024]{1,0:T(8,128)(2,1)} collective-permute-done((bf16[512,1024]{1,0:T(8,128)(2,1)}, bf16[512,1024]{1,0:T(8,128)(2,1)}, u32[]{:S(2)}, u32[]{:S(2)}) %collective-permute-start.1) | collective-permute-done | bytes 1048608 | tf_op jit(solution)/shard_map/ppermute | solution.py:705
  71.9 3.8 broadcast_select_fusion.4
  75.7 3.8 qkv_rope.8
  79.5 3.8 qkv_rope.9
  83.3 3.8 qkv_rope.10
  89.4 5.4 qkv_rope.11
  94.8 13.6 %attend.2 = (bf16[512,256]{1,0:T(8,128)(2,1)}, bf16[512,256]{1,0:T(8,128)(2,1)}, bf16[512,256]{1,0:T(8,128)(2,1)}, bf16[512,256]{1,0:T(8,128)(2,1)}, f32[4,2048]{1,0:T(4,128)}) custom-call(s32[3]{0:T(128)} %pad_add_fusion.info_ref, bf16[2048,256]{1,0:T(8,128)(2,1)} %get-tuple-element.165.q_ref, bf16[2048,256]{1,0:T(8,128)(2,1)} %get-tuple-element.166.k_ref, ...), custom_call_target="tpu_custom_call" | custom-call | flops 20700000256 | bytes 1048576 | tf_op jit(solution)/shard_map/attend/pallas_call | solution.py:205
  108.4 36.4 %all-gather.5.cloned.1.call-done = bf16[4736,1024]{1,0:T(8,128)(2,1)} async-done(((bf16[1184,1024]{1,0:T(8,128)(2,1)}), bf16[4736,1024]{1,0:T(8,128)(2,1)}) %all-gather.5.cloned.1.call-update) | async-done | bytes 9699344 | tf_op jit(solution)/shard_map/all_gather | solution.py:917
  150.4 6.6 collective-permute-done.10.refs_3_
  157.1 7.9 collective-permute-done.8.refs_1_
  166.1 6.5 out_project.2
  172.7 11.1 %ffn.4 = (f32[512,1024]{1,0:T(8,128)}, bf16[512,1408]{1,0:T(8,128)(2,1)}, bf16[512,1408]{1,0:T(8,128)(2,1)}, bf16[512,1408]{1,0:T(8,128)(2,1)}) custom-call(bf16[512,1024]{1,0:T(8,128)(2,1)} %get-tuple-element.181.x_ref.refs_6_, f32[512,1024]{1,0:T(8,128)} %get-tuple-element.182.base_ref, bf16[4,1184,1024]{2,1,0:T(8,128)(2,1)} %bitcast.121), custom_call_target="tpu_custom_call" | custom-call | flops 10350000128 | bytes 1048576 | tf_op jit(solution)/shard_map/ffn/pallas_call | solution.py:478
  183.8 11.2 %ffn.5 = (f32[512,1024]{1,0:T(8,128)}, bf16[512,1408]{1,0:T(8,128)(2,1)}, bf16[512,1408]{1,0:T(8,128)(2,1)}, bf16[512,1408]{1,0:T(8,128)(2,1)}) custom-call(bf16[512,1024]{1,0:T(8,128)(2,1)} %get-tuple-element.181.x_ref.refs_6_, f32[512,1024]{1,0:T(8,128)} %get-tuple-element.183.base_ref, bf16[4,1184,1024]{2,1,0:T(8,128)(2,1)} %collective-permute-done.11.pieces_ref.refs_4_), custom_call_target="tpu_custom_call" | custom-call | flops 10350000128 | bytes 1048576 | tf_op jit(solution)/shard_map/ffn/pallas_call | solution.py:478
  200.5 4.3 qkv_rope.12
  204.8 41.5 %collective-permute-done.12.refs_0_.refs_2_ = bf16[512,1024]{1,0:T(8,128)(2,1)S(1)} collective-permute-done((bf16[512,1024]{1,0:T(8,128)(2,1)S(1)}, bf16[512,1024]{1,0:T(8,128)(2,1)S(1)}, u32[]{:S(2)}, u32[]{:S(2)}) %collective-permute-start.12) | collective-permute-done | bytes 1048608 | tf_op jit(solution)/shard_map/ppermute | solution.py:705
  248.6 3.9 qkv_rope.13
  252.5 3.9 qkv_rope.14
  256.4 15.3 %collective-permute-done.13.refs_0_.refs_3_ = bf16[256,1024]{1,0:T(8,128)(2,1)S(1)} collective-permute-done((bf16[256,1024]{1,0:T(8,128)(2,1)S(1)}, bf16[256,1024]{1,0:T(8,128)(2,1)S(1)}, u32[]{:S(2)}, u32[]{:S(2)}) %collective-permute-start.13) | collective-permute-done | bytes 524320 | tf_op jit(solution)/shard_map/ppermute | solution.py:705
  273.9 4.2 qkv_rope.15
  278.0 13.7 %attend.3 = (bf16[512,256]{1,0:T(8,128)(2,1)}, bf16[512,256]{1,0:T(8,128)(2,1)}, bf16[512,256]{1,0:T(8,128)(2,1)}, bf16[512,256]{1,0:T(8,128)(2,1)}, f32[4,2048]{1,0:T(4,128)}) custom-call(s32[3]{0:T(128)} %pad_add_fusion.info_ref, bf16[2048,256]{1,0:T(8,128)(2,1)} %get-tuple-element.194.q_ref, bf16[2048,256]{1,0:T(8,128)(2,1)} %get-tuple-element.195.k_ref, ...), custom_call_target="tpu_custom_call" | custom-call | flops 20700000256 | bytes 1048576 | tf_op jit(solution)/shard_map/attend/pallas_call | solution.py:205
  291.8 4.6 collective-permute-start.20
  307.0 4.7 collective-permute-done.18.refs_2_
  313.5 6.5 out_project.3
  320.1 11.1 %ffn.6 = (f32[512,1024]{1,0:T(8,128)}, bf16[512,1408]{1,0:T(8,128)(2,1)}, bf16[512,1408]{1,0:T(8,128)(2,1)}, bf16[512,1408]{1,0:T(8,128)(2,1)}) custom-call(bf16[512,1024]{1,0:T(8,128)(2,1)} %get-tuple-element.206.x_ref.refs_6_, f32[512,1024]{1,0:T(8,128)} %get-tuple-element.207.base_ref, bf16[4,1184,1024]{2,1,0:T(8,128)(2,1)} %bitcast.125), custom_call_target="tpu_custom_call" | custom-call | flops 10350000128 | bytes 1048576 | tf_op jit(solution)/shard_map/ffn/pallas_call | solution.py:478
  331.2 11.1 %ffn_back.4 = (f32[512,1024]{1,0:T(8,128)}, bf16[512,1408]{1,0:T(8,128)(2,1)}, bf16[512,1408]{1,0:T(8,128)(2,1)}) custom-call(bf16[512,1024]{1,0:T(8,128)(2,1)} %bitcast_convert_fusion.refs_0_.refs_1_.refs_8_, bf16[512,1408]{1,0:T(8,128)(2,1)} %get-tuple-element.210.refs_1_, bf16[512,1408]{1,0:T(8,128)(2,1)} %get-tuple-element.211.refs_2_, ...), custom_call_target="tpu_custom_call" | custom-call | flops 1150000000 | bytes 1048576 | tf_op jit(solution)/shard_map/ffn_back/pallas_call | solution.py:527
  342.6 11.3 %ffn.7 = (f32[512,1024]{1,0:T(8,128)}, bf16[512,1408]{1,0:T(8,128)(2,1)}, bf16[512,1408]{1,0:T(8,128)(2,1)}, bf16[512,1408]{1,0:T(8,128)(2,1)}) custom-call(bf16[512,1024]{1,0:T(8,128)(2,1)} %get-tuple-element.206.x_ref.refs_6_, f32[512,1024]{1,0:T(8,128)} %get-tuple-element.208.base_ref, bf16[4,1184,1024]{2,1,0:T(8,128)(2,1)} %collective-permute-done.20.pieces_ref.refs_4_), custom_call_target="tpu_custom_call" | custom-call | flops 10350000128 | bytes 1048576 | tf_op jit(solution)/shard_map/ffn/pallas_call | solution.py:478
  353.9 11.6 %ffn_back.5 = (f32[512,1024]{1,0:T(8,128)}, bf16[512,1408]{1,0:T(8,128)(2,1)}, bf16[512,1408]{1,0:T(8,128)(2,1)}) custom-call(f32[512,1024]{1,0:T(8,128)} %get-tuple-element.212.refs_0_, bf16[512,1024]{1,0:T(8,128)(2,1)} %bitcast_convert_fusion.refs_0_.refs_1_.refs_8_, bf16[512,1408]{1,0:T(8,128)(2,1)} %get-tuple-element.213.refs_2_, ...), custom_call_target="tpu_custom_call" | custom-call | flops 1150000000 | bytes 1048576 | tf_op jit(solution)/shard_map/ffn_back/pallas_call | solution.py:527
  375.0 3.0 convolution_convert_fusion.11
  382.1 3.5 collective-permute-done.23.refs_3_
  391.5 16.9 %pack_grads.2 = (bf16[4,592,1024]{2,1,0:T(8,128)(2,1)}, bf16[4,592,1024]{2,1,0:T(8,128)(2,1)}) custom-call(s32[1]{0:T(128)} %bitcast.31.info_ref.which_ref, bf16[512,1408]{1,0:T(8,128)(2,1)} %get-tuple-element.221.refs_0_, bf16[512,1408]{1,0:T(8,128)(2,1)} %copy-done.82, bf16[512,1408]{1,0:T(8,128)(2,1)} %get-tuple-element.223.refs_2_, ...), custom_call_target="tpu_custom_call" | custom-call | flops 17250000896 | bytes 1048576 | tf_op jit(solution)/shard_map/pack_grads/pallas_call | solution.py:587
  409.8 25.7 %attend_back.2 = (bf16[512,768]{1,0:T(8,128)(2,1)}, bf16[512,768]{1,0:T(8,128)(2,1)}, bf16[512,768]{1,0:T(8,128)(2,1)}, bf16[512,768]{1,0:T(8,128)(2,1)}) custom-call(s32[3]{0:T(128)} %pad_add_fusion.info_ref, bf16[2048,256]{1,0:T(8,128)(2,1)} %get-tuple-element.194.q_ref, bf16[2048,256]{1,0:T(8,128)(2,1)} %get-tuple-element.195.k_ref, ...), custom_call_target="tpu_custom_call" | custom-call | flops 41400000512 | bytes 1048576 | tf_op jit(solution)/shard_map/attend_back/pallas_call | solution.py:362
  448.7 8.9 collective-permute-done.32
  459.6 9.2 %collective-permute-done.35 = bf16[256,1024]{1,0:T(8,128)(2,1)S(1)} collective-permute-done((bf16[256,1024]{1,0:T(8,128)(2,1)S(1)}, bf16[256,1024]{1,0:T(8,128)(2,1)S(1)}, u32[]{:S(2)}, u32[]{:S(2)}) %collective-permute-start.35) | collective-permute-done | bytes 524320 | tf_op jit(solution)/shard_map/ppermute | solution.py:705
  473.6 10.9 %ffn_back.6 = (f32[512,1024]{1,0:T(8,128)}, bf16[512,1408]{1,0:T(8,128)(2,1)}, bf16[512,1408]{1,0:T(8,128)(2,1)}) custom-call(bf16[512,1024]{1,0:T(8,128)(2,1)} %get-tuple-element.307.refs_0_.refs_1_.refs_8_, bf16[512,1408]{1,0:T(8,128)(2,1)} %get-tuple-element.237.refs_1_, bf16[512,1408]{1,0:T(8,128)(2,1)} %get-tuple-element.238.refs_2_, ...), custom_call_target="tpu_custom_call" | custom-call | flops 1150000000 | bytes 1048576 | tf_op jit(solution)/shard_map/ffn_back/pallas_call | solution.py:527
  484.6 11.8 %ffn_back.7 = (f32[512,1024]{1,0:T(8,128)}, bf16[512,1408]{1,0:T(8,128)(2,1)}, bf16[512,1408]{1,0:T(8,128)(2,1)}) custom-call(f32[512,1024]{1,0:T(8,128)} %get-tuple-element.239.refs_0_, bf16[512,1024]{1,0:T(8,128)(2,1)} %get-tuple-element.307.refs_0_.refs_1_.refs_8_, bf16[512,1408]{1,0:T(8,128)(2,1)} %get-tuple-element.240.refs_2_, ...), custom_call_target="tpu_custom_call" | custom-call | flops 1150000000 | bytes 1048576 | tf_op jit(solution)/shard_map/ffn_back/pallas_call | solution.py:527
  496.3 18.5 %collective-permute-done.37 = bf16[4,592,1024]{2,1,0:T(8,128)(2,1)} collective-permute-done((bf16[4,592,1024]{2,1,0:T(8,128)(2,1)}, bf16[4,592,1024]{2,1,0:T(8,128)(2,1)}, u32[]{:S(2)}, u32[]{:S(2)}) %collective-permute-start.37) | collective-permute-done | bytes 4849696 | tf_op jit(solution)/shard_map/ppermute | solution.py:705
  514.9 8.6 add_convert_fusion
  541.0 17.4 %pack_grads.3 = (bf16[4,608,1024]{2,1,0:T(8,128)(2,1)}, bf16[4,288,1024]{2,1,0:T(8,128)(2,1)}, bf16[4,288,1024]{2,1,0:T(8,128)(2,1)}) custom-call(s32[1]{0:T(128)} %bitcast.31.info_ref.which_ref, bf16[512,1408]{1,0:T(8,128)(2,1)} %get-tuple-element.265.refs_0_, bf16[512,1408]{1,0:T(8,128)(2,1)} %copy-done.80, bf16[512,1408]{1,0:T(8,128)(2,1)} %get-tuple-element.267.refs_2_, ...), custom_call_target="tpu_custom_call" | custom-call | flops 17250000896 | bytes 1048576 | tf_op jit(solution)/shard_map/pack_grads/pallas_call | solution.py:587
  564.6 8.1 qkv_grad.2
  589.7 5.4 collective-permute-done.42.refs_7_
  595.1 4.4 collective-permute-start.54
  599.4 26.6 %attend_back.3 = (bf16[512,768]{1,0:T(8,128)(2,1)}, bf16[512,768]{1,0:T(8,128)(2,1)}, bf16[512,768]{1,0:T(8,128)(2,1)}, bf16[512,768]{1,0:T(8,128)(2,1)}) custom-call(s32[3]{0:T(128)} %pad_add_fusion.info_ref, bf16[2048,256]{1,0:T(8,128)(2,1)} %get-tuple-element.165.q_ref, bf16[2048,256]{1,0:T(8,128)(2,1)} %get-tuple-element.166.k_ref, ...), custom_call_target="tpu_custom_call" | custom-call | flops 41400000512 | bytes 1048576 | tf_op jit(solution)/shard_map/attend_back/pallas_call | solution.py:362
  627.0 18.8 %reduce-scatter.6.cloned.1.call-done = bf16[608,1024]{1,0:T(8,128)(2,1)} async-done(((bf16[2432,1024]{1,0:T(8,128)(2,1)}), bf16[608,1024]{1,0:T(8,128)(2,1)}) %reduce-scatter.6.cloned.1.call-update) | async-done | bytes 1245200 | tf_op jit(solution)/shard_map/reduce_scatter | solution.py:785
  652.5 11.1 %collective-permute-done.67 = bf16[4,288,1024]{2,1,0:T(8,128)(2,1)} collective-permute-done((bf16[4,288,1024]{2,1,0:T(8,128)(2,1)}, bf16[4,288,1024]{2,1,0:T(8,128)(2,1)}, u32[]{:S(2)}, u32[]{:S(2)}) %collective-permute-start.67) | collective-permute-done | bytes 2359328 | tf_op jit(solution)/shard_map/ppermute | solution.py:705
  663.6 7.4 qkv_grad.3
  678.7 4.2 add_convert_fusion.1
  686.1 4.8 collective-permute-done.63
  698.2 23.8 %collective-permute-done.49 = bf16[256,1024]{1,0:T(8,128)(2,1)S(1)} collective-permute-done((bf16[256,1024]{1,0:T(8,128)(2,1)S(1)}, bf16[256,1024]{1,0:T(8,128)(2,1)S(1)}, u32[]{:S(2)}, u32[]{:S(2)}) %collective-permute-start.49) | collective-permute-done | bytes 524320 | tf_op jit(solution)/shard_map/ppermute | solution.py:705
  732.8 10.8 %collective-permute-done.53 = bf16[256,1024]{1,0:T(8,128)(2,1)} collective-permute-done((bf16[256,1024]{1,0:T(8,128)(2,1)}, bf16[256,1024]{1,0:T(8,128)(2,1)}, u32[]{:S(2)}, u32[]{:S(2)}) %collective-permute-start.53) | collective-permute-done | bytes 524320 | tf_op jit(solution)/shard_map/ppermute | solution.py:705
  747.7 5.5 collective-permute-done.50
  763.7 3.6 collective-permute-start.73
  768.1 3.0 collective-permute-done.60
  774.9 16.9 %collective-permute-done.61 = f32[4128]{0:T(1024)S(1)} collective-permute-done((f32[4128]{0:T(1024)S(1)}, f32[4128]{0:T(1024)S(1)}, u32[]{:S(2)}, u32[]{:S(2)}) %collective-permute-start.61) | collective-permute-done | bytes 16544 | tf_op jit(solution)/shard_map/ppermute | solution.py:705
  795.9 3.4 collective-permute-start.74
  799.5 15.1 %collective-permute-done.74.second_ref = bf16[384,256]{1,0:T(8,128)(2,1)} collective-permute-done((bf16[384,256]{1,0:T(8,128)(2,1)S(1)}, bf16[384,256]{1,0:T(8,128)(2,1)}, u32[]{:S(2)}, u32[]{:S(2)}) %collective-permute-start.74) | collective-permute-done | bytes 196640 | tf_op jit(solution)/shard_map/ppermute | solution.py:705
  814.6 3.5 collective-permute-start.70
  820.0 22.6 %collective-permute-done.70 = bf16[384,256]{1,0:T(8,128)(2,1)S(1)} collective-permute-done((bf16[384,256]{1,0:T(8,128)(2,1)S(1)}, bf16[384,256]{1,0:T(8,128)(2,1)S(1)}, u32[]{:S(2)}, u32[]{:S(2)}) %collective-permute-start.70) | collective-permute-done | bytes 196640 | tf_op jit(solution)/shard_map/ppermute | solution.py:705
  849.7 5.2 collective-permute-done.71.second_ref
  858.8 3.2 place_two.15
  867.0 4.0 broadcast_select_fusion.2
  876.0 4.2 collective-permute-done.72.second_ref
  897.2 3.1 broadcast_select_fusion.1
  (556 shorter events, 244.2 us)
Async XLA Ops:
  7.2 137.6 %all-gather.5.cloned.1.call-start = ((), (), s32[]{:S(2)}) async-start(), calls=%async_computation.6 | async-start | bytes 12124160 | tf_op jit(solution)/shard_map/all_gather | solution.py:917
  21.7 270.1 %all-gather.7.cloned.1.call-start = ((), (), s32[]{:S(2)}) async-start(), calls=%async_computation.7 | async-start | bytes 12124160 | tf_op jit(solution)/shard_map/all_gather | solution.py:917
  23.1 48.8 %collective-permute-start.5 = (bf16[1024,768]{1,0:T(8,128)(2,1)S(1)}, bf16[1024,768]{1,0:T(8,128)(2,1)}, u32[]{:S(2)}, u32[]{:S(2)}) collective-permute-start(bf16[1024,768]{1,0:T(8,128)(2,1)S(1)} %pad_maximum_fusion.5), channel_id=1, source_target_pairs={{0,16},{16,0},{1,17},{17,1},{2,18},{18,2},{3,19},{19,3},{4,20},{20... | collective-permute-start | bytes 4718600 | tf_op jit(solution)/shard_map/ppermute | solution.py:701
  23.3 45.0 %collective-permute-start.3 = (bf16[512,1024]{1,0:T(8,128)(2,1)}, bf16[512,1024]{1,0:T(8,128)(2,1)}, u32[]{:S(2)}, u32[]{:S(2)}) collective-permute-start(bf16[512,1024]{1,0:T(8,128)(2,1)} %fusion.6.refs_0_), channel_id=1, source_target_pairs={{0,1},{1,0},{2,3},{3,2},{4,5},{5,4},{6,7},{7,6},{8,9},{9,8},{10,11... | collective-permute-start | bytes 3145736 | tf_op jit(solution)/shard_map/ppermute | solution.py:705
  26.2 40.9 %collective-permute-start.1 = (bf16[512,1024]{1,0:T(8,128)(2,1)}, bf16[512,1024]{1,0:T(8,128)(2,1)}, u32[]{:S(2)}, u32[]{:S(2)}) collective-permute-start(bf16[512,1024]{1,0:T(8,128)(2,1)} %fusion.6.refs_0_), channel_id=1, source_target_pairs={{0,2},{1,3},{2,0},{3,1},{4,6},{5,7},{6,4},{7,5},{8,10},{9,11},{10,... | collective-permute-start | bytes 3145736 | tf_op jit(solution)/shard_map/ppermute | solution.py:705
  68.2 18.9 %collective-permute-start.2 = (bf16[256,1024]{1,0:T(8,128)(2,1)S(1)}, bf16[256,1024]{1,0:T(8,128)(2,1)S(1)}, u32[]{:S(2)}, u32[]{:S(2)}) collective-permute-start(bf16[256,1024]{1,0:T(8,128)(2,1)S(1)} %slice.257), channel_id=1, source_target_pairs={{0,1},{1,0},{2,3},{3,2},{4,5},{5,4},{6,7},{7,6},{8,9},{9,8},{10,11... | collective-permute-start | bytes 1572872 | tf_op jit(solution)/shard_map/ppermute | solution.py:705
  69.4 19.2 %collective-permute-start.4 = (bf16[256,1024]{1,0:T(8,128)(2,1)S(1)}, bf16[256,1024]{1,0:T(8,128)(2,1)S(1)}, u32[]{:S(2)}, u32[]{:S(2)}) collective-permute-start(bf16[256,1024]{1,0:T(8,128)(2,1)S(1)} %slice.258), channel_id=1, source_target_pairs={{0,2},{1,3},{2,0},{3,1},{4,6},{5,7},{6,4},{7,5},{8,10},{9,11},{10,... | collective-permute-start | bytes 1572872 | tf_op jit(solution)/shard_map/ppermute | solution.py:705
  144.8 39.0 %collective-permute-start.11 = (bf16[4,1184,1024]{2,1,0:T(8,128)(2,1)}, bf16[4,1184,1024]{2,1,0:T(8,128)(2,1)}, u32[]{:S(2)}, u32[]{:S(2)}) collective-permute-start(bf16[4,1184,1024]{2,1,0:T(8,128)(2,1)} %bitcast.119), channel_id=1, source_target_pairs={{0,16},{16,0},{1,17},{17,1},{2,18},{18,2},{3,19},{19,3},{4,20},{20... | collective-permute-start | bytes 29097992 | tf_op jit(solution)/shard_map/ppermute | solution.py:701
  144.8 450.2 %reduce-scatter.4.cloned.1.call-start = ((), (), s32[]{:S(2)}) async-start(), calls=%async_computation.3 | async-start | bytes 6062080 | tf_op jit(solution)/shard_map/reduce_scatter | solution.py:785
  146.4 18.6 %collective-permute-start.7 = (bf16[4,128,1024]{2,1,0:T(8,128)(2,1)S(1)}, bf16[4,128,1024]{2,1,0:T(8,128)(2,1)S(1)}, u32[]{:S(2)}, u32[]{:S(2)}) collective-permute-start(bf16[4,128,1024]{2,1,0:T(8,128)(2,1)S(1)} %slice.199.own_ref), channel_id=1, source_target_pairs={{0,16},{16,0},{1,17},{17,1},{2,18},{18,2},{3,19},{19,3},{4,20},{20... | collective-permute-start | bytes 3145736 | tf_op jit(solution)/shard_map/ppermute | solution.py:701
  148.4 16.6 %collective-permute-start.8 = (bf16[512,256]{1,0:T(8,128)(2,1)S(1)}, bf16[512,256]{1,0:T(8,128)(2,1)S(1)}, u32[]{:S(2)}, u32[]{:S(2)}) collective-permute-start(bf16[512,256]{1,0:T(8,128)(2,1)S(1)} %copy-done.100), channel_id=1, source_target_pairs={{0,1},{1,0},{2,3},{3,2},{4,5},{5,4},{6,7},{7,6},{8,9},{9,8},{10,11... | collective-permute-start | bytes 786440 | tf_op jit(solution)/shard_map/ppermute | solution.py:705
  149.9 15.1 %collective-permute-start.9 = (bf16[512,256]{1,0:T(8,128)(2,1)S(1)}, bf16[512,256]{1,0:T(8,128)(2,1)S(1)}, u32[]{:S(2)}, u32[]{:S(2)}) collective-permute-start(bf16[512,256]{1,0:T(8,128)(2,1)S(1)} %copy-done.101), channel_id=1, source_target_pairs={{0,2},{1,3},{2,0},{3,1},{4,6},{5,7},{6,4},{7,5},{8,10},{9,11},{10,... | collective-permute-start | bytes 786440 | tf_op jit(solution)/shard_map/ppermute | solution.py:705
  198.3 48.0 %collective-permute-start.12 = (bf16[512,1024]{1,0:T(8,128)(2,1)S(1)}, bf16[512,1024]{1,0:T(8,128)(2,1)S(1)}, u32[]{:S(2)}, u32[]{:S(2)}) collective-permute-start(bf16[512,1024]{1,0:T(8,128)(2,1)S(1)} %fusion.4.refs_0_), channel_id=1, source_target_pairs={{0,2},{1,3},{2,0},{3,1},{4,6},{5,7},{6,4},{7,5},{8,10},{9,11},{10,... | collective-permute-start | bytes 3145736 | tf_op jit(solution)/shard_map/ppermute | solution.py:705
  199.6 48.0 %collective-permute-start.14 = (bf16[512,1024]{1,0:T(8,128)(2,1)S(1)}, bf16[512,1024]{1,0:T(8,128)(2,1)S(1)}, u32[]{:S(2)}, u32[]{:S(2)}) collective-permute-start(bf16[512,1024]{1,0:T(8,128)(2,1)S(1)} %fusion.4.refs_0_), channel_id=1, source_target_pairs={{0,1},{1,0},{2,3},{3,2},{4,5},{5,4},{6,7},{7,6},{8,9},{9,8},{10,11... | collective-permute-start | bytes 3145736 | tf_op jit(solution)/shard_map/ppermute | solution.py:705
  246.3 25.3 %collective-permute-start.13 = (bf16[256,1024]{1,0:T(8,128)(2,1)S(1)}, bf16[256,1024]{1,0:T(8,128)(2,1)S(1)}, u32[]{:S(2)}, u32[]{:S(2)}) collective-permute-start(bf16[256,1024]{1,0:T(8,128)(2,1)S(1)} %slice.261), channel_id=1, source_target_pairs={{0,1},{1,0},{2,3},{3,2},{4,5},{5,4},{6,7},{7,6},{8,9},{9,8},{10,11... | collective-permute-start | bytes 1572872 | tf_op jit(solution)/shard_map/ppermute | solution.py:705
  247.7 25.4 %collective-permute-start.15 = (bf16[256,1024]{1,0:T(8,128)(2,1)S(1)}, bf16[256,1024]{1,0:T(8,128)(2,1)S(1)}, u32[]{:S(2)}, u32[]{:S(2)}) collective-permute-start(bf16[256,1024]{1,0:T(8,128)(2,1)S(1)} %slice.262), channel_id=1, source_target_pairs={{0,2},{1,3},{2,0},{3,1},{4,6},{5,7},{6,4},{7,5},{8,10},{9,11},{10,... | collective-permute-start | bytes 1572872 | tf_op jit(solution)/shard_map/ppermute | solution.py:705
  291.8 50.7 %collective-permute-start.20 = (bf16[4,1184,1024]{2,1,0:T(8,128)(2,1)}, bf16[4,1184,1024]{2,1,0:T(8,128)(2,1)}, u32[]{:S(2)}, u32[]{:S(2)}) collective-permute-start(bf16[4,1184,1024]{2,1,0:T(8,128)(2,1)} %bitcast.123), channel_id=1, source_target_pairs={{0,16},{16,0},{1,17},{17,1},{2,18},{18,2},{3,19},{19,3},{4,20},{20... | collective-permute-start | bytes 29097992 | tf_op jit(solution)/shard_map/ppermute | solution.py:701
  297.7 14.9 %collective-permute-start.16 = (bf16[4,128,1024]{2,1,0:T(8,128)(2,1)S(1)}, bf16[4,128,1024]{2,1,0:T(8,128)(2,1)S(1)}, u32[]{:S(2)}, u32[]{:S(2)}) collective-permute-start(bf16[4,128,1024]{2,1,0:T(8,128)(2,1)S(1)} %slice.204.own_ref), channel_id=1, source_target_pairs={{0,16},{16,0},{1,17},{17,1},{2,18},{18,2},{3,19},{19,3},{4,20},{20... | collective-permute-start | bytes 3145736 | tf_op jit(solution)/shard_map/ppermute | solution.py:701
  298.3 13.4 %collective-permute-start.18 = (bf16[512,256]{1,0:T(8,128)(2,1)S(1)}, bf16[512,256]{1,0:T(8,128)(2,1)S(1)}, u32[]{:S(2)}, u32[]{:S(2)}) collective-permute-start(bf16[512,256]{1,0:T(8,128)(2,1)S(1)} %copy-done.110), channel_id=1, source_target_pairs={{0,2},{1,3},{2,0},{3,1},{4,6},{5,7},{6,4},{7,5},{8,10},{9,11},{10,... | collective-permute-start | bytes 786440 | tf_op jit(solution)/shard_map/ppermute | solution.py:705
  300.1 12.2 %collective-permute-start.19 = (bf16[512,256]{1,0:T(8,128)(2,1)S(1)}, bf16[512,256]{1,0:T(8,128)(2,1)S(1)}, u32[]{:S(2)}, u32[]{:S(2)}) collective-permute-start(bf16[512,256]{1,0:T(8,128)(2,1)S(1)} %copy-done.111), channel_id=1, source_target_pairs={{0,3},{1,2},{2,1},{3,0},{4,7},{5,6},{6,5},{7,4},{8,11},{9,10},{10,... | collective-permute-start | bytes 786440 | tf_op jit(solution)/shard_map/ppermute | solution.py:705
  374.0 14.8 %collective-permute-start.29 = (bf16[512,1024]{1,0:T(8,128)(2,1)S(1)}, bf16[512,1024]{1,0:T(8,128)(2,1)}, u32[]{:S(2)}, u32[]{:S(2)}) collective-permute-start(bf16[512,1024]{1,0:T(8,128)(2,1)S(1)} %copy-done.9), channel_id=1, source_target_pairs={{0,16},{16,0},{1,17},{17,1},{2,18},{18,2},{3,19},{19,3},{4,20},{20... | collective-permute-start | bytes 3145736 | tf_op jit(solution)/shard_map/ppermute | solution.py:701
  374.3 15.7 %collective-permute-start.28 = (bf16[512,1024]{1,0:T(8,128)(2,1)}, bf16[512,1024]{1,0:T(8,128)(2,1)S(1)}, u32[]{:S(2)}, u32[]{:S(2)}) collective-permute-start(bf16[512,1024]{1,0:T(8,128)(2,1)} %get-tuple-element.206.x_ref.refs_6_), channel_id=1, source_target_pairs={{0,16},{16,0},{1,17},{17,1},{2,18},{18,2},{3,19},{19,3},{4,20},{20... | collective-permute-start | bytes 3145736 | tf_op jit(solution)/shard_map/ppermute | solution.py:701
  378.0 12.0 %collective-permute-start.27 = (bf16[512,1408]{1,0:T(8,128)(2,1)S(1)}, bf16[512,1408]{1,0:T(8,128)(2,1)S(1)}, u32[]{:S(2)}, u32[]{:S(2)}) collective-permute-start(bf16[512,1408]{1,0:T(8,128)(2,1)S(1)} %copy-done.79), channel_id=1, source_target_pairs={{0,16},{16,0},{1,17},{17,1},{2,18},{18,2},{3,19},{19,3},{4,20},{20... | collective-permute-start | bytes 4325384 | tf_op jit(solution)/shard_map/ppermute | solution.py:701
  386.5 21.9 %collective-permute-start.24 = (bf16[512,256]{1,0:T(8,128)(2,1)S(1)}, bf16[512,256]{1,0:T(8,128)(2,1)S(1)}, u32[]{:S(2)}, u32[]{:S(2)}) collective-permute-start(bf16[512,256]{1,0:T(8,128)(2,1)S(1)} %get-tuple-element.362), channel_id=1, source_target_pairs={{0,1},{1,0},{2,3},{3,2},{4,5},{5,4},{6,7},{7,6},{8,9},{9,8},{10,11... | collective-permute-start | bytes 786440 | tf_op jit(solution)/shard_map/ppermute | solution.py:705
  387.9 20.5 %collective-permute-start.25 = (bf16[512,256]{1,0:T(8,128)(2,1)S(1)}, bf16[512,256]{1,0:T(8,128)(2,1)S(1)}, u32[]{:S(2)}, u32[]{:S(2)}) collective-permute-start(bf16[512,256]{1,0:T(8,128)(2,1)S(1)} %get-tuple-element.361), channel_id=1, source_target_pairs={{0,2},{1,3},{2,0},{3,1},{4,6},{5,7},{6,4},{7,5},{8,10},{9,11},{10,... | collective-permute-start | bytes 786440 | tf_op jit(solution)/shard_map/ppermute | solution.py:705
  388.7 19.7 %collective-permute-start.26 = (bf16[512,256]{1,0:T(8,128)(2,1)S(1)}, bf16[512,256]{1,0:T(8,128)(2,1)S(1)}, u32[]{:S(2)}, u32[]{:S(2)}) collective-permute-start(bf16[512,256]{1,0:T(8,128)(2,1)S(1)} %get-tuple-element.360), channel_id=1, source_target_pairs={{0,3},{1,2},{2,1},{3,0},{4,7},{5,6},{6,5},{7,4},{8,11},{9,10},{10,... | collective-permute-start | bytes 786440 | tf_op jit(solution)/shard_map/ppermute | solution.py:705
  408.5 106.4 %collective-permute-start.37 = (bf16[4,592,1024]{2,1,0:T(8,128)(2,1)}, bf16[4,592,1024]{2,1,0:T(8,128)(2,1)}, u32[]{:S(2)}, u32[]{:S(2)}) collective-permute-start(bf16[4,592,1024]{2,1,0:T(8,128)(2,1)} %get-tuple-element.244), channel_id=1, source_target_pairs={{0,4},{4,0},{8,12},{12,8},{1,5},{5,1},{9,13},{13,9},{2,6},{6,2},{1... | collective-permute-start | bytes 14549000 | tf_op jit(solution)/shard_map/ppermute | solution.py:705
  440.6 19.0 %collective-permute-start.31 = (bf16[256,1024]{1,0:T(8,128)(2,1)S(1)}, bf16[256,1024]{1,0:T(8,128)(2,1)S(1)}, u32[]{:S(2)}, u32[]{:S(2)}) collective-permute-start(bf16[256,1024]{1,0:T(8,128)(2,1)S(1)} %slice.271), channel_id=1, source_target_pairs={{0,1},{1,0},{2,3},{3,2},{4,5},{5,4},{6,7},{7,6},{8,9},{9,8},{10,11... | collective-permute-start | bytes 1572872 | tf_op jit(solution)/shard_map/ppermute | solution.py:705
  441.3 16.2 %collective-permute-start.32 = (bf16[256,1024]{1,0:T(8,128)(2,1)S(1)}, bf16[256,1024]{1,0:T(8,128)(2,1)S(1)}, u32[]{:S(2)}, u32[]{:S(2)}) collective-permute-start(bf16[256,1024]{1,0:T(8,128)(2,1)S(1)} %get-tuple-element.352), channel_id=1, source_target_pairs={{0,1},{1,0},{2,3},{3,2},{4,5},{5,4},{6,7},{7,6},{8,9},{9,8},{10,11... | collective-permute-start | bytes 1572872 | tf_op jit(solution)/shard_map/ppermute | solution.py:705
  443.8 15.8 %collective-permute-start.36 = (bf16[256,1024]{1,0:T(8,128)(2,1)S(1)}, bf16[256,1024]{1,0:T(8,128)(2,1)S(1)}, u32[]{:S(2)}, u32[]{:S(2)}) collective-permute-start(bf16[256,1024]{1,0:T(8,128)(2,1)S(1)} %slice.277), channel_id=1, source_target_pairs={{0,2},{1,3},{2,0},{3,1},{4,6},{5,7},{6,4},{7,5},{8,10},{9,11},{10,... | collective-permute-start | bytes 1572872 | tf_op jit(solution)/shard_map/ppermute | solution.py:705
  447.2 21.6 %collective-permute-start.35 = (bf16[256,1024]{1,0:T(8,128)(2,1)S(1)}, bf16[256,1024]{1,0:T(8,128)(2,1)S(1)}, u32[]{:S(2)}, u32[]{:S(2)}) collective-permute-start(bf16[256,1024]{1,0:T(8,128)(2,1)S(1)} %add_convert_fusion.9), channel_id=1, source_target_pairs={{0,1},{1,0},{2,3},{3,2},{4,5},{5,4},{6,7},{7,6},{8,9},{9,8},{10,11... | collective-permute-start | bytes 1572872 | tf_op jit(solution)/shard_map/ppermute | solution.py:705
  457.8 12.1 %collective-permute-start.33 = (bf16[256,1024]{1,0:T(8,128)(2,1)S(1)}, bf16[256,1024]{1,0:T(8,128)(2,1)S(1)}, u32[]{:S(2)}, u32[]{:S(2)}) collective-permute-start(bf16[256,1024]{1,0:T(8,128)(2,1)S(1)} %add_convert_fusion.10), channel_id=1, source_target_pairs={{0,2},{1,3},{2,0},{3,1},{4,6},{5,7},{6,4},{7,5},{8,10},{9,11},{10,... | collective-permute-start | bytes 1572872 | tf_op jit(solution)/shard_map/ppermute | solution.py:705
  523.6 122.3 %reduce-scatter.6.cloned.1.call-start = ((), (), s32[]{:S(2)}) async-start(), calls=%async_computation.4 | async-start | bytes 6225920 | tf_op jit(solution)/shard_map/reduce_scatter | solution.py:785
  558.4 240.8 %reduce-scatter.8.cloned.1.call-start = ((), (), s32[]{:S(2)}) async-start(), calls=%async_computation.5 | async-start | bytes 2949120 | tf_op jit(solution)/shard_map/reduce_scatter | solution.py:785
  564.3 11.4 %collective-permute-start.21 = (bf16[512,1024]{1,0:T(8,128)(2,1)}, bf16[512,1024]{1,0:T(8,128)(2,1)}, u32[]{:S(2)}, u32[]{:S(2)}) collective-permute-start(bf16[512,1024]{1,0:T(8,128)(2,1)} %broadcast_select_fusion.7), channel_id=1, source_target_pairs={{0,16},{16,0},{1,17},{17,1},{2,18},{18,2},{3,19},{19,3},{4,20},{20... | collective-permute-start | bytes 3145736 | tf_op jit(solution)/shard_map/ppermute | solution.py:701
  581.3 13.8 %collective-permute-start.42 = (bf16[512,256]{1,0:T(8,128)(2,1)S(1)}, bf16[512,256]{1,0:T(8,128)(2,1)}, u32[]{:S(2)}, u32[]{:S(2)}) collective-permute-start(bf16[512,256]{1,0:T(8,128)(2,1)S(1)} %get-tuple-element.348), channel_id=1, source_target_pairs={{0,3},{1,2},{2,1},{3,0},{4,7},{5,6},{6,5},{7,4},{8,11},{9,10},{10,... | collective-permute-start | bytes 786440 | tf_op jit(solution)/shard_map/ppermute | solution.py:705
  584.8 78.8 %collective-permute-start.67 = (bf16[4,288,1024]{2,1,0:T(8,128)(2,1)}, bf16[4,288,1024]{2,1,0:T(8,128)(2,1)}, u32[]{:S(2)}, u32[]{:S(2)}) collective-permute-start(bf16[4,288,1024]{2,1,0:T(8,128)(2,1)} %get-tuple-element.282), channel_id=1, source_target_pairs={{0,4},{4,0},{8,12},{12,8},{1,5},{5,1},{9,13},{13,9},{2,6},{6,2},{1... | collective-permute-start | bytes 7077896 | tf_op jit(solution)/shard_map/ppermute | solution.py:705
  595.1 160.9 %collective-permute-start.54 = (bf16[592,1024]{1,0:T(8,128)(2,1)}, bf16[592,1024]{1,0:T(8,128)(2,1)}, u32[]{:S(2)}, u32[]{:S(2)}) collective-permute-start(bf16[592,1024]{1,0:T(8,128)(2,1)} %reduce-scatter.4.cloned.1.call-done), channel_id=1, source_target_pairs={{0,8},{4,12},{8,0},{12,4},{1,9},{5,13},{9,1},{13,5},{2,10},{6,14},... | collective-permute-start | bytes 3637256 | tf_op jit(solution)/shard_map/ppermute | solution.py:705
  673.2 50.2 %collective-permute-start.68 = (bf16[512,768]{1,0:T(8,128)(2,1)}, bf16[512,768]{1,0:T(8,128)(2,1)}, u32[]{:S(2)}, u32[]{:S(2)}) collective-permute-start(bf16[512,768]{1,0:T(8,128)(2,1)} %constant_dynamic-slice_fusion.5), channel_id=1, source_target_pairs={{0,16},{16,0},{1,17},{17,1},{2,18},{18,2},{3,19},{19,3},{4,20},{20... | collective-permute-start | bytes 2359304 | tf_op jit(solution)/shard_map/ppermute | solution.py:701
  674.1 16.8 %collective-permute-start.63 = (bf16[608,512]{1,0:T(8,128)(2,1)}, bf16[608,512]{1,0:T(8,128)(2,1)}, u32[]{:S(2)}, u32[]{:S(2)}) collective-permute-start(bf16[608,512]{1,0:T(8,128)(2,1)} %constant_dynamic-slice_fusion.7), channel_id=1, source_target_pairs={{0,4},{4,0},{8,12},{12,8},{1,5},{5,1},{9,13},{13,9},{2,6},{6,2},{1... | collective-permute-start | bytes 1867784 | tf_op jit(solution)/shard_map/ppermute | solution.py:705
  675.1 18.4 %collective-permute-start.51 = (bf16[256,1024]{1,0:T(8,128)(2,1)}, bf16[256,1024]{1,0:T(8,128)(2,1)}, u32[]{:S(2)}, u32[]{:S(2)}) collective-permute-start(bf16[256,1024]{1,0:T(8,128)(2,1)} %get-tuple-element.341), channel_id=1, source_target_pairs={{0,2},{1,3},{2,0},{3,1},{4,6},{5,7},{6,4},{7,5},{8,10},{9,11},{10,... | collective-permute-start | bytes 1572872 | tf_op jit(solution)/shard_map/ppermute | solution.py:705
  683.9 47.1 %collective-permute-start.48 = (bf16[256,1024]{1,0:T(8,128)(2,1)}, bf16[256,1024]{1,0:T(8,128)(2,1)}, u32[]{:S(2)}, u32[]{:S(2)}) collective-permute-start(bf16[256,1024]{1,0:T(8,128)(2,1)} %slice.285), channel_id=1, source_target_pairs={{0,1},{1,0},{2,3},{3,2},{4,5},{5,4},{6,7},{7,6},{8,9},{9,8},{10,11... | collective-permute-start | bytes 1572872 | tf_op jit(solution)/shard_map/ppermute | solution.py:705
  690.9 31.1 %collective-permute-start.49 = (bf16[256,1024]{1,0:T(8,128)(2,1)S(1)}, bf16[256,1024]{1,0:T(8,128)(2,1)S(1)}, u32[]{:S(2)}, u32[]{:S(2)}) collective-permute-start(bf16[256,1024]{1,0:T(8,128)(2,1)S(1)} %copy-done.53), channel_id=1, source_target_pairs={{0,1},{1,0},{2,3},{3,2},{4,5},{5,4},{6,7},{7,6},{8,9},{9,8},{10,11... | collective-permute-start | bytes 1572872 | tf_op jit(solution)/shard_map/ppermute | solution.py:705
  693.6 31.2 %collective-permute-start.64 = (bf16[608,256]{1,0:T(8,128)(2,1)S(1)}, bf16[608,256]{1,0:T(8,128)(2,1)S(1)}, u32[]{:S(2)}, u32[]{:S(2)}) collective-permute-start(bf16[608,256]{1,0:T(8,128)(2,1)S(1)} %constant_dynamic-slice_fusion.6), channel_id=1, source_target_pairs={{0,8},{4,12},{8,0},{12,4},{1,9},{5,13},{9,1},{13,5},{2,10},{6,14},... | collective-permute-start | bytes 933896 | tf_op jit(solution)/shard_map/ppermute | solution.py:705
  722.0 21.5 %collective-permute-start.53 = (bf16[256,1024]{1,0:T(8,128)(2,1)}, bf16[256,1024]{1,0:T(8,128)(2,1)}, u32[]{:S(2)}, u32[]{:S(2)}) collective-permute-start(bf16[256,1024]{1,0:T(8,128)(2,1)} %slice.291), channel_id=1, source_target_pairs={{0,2},{1,3},{2,0},{3,1},{4,6},{5,7},{6,4},{7,5},{8,10},{9,11},{10,... | collective-permute-start | bytes 1572872 | tf_op jit(solution)/shard_map/ppermute | solution.py:705
  723.4 21.8 %collective-permute-start.52 = (bf16[256,1024]{1,0:T(8,128)(2,1)}, bf16[256,1024]{1,0:T(8,128)(2,1)}, u32[]{:S(2)}, u32[]{:S(2)}) collective-permute-start(bf16[256,1024]{1,0:T(8,128)(2,1)} %add_convert_fusion.7), channel_id=1, source_target_pairs={{0,1},{1,0},{2,3},{3,2},{4,5},{5,4},{6,7},{7,6},{8,9},{9,8},{10,11... | collective-permute-start | bytes 1572872 | tf_op jit(solution)/shard_map/ppermute | solution.py:705
  725.5 27.6 %collective-permute-start.50 = (bf16[256,1024]{1,0:T(8,128)(2,1)}, bf16[256,1024]{1,0:T(8,128)(2,1)}, u32[]{:S(2)}, u32[]{:S(2)}) collective-permute-start(bf16[256,1024]{1,0:T(8,128)(2,1)} %add_convert_fusion.8), channel_id=1, source_target_pairs={{0,2},{1,3},{2,0},{3,1},{4,6},{5,7},{6,4},{7,5},{8,10},{9,11},{10,... | collective-permute-start | bytes 1572872 | tf_op jit(solution)/shard_map/ppermute | solution.py:705
  731.0 30.3 %collective-permute-start.55 = (bf16[384,512]{1,0:T(8,128)(2,1)}, bf16[384,512]{1,0:T(8,128)(2,1)S(1)}, u32[]{:S(2)}, u32[]{:S(2)}) collective-permute-start(bf16[384,512]{1,0:T(8,128)(2,1)} %get-tuple-element.364), channel_id=1, source_target_pairs={{0,4},{4,0},{8,12},{12,8},{1,5},{5,1},{9,13},{13,9},{2,6},{6,2},{1... | collective-permute-start | bytes 1179656 | tf_op jit(solution)/shard_map/ppermute | solution.py:705
  743.5 55.7 %collective-permute-start.69 = (bf16[384,512]{1,0:T(8,128)(2,1)S(1)}, bf16[384,512]{1,0:T(8,128)(2,1)S(1)}, u32[]{:S(2)}, u32[]{:S(2)}) collective-permute-start(bf16[384,512]{1,0:T(8,128)(2,1)S(1)} %constant_dynamic-slice_fusion.4), channel_id=1, source_target_pairs={{0,4},{4,0},{8,12},{12,8},{1,5},{5,1},{9,13},{13,9},{2,6},{6,2},{1... | collective-permute-start | bytes 1179656 | tf_op jit(solution)/shard_map/ppermute | solution.py:705
  745.3 46.5 %collective-permute-start.65 = (bf16[608,256]{1,0:T(8,128)(2,1)S(1)}, bf16[608,256]{1,0:T(8,128)(2,1)S(1)}, u32[]{:S(2)}, u32[]{:S(2)}) collective-permute-start(bf16[608,256]{1,0:T(8,128)(2,1)S(1)} %add_convert_fusion.13.first_ref), channel_id=1, source_target_pairs={{0,8},{4,12},{8,0},{12,4},{1,9},{5,13},{9,1},{13,5},{2,10},{6,14},... | collective-permute-start | bytes 933896 | tf_op jit(solution)/shard_map/ppermute | solution.py:705
  759.8 97.8 %collective-permute-start.79 = (bf16[592,1024]{1,0:T(8,128)(2,1)}, bf16[592,1024]{1,0:T(8,128)(2,1)}, u32[]{:S(2)}, u32[]{:S(2)}) collective-permute-start(bf16[592,1024]{1,0:T(8,128)(2,1)} %add_convert_fusion.2.first_ref), channel_id=1, source_target_pairs={{0,4},{4,0},{8,12},{12,8},{1,5},{5,1},{9,13},{13,9},{2,6},{6,2},{1... | collective-permute-start | bytes 3637256 | tf_op jit(solution)/shard_map/ppermute | solution.py:705
  763.7 32.1 %collective-permute-start.73 = (bf16[384,256]{1,0:T(8,128)(2,1)S(1)}, bf16[384,256]{1,0:T(8,128)(2,1)S(1)}, u32[]{:S(2)}, u32[]{:S(2)}) collective-permute-start(bf16[384,256]{1,0:T(8,128)(2,1)S(1)} %constant_dynamic-slice_fusion.1), channel_id=1, source_target_pairs={{0,8},{4,12},{8,0},{12,4},{1,9},{5,13},{9,1},{13,5},{2,10},{6,14},... | collective-permute-start | bytes 589832 | tf_op jit(solution)/shard_map/ppermute | solution.py:705
  771.2 20.6 %collective-permute-start.61 = (f32[4128]{0:T(1024)S(1)}, f32[4128]{0:T(1024)S(1)}, u32[]{:S(2)}, u32[]{:S(2)}) collective-permute-start(f32[4128]{0:T(1024)S(1)} %add.282), channel_id=1, source_target_pairs={{0,4},{4,0},{8,12},{12,8},{1,5},{5,1},{9,13},{13,9},{2,6},{6,2},{1... | collective-permute-start | bytes 49544 | tf_op jit(solution)/shard_map/ppermute | solution.py:705
  791.8 92.0 %collective-permute-start.56 = (bf16[512,1024]{1,0:T(8,128)(2,1)}, bf16[512,1024]{1,0:T(8,128)(2,1)}, u32[]{:S(2)}, u32[]{:S(2)}) collective-permute-start(bf16[512,1024]{1,0:T(8,128)(2,1)} %get-tuple-element.305), channel_id=1, source_target_pairs={{0,16},{16,0},{1,17},{17,1},{2,18},{18,2},{3,19},{19,3},{4,20},{20... | collective-permute-start | bytes 3145736 | tf_op jit(solution)/shard_map/ppermute | solution.py:701
  794.6 47.9 %collective-permute-start.66 = (bf16[608,512]{1,0:T(8,128)(2,1)}, bf16[608,512]{1,0:T(8,128)(2,1)}, u32[]{:S(2)}, u32[]{:S(2)}) collective-permute-start(bf16[608,512]{1,0:T(8,128)(2,1)} %place_two.8.first_ref), channel_id=1, source_target_pairs={{0,4},{4,0},{8,12},{12,8},{1,5},{5,1},{9,13},{13,9},{2,6},{6,2},{1... | collective-permute-start | bytes 1867784 | tf_op jit(solution)/shard_map/ppermute | solution.py:705
  795.9 18.7 %collective-permute-start.74 = (bf16[384,256]{1,0:T(8,128)(2,1)S(1)}, bf16[384,256]{1,0:T(8,128)(2,1)}, u32[]{:S(2)}, u32[]{:S(2)}) collective-permute-start(bf16[384,256]{1,0:T(8,128)(2,1)S(1)} %add_convert_fusion.14.first_ref), channel_id=1, source_target_pairs={{0,8},{4,12},{8,0},{12,4},{1,9},{5,13},{9,1},{13,5},{2,10},{6,14},... | collective-permute-start | bytes 589832 | tf_op jit(solution)/shard_map/ppermute | solution.py:705
  799.3 46.3 %collective-permute-start.77 = (bf16[288,1024]{1,0:T(8,128)(2,1)}, bf16[288,1024]{1,0:T(8,128)(2,1)S(1)}, u32[]{:S(2)}, u32[]{:S(2)}) collective-permute-start(bf16[288,1024]{1,0:T(8,128)(2,1)} %reduce-scatter.8.cloned.1.call-done), channel_id=1, source_target_pairs={{0,8},{4,12},{8,0},{12,4},{1,9},{5,13},{9,1},{13,5},{2,10},{6,14},... | collective-permute-start | bytes 1769480 | tf_op jit(solution)/shard_map/ppermute | solution.py:705
  814.6 27.9 %collective-permute-start.70 = (bf16[384,256]{1,0:T(8,128)(2,1)S(1)}, bf16[384,256]{1,0:T(8,128)(2,1)S(1)}, u32[]{:S(2)}, u32[]{:S(2)}) collective-permute-start(bf16[384,256]{1,0:T(8,128)(2,1)S(1)} %get-tuple-element.366), channel_id=1, source_target_pairs={{0,8},{4,12},{8,0},{12,4},{1,9},{5,13},{9,1},{13,5},{2,10},{6,14},... | collective-permute-start | bytes 589832 | tf_op jit(solution)/shard_map/ppermute | solution.py:705
  842.5 30.0 %collective-permute-start.62 = (f32[4128]{0:T(1024)S(1)}, f32[4128]{0:T(1024)S(1)}, u32[]{:S(2)}, u32[]{:S(2)}) collective-permute-start(f32[4128]{0:T(1024)S(1)} %add.283), channel_id=1, source_target_pairs={{0,8},{4,12},{8,0},{12,4},{1,9},{5,13},{9,1},{13,5},{2,10},{6,14},... | collective-permute-start | bytes 49544 | tf_op jit(solution)/shard_map/ppermute | solution.py:705
  842.6 12.3 %collective-permute-start.71 = (bf16[384,256]{1,0:T(8,128)(2,1)S(1)}, bf16[384,256]{1,0:T(8,128)(2,1)S(1)}, u32[]{:S(2)}, u32[]{:S(2)}) collective-permute-start(bf16[384,256]{1,0:T(8,128)(2,1)S(1)} %add_convert_fusion.15.first_ref), channel_id=1, source_target_pairs={{0,8},{4,12},{8,0},{12,4},{1,9},{5,13},{9,1},{13,5},{2,10},{6,14},... | collective-permute-start | bytes 589832 | tf_op jit(solution)/shard_map/ppermute | solution.py:705
  845.8 18.0 %collective-permute-start.78 = (bf16[288,1024]{1,0:T(8,128)(2,1)S(1)}, bf16[288,1024]{1,0:T(8,128)(2,1)S(1)}, u32[]{:S(2)}, u32[]{:S(2)}) collective-permute-start(bf16[288,1024]{1,0:T(8,128)(2,1)S(1)} %add_convert_fusion.6.first_ref), channel_id=1, source_target_pairs={{0,4},{4,0},{8,12},{12,8},{1,5},{5,1},{9,13},{13,9},{2,6},{6,2},{1... | collective-permute-start | bytes 1769480 | tf_op jit(solution)/shard_map/ppermute | solution.py:705
  854.9 18.3 %collective-permute-start.75 = (bf16[384,512]{1,0:T(8,128)(2,1)S(1)}, bf16[384,512]{1,0:T(8,128)(2,1)S(1)}, u32[]{:S(2)}, u32[]{:S(2)}) collective-permute-start(bf16[384,512]{1,0:T(8,128)(2,1)S(1)} %copy-done.97), channel_id=1, source_target_pairs={{0,4},{4,0},{8,12},{12,8},{1,5},{5,1},{9,13},{13,9},{2,6},{6,2},{1... | collective-permute-start | bytes 1179656 | tf_op jit(solution)/shard_map/ppermute | solution.py:705
  857.6 22.6 %collective-permute-start.72 = (bf16[384,512]{1,0:T(8,128)(2,1)}, bf16[384,512]{1,0:T(8,128)(2,1)}, u32[]{:S(2)}, u32[]{:S(2)}) collective-permute-start(bf16[384,512]{1,0:T(8,128)(2,1)} %place_two.9.first_ref), channel_id=1, source_target_pairs={{0,4},{4,0},{8,12},{12,8},{1,5},{5,1},{9,13},{13,9},{2,6},{6,2},{1... | collective-permute-start | bytes 1179656 | tf_op jit(solution)/shard_map/ppermute | solution.py:705
  871.0 24.4 %collective-permute-start.80 = (bf16[1184,1024]{1,0:T(8,128)(2,1)}, bf16[1184,1024]{1,0:T(8,128)(2,1)}, u32[]{:S(2)}, u32[]{:S(2)}) collective-permute-start(bf16[1184,1024]{1,0:T(8,128)(2,1)} %broadcast_select_fusion.2), channel_id=1, source_target_pairs={{0,16},{16,0},{1,17},{17,1},{2,18},{18,2},{3,19},{19,3},{4,20},{20... | collective-permute-start | bytes 7274504 | tf_op jit(solution)/shard_map/ppermute | solution.py:701
  (153 other events, 1039.3 us)
Sparse Core Ops, SparseCore 0:
  21.8 122.9 all-gather.4
  147.2 134.2 all-gather.6
  523.7 59.2 reduce-scatter.3
  585.9 59.9 reduce-scatter.5
  683.1 56.9 reduce-scatter.7

commit v5 on v4

--- a/solution.py
+++ b/solution.py
@@ -1062,14 +1062,6 @@
         (chains, chains + [grads_second[1]], [], chains + [grads_second[1]]),
     )
 
-    large, small = grads_first[0][0], grads_first[1]
-    while len(large.steps) > 1:
-        large.state = large.steps.pop(0)(large.state)
-    if large.steps:
-        large.state = large.steps.pop(0)(large.state)
-        small.state = small.steps.pop(0)(small.state)
-        large.state, small.state = lax.optimization_barrier((large.state, small.state))
-
     def ended(chains):
         return jnp.concatenate([chain.end() for chain in chains], axis=0)
 

time: 925 us -> 916 us (level)
  Pallas kernels: 284 us -> 318 us
  waiting for transfers between devices: 351 us -> 326 us
  starting transfers between devices: 86.7 us -> 72.4 us
    pallas_call x2, Pallas kernels: 52.3 us -> 74.7 us  [attend_back(): pl.pallas_call(functools.partial(attend_back_kernel, second, block, min(2...]
    pallas_call x2, Pallas kernels: 27.3 us -> 40.2 us  [attend(): pl.pallas_call(functools.partial(attend_kernel, block, group, parts), gri...]
    reduce_scatter x3, waiting for transfers between devices: 18.8 us -> 7.72 us  [scatter_parts(): return lax.psum_scatter(rows, 'mp', scatter_dimension=0, tiled=True)]
    ppermute x55, starting transfers between devices: 75.4 us -> 65.7 us  [across(): lax.ppermute(value, axis, [(i, i ^ bits) for i in range(lax.axis_size(axi...]
    unnamed x266 -> x264, local copies, waits for them, and re-layouts: 21.2 us -> 20.6 us
  transfers between devices with their start and end apart: 86 -> 86, of which waited for: 38 -> 39; matrix products, arithmetic and copies ran while one was open for 13% -> 13% of each run, Pallas kernels for 29% -> 33%
where the time goes in v5:
time: 916 us; the launch traced here: 905 us
  waiting for transfers between devices  326 us (36%)
  Pallas kernels  318 us (35%)
  other arithmetic  98.7 us (11%)
  starting transfers between devices  72.4 us (8%)
  local copies, waits for them, and re-layouts  50.3 us (5%)
  matrix products  21 us (2%)
  between operations  17.8 us (2%)
    ppermute x55, waiting for transfers between devices, across(): lax.ppermute(value, axis, [(i, i ^ bits) for i in range(lax.axis_size(axi...  278 us
    pallas_call x2, Pallas kernels, attend_back(): pl.pallas_call(functools.partial(attend_back_kernel, second, block, min(2...  74.7 us
    ppermute x55, starting transfers between devices, across(): lax.ppermute(value, axis, [(i, i ^ bits) for i in range(lax.axis_size(axi...  65.7 us
    pallas_call x4, Pallas kernels, ffn_backward(): pl.pallas_call(functools.partial(ffn_back_kernel, more), grid=(1,), in_sp...  45.5 us
    pallas_call x4, Pallas kernels, ffn_forward(): pl.pallas_call(ffn_kernel, grid=(1,), in_specs=[whole, whole, pl.BlockSpe...  45 us
    pallas_call x2, Pallas kernels, attend(): pl.pallas_call(functools.partial(attend_kernel, block, group, parts), gri...  40.2 us
    pallas_call x2, Pallas kernels, pack_grads(): pl.pallas_call(functools.partial(pack_grads_kernel, size, plain, halves),...  34.3 us
    pallas_call x8, Pallas kernels, project_qkv(): pl.pallas_call(functools.partial(qkv_kernel, second, group, parts, fresh)...  32.5 us
  transfers between devices with their start and end apart: 86, of which 39 were waited for; matrix products, arithmetic and copies ran while one was open for 13% of the time, Pallas kernels for 33%

profile of v5, /device:TPU:0, one launch (start us, length us, event | category | flops | bytes accessed | tf_op | source)
XLA Modules:
  0.0 904.7 jit_solution(18275367338947305494)
XLA Ops:
  14.6 4.6 collective-permute-done.6
  31.1 3.7 fusion.46
  34.8 3.0 pad_maximum_fusion.6
  37.9 29.3 %collective-permute-done.1.refs_0_.refs_2_ = bf16[512,1024]{1,0:T(8,128)(2,1)} collective-permute-done((bf16[512,1024]{1,0:T(8,128)(2,1)}, bf16[512,1024]{1,0:T(8,128)(2,1)}, u32[]{:S(2)}, u32[]{:S(2)}) %collective-permute-start.1) | collective-permute-done | bytes 1048608 | tf_op jit(solution)/shard_map/ppermute | solution.py:705
  72.0 3.7 broadcast_select_fusion.4
  75.7 3.8 qkv_rope.8
  79.5 3.8 qkv_rope.9
  83.3 3.8 qkv_rope.10
  89.4 5.1 qkv_rope.11
  94.5 19.9 %attend.2 = (bf16[512,256]{1,0:T(8,128)(2,1)}, bf16[512,256]{1,0:T(8,128)(2,1)}, bf16[512,256]{1,0:T(8,128)(2,1)}, bf16[512,256]{1,0:T(8,128)(2,1)}, f32[4,2048]{1,0:T(4,128)}) custom-call(s32[3]{0:T(128)} %pad_add_fusion.info_ref, bf16[2048,256]{1,0:T(8,128)(2,1)} %get-tuple-element.161.q_ref, bf16[2048,256]{1,0:T(8,128)(2,1)} %get-tuple-element.162.k_ref, ...), custom_call_target="tpu_custom_call" | custom-call | flops 20700000256 | bytes 1048576 | tf_op jit(solution)/shard_map/attend/pallas_call | solution.py:205
  114.4 30.4 %all-gather.5.cloned.1.call-done = bf16[4736,1024]{1,0:T(8,128)(2,1)} async-done(((bf16[1184,1024]{1,0:T(8,128)(2,1)}), bf16[4736,1024]{1,0:T(8,128)(2,1)}) %all-gather.5.cloned.1.call-update) | async-done | bytes 9699344 | tf_op jit(solution)/shard_map/all_gather | solution.py:917
  150.7 6.6 collective-permute-done.10.refs_3_
  157.3 8.2 collective-permute-done.8.refs_1_
  166.6 6.5 out_project.2
  173.1 11.1 %ffn.4 = (f32[512,1024]{1,0:T(8,128)}, bf16[512,1408]{1,0:T(8,128)(2,1)}, bf16[512,1408]{1,0:T(8,128)(2,1)}, bf16[512,1408]{1,0:T(8,128)(2,1)}) custom-call(bf16[512,1024]{1,0:T(8,128)(2,1)} %get-tuple-element.177.x_ref.refs_6_, f32[512,1024]{1,0:T(8,128)} %get-tuple-element.178.base_ref, bf16[4,1184,1024]{2,1,0:T(8,128)(2,1)} %bitcast.121), custom_call_target="tpu_custom_call" | custom-call | flops 10350000128 | bytes 1048576 | tf_op jit(solution)/shard_map/ffn/pallas_call | solution.py:478
  184.3 11.5 %ffn.5 = (f32[512,1024]{1,0:T(8,128)}, bf16[512,1408]{1,0:T(8,128)(2,1)}, bf16[512,1408]{1,0:T(8,128)(2,1)}, bf16[512,1408]{1,0:T(8,128)(2,1)}) custom-call(bf16[512,1024]{1,0:T(8,128)(2,1)} %get-tuple-element.177.x_ref.refs_6_, f32[512,1024]{1,0:T(8,128)} %get-tuple-element.179.base_ref, bf16[4,1184,1024]{2,1,0:T(8,128)(2,1)} %collective-permute-done.11.pieces_ref.refs_4_), custom_call_target="tpu_custom_call" | custom-call | flops 10350000128 | bytes 1048576 | tf_op jit(solution)/shard_map/ffn/pallas_call | solution.py:478
  201.0 4.1 qkv_rope.12
  205.0 41.7 %collective-permute-done.12.refs_0_.refs_2_ = bf16[512,1024]{1,0:T(8,128)(2,1)S(1)} collective-permute-done((bf16[512,1024]{1,0:T(8,128)(2,1)S(1)}, bf16[512,1024]{1,0:T(8,128)(2,1)S(1)}, u32[]{:S(2)}, u32[]{:S(2)}) %collective-permute-start.12) | collective-permute-done | bytes 1048608 | tf_op jit(solution)/shard_map/ppermute | solution.py:705
  249.1 3.9 qkv_rope.13
  253.0 3.9 qkv_rope.14
  256.9 15.3 %collective-permute-done.13.refs_0_.refs_3_ = bf16[256,1024]{1,0:T(8,128)(2,1)S(1)} collective-permute-done((bf16[256,1024]{1,0:T(8,128)(2,1)S(1)}, bf16[256,1024]{1,0:T(8,128)(2,1)S(1)}, u32[]{:S(2)}, u32[]{:S(2)}) %collective-permute-start.13) | collective-permute-done | bytes 524320 | tf_op jit(solution)/shard_map/ppermute | solution.py:705
  274.3 4.2 qkv_rope.15
  278.5 20.3 %attend.3 = (bf16[512,256]{1,0:T(8,128)(2,1)}, bf16[512,256]{1,0:T(8,128)(2,1)}, bf16[512,256]{1,0:T(8,128)(2,1)}, bf16[512,256]{1,0:T(8,128)(2,1)}, f32[4,2048]{1,0:T(4,128)}) custom-call(s32[3]{0:T(128)} %pad_add_fusion.info_ref, bf16[2048,256]{1,0:T(8,128)(2,1)} %get-tuple-element.190.q_ref, bf16[2048,256]{1,0:T(8,128)(2,1)} %get-tuple-element.191.k_ref, ...), custom_call_target="tpu_custom_call" | custom-call | flops 20700000256 | bytes 1048576 | tf_op jit(solution)/shard_map/attend/pallas_call | solution.py:205
  310.0 5.2 collective-permute-done.18.refs_2_
  316.5 6.5 out_project.3
  323.0 11.1 %ffn.6 = (f32[512,1024]{1,0:T(8,128)}, bf16[512,1408]{1,0:T(8,128)(2,1)}, bf16[512,1408]{1,0:T(8,128)(2,1)}, bf16[512,1408]{1,0:T(8,128)(2,1)}) custom-call(bf16[512,1024]{1,0:T(8,128)(2,1)} %get-tuple-element.202.x_ref.refs_6_, f32[512,1024]{1,0:T(8,128)} %get-tuple-element.203.base_ref, bf16[4,1184,1024]{2,1,0:T(8,128)(2,1)} %bitcast.125), custom_call_target="tpu_custom_call" | custom-call | flops 10350000128 | bytes 1048576 | tf_op jit(solution)/shard_map/ffn/pallas_call | solution.py:478
  334.1 11.2 %ffn_back.4 = (f32[512,1024]{1,0:T(8,128)}, bf16[512,1408]{1,0:T(8,128)(2,1)}, bf16[512,1408]{1,0:T(8,128)(2,1)}) custom-call(bf16[512,1024]{1,0:T(8,128)(2,1)} %bitcast_convert_fusion.refs_0_.refs_1_.refs_8_, bf16[512,1408]{1,0:T(8,128)(2,1)} %get-tuple-element.206.refs_1_, bf16[512,1408]{1,0:T(8,128)(2,1)} %get-tuple-element.207.refs_2_, ...), custom_call_target="tpu_custom_call" | custom-call | flops 1150000000 | bytes 1048576 | tf_op jit(solution)/shard_map/ffn_back/pallas_call | solution.py:527
  345.5 11.3 %ffn.7 = (f32[512,1024]{1,0:T(8,128)}, bf16[512,1408]{1,0:T(8,128)(2,1)}, bf16[512,1408]{1,0:T(8,128)(2,1)}, bf16[512,1408]{1,0:T(8,128)(2,1)}) custom-call(bf16[512,1024]{1,0:T(8,128)(2,1)} %get-tuple-element.202.x_ref.refs_6_, f32[512,1024]{1,0:T(8,128)} %get-tuple-element.204.base_ref, bf16[4,1184,1024]{2,1,0:T(8,128)(2,1)} %collective-permute-done.20.pieces_ref.refs_4_), custom_call_target="tpu_custom_call" | custom-call | flops 10350000128 | bytes 1048576 | tf_op jit(solution)/shard_map/ffn/pallas_call | solution.py:478
  356.8 11.6 %ffn_back.5 = (f32[512,1024]{1,0:T(8,128)}, bf16[512,1408]{1,0:T(8,128)(2,1)}, bf16[512,1408]{1,0:T(8,128)(2,1)}) custom-call(f32[512,1024]{1,0:T(8,128)} %get-tuple-element.208.refs_0_, bf16[512,1024]{1,0:T(8,128)(2,1)} %bitcast_convert_fusion.refs_0_.refs_1_.refs_8_, bf16[512,1408]{1,0:T(8,128)(2,1)} %get-tuple-element.209.refs_2_, ...), custom_call_target="tpu_custom_call" | custom-call | flops 1150000000 | bytes 1048576 | tf_op jit(solution)/shard_map/ffn_back/pallas_call | solution.py:527
  377.9 3.0 convolution_convert_fusion.11
  384.7 3.8 collective-permute-done.23.refs_3_
  394.4 16.9 %pack_grads.2 = (bf16[4,592,1024]{2,1,0:T(8,128)(2,1)}, bf16[4,592,1024]{2,1,0:T(8,128)(2,1)}) custom-call(s32[1]{0:T(128)} %bitcast.31.info_ref.which_ref, bf16[512,1408]{1,0:T(8,128)(2,1)} %get-tuple-element.217.refs_0_, bf16[512,1408]{1,0:T(8,128)(2,1)} %copy-done.80, bf16[512,1408]{1,0:T(8,128)(2,1)} %get-tuple-element.219.refs_2_, ...), custom_call_target="tpu_custom_call" | custom-call | flops 17250000896 | bytes 1048576 | tf_op jit(solution)/shard_map/pack_grads/pallas_call | solution.py:587
  412.7 37.0 %attend_back.2 = (bf16[512,768]{1,0:T(8,128)(2,1)}, bf16[512,768]{1,0:T(8,128)(2,1)}, bf16[512,768]{1,0:T(8,128)(2,1)}, bf16[512,768]{1,0:T(8,128)(2,1)}) custom-call(s32[3]{0:T(128)} %pad_add_fusion.info_ref, bf16[2048,256]{1,0:T(8,128)(2,1)} %get-tuple-element.190.q_ref, bf16[2048,256]{1,0:T(8,128)(2,1)} %get-tuple-element.191.k_ref, ...), custom_call_target="tpu_custom_call" | custom-call | flops 41400000512 | bytes 1048576 | tf_op jit(solution)/shard_map/attend_back/pallas_call | solution.py:362
  458.7 4.7 collective-permute-done.34
  464.9 7.7 collective-permute-done.32
  475.2 3.0 collective-permute-done.35
  478.3 3.8 collective-permute-done.33
  485.8 10.9 %ffn_back.6 = (f32[512,1024]{1,0:T(8,128)}, bf16[512,1408]{1,0:T(8,128)(2,1)}, bf16[512,1408]{1,0:T(8,128)(2,1)}) custom-call(bf16[512,1024]{1,0:T(8,128)(2,1)} %get-tuple-element.299.refs_0_.refs_1_.refs_8_, bf16[512,1408]{1,0:T(8,128)(2,1)} %get-tuple-element.233.refs_1_, bf16[512,1408]{1,0:T(8,128)(2,1)} %get-tuple-element.234.refs_2_, ...), custom_call_target="tpu_custom_call" | custom-call | flops 1150000000 | bytes 1048576 | tf_op jit(solution)/shard_map/ffn_back/pallas_call | solution.py:527
  496.8 11.8 %ffn_back.7 = (f32[512,1024]{1,0:T(8,128)}, bf16[512,1408]{1,0:T(8,128)(2,1)}, bf16[512,1408]{1,0:T(8,128)(2,1)}) custom-call(f32[512,1024]{1,0:T(8,128)} %get-tuple-element.235.refs_0_, bf16[512,1024]{1,0:T(8,128)(2,1)} %get-tuple-element.299.refs_0_.refs_1_.refs_8_, bf16[512,1408]{1,0:T(8,128)(2,1)} %get-tuple-element.236.refs_2_, ...), custom_call_target="tpu_custom_call" | custom-call | flops 1150000000 | bytes 1048576 | tf_op jit(solution)/shard_map/ffn_back/pallas_call | solution.py:527
  508.6 9.0 collective-permute-done.37
  517.6 8.6 add_convert_fusion
  543.3 17.3 %pack_grads.3 = (bf16[4,608,1024]{2,1,0:T(8,128)(2,1)}, bf16[4,288,1024]{2,1,0:T(8,128)(2,1)}, bf16[4,288,1024]{2,1,0:T(8,128)(2,1)}) custom-call(s32[1]{0:T(128)} %bitcast.31.info_ref.which_ref, bf16[512,1408]{1,0:T(8,128)(2,1)} %get-tuple-element.261.refs_0_, bf16[512,1408]{1,0:T(8,128)(2,1)} %copy-done.78, bf16[512,1408]{1,0:T(8,128)(2,1)} %get-tuple-element.263.refs_2_, ...), custom_call_target="tpu_custom_call" | custom-call | flops 17250000896 | bytes 1048576 | tf_op jit(solution)/shard_map/pack_grads/pallas_call | solution.py:587
  567.3 7.4 qkv_grad.2
  590.8 5.6 collective-permute-done.41.refs_6_
  600.0 37.7 %attend_back.3 = (bf16[512,768]{1,0:T(8,128)(2,1)}, bf16[512,768]{1,0:T(8,128)(2,1)}, bf16[512,768]{1,0:T(8,128)(2,1)}, bf16[512,768]{1,0:T(8,128)(2,1)}) custom-call(s32[3]{0:T(128)} %pad_add_fusion.info_ref, bf16[2048,256]{1,0:T(8,128)(2,1)} %get-tuple-element.161.q_ref, bf16[2048,256]{1,0:T(8,128)(2,1)} %get-tuple-element.162.k_ref, ...), custom_call_target="tpu_custom_call" | custom-call | flops 41400000512 | bytes 1048576 | tf_op jit(solution)/shard_map/attend_back/pallas_call | solution.py:362
  638.8 7.7 reduce-scatter.6.cloned.1.call-done
  654.6 12.4 %collective-permute-done.63 = bf16[4,288,1024]{2,1,0:T(8,128)(2,1)} collective-permute-done((bf16[4,288,1024]{2,1,0:T(8,128)(2,1)}, bf16[4,288,1024]{2,1,0:T(8,128)(2,1)}, u32[]{:S(2)}, u32[]{:S(2)}) %collective-permute-start.63) | collective-permute-done | bytes 2359328 | tf_op jit(solution)/shard_map/ppermute | solution.py:705
  667.0 4.2 add_convert_fusion.1
  677.0 7.8 qkv_grad.3
  692.8 17.2 %collective-permute-done.49 = bf16[256,1024]{1,0:T(8,128)(2,1)S(1)} collective-permute-done((bf16[256,1024]{1,0:T(8,128)(2,1)S(1)}, bf16[256,1024]{1,0:T(8,128)(2,1)S(1)}, u32[]{:S(2)}, u32[]{:S(2)}) %collective-permute-start.49) | collective-permute-done | bytes 524320 | tf_op jit(solution)/shard_map/ppermute | solution.py:705
  719.6 11.2 %collective-permute-done.53 = bf16[256,1024]{1,0:T(8,128)(2,1)} collective-permute-done((bf16[256,1024]{1,0:T(8,128)(2,1)}, bf16[256,1024]{1,0:T(8,128)(2,1)}, u32[]{:S(2)}, u32[]{:S(2)}) %collective-permute-start.53) | collective-permute-done | bytes 524320 | tf_op jit(solution)/shard_map/ppermute | solution.py:705
  733.4 3.7 collective-permute-done.50
  750.0 3.5 collective-permute-done.60
  757.9 14.7 %collective-permute-done.61 = f32[4128]{0:T(1024)S(1)} collective-permute-done((f32[4128]{0:T(1024)S(1)}, f32[4128]{0:T(1024)S(1)}, u32[]{:S(2)}, u32[]{:S(2)}) %collective-permute-start.61) | collective-permute-done | bytes 16544 | tf_op jit(solution)/shard_map/ppermute | solution.py:705
  778.5 20.4 %collective-permute-done.66 = bf16[384,256]{1,0:T(8,128)(2,1)S(1)} collective-permute-done((bf16[384,256]{1,0:T(8,128)(2,1)S(1)}, bf16[384,256]{1,0:T(8,128)(2,1)S(1)}, u32[]{:S(2)}, u32[]{:S(2)}) %collective-permute-start.66) | collective-permute-done | bytes 196640 | tf_op jit(solution)/shard_map/ppermute | solution.py:705
  799.0 20.5 %collective-permute-done.70.second_ref = bf16[384,256]{1,0:T(8,128)(2,1)S(1)} collective-permute-done((bf16[384,256]{1,0:T(8,128)(2,1)S(1)}, bf16[384,256]{1,0:T(8,128)(2,1)S(1)}, u32[]{:S(2)}, u32[]{:S(2)}) %collective-permute-start.70) | collective-permute-done | bytes 196640 | tf_op jit(solution)/shard_map/ppermute | solution.py:705
  824.1 13.2 %collective-permute-done.67.second_ref = bf16[384,256]{1,0:T(8,128)(2,1)S(1)} collective-permute-done((bf16[384,256]{1,0:T(8,128)(2,1)S(1)}, bf16[384,256]{1,0:T(8,128)(2,1)S(1)}, u32[]{:S(2)}, u32[]{:S(2)}) %collective-permute-start.67) | collective-permute-done | bytes 196640 | tf_op jit(solution)/shard_map/ppermute | solution.py:705
  837.3 3.0 collective-permute-start.78
  846.5 3.2 place_two.15
  849.7 4.9 collective-permute-done.78.second_ref
  856.9 4.0 broadcast_select_fusion.2
  865.2 4.4 collective-permute-done.68.second_ref
  881.0 3.0 reshape.279
  887.5 3.1 broadcast_select_fusion.1
  (554 shorter events, 231.1 us)
Async XLA Ops:
  7.2 137.6 %all-gather.5.cloned.1.call-start = ((), (), s32[]{:S(2)}) async-start(), calls=%async_computation.6 | async-start | bytes 12124160 | tf_op jit(solution)/shard_map/all_gather | solution.py:917
  21.7 277.2 %all-gather.7.cloned.1.call-start = ((), (), s32[]{:S(2)}) async-start(), calls=%async_computation.7 | async-start | bytes 12124160 | tf_op jit(solution)/shard_map/all_gather | solution.py:917
  23.2 48.8 %collective-permute-start.5 = (bf16[1024,768]{1,0:T(8,128)(2,1)S(1)}, bf16[1024,768]{1,0:T(8,128)(2,1)}, u32[]{:S(2)}, u32[]{:S(2)}) collective-permute-start(bf16[1024,768]{1,0:T(8,128)(2,1)S(1)} %pad_maximum_fusion.5), channel_id=1, source_target_pairs={{0,16},{16,0},{1,17},{17,1},{2,18},{18,2},{3,19},{19,3},{4,20},{20... | collective-permute-start | bytes 4718600 | tf_op jit(solution)/shard_map/ppermute | solution.py:701
  23.4 45.0 %collective-permute-start.3 = (bf16[512,1024]{1,0:T(8,128)(2,1)}, bf16[512,1024]{1,0:T(8,128)(2,1)}, u32[]{:S(2)}, u32[]{:S(2)}) collective-permute-start(bf16[512,1024]{1,0:T(8,128)(2,1)} %fusion.6.refs_0_), channel_id=1, source_target_pairs={{0,1},{1,0},{2,3},{3,2},{4,5},{5,4},{6,7},{7,6},{8,9},{9,8},{10,11... | collective-permute-start | bytes 3145736 | tf_op jit(solution)/shard_map/ppermute | solution.py:705
  26.2 40.9 %collective-permute-start.1 = (bf16[512,1024]{1,0:T(8,128)(2,1)}, bf16[512,1024]{1,0:T(8,128)(2,1)}, u32[]{:S(2)}, u32[]{:S(2)}) collective-permute-start(bf16[512,1024]{1,0:T(8,128)(2,1)} %fusion.6.refs_0_), channel_id=1, source_target_pairs={{0,2},{1,3},{2,0},{3,1},{4,6},{5,7},{6,4},{7,5},{8,10},{9,11},{10,... | collective-permute-start | bytes 3145736 | tf_op jit(solution)/shard_map/ppermute | solution.py:705
  68.2 18.9 %collective-permute-start.2 = (bf16[256,1024]{1,0:T(8,128)(2,1)S(1)}, bf16[256,1024]{1,0:T(8,128)(2,1)S(1)}, u32[]{:S(2)}, u32[]{:S(2)}) collective-permute-start(bf16[256,1024]{1,0:T(8,128)(2,1)S(1)} %slice.257), channel_id=1, source_target_pairs={{0,1},{1,0},{2,3},{3,2},{4,5},{5,4},{6,7},{7,6},{8,9},{9,8},{10,11... | collective-permute-start | bytes 1572872 | tf_op jit(solution)/shard_map/ppermute | solution.py:705
  69.4 19.2 %collective-permute-start.4 = (bf16[256,1024]{1,0:T(8,128)(2,1)S(1)}, bf16[256,1024]{1,0:T(8,128)(2,1)S(1)}, u32[]{:S(2)}, u32[]{:S(2)}) collective-permute-start(bf16[256,1024]{1,0:T(8,128)(2,1)S(1)} %slice.258), channel_id=1, source_target_pairs={{0,2},{1,3},{2,0},{3,1},{4,6},{5,7},{6,4},{7,5},{8,10},{9,11},{10,... | collective-permute-start | bytes 1572872 | tf_op jit(solution)/shard_map/ppermute | solution.py:705
  144.8 39.5 %collective-permute-start.11 = (bf16[4,1184,1024]{2,1,0:T(8,128)(2,1)}, bf16[4,1184,1024]{2,1,0:T(8,128)(2,1)}, u32[]{:S(2)}, u32[]{:S(2)}) collective-permute-start(bf16[4,1184,1024]{2,1,0:T(8,128)(2,1)} %bitcast.119), channel_id=1, source_target_pairs={{0,16},{16,0},{1,17},{17,1},{2,18},{18,2},{3,19},{19,3},{4,20},{20... | collective-permute-start | bytes 29097992 | tf_op jit(solution)/shard_map/ppermute | solution.py:701
  144.8 453.1 %reduce-scatter.4.cloned.1.call-start = ((), (), s32[]{:S(2)}) async-start(), calls=%async_computation.3 | async-start | bytes 6062080 | tf_op jit(solution)/shard_map/reduce_scatter | solution.py:785
  146.6 18.9 %collective-permute-start.7 = (bf16[4,128,1024]{2,1,0:T(8,128)(2,1)S(1)}, bf16[4,128,1024]{2,1,0:T(8,128)(2,1)S(1)}, u32[]{:S(2)}, u32[]{:S(2)}) collective-permute-start(bf16[4,128,1024]{2,1,0:T(8,128)(2,1)S(1)} %slice.199.own_ref), channel_id=1, source_target_pairs={{0,16},{16,0},{1,17},{17,1},{2,18},{18,2},{3,19},{19,3},{4,20},{20... | collective-permute-start | bytes 3145736 | tf_op jit(solution)/shard_map/ppermute | solution.py:701
  148.6 16.8 %collective-permute-start.8 = (bf16[512,256]{1,0:T(8,128)(2,1)S(1)}, bf16[512,256]{1,0:T(8,128)(2,1)S(1)}, u32[]{:S(2)}, u32[]{:S(2)}) collective-permute-start(bf16[512,256]{1,0:T(8,128)(2,1)S(1)} %copy-done.98), channel_id=1, source_target_pairs={{0,1},{1,0},{2,3},{3,2},{4,5},{5,4},{6,7},{7,6},{8,9},{9,8},{10,11... | collective-permute-start | bytes 786440 | tf_op jit(solution)/shard_map/ppermute | solution.py:705
  150.1 15.4 %collective-permute-start.9 = (bf16[512,256]{1,0:T(8,128)(2,1)S(1)}, bf16[512,256]{1,0:T(8,128)(2,1)S(1)}, u32[]{:S(2)}, u32[]{:S(2)}) collective-permute-start(bf16[512,256]{1,0:T(8,128)(2,1)S(1)} %copy-done.99), channel_id=1, source_target_pairs={{0,2},{1,3},{2,0},{3,1},{4,6},{5,7},{6,4},{7,5},{8,10},{9,11},{10,... | collective-permute-start | bytes 786440 | tf_op jit(solution)/shard_map/ppermute | solution.py:705
  198.8 48.0 %collective-permute-start.12 = (bf16[512,1024]{1,0:T(8,128)(2,1)S(1)}, bf16[512,1024]{1,0:T(8,128)(2,1)S(1)}, u32[]{:S(2)}, u32[]{:S(2)}) collective-permute-start(bf16[512,1024]{1,0:T(8,128)(2,1)S(1)} %fusion.4.refs_0_), channel_id=1, source_target_pairs={{0,2},{1,3},{2,0},{3,1},{4,6},{5,7},{6,4},{7,5},{8,10},{9,11},{10,... | collective-permute-start | bytes 3145736 | tf_op jit(solution)/shard_map/ppermute | solution.py:705
  200.1 48.0 %collective-permute-start.14 = (bf16[512,1024]{1,0:T(8,128)(2,1)S(1)}, bf16[512,1024]{1,0:T(8,128)(2,1)S(1)}, u32[]{:S(2)}, u32[]{:S(2)}) collective-permute-start(bf16[512,1024]{1,0:T(8,128)(2,1)S(1)} %fusion.4.refs_0_), channel_id=1, source_target_pairs={{0,1},{1,0},{2,3},{3,2},{4,5},{5,4},{6,7},{7,6},{8,9},{9,8},{10,11... | collective-permute-start | bytes 3145736 | tf_op jit(solution)/shard_map/ppermute | solution.py:705
  246.8 25.3 %collective-permute-start.13 = (bf16[256,1024]{1,0:T(8,128)(2,1)S(1)}, bf16[256,1024]{1,0:T(8,128)(2,1)S(1)}, u32[]{:S(2)}, u32[]{:S(2)}) collective-permute-start(bf16[256,1024]{1,0:T(8,128)(2,1)S(1)} %slice.261), channel_id=1, source_target_pairs={{0,1},{1,0},{2,3},{3,2},{4,5},{5,4},{6,7},{7,6},{8,9},{9,8},{10,11... | collective-permute-start | bytes 1572872 | tf_op jit(solution)/shard_map/ppermute | solution.py:705
  248.2 25.4 %collective-permute-start.15 = (bf16[256,1024]{1,0:T(8,128)(2,1)S(1)}, bf16[256,1024]{1,0:T(8,128)(2,1)S(1)}, u32[]{:S(2)}, u32[]{:S(2)}) collective-permute-start(bf16[256,1024]{1,0:T(8,128)(2,1)S(1)} %slice.262), channel_id=1, source_target_pairs={{0,2},{1,3},{2,0},{3,1},{4,6},{5,7},{6,4},{7,5},{8,10},{9,11},{10,... | collective-permute-start | bytes 1572872 | tf_op jit(solution)/shard_map/ppermute | solution.py:705
  298.9 46.6 %collective-permute-start.20 = (bf16[4,1184,1024]{2,1,0:T(8,128)(2,1)}, bf16[4,1184,1024]{2,1,0:T(8,128)(2,1)}, u32[]{:S(2)}, u32[]{:S(2)}) collective-permute-start(bf16[4,1184,1024]{2,1,0:T(8,128)(2,1)} %bitcast.123), channel_id=1, source_target_pairs={{0,16},{16,0},{1,17},{17,1},{2,18},{18,2},{3,19},{19,3},{4,20},{20... | collective-permute-start | bytes 29097992 | tf_op jit(solution)/shard_map/ppermute | solution.py:701
  300.4 15.1 %collective-permute-start.16 = (bf16[4,128,1024]{2,1,0:T(8,128)(2,1)S(1)}, bf16[4,128,1024]{2,1,0:T(8,128)(2,1)S(1)}, u32[]{:S(2)}, u32[]{:S(2)}) collective-permute-start(bf16[4,128,1024]{2,1,0:T(8,128)(2,1)S(1)} %slice.204.own_ref), channel_id=1, source_target_pairs={{0,16},{16,0},{1,17},{17,1},{2,18},{18,2},{3,19},{19,3},{4,20},{20... | collective-permute-start | bytes 3145736 | tf_op jit(solution)/shard_map/ppermute | solution.py:701
  301.6 13.6 %collective-permute-start.18 = (bf16[512,256]{1,0:T(8,128)(2,1)S(1)}, bf16[512,256]{1,0:T(8,128)(2,1)S(1)}, u32[]{:S(2)}, u32[]{:S(2)}) collective-permute-start(bf16[512,256]{1,0:T(8,128)(2,1)S(1)} %copy-done.108), channel_id=1, source_target_pairs={{0,2},{1,3},{2,0},{3,1},{4,6},{5,7},{6,4},{7,5},{8,10},{9,11},{10,... | collective-permute-start | bytes 786440 | tf_op jit(solution)/shard_map/ppermute | solution.py:705
  303.1 12.1 %collective-permute-start.19 = (bf16[512,256]{1,0:T(8,128)(2,1)S(1)}, bf16[512,256]{1,0:T(8,128)(2,1)S(1)}, u32[]{:S(2)}, u32[]{:S(2)}) collective-permute-start(bf16[512,256]{1,0:T(8,128)(2,1)S(1)} %copy-done.109), channel_id=1, source_target_pairs={{0,3},{1,2},{2,1},{3,0},{4,7},{5,6},{6,5},{7,4},{8,11},{9,10},{10,... | collective-permute-start | bytes 786440 | tf_op jit(solution)/shard_map/ppermute | solution.py:705
  376.8 14.8 %collective-permute-start.29 = (bf16[512,1024]{1,0:T(8,128)(2,1)S(1)}, bf16[512,1024]{1,0:T(8,128)(2,1)}, u32[]{:S(2)}, u32[]{:S(2)}) collective-permute-start(bf16[512,1024]{1,0:T(8,128)(2,1)S(1)} %copy-done.9), channel_id=1, source_target_pairs={{0,16},{16,0},{1,17},{17,1},{2,18},{18,2},{3,19},{19,3},{4,20},{20... | collective-permute-start | bytes 3145736 | tf_op jit(solution)/shard_map/ppermute | solution.py:701
  377.0 15.9 %collective-permute-start.28 = (bf16[512,1024]{1,0:T(8,128)(2,1)}, bf16[512,1024]{1,0:T(8,128)(2,1)S(1)}, u32[]{:S(2)}, u32[]{:S(2)}) collective-permute-start(bf16[512,1024]{1,0:T(8,128)(2,1)} %get-tuple-element.202.x_ref.refs_6_), channel_id=1, source_target_pairs={{0,16},{16,0},{1,17},{17,1},{2,18},{18,2},{3,19},{19,3},{4,20},{20... | collective-permute-start | bytes 3145736 | tf_op jit(solution)/shard_map/ppermute | solution.py:701
  380.9 12.0 %collective-permute-start.27 = (bf16[512,1408]{1,0:T(8,128)(2,1)S(1)}, bf16[512,1408]{1,0:T(8,128)(2,1)S(1)}, u32[]{:S(2)}, u32[]{:S(2)}) collective-permute-start(bf16[512,1408]{1,0:T(8,128)(2,1)S(1)} %copy-done.77), channel_id=1, source_target_pairs={{0,16},{16,0},{1,17},{17,1},{2,18},{18,2},{3,19},{19,3},{4,20},{20... | collective-permute-start | bytes 4325384 | tf_op jit(solution)/shard_map/ppermute | solution.py:701
  389.4 21.9 %collective-permute-start.24 = (bf16[512,256]{1,0:T(8,128)(2,1)S(1)}, bf16[512,256]{1,0:T(8,128)(2,1)S(1)}, u32[]{:S(2)}, u32[]{:S(2)}) collective-permute-start(bf16[512,256]{1,0:T(8,128)(2,1)S(1)} %get-tuple-element.354), channel_id=1, source_target_pairs={{0,1},{1,0},{2,3},{3,2},{4,5},{5,4},{6,7},{7,6},{8,9},{9,8},{10,11... | collective-permute-start | bytes 786440 | tf_op jit(solution)/shard_map/ppermute | solution.py:705
  390.5 20.8 %collective-permute-start.25 = (bf16[512,256]{1,0:T(8,128)(2,1)S(1)}, bf16[512,256]{1,0:T(8,128)(2,1)S(1)}, u32[]{:S(2)}, u32[]{:S(2)}) collective-permute-start(bf16[512,256]{1,0:T(8,128)(2,1)S(1)} %get-tuple-element.353), channel_id=1, source_target_pairs={{0,2},{1,3},{2,0},{3,1},{4,6},{5,7},{6,4},{7,5},{8,10},{9,11},{10,... | collective-permute-start | bytes 786440 | tf_op jit(solution)/shard_map/ppermute | solution.py:705
  391.6 19.7 %collective-permute-start.26 = (bf16[512,256]{1,0:T(8,128)(2,1)S(1)}, bf16[512,256]{1,0:T(8,128)(2,1)S(1)}, u32[]{:S(2)}, u32[]{:S(2)}) collective-permute-start(bf16[512,256]{1,0:T(8,128)(2,1)S(1)} %get-tuple-element.352), channel_id=1, source_target_pairs={{0,3},{1,2},{2,1},{3,0},{4,7},{5,6},{6,5},{7,4},{8,11},{9,10},{10,... | collective-permute-start | bytes 786440 | tf_op jit(solution)/shard_map/ppermute | solution.py:705
  411.4 106.2 %collective-permute-start.37 = (bf16[4,592,1024]{2,1,0:T(8,128)(2,1)}, bf16[4,592,1024]{2,1,0:T(8,128)(2,1)}, u32[]{:S(2)}, u32[]{:S(2)}) collective-permute-start(bf16[4,592,1024]{2,1,0:T(8,128)(2,1)} %get-tuple-element.240), channel_id=1, source_target_pairs={{0,4},{4,0},{8,12},{12,8},{1,5},{5,1},{9,13},{13,9},{2,6},{6,2},{1... | collective-permute-start | bytes 14549000 | tf_op jit(solution)/shard_map/ppermute | solution.py:705
  451.9 11.5 %collective-permute-start.34 = (bf16[256,1024]{1,0:T(8,128)(2,1)S(1)}, bf16[256,1024]{1,0:T(8,128)(2,1)S(1)}, u32[]{:S(2)}, u32[]{:S(2)}) collective-permute-start(bf16[256,1024]{1,0:T(8,128)(2,1)S(1)} %get-tuple-element.345), channel_id=1, source_target_pairs={{0,2},{1,3},{2,0},{3,1},{4,6},{5,7},{6,4},{7,5},{8,10},{9,11},{10,... | collective-permute-start | bytes 1572872 | tf_op jit(solution)/shard_map/ppermute | solution.py:705
  454.5 20.7 %collective-permute-start.31 = (bf16[256,1024]{1,0:T(8,128)(2,1)S(1)}, bf16[256,1024]{1,0:T(8,128)(2,1)S(1)}, u32[]{:S(2)}, u32[]{:S(2)}) collective-permute-start(bf16[256,1024]{1,0:T(8,128)(2,1)S(1)} %slice.271), channel_id=1, source_target_pairs={{0,1},{1,0},{2,3},{3,2},{4,5},{5,4},{6,7},{7,6},{8,9},{9,8},{10,11... | collective-permute-start | bytes 1572872 | tf_op jit(solution)/shard_map/ppermute | solution.py:705
  455.4 17.3 %collective-permute-start.32 = (bf16[256,1024]{1,0:T(8,128)(2,1)S(1)}, bf16[256,1024]{1,0:T(8,128)(2,1)S(1)}, u32[]{:S(2)}, u32[]{:S(2)}) collective-permute-start(bf16[256,1024]{1,0:T(8,128)(2,1)S(1)} %get-tuple-element.344), channel_id=1, source_target_pairs={{0,1},{1,0},{2,3},{3,2},{4,5},{5,4},{6,7},{7,6},{8,9},{9,8},{10,11... | collective-permute-start | bytes 1572872 | tf_op jit(solution)/shard_map/ppermute | solution.py:705
  457.7 17.6 %collective-permute-start.36 = (bf16[256,1024]{1,0:T(8,128)(2,1)S(1)}, bf16[256,1024]{1,0:T(8,128)(2,1)S(1)}, u32[]{:S(2)}, u32[]{:S(2)}) collective-permute-start(bf16[256,1024]{1,0:T(8,128)(2,1)S(1)} %slice.277), channel_id=1, source_target_pairs={{0,2},{1,3},{2,0},{3,1},{4,6},{5,7},{6,4},{7,5},{8,10},{9,11},{10,... | collective-permute-start | bytes 1572872 | tf_op jit(solution)/shard_map/ppermute | solution.py:705
  463.6 14.6 %collective-permute-start.35 = (bf16[256,1024]{1,0:T(8,128)(2,1)S(1)}, bf16[256,1024]{1,0:T(8,128)(2,1)S(1)}, u32[]{:S(2)}, u32[]{:S(2)}) collective-permute-start(bf16[256,1024]{1,0:T(8,128)(2,1)S(1)} %add_convert_fusion.9), channel_id=1, source_target_pairs={{0,1},{1,0},{2,3},{3,2},{4,5},{5,4},{6,7},{7,6},{8,9},{9,8},{10,11... | collective-permute-start | bytes 1572872 | tf_op jit(solution)/shard_map/ppermute | solution.py:705
  526.2 120.3 %reduce-scatter.6.cloned.1.call-start = ((), (), s32[]{:S(2)}) async-start(), calls=%async_computation.4 | async-start | bytes 6225920 | tf_op jit(solution)/shard_map/reduce_scatter | solution.py:785
  560.7 217.1 %reduce-scatter.8.cloned.1.call-start = ((), (), s32[]{:S(2)}) async-start(), calls=%async_computation.5 | async-start | bytes 2949120 | tf_op jit(solution)/shard_map/reduce_scatter | solution.py:785
  582.7 13.6 %collective-permute-start.41 = (bf16[512,256]{1,0:T(8,128)(2,1)S(1)}, bf16[512,256]{1,0:T(8,128)(2,1)}, u32[]{:S(2)}, u32[]{:S(2)}) collective-permute-start(bf16[512,256]{1,0:T(8,128)(2,1)S(1)} %get-tuple-element.341), channel_id=1, source_target_pairs={{0,2},{1,3},{2,0},{3,1},{4,6},{5,7},{6,4},{7,5},{8,10},{9,11},{10,... | collective-permute-start | bytes 786440 | tf_op jit(solution)/shard_map/ppermute | solution.py:705
  584.1 13.8 %collective-permute-start.42 = (bf16[512,256]{1,0:T(8,128)(2,1)S(1)}, bf16[512,256]{1,0:T(8,128)(2,1)}, u32[]{:S(2)}, u32[]{:S(2)}) collective-permute-start(bf16[512,256]{1,0:T(8,128)(2,1)S(1)} %get-tuple-element.340), channel_id=1, source_target_pairs={{0,3},{1,2},{2,1},{3,0},{4,7},{5,6},{6,5},{7,4},{8,11},{9,10},{10,... | collective-permute-start | bytes 786440 | tf_op jit(solution)/shard_map/ppermute | solution.py:705
  586.5 80.5 %collective-permute-start.63 = (bf16[4,288,1024]{2,1,0:T(8,128)(2,1)}, bf16[4,288,1024]{2,1,0:T(8,128)(2,1)}, u32[]{:S(2)}, u32[]{:S(2)}) collective-permute-start(bf16[4,288,1024]{2,1,0:T(8,128)(2,1)} %get-tuple-element.277), channel_id=1, source_target_pairs={{0,4},{4,0},{8,12},{12,8},{1,5},{5,1},{9,13},{13,9},{2,6},{6,2},{1... | collective-permute-start | bytes 7077896 | tf_op jit(solution)/shard_map/ppermute | solution.py:705
  597.9 142.0 %collective-permute-start.54 = (bf16[592,1024]{1,0:T(8,128)(2,1)}, bf16[592,1024]{1,0:T(8,128)(2,1)}, u32[]{:S(2)}, u32[]{:S(2)}) collective-permute-start(bf16[592,1024]{1,0:T(8,128)(2,1)} %reduce-scatter.4.cloned.1.call-done), channel_id=1, source_target_pairs={{0,8},{4,12},{8,0},{12,4},{1,9},{5,13},{9,1},{13,5},{2,10},{6,14},... | collective-permute-start | bytes 3637256 | tf_op jit(solution)/shard_map/ppermute | solution.py:705
  648.5 40.7 %collective-permute-start.73 = (bf16[608,512]{1,0:T(8,128)(2,1)}, bf16[608,512]{1,0:T(8,128)(2,1)}, u32[]{:S(2)}, u32[]{:S(2)}) collective-permute-start(bf16[608,512]{1,0:T(8,128)(2,1)} %constant_dynamic-slice_fusion.2), channel_id=1, source_target_pairs={{0,4},{4,0},{8,12},{12,8},{1,5},{5,1},{9,13},{13,9},{2,6},{6,2},{1... | collective-permute-start | bytes 1867784 | tf_op jit(solution)/shard_map/ppermute | solution.py:705
  672.5 18.7 %collective-permute-start.51 = (bf16[256,1024]{1,0:T(8,128)(2,1)S(1)}, bf16[256,1024]{1,0:T(8,128)(2,1)S(1)}, u32[]{:S(2)}, u32[]{:S(2)}) collective-permute-start(bf16[256,1024]{1,0:T(8,128)(2,1)S(1)} %get-tuple-element.333), channel_id=1, source_target_pairs={{0,2},{1,3},{2,0},{3,1},{4,6},{5,7},{6,4},{7,5},{8,10},{9,11},{10,... | collective-permute-start | bytes 1572872 | tf_op jit(solution)/shard_map/ppermute | solution.py:705
  675.0 43.7 %collective-permute-start.48 = (bf16[256,1024]{1,0:T(8,128)(2,1)}, bf16[256,1024]{1,0:T(8,128)(2,1)}, u32[]{:S(2)}, u32[]{:S(2)}) collective-permute-start(bf16[256,1024]{1,0:T(8,128)(2,1)} %slice.285), channel_id=1, source_target_pairs={{0,1},{1,0},{2,3},{3,2},{4,5},{5,4},{6,7},{7,6},{8,9},{9,8},{10,11... | collective-permute-start | bytes 1572872 | tf_op jit(solution)/shard_map/ppermute | solution.py:705
  676.2 33.7 %collective-permute-start.49 = (bf16[256,1024]{1,0:T(8,128)(2,1)S(1)}, bf16[256,1024]{1,0:T(8,128)(2,1)S(1)}, u32[]{:S(2)}, u32[]{:S(2)}) collective-permute-start(bf16[256,1024]{1,0:T(8,128)(2,1)S(1)} %get-tuple-element.332), channel_id=1, source_target_pairs={{0,1},{1,0},{2,3},{3,2},{4,5},{5,4},{6,7},{7,6},{8,9},{9,8},{10,11... | collective-permute-start | bytes 1572872 | tf_op jit(solution)/shard_map/ppermute | solution.py:705
  689.2 22.0 %collective-permute-start.64 = (bf16[512,768]{1,0:T(8,128)(2,1)S(1)}, bf16[512,768]{1,0:T(8,128)(2,1)S(1)}, u32[]{:S(2)}, u32[]{:S(2)}) collective-permute-start(bf16[512,768]{1,0:T(8,128)(2,1)S(1)} %constant_dynamic-slice_fusion.6), channel_id=1, source_target_pairs={{0,16},{16,0},{1,17},{17,1},{2,18},{18,2},{3,19},{19,3},{4,20},{20... | collective-permute-start | bytes 2359304 | tf_op jit(solution)/shard_map/ppermute | solution.py:701
  691.2 21.1 %collective-permute-start.74 = (bf16[608,256]{1,0:T(8,128)(2,1)S(1)}, bf16[608,256]{1,0:T(8,128)(2,1)S(1)}, u32[]{:S(2)}, u32[]{:S(2)}) collective-permute-start(bf16[608,256]{1,0:T(8,128)(2,1)S(1)} %constant_dynamic-slice_fusion.1), channel_id=1, source_target_pairs={{0,8},{4,12},{8,0},{12,4},{1,9},{5,13},{9,1},{13,5},{2,10},{6,14},... | collective-permute-start | bytes 933896 | tf_op jit(solution)/shard_map/ppermute | solution.py:705
  710.0 20.9 %collective-permute-start.53 = (bf16[256,1024]{1,0:T(8,128)(2,1)}, bf16[256,1024]{1,0:T(8,128)(2,1)}, u32[]{:S(2)}, u32[]{:S(2)}) collective-permute-start(bf16[256,1024]{1,0:T(8,128)(2,1)} %slice.291), channel_id=1, source_target_pairs={{0,2},{1,3},{2,0},{3,1},{4,6},{5,7},{6,4},{7,5},{8,10},{9,11},{10,... | collective-permute-start | bytes 1572872 | tf_op jit(solution)/shard_map/ppermute | solution.py:705
  711.1 19.7 %collective-permute-start.52 = (bf16[256,1024]{1,0:T(8,128)(2,1)}, bf16[256,1024]{1,0:T(8,128)(2,1)}, u32[]{:S(2)}, u32[]{:S(2)}) collective-permute-start(bf16[256,1024]{1,0:T(8,128)(2,1)} %add_convert_fusion.7), channel_id=1, source_target_pairs={{0,1},{1,0},{2,3},{3,2},{4,5},{5,4},{6,7},{7,6},{8,9},{9,8},{10,11... | collective-permute-start | bytes 1572872 | tf_op jit(solution)/shard_map/ppermute | solution.py:705
  713.1 24.1 %collective-permute-start.50 = (bf16[256,1024]{1,0:T(8,128)(2,1)}, bf16[256,1024]{1,0:T(8,128)(2,1)}, u32[]{:S(2)}, u32[]{:S(2)}) collective-permute-start(bf16[256,1024]{1,0:T(8,128)(2,1)} %add_convert_fusion.8), channel_id=1, source_target_pairs={{0,2},{1,3},{2,0},{3,1},{4,6},{5,7},{6,4},{7,5},{8,10},{9,11},{10,... | collective-permute-start | bytes 1572872 | tf_op jit(solution)/shard_map/ppermute | solution.py:705
  718.7 25.1 %collective-permute-start.55 = (bf16[384,512]{1,0:T(8,128)(2,1)}, bf16[384,512]{1,0:T(8,128)(2,1)S(1)}, u32[]{:S(2)}, u32[]{:S(2)}) collective-permute-start(bf16[384,512]{1,0:T(8,128)(2,1)} %get-tuple-element.356), channel_id=1, source_target_pairs={{0,4},{4,0},{8,12},{12,8},{1,5},{5,1},{9,13},{13,9},{2,6},{6,2},{1... | collective-permute-start | bytes 1179656 | tf_op jit(solution)/shard_map/ppermute | solution.py:705
  730.9 41.8 %collective-permute-start.65 = (bf16[384,512]{1,0:T(8,128)(2,1)S(1)}, bf16[384,512]{1,0:T(8,128)(2,1)S(1)}, u32[]{:S(2)}, u32[]{:S(2)}) collective-permute-start(bf16[384,512]{1,0:T(8,128)(2,1)S(1)} %constant_dynamic-slice_fusion.5), channel_id=1, source_target_pairs={{0,4},{4,0},{8,12},{12,8},{1,5},{5,1},{9,13},{13,9},{2,6},{6,2},{1... | collective-permute-start | bytes 1179656 | tf_op jit(solution)/shard_map/ppermute | solution.py:705
  730.9 42.5 %collective-permute-start.75 = (bf16[608,256]{1,0:T(8,128)(2,1)S(1)}, bf16[608,256]{1,0:T(8,128)(2,1)S(1)}, u32[]{:S(2)}, u32[]{:S(2)}) collective-permute-start(bf16[608,256]{1,0:T(8,128)(2,1)S(1)} %add_convert_fusion.13.first_ref), channel_id=1, source_target_pairs={{0,8},{4,12},{8,0},{12,4},{1,9},{5,13},{9,1},{13,5},{2,10},{6,14},... | collective-permute-start | bytes 933896 | tf_op jit(solution)/shard_map/ppermute | solution.py:705
  743.8 101.4 %collective-permute-start.79 = (bf16[592,1024]{1,0:T(8,128)(2,1)}, bf16[592,1024]{1,0:T(8,128)(2,1)}, u32[]{:S(2)}, u32[]{:S(2)}) collective-permute-start(bf16[592,1024]{1,0:T(8,128)(2,1)} %add_convert_fusion.2.first_ref), channel_id=1, source_target_pairs={{0,4},{4,0},{8,12},{12,8},{1,5},{5,1},{9,13},{13,9},{2,6},{6,2},{1... | collective-permute-start | bytes 3637256 | tf_op jit(solution)/shard_map/ppermute | solution.py:705
  747.0 30.8 %collective-permute-start.69 = (bf16[384,256]{1,0:T(8,128)(2,1)S(1)}, bf16[384,256]{1,0:T(8,128)(2,1)S(1)}, u32[]{:S(2)}, u32[]{:S(2)}) collective-permute-start(bf16[384,256]{1,0:T(8,128)(2,1)S(1)} %constant_dynamic-slice_fusion.3), channel_id=1, source_target_pairs={{0,8},{4,12},{8,0},{12,4},{1,9},{5,13},{9,1},{13,5},{2,10},{6,14},... | collective-permute-start | bytes 589832 | tf_op jit(solution)/shard_map/ppermute | solution.py:705
  753.5 19.1 %collective-permute-start.61 = (f32[4128]{0:T(1024)S(1)}, f32[4128]{0:T(1024)S(1)}, u32[]{:S(2)}, u32[]{:S(2)}) collective-permute-start(f32[4128]{0:T(1024)S(1)} %add.282), channel_id=1, source_target_pairs={{0,4},{4,0},{8,12},{12,8},{1,5},{5,1},{9,13},{13,9},{2,6},{6,2},{1... | collective-permute-start | bytes 49544 | tf_op jit(solution)/shard_map/ppermute | solution.py:705
  772.6 100.8 %collective-permute-start.56 = (bf16[512,1024]{1,0:T(8,128)(2,1)}, bf16[512,1024]{1,0:T(8,128)(2,1)}, u32[]{:S(2)}, u32[]{:S(2)}) collective-permute-start(bf16[512,1024]{1,0:T(8,128)(2,1)} %get-tuple-element.297), channel_id=1, source_target_pairs={{0,16},{16,0},{1,17},{17,1},{2,18},{18,2},{3,19},{19,3},{4,20},{20... | collective-permute-start | bytes 3145736 | tf_op jit(solution)/shard_map/ppermute | solution.py:701
  772.6 89.8 %collective-permute-start.62 = (f32[4128]{0:T(1024)S(1)}, f32[4128]{0:T(1024)S(1)}, u32[]{:S(2)}, u32[]{:S(2)}) collective-permute-start(f32[4128]{0:T(1024)S(1)} %add.283), channel_id=1, source_target_pairs={{0,8},{4,12},{8,0},{12,4},{1,9},{5,13},{9,1},{13,5},{2,10},{6,14},... | collective-permute-start | bytes 49544 | tf_op jit(solution)/shard_map/ppermute | solution.py:705
  773.4 25.6 %collective-permute-start.66 = (bf16[384,256]{1,0:T(8,128)(2,1)S(1)}, bf16[384,256]{1,0:T(8,128)(2,1)S(1)}, u32[]{:S(2)}, u32[]{:S(2)}) collective-permute-start(bf16[384,256]{1,0:T(8,128)(2,1)S(1)} %constant_dynamic-slice_fusion.4), channel_id=1, source_target_pairs={{0,8},{4,12},{8,0},{12,4},{1,9},{5,13},{9,1},{13,5},{2,10},{6,14},... | collective-permute-start | bytes 589832 | tf_op jit(solution)/shard_map/ppermute | solution.py:705
  777.8 44.2 %collective-permute-start.77 = (bf16[288,1024]{1,0:T(8,128)(2,1)}, bf16[288,1024]{1,0:T(8,128)(2,1)S(1)}, u32[]{:S(2)}, u32[]{:S(2)}) collective-permute-start(bf16[288,1024]{1,0:T(8,128)(2,1)} %reduce-scatter.8.cloned.1.call-done), channel_id=1, source_target_pairs={{0,8},{4,12},{8,0},{12,4},{1,9},{5,13},{9,1},{13,5},{2,10},{6,14},... | collective-permute-start | bytes 1769480 | tf_op jit(solution)/shard_map/ppermute | solution.py:705
  798.9 20.6 %collective-permute-start.70 = (bf16[384,256]{1,0:T(8,128)(2,1)S(1)}, bf16[384,256]{1,0:T(8,128)(2,1)S(1)}, u32[]{:S(2)}, u32[]{:S(2)}) collective-permute-start(bf16[384,256]{1,0:T(8,128)(2,1)S(1)} %add_convert_fusion.14.first_ref), channel_id=1, source_target_pairs={{0,8},{4,12},{8,0},{12,4},{1,9},{5,13},{9,1},{13,5},{2,10},{6,14},... | collective-permute-start | bytes 589832 | tf_op jit(solution)/shard_map/ppermute | solution.py:705
  819.5 22.5 %collective-permute-start.76 = (bf16[608,512]{1,0:T(8,128)(2,1)}, bf16[608,512]{1,0:T(8,128)(2,1)S(1)}, u32[]{:S(2)}, u32[]{:S(2)}) collective-permute-start(bf16[608,512]{1,0:T(8,128)(2,1)} %place_two.12.first_ref), channel_id=1, source_target_pairs={{0,4},{4,0},{8,12},{12,8},{1,5},{5,1},{9,13},{13,9},{2,6},{6,2},{1... | collective-permute-start | bytes 1867784 | tf_op jit(solution)/shard_map/ppermute | solution.py:705
  822.0 15.3 %collective-permute-start.67 = (bf16[384,256]{1,0:T(8,128)(2,1)S(1)}, bf16[384,256]{1,0:T(8,128)(2,1)S(1)}, u32[]{:S(2)}, u32[]{:S(2)}) collective-permute-start(bf16[384,256]{1,0:T(8,128)(2,1)S(1)} %add_convert_fusion.15.first_ref), channel_id=1, source_target_pairs={{0,8},{4,12},{8,0},{12,4},{1,9},{5,13},{9,1},{13,5},{2,10},{6,14},... | collective-permute-start | bytes 589832 | tf_op jit(solution)/shard_map/ppermute | solution.py:705
  837.3 17.3 %collective-permute-start.78 = (bf16[288,1024]{1,0:T(8,128)(2,1)S(1)}, bf16[288,1024]{1,0:T(8,128)(2,1)}, u32[]{:S(2)}, u32[]{:S(2)}) collective-permute-start(bf16[288,1024]{1,0:T(8,128)(2,1)S(1)} %add_convert_fusion.6.first_ref), channel_id=1, source_target_pairs={{0,4},{4,0},{8,12},{12,8},{1,5},{5,1},{9,13},{13,9},{2,6},{6,2},{1... | collective-permute-start | bytes 1769480 | tf_op jit(solution)/shard_map/ppermute | solution.py:705
  842.1 21.1 %collective-permute-start.71 = (bf16[384,512]{1,0:T(8,128)(2,1)S(1)}, bf16[384,512]{1,0:T(8,128)(2,1)}, u32[]{:S(2)}, u32[]{:S(2)}) collective-permute-start(bf16[384,512]{1,0:T(8,128)(2,1)S(1)} %copy-done.95), channel_id=1, source_target_pairs={{0,4},{4,0},{8,12},{12,8},{1,5},{5,1},{9,13},{13,9},{2,6},{6,2},{1... | collective-permute-start | bytes 1179656 | tf_op jit(solution)/shard_map/ppermute | solution.py:705
  845.3 24.3 %collective-permute-start.68 = (bf16[384,512]{1,0:T(8,128)(2,1)}, bf16[384,512]{1,0:T(8,128)(2,1)S(1)}, u32[]{:S(2)}, u32[]{:S(2)}) collective-permute-start(bf16[384,512]{1,0:T(8,128)(2,1)} %place_two.8.first_ref), channel_id=1, source_target_pairs={{0,4},{4,0},{8,12},{12,8},{1,5},{5,1},{9,13},{13,9},{2,6},{6,2},{1... | collective-permute-start | bytes 1179656 | tf_op jit(solution)/shard_map/ppermute | solution.py:705
  860.9 24.8 %collective-permute-start.80 = (bf16[1184,1024]{1,0:T(8,128)(2,1)}, bf16[1184,1024]{1,0:T(8,128)(2,1)}, u32[]{:S(2)}, u32[]{:S(2)}) collective-permute-start(bf16[1184,1024]{1,0:T(8,128)(2,1)} %broadcast_select_fusion.2), channel_id=1, source_target_pairs={{0,16},{16,0},{1,17},{17,1},{2,18},{18,2},{3,19},{19,3},{4,20},{20... | collective-permute-start | bytes 7274504 | tf_op jit(solution)/shard_map/ppermute | solution.py:701
  (152 other events, 1014.6 us)
Sparse Core Ops, SparseCore 0:
  21.8 122.9 all-gather.4
  147.2 134.4 all-gather.6
  526.3 57.2 reduce-scatter.3
  586.6 59.8 reduce-scatter.5
  671.4 55.6 reduce-scatter.7
